TPU v7x, 32 devices: a whole 2x2x4 slice. The times are simulated.
32 devices in a mesh: dom: 8 (over z, x), orb: 4 (over y, core).
Axes of the slice: x: 2, y: 2, z: 4, core: 2. Of those that a mesh axis runs over, the one named last changes fastest.
Arguments:
- orbitals: float32 [16, 96, 64, 128], P('orb', 'dom'), may hold values from -400 to 400
- potential: float32 [96, 64, 128], P('dom'), may hold values from -8 to 8
Outputs:
- filtered_basis: float32 [16, 96, 64, 128], P('orb', 'dom')
All inputs are finite; a program needn't handle non-finite values.
Results may differ from a plain program's by a relative error of at most 0.0003.
Values sent between devices are 32-bit elements; how exact they have to be, the bound alone decides.
No kernel may reach another device: no remote copies, remote signals or barrier semaphores. Data moves between devices by JAX's collectives and lax.ppermute only.
A program may use at most 64 MiB of HBM per device.

v0:
```python
import jax
import jax.numpy as jnp
from jax import lax
from jax.sharding import PartitionSpec as P

coefficients = (-49.0 / 18.0, 1.5, -0.15, 1.0 / 90.0)
spacing = 0.5
filter_centre = 23.0
filter_half = 23.0


def extended(block, sides, width):
    for axis, dim in sides:
        count = lax.axis_size(axis)
        forward = [(i, i + 1) for i in range(count - 1)]
        forward.append((count - 1, 0))
        backward = [(target, source) for source, target in forward]
        low = lax.ppermute(
            lax.slice_in_dim(block, block.shape[dim] - width, None, axis=dim), axis, forward
        )
        high = lax.ppermute(lax.slice_in_dim(block, 0, width, axis=dim), axis, backward)
        block = jnp.concatenate([low, block, high], axis=dim)
    return block


def hamiltonian(padded, row_count, near_potential, plane_margin):
    col_count = padded.shape[2] - 2 * plane_margin

    def portion(shift_rows, shift_cols):
        return padded[
            :,
            3 + shift_rows : 3 + shift_rows + row_count,
            plane_margin + shift_cols : plane_margin + shift_cols + col_count,
        ]

    centre_part = portion(0, 0)
    laplace = 3.0 * coefficients[0] * centre_part
    for offset in range(1, 4):
        laplace = laplace + coefficients[offset] * (portion(offset, 0) + portion(-offset, 0))
        laplace = laplace + coefficients[offset] * (
            jnp.roll(centre_part, offset, 2) + jnp.roll(centre_part, -offset, 2)
        )
        laplace = laplace + coefficients[offset] * (
            jnp.roll(centre_part, offset, 3) + jnp.roll(centre_part, -offset, 3)
        )
    return (-0.5 / (spacing * spacing) * laplace + near_potential * centre_part, centre_part)


def chain_steps(block, potential, extend, plane_margin):
    row_count = block.shape[1]

    def applied(vector):
        result, centre_part = hamiltonian(extend(vector), row_count, potential, plane_margin)
        return result

    first = (applied(block) - filter_centre * block) / filter_half
    second = 2.0 * (applied(first) - filter_centre * first) / filter_half - block
    third = 2.0 * (applied(second) - filter_centre * second) / filter_half - first
    return third


def orthonormal(flat, cell_total):
    local_gram = jnp.dot(
        flat, flat.T, precision=lax.Precision.HIGHEST, preferred_element_type=jnp.float32
    )
    gram = lax.psum(local_gram, ("dom", "orb")) / cell_total
    lower = jnp.linalg.cholesky(gram)
    return lax.linalg.triangular_solve(lower, flat, left_side=True, lower=True)


def regroup(block):
    return lax.all_to_all(block, "orb", split_axis=2, concat_axis=0, tiled=True)


def on_device(orbitals, potential):

    def extend_slab(vector):
        return extended(vector, (("dom", 1),), 3)

    filtered = chain_steps(orbitals, potential, extend_slab, 0)
    grouped = regroup(filtered)
    cell_total = (
        grouped.shape[1]
        * grouped.shape[2]
        * grouped.shape[3]
        * lax.axis_size("dom")
        * lax.axis_size("orb")
    )
    flat = grouped.reshape(grouped.shape[0], -1)
    basis = orthonormal(orthonormal(flat, cell_total), cell_total).reshape(grouped.shape)
    return lax.all_to_all(basis, "orb", split_axis=0, concat_axis=2, tiled=True)


def solution(mesh):
    return jax.shard_map(
        on_device,
        mesh=mesh,
        in_specs=(P("orb", "dom", None, None), P("dom", None, None)),
        out_specs=P("orb", "dom", None, None),
        check_vma=False,
    )
```

profile of v0, /device:TPU:0, one launch (start us, length us, event | category | flops | bytes accessed | tf_op | source)
XLA Modules:
  0.0 288.6 jit_solution(260849028277319936)
XLA Ops:
  1.3 3.0 %collective-permute-start.1 = (f32[4,3,64,128]{3,2,1,0:T(8,128)S(1)}, f32[4,3,64,128]{3,2,1,0:T(8,128)S(1)}, u32[]{:S(2)}, u32[]{:S(2)}) collective-permute-start(f32[4,3,64,128]{3,2,1,0:T(8,128)S(1)} %get-tuple-element.78), channel_id=1, source_target_pairs={{0,4},{4,8},{8,12},{12,16},{16,20},{20,24},{24,28},{28,0},{1,5},{5... | collective-permute-start | bytes 1179656 | tf_op jit(solution)/shard_map/ppermute | solution.py:18
  4.3 3.1 %collective-permute-start = (f32[4,3,64,128]{3,2,1,0:T(8,128)S(1)}, f32[4,3,64,128]{3,2,1,0:T(8,128)S(1)}, u32[]{:S(2)}, u32[]{:S(2)}) collective-permute-start(f32[4,3,64,128]{3,2,1,0:T(8,128)S(1)} %get-tuple-element.77), channel_id=1, source_target_pairs={{4,0},{8,4},{12,8},{16,12},{20,16},{24,20},{28,24},{0,28},{5,1},{9... | collective-permute-start | bytes 1179656 | tf_op jit(solution)/shard_map/ppermute | solution.py:21
  14.1 2.3 fusion.123
  16.4 2.3 fusion.124
  20.7 2.3 fusion.128
  26.6 10.7 %broadcast_multiply_fusion = (f32[4,12,64,128]{3,2,1,0:T(8,128)S(1)}, f32[4,12,64,128]{3,2,1,0:T(8,128)S(1)}) fusion(f32[4,12,64,128]{3,2,1,0:T(8,128)S(1)} %copy-done, f32[12,64,128]{2,1,0:T(8,128)S(1)} %copy-done.1, f32[4,12,64,3]{3,2,1,0:T(8,128)} %get-tuple-element.86, f32[4,12,64,125]{3,2,1,0:T(8,128)} %get-tuple-element.88, ...), kind=kLoop, calls=%fused_computation.124 | loop fusion | flops 18087936 | bytes 33423360 | tf_op jit(solution)/shard_map/div | solution.py:56
  37.3 2.2 fusion.104
  39.6 2.3 fusion.105
  43.8 2.3 fusion.108
  50.3 2.2 fusion.112
  52.6 2.3 fusion.113
  60.9 14.4 %collective-permute-done.2 = f32[4,3,64,128]{3,2,1,0:T(8,128)S(1)} collective-permute-done((f32[4,3,64,128]{3,2,1,0:T(8,128)S(1)}, f32[4,3,64,128]{3,2,1,0:T(8,128)S(1)}, u32[]{:S(2)}, u32[]{:S(2)}) %collective-permute-start.2) | collective-permute-done | bytes 393248 | tf_op jit(solution)/shard_map/ppermute | solution.py:21
  76.2 12.4 %fusion.35 = f32[4,12,64,128]{3,2,1,0:T(8,128)S(1)} fusion(f32[4,12,64,128]{3,2,1,0:T(8,128)S(1)} %copy-done, f32[4,12,64,128]{3,2,1,0:T(8,128)S(1)} %get-tuple-element.8, f32[4,12,64,128]{3,2,1,0:T(8,128)S(1)} %get-tuple-element.6, f32[4,3,64,128]{3,2,1,0:T(8,128)} %copy-done.4, f32[4,3,64,128]{3,2,1,0:T(8,128)} %copy-done.2, ...), kind=kLoop, calls=%fused_computation.51 | loop fusion | flops 20447232 | bytes 26345472 | tf_op jit(solution)/shard_map/sub | solution.py:57
  90.3 2.3 fusion.92
  94.6 2.3 fusion.95
  101.1 2.2 fusion.99
  103.3 2.3 fusion.100
  107.1 2.7 collective-permute-start.4
  112.4 12.9 %collective-permute-done.4 = f32[4,3,64,128]{3,2,1,0:T(8,128)S(1)} collective-permute-done((f32[4,3,64,128]{3,2,1,0:T(8,128)S(1)}, f32[4,3,64,128]{3,2,1,0:T(8,128)S(1)}, u32[]{:S(2)}, u32[]{:S(2)}) %collective-permute-start.4) | collective-permute-done | bytes 393248 | tf_op jit(solution)/shard_map/ppermute | solution.py:21
  126.2 11.8 %fusion.13 = f32[4,12,64,128]{3,2,1,0:T(8,128)S(1)} fusion(f32[4,12,64,128]{3,2,1,0:T(8,128)S(1)} %fusion.35, f32[4,3,64,128]{3,2,1,0:T(8,128)} %copy-done.5, f32[4,3,64,128]{3,2,1,0:T(8,128)} %copy-done.3, f32[4,12,63,128]{3,2,1,0:T(8,128)} %get-tuple-element.30, f32[4,12,1,128]{3,2,1,0:T(1,128)} %get-tuple-element.32, ...), kind=kLoop, calls=%fused_computation.29 | loop fusion | flops 21233664 | bytes 24772608 | tf_op jit(solution)/shard_map/sub | solution.py:58
  139.0 28.1 %all_to_all.33 = f32[4,12,64,128]{3,1,0,2:T(8,128)S(1)} all-to-all(f32[4,12,64,128]{3,1,0,2:T(8,128)S(1)} %copy.54), channel_id=1, replica_groups=mesh['dom'=8,'orb'=4] {'orb'}, dimensions={2} | all-to-all | bytes 3145728 | tf_op jit(solution)/shard_map/all_to_all | solution.py:72
  170.4 38.7 %psum.14 = f32[16,16]{0,1:T(8,128)S(1)} all-reduce(f32[16,16]{0,1:T(8,128)S(1)} %fusion.130), channel_id=1, replica_groups=mesh['dom'=8,'orb'=4] {'dom','orb'}, use_global_device_ids=true, to_apply=%region_0.1 | all-reduce | flops 256 | bytes 2048 | tf_op jit(solution)/shard_map/psum | solution.py:66
  216.7 41.2 %psum.15 = f32[16,16]{0,1:T(8,128)S(1)} all-reduce(f32[16,16]{0,1:T(8,128)S(1)} %fusion.131), channel_id=1, replica_groups=mesh['dom'=8,'orb'=4] {'dom','orb'}, use_global_device_ids=true, to_apply=%region_3.6 | all-reduce | flops 256 | bytes 2048 | tf_op jit(solution)/shard_map/psum | solution.py:66
  263.8 23.4 %all_to_all.34 = f32[16,12,16,128]{3,2,1,0:T(8,128)S(1)} all-to-all(f32[16,12,16,128]{3,2,1,0:T(8,128)S(1)} %bitcast.40), channel_id=1, replica_groups=mesh['dom'=8,'orb'=4] {'orb'}, dimensions={0} | all-to-all | bytes 3145728 | tf_op jit(solution)/shard_map/all_to_all | solution.py:91
  (75 shorter events, 58.7 us)
Async XLA Ops:
  0.0 7.4 %copy-start = (f32[4,12,64,128]{3,2,1,0:T(8,128)S(1)}, f32[4,12,64,128]{3,2,1,0:T(8,128)}, u32[]{:S(2)}) copy-start(f32[4,12,64,128]{3,2,1,0:T(8,128)} %param.5) | copy-start | bytes 4718596
  1.3 24.8 %collective-permute-start.1 = (f32[4,3,64,128]{3,2,1,0:T(8,128)S(1)}, f32[4,3,64,128]{3,2,1,0:T(8,128)S(1)}, u32[]{:S(2)}, u32[]{:S(2)}) collective-permute-start(f32[4,3,64,128]{3,2,1,0:T(8,128)S(1)} %get-tuple-element.78), channel_id=1, source_target_pairs={{0,4},{4,8},{8,12},{12,16},{16,20},{20,24},{24,28},{28,0},{1,5},{5... | collective-permute-start | bytes 1179656 | tf_op jit(solution)/shard_map/ppermute | solution.py:18
  4.3 22.2 %collective-permute-start = (f32[4,3,64,128]{3,2,1,0:T(8,128)S(1)}, f32[4,3,64,128]{3,2,1,0:T(8,128)S(1)}, u32[]{:S(2)}, u32[]{:S(2)}) collective-permute-start(f32[4,3,64,128]{3,2,1,0:T(8,128)S(1)} %get-tuple-element.77), channel_id=1, source_target_pairs={{4,0},{8,4},{12,8},{16,12},{20,16},{24,20},{28,24},{0,28},{5,1},{9... | collective-permute-start | bytes 1179656 | tf_op jit(solution)/shard_map/ppermute | solution.py:21
  22.9 2.3 copy-start.1
  56.3 19.0 %collective-permute-start.2 = (f32[4,3,64,128]{3,2,1,0:T(8,128)S(1)}, f32[4,3,64,128]{3,2,1,0:T(8,128)S(1)}, u32[]{:S(2)}, u32[]{:S(2)}) collective-permute-start(f32[4,3,64,128]{3,2,1,0:T(8,128)S(1)} %get-tuple-element.59), channel_id=1, source_target_pairs={{4,0},{8,4},{12,8},{16,12},{20,16},{24,20},{28,24},{0,28},{5,1},{9... | collective-permute-start | bytes 1179656 | tf_op jit(solution)/shard_map/ppermute | solution.py:21
  58.3 17.0 %collective-permute-start.3 = (f32[4,3,64,128]{3,2,1,0:T(8,128)S(1)}, f32[4,3,64,128]{3,2,1,0:T(8,128)S(1)}, u32[]{:S(2)}, u32[]{:S(2)}) collective-permute-start(f32[4,3,64,128]{3,2,1,0:T(8,128)S(1)} %get-tuple-element.60), channel_id=1, source_target_pairs={{0,4},{4,8},{8,12},{12,16},{16,20},{20,24},{24,28},{28,0},{1,5},{5... | collective-permute-start | bytes 1179656 | tf_op jit(solution)/shard_map/ppermute | solution.py:18
  75.3 0.7 copy-start.2
  75.3 0.9 copy-start.4
  107.1 18.1 %collective-permute-start.4 = (f32[4,3,64,128]{3,2,1,0:T(8,128)S(1)}, f32[4,3,64,128]{3,2,1,0:T(8,128)S(1)}, u32[]{:S(2)}, u32[]{:S(2)}) collective-permute-start(f32[4,3,64,128]{3,2,1,0:T(8,128)S(1)} %get-tuple-element.33), channel_id=1, source_target_pairs={{4,0},{8,4},{12,8},{16,12},{20,16},{24,20},{28,24},{0,28},{5,1},{9... | collective-permute-start | bytes 1179656 | tf_op jit(solution)/shard_map/ppermute | solution.py:21
  109.8 15.4 %collective-permute-start.5 = (f32[4,3,64,128]{3,2,1,0:T(8,128)S(1)}, f32[4,3,64,128]{3,2,1,0:T(8,128)S(1)}, u32[]{:S(2)}, u32[]{:S(2)}) collective-permute-start(f32[4,3,64,128]{3,2,1,0:T(8,128)S(1)} %get-tuple-element.34), channel_id=1, source_target_pairs={{0,4},{4,8},{8,12},{12,16},{16,20},{20,24},{24,28},{28,0},{1,5},{5... | collective-permute-start | bytes 1179656 | tf_op jit(solution)/shard_map/ppermute | solution.py:18
  125.2 0.7 copy-start.3
  125.2 0.9 copy-start.5
where the time goes:
time: 289 us
  blocking collectives  131 us (45%)
  local copies, waits for them, and re-layouts  68 us (24%)
  other arithmetic  43.8 us (15%)
  waiting for transfers between devices  27.3 us (9%)
  starting transfers between devices  10.9 us (4%)
  matrix products  7.13 us (2%)
    psum x2, blocking collectives, orthonormal(): gram = lax.psum(local_gram, ('dom', 'orb')) / cell_total  79.9 us
    all_to_all x1, blocking collectives, regroup(): return lax.all_to_all(block, 'orb', split_axis=2, concat_axis=0, tiled=True)  28.1 us
    ppermute x3, waiting for transfers between devices, extended(): lax.ppermute(lax.slice_in_dim(block, 0, width, axis=dim), axis, backward)  27.3 us
    slice x12, local copies, waits for them, and re-layouts, hamiltonian(): jnp.roll(centre_part, -offset, 3)  26.6 us
    all_to_all x1, blocking collectives, on_device(): return lax.all_to_all(basis, 'orb', split_axis=0, concat_axis=2, tiled=True)  23.4 us
    slice x12, local copies, waits for them, and re-layouts, hamiltonian(): jnp.roll(centre_part, -offset, 2)  15.9 us
    slice x6, local copies, waits for them, and re-layouts, hamiltonian(): jnp.roll(centre_part, offset, 3) + jnp.roll(centre_part, -offset, 3)  13.5 us
    sub x1, other arithmetic, chain_steps(): 2.0 * (applied(first) - filter_centre * first) / filter_half - block  12.4 us
  transfers between devices with their start and end apart: 6, of which 2 were waited for; matrix products, arithmetic and copies ran while one was open for 8% of the time, Pallas kernels for 0%

commit v1 on v0

v1 whole, which is shorter than its diff:
```python
import functools

import jax
import jax.numpy as jnp
from jax import lax
from jax.experimental import pallas as pl
from jax.experimental.pallas import tpu as pltpu
from jax.sharding import Mesh
from jax.sharding import PartitionSpec as P

coefficients = (-49.0 / 18.0, 1.5, -0.15, 1.0 / 90.0)
spacing = 0.5
filter_centre = 23.0
filter_half = 23.0

REACH = 3
STEPS = 3
DEEP = REACH * STEPS
WIDE = REACH * (STEPS - 1)
EIGHT = 8
GROUP = 6
ALL = ("pair", "side", "orb")

VMEM = pl.BlockSpec(memory_space=pltpu.VMEM)
SMEM = pl.BlockSpec(memory_space=pltpu.SMEM)

kinetic = -0.5 / (spacing * spacing)
taps = tuple(kinetic * c / filter_half for c in coefficients)
shift = (kinetic * 3.0 * coefficients[0] - filter_centre) / filter_half


def filter_kernel(side_ref, own, swapped, slanted, straight, own_pot, pot_far, out, field, first, second, weight):
    side = side_ref[0]
    kept, rows, cols, _ = swapped.shape
    both = 2 * rows
    strips = cols // EIGHT

    def keep(ref, orbital, row, strip, value):
        ref[orbital, row, pl.ds(EIGHT * (strip + 1), EIGHT), :] = value
        if strip == 0:
            ref[orbital, row, pl.ds(cols + EIGHT, EIGHT), :] = value
        if strip == strips - 1:
            ref[orbital, row, pl.ds(0, EIGHT), :] = value

    def gather(source, orbital_from, count, row_to):
        for orbital in range(kept):

            def body(row, carry, orbital=orbital):
                for strip in range(strips):
                    value = source[orbital_from + orbital, row, pl.ds(EIGHT * strip, EIGHT), :]
                    keep(field, orbital, row_to + row, strip, value)
                return carry

            lax.fori_loop(0, count, body, 0)

    gather(own, side * kept, rows, DEEP + side * rows)
    gather(swapped, 0, rows, DEEP + (1 - side) * rows)
    gather(slanted, 0, DEEP, side * (both + DEEP))
    gather(straight, 0, DEEP, (1 - side) * (both + DEEP))

    def weigh(values):
        return values * (1.0 / filter_half) + shift

    weight[pl.ds(WIDE + side * rows, rows)] = weigh(own_pot[...])
    weight[pl.ds(WIDE + (1 - side) * rows, rows)] = weigh(pot_far[pl.ds(0, rows)])
    weight[pl.ds(side * (both + WIDE), WIDE)] = weigh(pot_far[pl.ds(rows, WIDE)])
    weight[pl.ds((1 - side) * (both + WIDE), WIDE)] = weigh(pot_far[pl.ds(rows + WIDE, WIDE)])

    def step(source, before, before_at, weight_at, total, store):
        width = source.shape[3]
        blocks = total // GROUP

        def body(index, carry):
            orbital = index // blocks
            base = (index % blocks) * GROUP
            for strip in range(strips):
                start = EIGHT * (strip + 1)
                window = [source[orbital, base + i, pl.ds(start, EIGHT), :] for i in range(GROUP + 2 * REACH)]
                for i in range(GROUP):
                    row = base + i
                    centre = window[i + REACH]
                    value = centre * weight[weight_at + row, pl.ds(EIGHT * strip, EIGHT), :]
                    for k in range(1, REACH + 1):
                        near = window[i + REACH - k] + window[i + REACH + k]
                        near = near + (
                            source[orbital, row + REACH, pl.ds(start - k, EIGHT), :]
                            + source[orbital, row + REACH, pl.ds(start + k, EIGHT), :]
                        )
                        near = near + (pltpu.roll(centre, k, 1) + pltpu.roll(centre, width - k, 1))
                        value = value + taps[k] * near
                    if before is not None:
                        value = 2.0 * value - before[orbital, before_at + row, pl.ds(start, EIGHT), :]
                    store(orbital, row, strip, value)
            return carry

        lax.fori_loop(0, kept * blocks, body, 0)

    step(field, None, 0, 0, both + 2 * WIDE, functools.partial(keep, first))
    step(first, field, 2 * REACH, REACH, both + 2 * REACH, functools.partial(keep, second))
    piece = out.shape[3]

    def store_out(orbital, row, strip, value):
        to = (EIGHT * strip) // piece
        half = row // rows
        out[2 * to + half, orbital, row - half * rows, pl.ds(EIGHT * strip - to * piece, EIGHT), :] = value

    step(second, first, 2 * REACH, 2 * REACH, both, store_out)


def filtered_pieces(side, own, swapped, slanted, straight, own_pot, pot_far, orb_count):
    kept, rows, cols, width = swapped.shape
    both = 2 * rows

    def scratch(margin):
        return pltpu.VMEM((kept, both + 2 * margin, cols + 2 * EIGHT, width), jnp.float32)

    return pl.pallas_call(
        filter_kernel,
        out_shape=jax.ShapeDtypeStruct((2 * orb_count, kept, rows, cols // orb_count, width), jnp.float32),
        in_specs=[SMEM] + [VMEM] * 6,
        out_specs=VMEM,
        scratch_shapes=[
            scratch(DEEP),
            scratch(WIDE),
            scratch(REACH),
            pltpu.VMEM((both + 2 * WIDE, cols, width), jnp.float32),
        ],
    )(side[None], own, swapped, slanted, straight, own_pot, pot_far)


def summed_everywhere(part, devices):
    copies = lax.all_to_all(jnp.broadcast_to(part[None], (devices,) + part.shape), ALL, 0, 0)
    return jnp.sum(copies, axis=0)


def orthonormal(flat, cell_total, devices):
    local_gram = jnp.dot(flat, flat.T, precision=lax.Precision.HIGHEST, preferred_element_type=jnp.float32)
    gram = summed_everywhere(local_gram, devices) / cell_total
    lower = jnp.linalg.cholesky(gram)
    return lax.linalg.triangular_solve(lower, flat, left_side=True, lower=True)


def on_device(orbitals, potential):
    pair_count, orb_count = lax.axis_size("pair"), lax.axis_size("orb")
    slabs = 2 * pair_count
    side, orb = lax.axis_index("side"), lax.axis_index("orb")
    held, rows, cols, width = orbitals.shape
    kept = held // 2
    part = cols // orb_count

    slant = [(i, (i + (1 if i % 2 else -1)) % slabs) for i in range(slabs)]
    ahead = [(i, (i + (2 if i % 2 else -2)) % slabs) for i in range(slabs)]
    swap = [(0, 1), (1, 0)]
    slab_axes = ("pair", "side")

    mine = lax.dynamic_slice_in_dim(potential, orb * part, part, axis=1)
    edge = lax.dynamic_slice_in_dim(mine, side * (rows - WIDE), WIDE, axis=0)
    pot_far = jnp.concatenate(
        [
            lax.ppermute(mine, "side", swap),
            lax.ppermute(edge, slab_axes, slant),
            lax.ppermute(edge, slab_axes, ahead),
        ],
        axis=0,
    )
    reach = 1
    while reach < orb_count:
        other = lax.ppermute(pot_far, "orb", [(i, i ^ reach) for i in range(orb_count)])
        low = (orb // reach) % 2 == 0
        pot_far = jnp.concatenate([jnp.where(low, pot_far, other), jnp.where(low, other, pot_far)], axis=1)
        reach *= 2

    given = lax.dynamic_slice_in_dim(orbitals, (1 - side) * kept, kept, axis=0)
    edges = lax.dynamic_slice_in_dim(orbitals, side * (rows - DEEP), DEEP, axis=1)
    given_edge = lax.dynamic_slice_in_dim(edges, (1 - side) * kept, kept, axis=0)
    kept_edge = lax.dynamic_slice_in_dim(edges, side * kept, kept, axis=0)
    swapped = lax.ppermute(given, "side", swap)
    slanted = lax.ppermute(given_edge, slab_axes, slant)
    straight = lax.ppermute(kept_edge, slab_axes, ahead)

    pieces = filtered_pieces(side, orbitals, swapped, slanted, straight, potential, pot_far, orb_count)
    grouped = lax.all_to_all(pieces, ("orb", "side"), 0, 0)
    total = held * orb_count
    devices = slabs * orb_count
    flat = grouped.reshape(total, -1)
    cell_total = flat.shape[1] * devices
    basis = orthonormal(orthonormal(flat, cell_total, devices), cell_total, devices)
    basis = basis.reshape(total, rows, part, width)
    return lax.all_to_all(basis, "orb", split_axis=0, concat_axis=2, tiled=True)


def solution(mesh):
    slabs, orb_count = mesh.shape["dom"], mesh.shape["orb"]
    fine = Mesh(mesh.devices.reshape(slabs // 2, 2, orb_count), ALL)
    spec = P("orb", ("pair", "side"), None, None)
    return jax.shard_map(
        on_device,
        mesh=fine,
        in_specs=(spec, P(("pair", "side"), None, None)),
        out_specs=spec,
        check_vma=False,
    )
```

time: 289 us -> 153 us (0.53)
  blocking collectives: 131 us -> 67.5 us
  local copies, waits for them, and re-layouts: 68 us -> 8.68 us
  other arithmetic: 43.8 us -> 13.5 us
  Pallas kernels: 0 us -> 15.6 us
    psum x2 -> x0, blocking collectives: 79.9 us -> none  [orthonormal(): gram = lax.psum(local_gram, ('dom', 'orb')) / cell_total]
    slice x39 -> x0, local copies, waits for them, and re-layouts: 61.7 us -> none  [the longest x12 26.6 us: hamiltonian(): jnp.roll(centre_part, -offset, 3)]
    sub x2 -> x0, other arithmetic: 24.2 us -> none  [the longest x1 12.4 us: chain_steps(): 2.0 * (applied(first) - filter_centre * first) / filter_half - block]
    all_to_all x1 -> x3, blocking collectives: 28.1 us -> 45.1 us  [the longest x1 24.7 us: on_device(): grouped = lax.all_to_all(pieces, ('orb', 'side'), 0, 0)]
    pallas_call x0 -> x1, Pallas kernels: none -> 15.6 us  [filtered_pieces(): pl.pallas_call(filter_kernel, out_shape=jax.ShapeDtypeStruct((2 * orb_cou...]
    div x3 -> x2, other arithmetic: 10.7 us -> 0.01 us  [orthonormal(): gram = summed_everywhere(local_gram, devices) / cell_total]
    dynamic_slice x0 -> x4, local copies, waits for them, and re-layouts: none -> 4.19 us  [the longest x1 1.31 us: on_device(): given = lax.dynamic_slice_in_dim(orbitals, (1 - side) * kept, kept, axis=0)]
    ppermute x6 -> x8, starting transfers between devices: 10.9 us -> 12.4 us  [the longest x1 3.57 us: on_device(): lax.ppermute(edge, slab_axes, slant)]
  transfers between devices with their start and end apart: 6 -> 8, of which waited for: 2 -> 5; matrix products, arithmetic and copies ran while one was open for 8% -> 5% of each run, Pallas kernels for 0% -> 0%
where the time goes in v1:
time: 153 us
  blocking collectives  67.5 us (44%)
  waiting for transfers between devices  27.3 us (18%)
  Pallas kernels  15.6 us (10%)
  other arithmetic  13.5 us (9%)
  starting transfers between devices  12.4 us (8%)
  local copies, waits for them, and re-layouts  8.68 us (6%)
  matrix products  7.31 us (5%)
    all_to_all x1, blocking collectives, on_device(): grouped = lax.all_to_all(pieces, ('orb', 'side'), 0, 0)  24.7 us
    all_to_all x1, blocking collectives, on_device(): return lax.all_to_all(basis, 'orb', split_axis=0, concat_axis=2, tiled=True)  22.5 us
    all_to_all x2, blocking collectives, summed_everywhere(): lax.all_to_all(jnp.broadcast_to(part[None], (devices,) + part.shape), ALL...  20.3 us
    pallas_call x1, Pallas kernels, filtered_pieces(): pl.pallas_call(filter_kernel, out_shape=jax.ShapeDtypeStruct((2 * orb_cou...  15.6 us
    ppermute x1, waiting for transfers between devices, on_device(): straight = lax.ppermute(kept_edge, slab_axes, ahead)  9.09 us
    ppermute x1, waiting for transfers between devices, on_device(): slanted = lax.ppermute(given_edge, slab_axes, slant)  8.2 us
    ppermute x2, waiting for transfers between devices, on_device(): lax.ppermute(pot_far, 'orb', [(i, i ^ reach) for i in range(orb_count)])  6.4 us
    another operation x6, other arithmetic, orthonormal(): lower = jnp.linalg.cholesky(gram)  4.34 us
  transfers between devices with their start and end apart: 8, of which 5 were waited for; matrix products, arithmetic and copies ran while one was open for 5% of the time, Pallas kernels for 0%

profile of v1, /device:TPU:0, one launch (start us, length us, event | category | flops | bytes accessed | tf_op | source)
XLA Modules:
  0.0 152.6 jit_solution(6603941879549067285)
XLA Ops:
  0.9 3.0 %collective-permute-start.3 = (f32[12,16,128]{2,1,0:T(8,128)S(1)}, f32[12,16,128]{2,1,0:T(8,128)S(1)}, u32[]{:S(2)}, u32[]{:S(2)}) collective-permute-start(f32[12,16,128]{2,1,0:T(8,128)S(1)} %constant_dynamic-slice_fusion.1), channel_id=1, source_target_pairs={{0,4},{4,0},{1,5},{5,1},{2,6},{6,2},{3,7},{7,3},{8,12},{12,8},{9,1... | collective-permute-start | bytes 294920 | tf_op jit(solution)/shard_map/ppermute | solution.py:160
  4.8 3.6 %collective-permute-start.4 = (f32[6,16,128]{2,1,0:T(8,128)S(1)}, f32[6,16,128]{2,1,0:T(8,128)S(1)}, u32[]{:S(2)}, u32[]{:S(2)}) collective-permute-start(f32[6,16,128]{2,1,0:T(8,128)S(1)} %constant_dynamic-slice_fusion), channel_id=1, source_target_pairs={{0,28},{4,8},{8,4},{12,16},{16,12},{20,24},{24,20},{28,0},{1,29},{... | collective-permute-start | bytes 147464 | tf_op jit(solution)/shard_map/ppermute | solution.py:161
  8.8 3.2 %collective-permute-done.4 = f32[6,16,128]{2,1,0:T(8,128)S(1)} collective-permute-done((f32[6,16,128]{2,1,0:T(8,128)S(1)}, f32[6,16,128]{2,1,0:T(8,128)S(1)}, u32[]{:S(2)}, u32[]{:S(2)}) %collective-permute-start.4) | collective-permute-done | bytes 49184 | tf_op jit(solution)/shard_map/ppermute | solution.py:161
  12.5 1.3 constant_dynamic-slice_fusion.4
  13.8 1.3 collective-permute-start
  17.0 1.5 collective-permute-start.7
  19.6 2.5 %collective-permute-start.1 = (f32[2,9,64,128]{3,2,1,0:T(8,128)}, f32[2,9,64,128]{3,2,1,0:T(8,128)S(1)}, u32[]{:S(2)}, u32[]{:S(2)}) collective-permute-start(f32[2,9,64,128]{3,2,1,0:T(8,128)} %get-tuple-element.8), channel_id=1, source_target_pairs={{0,28},{4,8},{8,4},{12,16},{16,12},{20,24},{24,20},{28,0},{1,29},{... | collective-permute-start | bytes 1769480 | tf_op jit(solution)/shard_map/ppermute | solution.py:178
  22.1 6.4 %collective-permute-done.7 = f32[24,32,128]{2,1,0:T(8,128)} collective-permute-done((f32[24,32,128]{2,1,0:T(8,128)}, f32[24,32,128]{2,1,0:T(8,128)}, u32[]{:S(2)}, u32[]{:S(2)}) %collective-permute-start.7) | collective-permute-done | bytes 393248 | tf_op jit(solution)/shard_map/ppermute | solution.py:168
  30.6 8.2 %collective-permute-done.1.slanted = f32[2,9,64,128]{3,2,1,0:T(8,128)S(1)} collective-permute-done((f32[2,9,64,128]{3,2,1,0:T(8,128)}, f32[2,9,64,128]{3,2,1,0:T(8,128)S(1)}, u32[]{:S(2)}, u32[]{:S(2)}) %collective-permute-start.1) | collective-permute-done | bytes 589856 | tf_op jit(solution)/shard_map/ppermute | solution.py:178
  38.8 9.1 %collective-permute-done.2.straight = f32[2,9,64,128]{3,2,1,0:T(8,128)S(1)} collective-permute-done((f32[2,9,64,128]{3,2,1,0:T(8,128)}, f32[2,9,64,128]{3,2,1,0:T(8,128)S(1)}, u32[]{:S(2)}, u32[]{:S(2)}) %collective-permute-start.2) | collective-permute-done | bytes 589856 | tf_op jit(solution)/shard_map/ppermute | solution.py:179
  49.0 15.6 %shard_map.28 = f32[8,2,12,16,128]{4,3,2,1,0:T(8,128)} custom-call(s32[1]{0:T(128)} %bitcast.side_ref, f32[4,12,64,128]{3,2,1,0:T(8,128)} %own.1, f32[2,12,64,128]{3,2,1,0:T(8,128)} %copy-done.1, f32[2,9,64,128]{3,2,1,0:T(8,128)} %copy-done.2, f32[2,9,64,128]{3,2,1,0:T(8,128)} %copy-done.3, f32[12,64,128]{2,1,0:T(8,128)} %own_pot.1, ...), custom_call_target="tpu_custom_call" | custom-call | tf_op jit(solution)/shard_map/pallas_call | solution.py:117
  64.6 24.7 %all_to_all.33 = f32[8,2,12,16,128]{4,3,2,1,0:T(8,128)S(1)} all-to-all(f32[8,2,12,16,128]{4,3,2,1,0:T(8,128)} %shard_map.28), channel_id=1, replica_groups=mesh['pair'=4,'side'=2,'orb'=4] {'orb','side'}, dimensions={0} | all-to-all | bytes 3145728 | tf_op jit(solution)/shard_map/all_to_all | solution.py:182
  89.6 2.1 %fusion.9 = f32[16,16]{1,0:T(8,128)S(1)} fusion(f32[16,24576]{1,0:T(8,128)S(1)} %reshape.19), kind=kOutput, calls=%fused_computation.35 | convolution fusion | flops 75497472 | bytes 1573888 | tf_op jit(solution)/shard_map/dot_general | solution.py:137
  91.9 11.4 %all_to_all.34 = f32[32,1,256]{2,1,0:T(1,128)S(1)} all-to-all(f32[32,1,256]{2,1,0:T(1,128)S(1)} %reshape.27), channel_id=1, replica_groups=mesh['pair'=4,'side'=2,'orb'=4] {'pair','side','orb'}, dimensions={0} | all-to-all | bytes 65536 | tf_op jit(solution)/shard_map/all_to_all | solution.py:132
  104.8 1.5 cholesky.44
  107.8 1.2 custom-call.6
  109.0 1.5 fusion.4
  110.5 2.2 %fusion.10 = f32[16,16]{1,0:T(8,128)S(1)} fusion(f32[16,24576]{1,0:T(8,128)S(1)} %fusion.4), kind=kOutput, calls=%fused_computation.36 | convolution fusion | flops 75497472 | bytes 1573888 | tf_op jit(solution)/shard_map/dot_general | solution.py:137
  112.9 9.0 %all_to_all.35 = f32[32,1,256]{2,1,0:T(1,128)S(1)} all-to-all(f32[32,1,256]{2,1,0:T(1,128)S(1)} %reshape.29), channel_id=1, replica_groups=mesh['pair'=4,'side'=2,'orb'=4] {'pair','side','orb'}, dimensions={0} | all-to-all | bytes 65536 | tf_op jit(solution)/shard_map/all_to_all | solution.py:132
  122.9 1.5 cholesky.55
  125.7 1.2 custom-call.7
  126.9 1.5 convolution_bitcast_fusion
  128.7 22.5 %all_to_all.36 = f32[16,12,16,128]{3,2,1,0:T(8,128)S(1)} all-to-all(f32[16,12,16,128]{3,2,1,0:T(8,128)S(1)} %bitcast.35), channel_id=1, replica_groups=mesh['pair'=4,'side'=2,'orb'=4] {'orb'}, dimensions={0} | all-to-all | bytes 3145728 | tf_op jit(solution)/shard_map/all_to_all | solution.py:189
  151.2 1.4 copy.17
  (54 shorter events, 15.2 us)
Async XLA Ops:
  0.9 7.9 %collective-permute-start.3 = (f32[12,16,128]{2,1,0:T(8,128)S(1)}, f32[12,16,128]{2,1,0:T(8,128)S(1)}, u32[]{:S(2)}, u32[]{:S(2)}) collective-permute-start(f32[12,16,128]{2,1,0:T(8,128)S(1)} %constant_dynamic-slice_fusion.1), channel_id=1, source_target_pairs={{0,4},{4,0},{1,5},{5,1},{2,6},{6,2},{3,7},{7,3},{8,12},{12,8},{9,1... | collective-permute-start | bytes 294920 | tf_op jit(solution)/shard_map/ppermute | solution.py:160
  4.8 7.2 %collective-permute-start.4 = (f32[6,16,128]{2,1,0:T(8,128)S(1)}, f32[6,16,128]{2,1,0:T(8,128)S(1)}, u32[]{:S(2)}, u32[]{:S(2)}) collective-permute-start(f32[6,16,128]{2,1,0:T(8,128)S(1)} %constant_dynamic-slice_fusion), channel_id=1, source_target_pairs={{0,28},{4,8},{8,4},{12,16},{16,12},{20,24},{24,20},{28,0},{1,29},{... | collective-permute-start | bytes 147464 | tf_op jit(solution)/shard_map/ppermute | solution.py:161
  8.3 4.1 %collective-permute-start.5 = (f32[6,16,128]{2,1,0:T(8,128)S(1)}, f32[6,16,128]{2,1,0:T(8,128)S(1)}, u32[]{:S(2)}, u32[]{:S(2)}) collective-permute-start(f32[6,16,128]{2,1,0:T(8,128)S(1)} %constant_dynamic-slice_fusion), channel_id=1, source_target_pairs={{0,24},{4,12},{8,0},{12,20},{16,8},{20,28},{24,16},{28,4},{1,25},{... | collective-permute-start | bytes 147464 | tf_op jit(solution)/shard_map/ppermute | solution.py:162
  12.4 2.7 %copy-start.4 = (f32[24,16,128]{2,1,0:T(8,128)}, f32[24,16,128]{2,1,0:T(8,128)S(1)}, u32[]{:S(2)}) copy-start(f32[24,16,128]{2,1,0:T(8,128)S(1)} %constant_dynamic-update-slice_fusion) | copy-start | bytes 589828
  12.4 2.7 %collective-permute-start.6 = (f32[24,16,128]{2,1,0:T(8,128)S(1)}, f32[24,16,128]{2,1,0:T(8,128)}, u32[]{:S(2)}, u32[]{:S(2)}) collective-permute-start(f32[24,16,128]{2,1,0:T(8,128)S(1)} %constant_dynamic-update-slice_fusion), channel_id=1, source_target_pairs={{0,1},{1,0},{2,3},{3,2},{4,5},{5,4},{6,7},{7,6},{8,9},{9,8},{10,11... | collective-permute-start | bytes 589832 | tf_op jit(solution)/shard_map/ppermute | solution.py:168
  12.5 6.0 %copy-start = (f32[4,12,64,128]{3,2,1,0:T(8,128)S(1)}, f32[4,12,64,128]{3,2,1,0:T(8,128)}, u32[]{:S(2)}) copy-start(f32[4,12,64,128]{3,2,1,0:T(8,128)} %own.1) | copy-start | bytes 4718596
  13.8 34.0 %collective-permute-start = (f32[2,12,64,128]{3,2,1,0:T(8,128)S(1)}, f32[2,12,64,128]{3,2,1,0:T(8,128)S(1)}, u32[]{:S(2)}, u32[]{:S(2)}) collective-permute-start(f32[2,12,64,128]{3,2,1,0:T(8,128)S(1)} %constant_dynamic-slice_fusion.4), channel_id=1, source_target_pairs={{0,4},{4,0},{1,5},{5,1},{2,6},{6,2},{3,7},{7,3},{8,12},{12,8},{9,1... | collective-permute-start | bytes 2359304 | tf_op jit(solution)/shard_map/ppermute | solution.py:177
  17.0 11.5 %collective-permute-start.7 = (f32[24,32,128]{2,1,0:T(8,128)}, f32[24,32,128]{2,1,0:T(8,128)}, u32[]{:S(2)}, u32[]{:S(2)}) collective-permute-start(f32[24,32,128]{2,1,0:T(8,128)} %pad_maximum_fusion.1), channel_id=1, source_target_pairs={{0,2},{1,3},{2,0},{3,1},{4,6},{5,7},{6,4},{7,5},{8,10},{9,11},{10,... | collective-permute-start | bytes 1179656 | tf_op jit(solution)/shard_map/ppermute | solution.py:168
  19.6 19.2 %collective-permute-start.1 = (f32[2,9,64,128]{3,2,1,0:T(8,128)}, f32[2,9,64,128]{3,2,1,0:T(8,128)S(1)}, u32[]{:S(2)}, u32[]{:S(2)}) collective-permute-start(f32[2,9,64,128]{3,2,1,0:T(8,128)} %get-tuple-element.8), channel_id=1, source_target_pairs={{0,28},{4,8},{8,4},{12,16},{16,12},{20,24},{24,20},{28,0},{1,29},{... | collective-permute-start | bytes 1769480 | tf_op jit(solution)/shard_map/ppermute | solution.py:178
  22.1 25.7 %collective-permute-start.2 = (f32[2,9,64,128]{3,2,1,0:T(8,128)}, f32[2,9,64,128]{3,2,1,0:T(8,128)S(1)}, u32[]{:S(2)}, u32[]{:S(2)}) collective-permute-start(f32[2,9,64,128]{3,2,1,0:T(8,128)} %get-tuple-element.6), channel_id=1, source_target_pairs={{0,24},{4,12},{8,0},{12,20},{16,8},{20,28},{24,16},{28,4},{1,25},{... | collective-permute-start | bytes 1769480 | tf_op jit(solution)/shard_map/ppermute | solution.py:179
  38.8 9.1 %copy-start.2 = (f32[2,9,64,128]{3,2,1,0:T(8,128)}, f32[2,9,64,128]{3,2,1,0:T(8,128)S(1)}, u32[]{:S(2)}) copy-start(f32[2,9,64,128]{3,2,1,0:T(8,128)S(1)} %collective-permute-done.1.slanted) | copy-start | bytes 1769476
  47.9 0.8 copy-start.3
  47.9 1.1 copy-start.1

commit v2 on v1

--- a/solution.py
+++ b/solution.py
@@ -80,13 +80,18 @@
                     row = base + i
                     centre = window[i + REACH]
                     value = centre * weight[weight_at + row, pl.ds(EIGHT * strip, EIGHT), :]
+                    left, right = pltpu.roll(centre, 1, 1), pltpu.roll(centre, width - 1, 1)
+                    far = taps[3] * centre
+                    value = value + pltpu.roll(taps[2] * right + far, 3, 1)
+                    value = value + pltpu.roll(taps[2] * left + far, width - 3, 1)
                     for k in range(1, REACH + 1):
                         near = window[i + REACH - k] + window[i + REACH + k]
                         near = near + (
                             source[orbital, row + REACH, pl.ds(start - k, EIGHT), :]
                             + source[orbital, row + REACH, pl.ds(start + k, EIGHT), :]
                         )
-                        near = near + (pltpu.roll(centre, k, 1) + pltpu.roll(centre, width - k, 1))
+                        if k == 1:
+                            near = near + (left + right)
                         value = value + taps[k] * near
                     if before is not None:
                         value = 2.0 * value - before[orbital, before_at + row, pl.ds(start, EIGHT), :]
@@ -128,19 +133,39 @@
     )(side[None], own, swapped, slanted, straight, own_pot, pot_far)
 
 
-def summed_everywhere(part, devices):
-    copies = lax.all_to_all(jnp.broadcast_to(part[None], (devices,) + part.shape), ALL, 0, 0)
-    return jnp.sum(copies, axis=0)
+def factor_kernel(cell_total, copies, inverse):
+    total = inverse.shape[0]
+    gram = jnp.sum(copies[...], axis=0) * (1.0 / cell_total)
+    lanes = 128
+    row = lax.broadcasted_iota(jnp.int32, (total, total), 0)
+    column = lax.broadcasted_iota(jnp.int32, (total, total), 1)
+    unit = jnp.where(row == column, 1.0, 0.0).astype(jnp.float32)
+    table = jnp.concatenate([gram, unit, jnp.zeros((total, lanes - 2 * total), jnp.float32)], axis=1)
+    index = lax.broadcasted_iota(jnp.int32, (total, lanes), 0)
+    for j in range(total):
+        pivot = table[j : j + 1, :]
+        scale = lax.rsqrt(table[j : j + 1, j : j + 1])
+        scale = scale * (1.5 - 0.5 * table[j : j + 1, j : j + 1] * scale * scale)
+        scaled = pivot * scale
+        factor = table[:, j : j + 1] * scale
+        table = jnp.where(index == j, scaled, jnp.where(index > j, table - factor * scaled, table))
+    inverse[...] = table[:, total : 2 * total]
 
 
 def orthonormal(flat, cell_total, devices):
+    total = flat.shape[0]
     local_gram = jnp.dot(flat, flat.T, precision=lax.Precision.HIGHEST, preferred_element_type=jnp.float32)
-    gram = summed_everywhere(local_gram, devices) / cell_total
-    lower = jnp.linalg.cholesky(gram)
-    return lax.linalg.triangular_solve(lower, flat, left_side=True, lower=True)
-
-
-def on_device(orbitals, potential):
+    copies = lax.all_to_all(jnp.broadcast_to(local_gram[None], (devices, total, total)), ALL, 0, 0)
+    inverse = pl.pallas_call(
+        functools.partial(factor_kernel, cell_total),
+        out_shape=jax.ShapeDtypeStruct((total, total), jnp.float32),
+        in_specs=[VMEM],
+        out_specs=VMEM,
+    )(copies)
+    return jnp.dot(inverse, flat, precision=lax.Precision.HIGHEST, preferred_element_type=jnp.float32)
+
+
+def whole(orbitals, potential):
     pair_count, orb_count = lax.axis_size("pair"), lax.axis_size("orb")
     slabs = 2 * pair_count
     side, orb = lax.axis_index("side"), lax.axis_index("orb")
@@ -156,11 +181,7 @@
     mine = lax.dynamic_slice_in_dim(potential, orb * part, part, axis=1)
     edge = lax.dynamic_slice_in_dim(mine, side * (rows - WIDE), WIDE, axis=0)
     pot_far = jnp.concatenate(
-        [
-            lax.ppermute(mine, "side", swap),
-            lax.ppermute(edge, slab_axes, slant),
-            lax.ppermute(edge, slab_axes, ahead),
-        ],
+        [lax.ppermute(mine, "side", swap), lax.ppermute(edge, slab_axes, slant), lax.ppermute(edge, slab_axes, ahead)],
         axis=0,
     )
     reach = 1
@@ -174,8 +195,8 @@
     edges = lax.dynamic_slice_in_dim(orbitals, side * (rows - DEEP), DEEP, axis=1)
     given_edge = lax.dynamic_slice_in_dim(edges, (1 - side) * kept, kept, axis=0)
     kept_edge = lax.dynamic_slice_in_dim(edges, side * kept, kept, axis=0)
+    slanted = lax.ppermute(given_edge, slab_axes, slant)
     swapped = lax.ppermute(given, "side", swap)
-    slanted = lax.ppermute(given_edge, slab_axes, slant)
     straight = lax.ppermute(kept_edge, slab_axes, ahead)
 
     pieces = filtered_pieces(side, orbitals, swapped, slanted, straight, potential, pot_far, orb_count)
@@ -194,7 +215,7 @@
     fine = Mesh(mesh.devices.reshape(slabs // 2, 2, orb_count), ALL)
     spec = P("orb", ("pair", "side"), None, None)
     return jax.shard_map(
-        on_device,
+        whole,
         mesh=fine,
         in_specs=(spec, P(("pair", "side"), None, None)),
         out_specs=spec,

time: 153 us -> 171 us (1.12)
  Pallas kernels: 15.6 us -> 39.2 us
  other arithmetic: 13.5 us -> 5.26 us
    pallas_call x1, Pallas kernels: 15.6 us -> 33.1 us  [filtered_pieces(): pl.pallas_call(filter_kernel, out_shape=jax.ShapeDtypeStruct((2 * orb_cou...]
    another operation x10 -> x0, other arithmetic: 8.14 us -> none  [the longest x6 4.34 us: orthonormal(): lower = jnp.linalg.cholesky(gram)]
    pallas_call x0 -> x2, Pallas kernels: none -> 6.13 us  [orthonormal(): pl.pallas_call(functools.partial(factor_kernel, cell_total), out_shape=ja...]
    dot_general x0 -> x2, matrix products: none -> 4.27 us  [orthonormal(): jnp.dot(inverse, flat, precision=lax.Precision.HIGHEST, preferred_element...]
    another operation x2 -> x0, matrix products: 2.97 us -> none  [orthonormal(): return lax.linalg.triangular_solve(lower, flat, left_side=True, lower=True)]
  transfers between devices with their start and end apart: 8 -> 8, of which waited for: 5 -> 5; matrix products, arithmetic and copies ran while one was open for 5% -> 4% of each run, Pallas kernels for 0% -> 0%
where the time goes in v2:
time: 171 us; the launch traced here: 170 us
  blocking collectives  67.4 us (39%)
  Pallas kernels  39.2 us (23%)
  waiting for transfers between devices  27.3 us (16%)
  starting transfers between devices  12.4 us (7%)
  local copies, waits for them, and re-layouts  9.9 us (6%)
  matrix products  8.72 us (5%)
  other arithmetic  5.26 us (3%)
    pallas_call x1, Pallas kernels, filtered_pieces(): pl.pallas_call(filter_kernel, out_shape=jax.ShapeDtypeStruct((2 * orb_cou...  33.1 us
    all_to_all x1, blocking collectives, whole(): grouped = lax.all_to_all(pieces, ('orb', 'side'), 0, 0)  24.7 us
    all_to_all x1, blocking collectives, whole(): return lax.all_to_all(basis, 'orb', split_axis=0, concat_axis=2, tiled=True)  22.5 us
    all_to_all x2, blocking collectives, orthonormal(): lax.all_to_all(jnp.broadcast_to(local_gram[None], (devices, total, total)...  20.2 us
    ppermute x1, waiting for transfers between devices, whole(): straight = lax.ppermute(kept_edge, slab_axes, ahead)  9.08 us
    ppermute x1, waiting for transfers between devices, whole(): slanted = lax.ppermute(given_edge, slab_axes, slant)  8.22 us
    ppermute x2, waiting for transfers between devices, whole(): lax.ppermute(pot_far, 'orb', [(i, i ^ reach) for i in range(orb_count)])  6.38 us
    pallas_call x2, Pallas kernels, orthonormal(): pl.pallas_call(functools.partial(factor_kernel, cell_total), out_shape=ja...  6.13 us
  transfers between devices with their start and end apart: 8, of which 5 were waited for; matrix products, arithmetic and copies ran while one was open for 4% of the time, Pallas kernels for 0%

profile of v2, /device:TPU:0, one launch (start us, length us, event | category | flops | bytes accessed | tf_op | source)
XLA Modules:
  0.0 170.4 jit_solution(13732399036748927689)
XLA Ops:
  0.9 3.0 %collective-permute-start.3 = (f32[12,16,128]{2,1,0:T(8,128)S(1)}, f32[12,16,128]{2,1,0:T(8,128)S(1)}, u32[]{:S(2)}, u32[]{:S(2)}) collective-permute-start(f32[12,16,128]{2,1,0:T(8,128)S(1)} %constant_dynamic-slice_fusion.1), channel_id=1, source_target_pairs={{0,4},{4,0},{1,5},{5,1},{2,6},{6,2},{3,7},{7,3},{8,12},{12,8},{9,1... | collective-permute-start | bytes 294920 | tf_op jit(solution)/shard_map/ppermute | solution.py:184
  4.8 3.6 %collective-permute-start.4 = (f32[6,16,128]{2,1,0:T(8,128)S(1)}, f32[6,16,128]{2,1,0:T(8,128)S(1)}, u32[]{:S(2)}, u32[]{:S(2)}) collective-permute-start(f32[6,16,128]{2,1,0:T(8,128)S(1)} %constant_dynamic-slice_fusion), channel_id=1, source_target_pairs={{0,28},{4,8},{8,4},{12,16},{16,12},{20,24},{24,20},{28,0},{1,29},{... | collective-permute-start | bytes 147464 | tf_op jit(solution)/shard_map/ppermute | solution.py:184
  8.8 3.2 %collective-permute-done.4 = f32[6,16,128]{2,1,0:T(8,128)S(1)} collective-permute-done((f32[6,16,128]{2,1,0:T(8,128)S(1)}, f32[6,16,128]{2,1,0:T(8,128)S(1)}, u32[]{:S(2)}, u32[]{:S(2)}) %collective-permute-start.4) | collective-permute-done | bytes 49184 | tf_op jit(solution)/shard_map/ppermute | solution.py:184
  12.5 1.3 constant_dynamic-slice_fusion.4
  13.8 1.3 collective-permute-start
  17.0 1.5 collective-permute-start.7
  18.5 1.1 constant_dynamic-slice_fusion.2
  19.7 2.5 %collective-permute-start.1 = (f32[2,9,64,128]{3,2,1,0:T(8,128)}, f32[2,9,64,128]{3,2,1,0:T(8,128)S(1)}, u32[]{:S(2)}, u32[]{:S(2)}) collective-permute-start(f32[2,9,64,128]{3,2,1,0:T(8,128)} %get-tuple-element.6), channel_id=1, source_target_pairs={{0,28},{4,8},{8,4},{12,16},{16,12},{20,24},{24,20},{28,0},{1,29},{... | collective-permute-start | bytes 1769480 | tf_op jit(solution)/shard_map/ppermute | solution.py:198
  22.2 6.4 %collective-permute-done.7 = f32[24,32,128]{2,1,0:T(8,128)} collective-permute-done((f32[24,32,128]{2,1,0:T(8,128)}, f32[24,32,128]{2,1,0:T(8,128)}, u32[]{:S(2)}, u32[]{:S(2)}) %collective-permute-start.7) | collective-permute-done | bytes 393248 | tf_op jit(solution)/shard_map/ppermute | solution.py:189
  28.6 1.1 broadcast_select_fusion.1
  30.6 8.2 %collective-permute-done.1.slanted = f32[2,9,64,128]{3,2,1,0:T(8,128)S(1)} collective-permute-done((f32[2,9,64,128]{3,2,1,0:T(8,128)}, f32[2,9,64,128]{3,2,1,0:T(8,128)S(1)}, u32[]{:S(2)}, u32[]{:S(2)}) %collective-permute-start.1) | collective-permute-done | bytes 589856 | tf_op jit(solution)/shard_map/ppermute | solution.py:198
  38.8 9.1 %collective-permute-done.2.straight = f32[2,9,64,128]{3,2,1,0:T(8,128)S(1)} collective-permute-done((f32[2,9,64,128]{3,2,1,0:T(8,128)}, f32[2,9,64,128]{3,2,1,0:T(8,128)S(1)}, u32[]{:S(2)}, u32[]{:S(2)}) %collective-permute-start.2) | collective-permute-done | bytes 589856 | tf_op jit(solution)/shard_map/ppermute | solution.py:200
  49.0 33.1 %shard_map.28 = f32[8,2,12,16,128]{4,3,2,1,0:T(8,128)} custom-call(s32[1]{0:T(128)} %bitcast.side_ref, f32[4,12,64,128]{3,2,1,0:T(8,128)} %own.1, f32[2,12,64,128]{3,2,1,0:T(8,128)} %copy-done.1, f32[2,9,64,128]{3,2,1,0:T(8,128)} %copy-done.2, f32[2,9,64,128]{3,2,1,0:T(8,128)} %copy-done.3, f32[12,64,128]{2,1,0:T(8,128)} %own_pot.1, ...), custom_call_target="tpu_custom_call" | custom-call | tf_op jit(solution)/shard_map/pallas_call | solution.py:122
  82.1 24.7 %all_to_all.33 = f32[8,2,12,16,128]{4,3,2,1,0:T(8,128)S(1)} all-to-all(f32[8,2,12,16,128]{4,3,2,1,0:T(8,128)} %shard_map.28), channel_id=1, replica_groups=mesh['pair'=4,'side'=2,'orb'=4] {'orb','side'}, dimensions={0} | all-to-all | bytes 3145728 | tf_op jit(solution)/shard_map/all_to_all | solution.py:203
  107.1 2.2 %fusion = f32[16,16]{1,0:T(8,128)S(1)} fusion(f32[16,24576]{1,0:T(8,128)S(1)} %reshape.8), kind=kOutput, calls=%fused_computation.15 | convolution fusion | flops 75497472 | bytes 1573888 | tf_op jit(solution)/shard_map/dot_general | solution.py:157
  109.5 11.3 %all_to_all.34 = f32[32,1,256]{2,1,0:T(1,128)S(1)} all-to-all(f32[32,1,256]{2,1,0:T(1,128)S(1)} %reshape.10), channel_id=1, replica_groups=mesh['pair'=4,'side'=2,'orb'=4] {'pair','side','orb'}, dimensions={0} | all-to-all | bytes 65536 | tf_op jit(solution)/shard_map/all_to_all | solution.py:158
  122.9 3.1 %shard_map.29 = f32[16,16]{1,0:T(8,128)} custom-call(f32[32,16,16]{2,1,0:T(8,128)} %reshape.11.copies), custom_call_target="tpu_custom_call" | custom-call | tf_op jit(solution)/shard_map/pallas_call | solution.py:159
  125.9 2.1 %fusion.1 = f32[16,24576]{1,0:T(8,128)S(1)} fusion(f32[16,16]{1,0:T(8,128)} %shard_map.29, f32[16,24576]{1,0:T(8,128)S(1)} %reshape.8), kind=kOutput, calls=%fused_computation.16 | convolution fusion | flops 75497472 | bytes 3146752 | tf_op jit(solution)/shard_map/dot_general | solution.py:165
  128.1 2.2 %fusion.2 = f32[16,16]{1,0:T(8,128)S(1)} fusion(f32[16,24576]{1,0:T(8,128)S(1)} %fusion.1), kind=kOutput, calls=%fused_computation.17 | convolution fusion | flops 75497472 | bytes 1573888 | tf_op jit(solution)/shard_map/dot_general | solution.py:157
  130.5 9.0 %all_to_all.35 = f32[32,1,256]{2,1,0:T(1,128)S(1)} all-to-all(f32[32,1,256]{2,1,0:T(1,128)S(1)} %reshape.12), channel_id=1, replica_groups=mesh['pair'=4,'side'=2,'orb'=4] {'pair','side','orb'}, dimensions={0} | all-to-all | bytes 65536 | tf_op jit(solution)/shard_map/all_to_all | solution.py:158
  141.0 3.1 %shard_map.30 = f32[16,16]{1,0:T(8,128)} custom-call(f32[32,16,16]{2,1,0:T(8,128)} %reshape.13.copies), custom_call_target="tpu_custom_call" | custom-call | tf_op jit(solution)/shard_map/pallas_call | solution.py:159
  144.1 2.1 %convolution_bitcast_fusion = f32[2,8,192,128]{3,1,2,0:T(8,128)S(1)} fusion(f32[16,16]{1,0:T(8,128)} %shard_map.30, f32[16,24576]{1,0:T(8,128)S(1)} %fusion.1), kind=kOutput, calls=%fused_computation | convolution fusion | flops 75497472 | bytes 3146752 | tf_op jit(solution)/shard_map/dot_general | solution.py:165
  146.5 22.5 %all_to_all.36 = f32[16,12,16,128]{3,2,1,0:T(8,128)S(1)} all-to-all(f32[16,12,16,128]{3,2,1,0:T(8,128)S(1)} %bitcast.19), channel_id=1, replica_groups=mesh['pair'=4,'side'=2,'orb'=4] {'orb'}, dimensions={0} | all-to-all | bytes 3145728 | tf_op jit(solution)/shard_map/all_to_all | solution.py:210
  169.0 1.4 copy.3
  (36 shorter events, 11.3 us)
Async XLA Ops:
  0.9 7.9 %collective-permute-start.3 = (f32[12,16,128]{2,1,0:T(8,128)S(1)}, f32[12,16,128]{2,1,0:T(8,128)S(1)}, u32[]{:S(2)}, u32[]{:S(2)}) collective-permute-start(f32[12,16,128]{2,1,0:T(8,128)S(1)} %constant_dynamic-slice_fusion.1), channel_id=1, source_target_pairs={{0,4},{4,0},{1,5},{5,1},{2,6},{6,2},{3,7},{7,3},{8,12},{12,8},{9,1... | collective-permute-start | bytes 294920 | tf_op jit(solution)/shard_map/ppermute | solution.py:184
  4.8 7.2 %collective-permute-start.4 = (f32[6,16,128]{2,1,0:T(8,128)S(1)}, f32[6,16,128]{2,1,0:T(8,128)S(1)}, u32[]{:S(2)}, u32[]{:S(2)}) collective-permute-start(f32[6,16,128]{2,1,0:T(8,128)S(1)} %constant_dynamic-slice_fusion), channel_id=1, source_target_pairs={{0,28},{4,8},{8,4},{12,16},{16,12},{20,24},{24,20},{28,0},{1,29},{... | collective-permute-start | bytes 147464 | tf_op jit(solution)/shard_map/ppermute | solution.py:184
  8.3 4.1 %collective-permute-start.5 = (f32[6,16,128]{2,1,0:T(8,128)S(1)}, f32[6,16,128]{2,1,0:T(8,128)S(1)}, u32[]{:S(2)}, u32[]{:S(2)}) collective-permute-start(f32[6,16,128]{2,1,0:T(8,128)S(1)} %constant_dynamic-slice_fusion), channel_id=1, source_target_pairs={{0,24},{4,12},{8,0},{12,20},{16,8},{20,28},{24,16},{28,4},{1,25},{... | collective-permute-start | bytes 147464 | tf_op jit(solution)/shard_map/ppermute | solution.py:184
  12.4 2.7 %copy-start.4 = (f32[24,16,128]{2,1,0:T(8,128)}, f32[24,16,128]{2,1,0:T(8,128)S(1)}, u32[]{:S(2)}) copy-start(f32[24,16,128]{2,1,0:T(8,128)S(1)} %constant_dynamic-update-slice_fusion) | copy-start | bytes 589828
  12.4 2.7 %collective-permute-start.6 = (f32[24,16,128]{2,1,0:T(8,128)S(1)}, f32[24,16,128]{2,1,0:T(8,128)}, u32[]{:S(2)}, u32[]{:S(2)}) collective-permute-start(f32[24,16,128]{2,1,0:T(8,128)S(1)} %constant_dynamic-update-slice_fusion), channel_id=1, source_target_pairs={{0,1},{1,0},{2,3},{3,2},{4,5},{5,4},{6,7},{7,6},{8,9},{9,8},{10,11... | collective-permute-start | bytes 589832 | tf_op jit(solution)/shard_map/ppermute | solution.py:189
  12.5 6.0 %copy-start = (f32[4,12,64,128]{3,2,1,0:T(8,128)S(1)}, f32[4,12,64,128]{3,2,1,0:T(8,128)}, u32[]{:S(2)}) copy-start(f32[4,12,64,128]{3,2,1,0:T(8,128)} %own.1) | copy-start | bytes 4718596
  13.8 34.1 %collective-permute-start = (f32[2,12,64,128]{3,2,1,0:T(8,128)S(1)}, f32[2,12,64,128]{3,2,1,0:T(8,128)S(1)}, u32[]{:S(2)}, u32[]{:S(2)}) collective-permute-start(f32[2,12,64,128]{3,2,1,0:T(8,128)S(1)} %constant_dynamic-slice_fusion.4), channel_id=1, source_target_pairs={{0,4},{4,0},{1,5},{5,1},{2,6},{6,2},{3,7},{7,3},{8,12},{12,8},{9,1... | collective-permute-start | bytes 2359304 | tf_op jit(solution)/shard_map/ppermute | solution.py:199
  17.0 11.5 %collective-permute-start.7 = (f32[24,32,128]{2,1,0:T(8,128)}, f32[24,32,128]{2,1,0:T(8,128)}, u32[]{:S(2)}, u32[]{:S(2)}) collective-permute-start(f32[24,32,128]{2,1,0:T(8,128)} %pad_maximum_fusion.1), channel_id=1, source_target_pairs={{0,2},{1,3},{2,0},{3,1},{4,6},{5,7},{6,4},{7,5},{8,10},{9,11},{10,... | collective-permute-start | bytes 1179656 | tf_op jit(solution)/shard_map/ppermute | solution.py:189
  19.7 19.2 %collective-permute-start.1 = (f32[2,9,64,128]{3,2,1,0:T(8,128)}, f32[2,9,64,128]{3,2,1,0:T(8,128)S(1)}, u32[]{:S(2)}, u32[]{:S(2)}) collective-permute-start(f32[2,9,64,128]{3,2,1,0:T(8,128)} %get-tuple-element.6), channel_id=1, source_target_pairs={{0,28},{4,8},{8,4},{12,16},{16,12},{20,24},{24,20},{28,0},{1,29},{... | collective-permute-start | bytes 1769480 | tf_op jit(solution)/shard_map/ppermute | solution.py:198
  22.2 25.7 %collective-permute-start.2 = (f32[2,9,64,128]{3,2,1,0:T(8,128)}, f32[2,9,64,128]{3,2,1,0:T(8,128)S(1)}, u32[]{:S(2)}, u32[]{:S(2)}) collective-permute-start(f32[2,9,64,128]{3,2,1,0:T(8,128)} %get-tuple-element.5), channel_id=1, source_target_pairs={{0,24},{4,12},{8,0},{12,20},{16,8},{20,28},{24,16},{28,4},{1,25},{... | collective-permute-start | bytes 1769480 | tf_op jit(solution)/shard_map/ppermute | solution.py:200
  38.8 9.1 %copy-start.2 = (f32[2,9,64,128]{3,2,1,0:T(8,128)}, f32[2,9,64,128]{3,2,1,0:T(8,128)S(1)}, u32[]{:S(2)}) copy-start(f32[2,9,64,128]{3,2,1,0:T(8,128)S(1)} %collective-permute-done.1.slanted) | copy-start | bytes 1769476
  47.9 0.8 copy-start.3
  47.9 1.1 copy-start.1

commit v3 on v2

v3 whole, which is shorter than its diff:
```python
import functools

import jax
import jax.numpy as jnp
from jax import lax
from jax.experimental import pallas as pl
from jax.experimental.pallas import tpu as pltpu
from jax.sharding import Mesh
from jax.sharding import PartitionSpec as P

coefficients = (-49.0 / 18.0, 1.5, -0.15, 1.0 / 90.0)
spacing = 0.5
filter_centre = 23.0
filter_half = 23.0

REACH = 3
STEPS = 3
DEEP = REACH * STEPS
WIDE = REACH * (STEPS - 1)
EIGHT = 8
BLOCKS = 3
ALL = ("pair", "side", "orb")

VMEM = pl.BlockSpec(memory_space=pltpu.VMEM)
SMEM = pl.BlockSpec(memory_space=pltpu.SMEM)

kinetic = -0.5 / (spacing * spacing)
taps = tuple(kinetic * c / filter_half for c in coefficients)
denominator = 180.0
whole_taps = tuple(round(denominator * c) for c in coefficients)
lane_scale = kinetic / filter_half / denominator
shift = (kinetic * 2.0 * coefficients[0] - filter_centre) / filter_half


def split_dot(values, table):
    high = values.astype(jnp.bfloat16)
    rest = values - high.astype(jnp.float32)
    middle = rest.astype(jnp.bfloat16)
    low = (rest - middle.astype(jnp.float32)).astype(jnp.bfloat16)
    wide = jnp.concatenate([high, middle], axis=1)
    twice = jnp.concatenate([table, table], axis=0)
    return jnp.dot(wide, twice, preferred_element_type=jnp.float32) + jnp.dot(
        low, table, preferred_element_type=jnp.float32
    )


def filter_kernel(at, place, own, swapped, slanted, straight, own_pot, pot_far, lane_table, *rest):
    outs, (field, first, second, weight, sorted_pieces) = rest[:-5], rest[-5:]
    side, me = place[0], place[1]
    rows, cols, _ = swapped.shape
    both = 2 * rows
    strips = cols // EIGHT

    def keep(ref, row, strip, value):
        ref[row, pl.ds(EIGHT * (strip + 1), EIGHT), :] = value
        if strip == 0:
            ref[row, pl.ds(cols + EIGHT, EIGHT), :] = value
        if strip == strips - 1:
            ref[row, pl.ds(0, EIGHT), :] = value

    def gather(load, count, row_to):
        def body(row, carry):
            for strip in range(strips):
                keep(field, row_to + row, strip, load(row, pl.ds(EIGHT * strip, EIGHT)))
            return carry

        lax.fori_loop(0, count, body, 0, unroll=3)

    kept = own.shape[0] // 2
    gather(lambda row, span: own[side * kept + at, row, span, :], rows, DEEP + side * rows)
    gather(lambda row, span: swapped[row, span, :], rows, DEEP + (1 - side) * rows)
    gather(lambda row, span: slanted[row, span, :], DEEP, side * (both + DEEP))
    gather(lambda row, span: straight[row, span, :], DEEP, (1 - side) * (both + DEEP))

    def weigh(values):
        return values * (1.0 / filter_half) + shift

    weight[pl.ds(WIDE + side * rows, rows)] = weigh(own_pot[...])
    weight[pl.ds(WIDE + (1 - side) * rows, rows)] = weigh(pot_far[pl.ds(0, rows)])
    weight[pl.ds(side * (both + WIDE), WIDE)] = weigh(pot_far[pl.ds(rows, WIDE)])
    weight[pl.ds((1 - side) * (both + WIDE), WIDE)] = weigh(pot_far[pl.ds(rows + WIDE, WIDE)])

    def step(source, before, before_at, weight_at, total, store):
        width = source.shape[2]
        count = total // BLOCKS

        def body(index, carry):
            base = index * count
            centres = source[pl.ds(base + REACH, count), pl.ds(EIGHT, cols), :]
            along = split_dot(centres.reshape(count * cols, width), lane_table[...])
            for strip in range(strips):
                start = EIGHT * (strip + 1)
                window = [source[base + i, pl.ds(start, EIGHT), :] for i in range(count + 2 * REACH)]
                for i in range(count):
                    row = base + i
                    value = window[i + REACH] * weight[weight_at + row, pl.ds(EIGHT * strip, EIGHT), :]
                    from_lanes = i * cols + EIGHT * strip
                    value = value + along[from_lanes : from_lanes + EIGHT] * lane_scale
                    for k in range(1, REACH + 1):
                        near = window[i + REACH - k] + window[i + REACH + k]
                        near = near + (
                            source[row + REACH, pl.ds(start - k, EIGHT), :]
                            + source[row + REACH, pl.ds(start + k, EIGHT), :]
                        )
                        value = value + taps[k] * near
                    if before is not None:
                        value = 2.0 * value - before[before_at + row, pl.ds(start, EIGHT), :]
                    store(row, strip, value)
            return carry

        lax.fori_loop(0, BLOCKS, body, 0)

    step(field, None, 0, 0, both + 2 * WIDE, functools.partial(keep, first))
    step(first, field, 2 * REACH, REACH, both + 2 * REACH, functools.partial(keep, second))
    piece = sorted_pieces.shape[2]

    def store_out(row, strip, value):
        to = (EIGHT * strip) // piece
        half = row // rows
        sorted_pieces[2 * to + half, row - half * rows, pl.ds(EIGHT * strip - to * piece, EIGHT), :] = value

    step(second, first, 2 * REACH, 2 * REACH, both, store_out)
    for apart, out in enumerate(outs):
        out[...] = sorted_pieces[me ^ apart]


def filtered_pieces(at, place, own, swapped, slanted, straight, own_pot, pot_far, group):
    rows, cols, width = swapped.shape
    both = 2 * rows
    apart = jnp.arange(width)[:, None] - jnp.arange(width)[None, :]
    lane_table = jnp.zeros((width, width), jnp.float32)
    for k, tap in enumerate(whole_taps):
        hit = (apart % width == k) | (-apart % width == k)
        lane_table = jnp.where(hit, float(tap), lane_table)

    def scratch(margin):
        return pltpu.VMEM((both + 2 * margin, cols + 2 * EIGHT, width), jnp.float32)

    piece = (rows, 2 * cols // group, width)
    return pl.pallas_call(
        functools.partial(filter_kernel, at),
        out_shape=[jax.ShapeDtypeStruct(piece, jnp.float32)] * group,
        in_specs=[SMEM] + [VMEM] * 7,
        out_specs=[VMEM] * group,
        scratch_shapes=[
            scratch(DEEP),
            scratch(WIDE),
            scratch(REACH),
            pltpu.VMEM((both + 2 * WIDE, cols, width), jnp.float32),
            pltpu.VMEM((group,) + piece, jnp.float32),
        ],
        compiler_params=pltpu.CompilerParams(vmem_limit_bytes=24 * 1024 * 1024),
    )(place, own, swapped, slanted, straight, own_pot, pot_far, lane_table.astype(jnp.bfloat16))


def sort_kernel(place, *refs):
    given, out = refs[:-1], refs[-1]
    kept = out.shape[1]
    for index, ref in enumerate(given):
        out[place[1] ^ (index // kept), index % kept] = ref[...]


def factor_kernel(cell_total, copies, inverse):
    total = inverse.shape[0]
    gram = jnp.sum(copies[...], axis=0) * (1.0 / cell_total)
    lanes = 128
    row = lax.broadcasted_iota(jnp.int32, (total, total), 0)
    column = lax.broadcasted_iota(jnp.int32, (total, total), 1)
    unit = jnp.where(row == column, 1.0, 0.0).astype(jnp.float32)
    table = jnp.concatenate([gram, unit, jnp.zeros((total, lanes - 2 * total), jnp.float32)], axis=1)
    index = lax.broadcasted_iota(jnp.int32, (total, lanes), 0)
    for j in range(total):
        pivot = table[j : j + 1, :]
        scale = lax.rsqrt(table[j : j + 1, j : j + 1])
        scale = scale * (1.5 - 0.5 * table[j : j + 1, j : j + 1] * scale * scale)
        scaled = pivot * scale
        factor = table[:, j : j + 1] * scale
        table = jnp.where(index == j, scaled, jnp.where(index > j, table - factor * scaled, table))
    inverse[...] = table[:, total : 2 * total]


def orthonormal(flat, cell_total, devices):
    total = flat.shape[0]
    local_gram = jnp.dot(flat, flat.T, precision=lax.Precision.HIGHEST, preferred_element_type=jnp.float32)
    copies = lax.all_to_all(jnp.broadcast_to(local_gram[None], (devices, total, total)), ALL, 0, 0)
    inverse = pl.pallas_call(
        functools.partial(factor_kernel, cell_total),
        out_shape=jax.ShapeDtypeStruct((total, total), jnp.float32),
        in_specs=[VMEM],
        out_specs=VMEM,
    )(copies)
    return jnp.dot(inverse, flat, precision=lax.Precision.HIGHEST, preferred_element_type=jnp.float32)


def whole(orbitals, potential):
    pair_count, orb_count = lax.axis_size("pair"), lax.axis_size("orb")
    slabs = 2 * pair_count
    side, orb = lax.axis_index("side"), lax.axis_index("orb")
    held, rows, cols, width = orbitals.shape
    kept = held // 2
    part = cols // orb_count

    slant = [(i, (i + (1 if i % 2 else -1)) % slabs) for i in range(slabs)]
    ahead = [(i, (i + (2 if i % 2 else -2)) % slabs) for i in range(slabs)]
    swap = [(0, 1), (1, 0)]
    slab_axes = ("pair", "side")

    mine = lax.dynamic_slice_in_dim(potential, orb * part, part, axis=1)
    edge = lax.dynamic_slice_in_dim(mine, side * (rows - WIDE), WIDE, axis=0)
    pot_far = [
        lax.ppermute(mine, "side", swap),
        lax.ppermute(edge, slab_axes, slant),
        lax.ppermute(edge, slab_axes, ahead),
    ]
    pot_far = jnp.concatenate(pot_far, axis=0)
    reach = 1
    while reach < orb_count:
        other = lax.ppermute(pot_far, "orb", [(i, i ^ reach) for i in range(orb_count)])
        low = (orb // reach) % 2 == 0
        pot_far = jnp.concatenate([jnp.where(low, pot_far, other), jnp.where(low, other, pot_far)], axis=1)
        reach *= 2

    fetched = []
    for at in range(kept):
        given = lax.dynamic_index_in_dim(orbitals, (1 - side) * kept + at, 0, keepdims=False)
        given_edge = lax.dynamic_slice_in_dim(given, side * (rows - DEEP), DEEP, axis=0)
        stays = lax.dynamic_index_in_dim(orbitals, side * kept + at, 0, keepdims=False)
        stays_edge = lax.dynamic_slice_in_dim(stays, side * (rows - DEEP), DEEP, axis=0)
        fetched.append(
            (
                lax.ppermute(given, "side", swap),
                lax.ppermute(given_edge, slab_axes, slant),
                lax.ppermute(stays_edge, slab_axes, ahead),
            )
        )

    group = 2 * orb_count
    me = 2 * orb + side

    def flat_of(index):
        return (index % 2) * orb_count + index // 2

    place = jnp.stack([side, me]).astype(jnp.int32)
    returned = []
    for at in range(kept):
        pieces = filtered_pieces(at, place, orbitals, *fetched[at], potential, pot_far, group)
        returned.append(
            [pieces[0]]
            + [
                lax.ppermute(pieces[m], ("side", "orb"), [(flat_of(i), flat_of(i ^ m)) for i in range(group)])
                for m in range(1, group)
            ]
        )
    grouped = pl.pallas_call(
        sort_kernel,
        out_shape=jax.ShapeDtypeStruct((group, kept, rows, part, width), jnp.float32),
        in_specs=[SMEM] + [VMEM] * (group * kept),
        out_specs=VMEM,
        compiler_params=pltpu.CompilerParams(vmem_limit_bytes=16 * 1024 * 1024),
    )(place, *[returned[at][m] for m in range(group) for at in range(kept)])
    total = held * orb_count
    devices = slabs * orb_count
    flat = grouped.reshape(total, -1)
    cell_total = flat.shape[1] * devices
    basis = orthonormal(orthonormal(flat, cell_total, devices), cell_total, devices)
    basis = basis.reshape(total, rows, part, width)
    return lax.all_to_all(basis, "orb", split_axis=0, concat_axis=2, tiled=True)


def solution(mesh):
    slabs, orb_count = mesh.shape["dom"], mesh.shape["orb"]
    fine = Mesh(mesh.devices.reshape(slabs // 2, 2, orb_count), ALL)
    spec = P("orb", ("pair", "side"), None, None)
    return jax.shard_map(
        whole,
        mesh=fine,
        in_specs=(spec, P(("pair", "side"), None, None)),
        out_specs=spec,
        check_vma=False,
    )
```

time: 171 us -> 142 us (0.83)
  blocking collectives: 67.4 us -> 42.1 us
  Pallas kernels: 39.2 us -> 16.1 us
  starting transfers between devices: 12.4 us -> 33.3 us
  waiting for transfers between devices: 27.3 us -> 29.3 us
    all_to_all x1 -> x0, blocking collectives: 24.7 us -> none  [whole(): grouped = lax.all_to_all(pieces, ('orb', 'side'), 0, 0)]
    pallas_call x1 -> x3, Pallas kernels: 33.1 us -> 10 us  [the longest x2 9.36 us: filtered_pieces(): pl.pallas_call(functools.partial(filter_kernel, at), out_shape=[jax.Shape...]
    ppermute x3 -> x20, starting transfers between devices: 3.85 us -> 24.8 us  [the longest x14 13.6 us: whole(): lax.ppermute(pieces[m], ('side', 'orb'), [(flat_of(i), flat_of(i ^ m)) fo...]
    ppermute x3 -> x20, waiting for transfers between devices: 17.3 us -> 24.2 us  [the longest x2 11.7 us: whole(): lax.ppermute(given, 'side', swap)]
    ppermute x2, waiting for transfers between devices: 6.38 us -> 1.41 us  [whole(): lax.ppermute(pot_far, 'orb', [(i, i ^ reach) for i in range(orb_count)])]
  transfers between devices with their start and end apart: 8 -> 25, of which waited for: 5 -> 10; matrix products, arithmetic and copies ran while one was open for 4% -> 3% of each run, Pallas kernels for 0% -> 7%
where the time goes in v3:
time: 142 us
  blocking collectives  42.1 us (30%)
  starting transfers between devices  33.3 us (23%)
  waiting for transfers between devices  29.3 us (21%)
  Pallas kernels  16.1 us (11%)
  matrix products  8.72 us (6%)
  local copies, waits for them, and re-layouts  8.53 us (6%)
  other arithmetic  3.7 us (3%)
    all_to_all x1, blocking collectives, whole(): return lax.all_to_all(basis, 'orb', split_axis=0, concat_axis=2, tiled=True)  22.5 us
    all_to_all x2, blocking collectives, orthonormal(): lax.all_to_all(jnp.broadcast_to(local_gram[None], (devices, total, total)...  19.6 us
    ppermute x14, starting transfers between devices, whole(): lax.ppermute(pieces[m], ('side', 'orb'), [(flat_of(i), flat_of(i ^ m)) fo...  13.6 us
    ppermute x2, waiting for transfers between devices, whole(): lax.ppermute(given, 'side', swap)  11.7 us
    pallas_call x2, Pallas kernels, filtered_pieces(): pl.pallas_call(functools.partial(filter_kernel, at), out_shape=[jax.Shape...  9.36 us
    ppermute x14, waiting for transfers between devices, whole(): lax.ppermute(pieces[m], ('side', 'orb'), [(flat_of(i), flat_of(i ^ m)) fo...  7.03 us
    ppermute x2, starting transfers between devices, whole(): lax.ppermute(stays_edge, slab_axes, ahead)  6.45 us
    pallas_call x2, Pallas kernels, orthonormal(): pl.pallas_call(functools.partial(factor_kernel, cell_total), out_shape=ja...  6.13 us
  transfers between devices with their start and end apart: 25, of which 10 were waited for; matrix products, arithmetic and copies ran while one was open for 3% of the time, Pallas kernels for 7%

profile of v3, /device:TPU:0, one launch (start us, length us, event | category | flops | bytes accessed | tf_op | source)
XLA Modules:
  0.0 142.1 jit_solution(9986721021192604968)
XLA Ops:
  1.0 3.0 %collective-permute-start.3 = (f32[12,16,128]{2,1,0:T(8,128)S(1)}, f32[12,16,128]{2,1,0:T(8,128)S(1)}, u32[]{:S(2)}, u32[]{:S(2)}) collective-permute-start(f32[12,16,128]{2,1,0:T(8,128)S(1)} %constant_dynamic-slice_fusion.1), channel_id=1, source_target_pairs={{0,4},{4,0},{1,5},{5,1},{2,6},{6,2},{3,7},{7,3},{8,12},{12,8},{9,1... | collective-permute-start | bytes 294920 | tf_op jit(solution)/shard_map/ppermute | solution.py:211
  4.9 3.6 %collective-permute-start.4 = (f32[6,16,128]{2,1,0:T(8,128)S(1)}, f32[6,16,128]{2,1,0:T(8,128)S(1)}, u32[]{:S(2)}, u32[]{:S(2)}) collective-permute-start(f32[6,16,128]{2,1,0:T(8,128)S(1)} %constant_dynamic-slice_fusion), channel_id=1, source_target_pairs={{0,28},{4,8},{8,4},{12,16},{16,12},{20,24},{24,20},{28,0},{1,29},{... | collective-permute-start | bytes 147464 | tf_op jit(solution)/shard_map/ppermute | solution.py:212
  8.9 3.2 %collective-permute-done.4 = f32[6,16,128]{2,1,0:T(8,128)S(1)} collective-permute-done((f32[6,16,128]{2,1,0:T(8,128)S(1)}, f32[6,16,128]{2,1,0:T(8,128)S(1)}, u32[]{:S(2)}, u32[]{:S(2)}) %collective-permute-start.4) | collective-permute-done | bytes 49184 | tf_op jit(solution)/shard_map/ppermute | solution.py:212
  17.4 2.3 %collective-permute-start.10 = (f32[9,64,128]{2,1,0:T(8,128)}, f32[9,64,128]{2,1,0:T(8,128)S(1)}, u32[]{:S(2)}, u32[]{:S(2)}) collective-permute-start(f32[9,64,128]{2,1,0:T(8,128)} %get-tuple-element.37), channel_id=1, source_target_pairs={{0,24},{4,12},{8,0},{12,20},{16,8},{20,28},{24,16},{28,4},{1,25},{... | collective-permute-start | bytes 884744 | tf_op jit(solution)/shard_map/ppermute | solution.py:233
  19.7 2.2 %collective-permute-start.9 = (f32[9,64,128]{2,1,0:T(8,128)}, f32[9,64,128]{2,1,0:T(8,128)S(1)}, u32[]{:S(2)}, u32[]{:S(2)}) collective-permute-start(f32[9,64,128]{2,1,0:T(8,128)} %get-tuple-element.38), channel_id=1, source_target_pairs={{0,28},{4,8},{8,4},{12,16},{16,12},{20,24},{24,20},{28,0},{1,29},{... | collective-permute-start | bytes 884744 | tf_op jit(solution)/shard_map/ppermute | solution.py:232
  22.9 2.5 %collective-permute-start.1 = (f32[9,64,128]{2,1,0:T(8,128)}, f32[9,64,128]{2,1,0:T(8,128)S(1)}, u32[]{:S(2)}, u32[]{:S(2)}) collective-permute-start(f32[9,64,128]{2,1,0:T(8,128)} %get-tuple-element.40), channel_id=1, source_target_pairs={{0,28},{4,8},{8,4},{12,16},{16,12},{20,24},{24,20},{28,0},{1,29},{... | collective-permute-start | bytes 884744 | tf_op jit(solution)/shard_map/ppermute | solution.py:232
  27.5 4.1 %collective-permute-start.2 = (f32[9,64,128]{2,1,0:T(8,128)}, f32[9,64,128]{2,1,0:T(8,128)S(1)}, u32[]{:S(2)}, u32[]{:S(2)}) collective-permute-start(f32[9,64,128]{2,1,0:T(8,128)} %get-tuple-element.39), channel_id=1, source_target_pairs={{0,24},{4,12},{8,0},{12,20},{16,8},{20,28},{24,16},{28,4},{1,25},{... | collective-permute-start | bytes 884744 | tf_op jit(solution)/shard_map/ppermute | solution.py:233
  32.8 3.6 %collective-permute-done.9.slanted = f32[9,64,128]{2,1,0:T(8,128)S(1)} collective-permute-done((f32[9,64,128]{2,1,0:T(8,128)}, f32[9,64,128]{2,1,0:T(8,128)S(1)}, u32[]{:S(2)}, u32[]{:S(2)}) %collective-permute-start.9) | collective-permute-done | bytes 294944 | tf_op jit(solution)/shard_map/ppermute | solution.py:232
  36.4 11.3 %collective-permute-done.8.swapped = f32[12,64,128]{2,1,0:T(8,128)S(1)} collective-permute-done((f32[12,64,128]{2,1,0:T(8,128)}, f32[12,64,128]{2,1,0:T(8,128)S(1)}, u32[]{:S(2)}, u32[]{:S(2)}) %collective-permute-start.8) | collective-permute-done | bytes 393248 | tf_op jit(solution)/shard_map/ppermute | solution.py:231
  47.7 4.7 %shard_map.29 = (f32[12,16,128]{2,1,0:T(8,128)S(1)}, f32[12,16,128]{2,1,0:T(8,128)S(1)}, f32[12,16,128]{2,1,0:T(8,128)S(1)}, f32[12,16,128]{2,1,0:T(8,128)S(1)},...) custom-call(s32[2]{0:T(128)S(1)} %pad_add_fusion.place, ...), custom_call_target="tpu_custom_call" | custom-call | tf_op jit(solution)/shard_map/pallas_call | solution.py:140
  56.2 4.7 %shard_map.28 = (f32[12,16,128]{2,1,0:T(8,128)S(1)}, f32[12,16,128]{2,1,0:T(8,128)S(1)}, f32[12,16,128]{2,1,0:T(8,128)S(1)}, f32[12,16,128]{2,1,0:T(8,128)S(1)},...) custom-call(s32[2]{0:T(128)S(1)} %pad_add_fusion.place, ...), custom_call_target="tpu_custom_call" | custom-call | tf_op jit(solution)/shard_map/pallas_call | solution.py:140
  61.0 3.1 %collective-permute-start.24 = (f32[12,16,128]{2,1,0:T(8,128)S(1)}, f32[12,16,128]{2,1,0:T(8,128)S(1)}, u32[]{:S(2)}, u32[]{:S(2)}) collective-permute-start(f32[12,16,128]{2,1,0:T(8,128)S(1)} %get-tuple-element.36), channel_id=1, source_target_pairs={{0,7},{4,3},{1,6},{5,2},{2,5},{6,1},{3,4},{7,0},{8,15},{12,11},{9,... | collective-permute-start | bytes 294920 | tf_op jit(solution)/shard_map/ppermute | solution.py:250
  68.1 2.7 %collective-permute-start.19 = (f32[12,16,128]{2,1,0:T(8,128)S(1)}, f32[12,16,128]{2,1,0:T(8,128)S(1)}, u32[]{:S(2)}, u32[]{:S(2)}) collective-permute-start(f32[12,16,128]{2,1,0:T(8,128)S(1)} %get-tuple-element.31), channel_id=1, source_target_pairs={{0,6},{4,2},{1,7},{5,3},{2,4},{6,0},{3,5},{7,1},{8,14},{12,10},{9,... | collective-permute-start | bytes 294920 | tf_op jit(solution)/shard_map/ppermute | solution.py:250
  70.8 2.1 %collective-permute-start.23 = (f32[12,16,128]{2,1,0:T(8,128)S(1)}, f32[12,16,128]{2,1,0:T(8,128)S(1)}, u32[]{:S(2)}, u32[]{:S(2)}) collective-permute-start(f32[12,16,128]{2,1,0:T(8,128)S(1)} %get-tuple-element.35), channel_id=1, source_target_pairs={{0,7},{4,3},{1,6},{5,2},{2,5},{6,1},{3,4},{7,0},{8,15},{12,11},{9,... | collective-permute-start | bytes 294920 | tf_op jit(solution)/shard_map/ppermute | solution.py:250
  72.9 4.9 %collective-permute-done.17.refs_8_ = f32[12,16,128]{2,1,0:T(8,128)S(1)} collective-permute-done((f32[12,16,128]{2,1,0:T(8,128)S(1)}, f32[12,16,128]{2,1,0:T(8,128)S(1)}, u32[]{:S(2)}, u32[]{:S(2)}) %collective-permute-start.17) | collective-permute-done | bytes 98336 | tf_op jit(solution)/shard_map/ppermute | solution.py:250
  79.2 2.2 %fusion.5 = f32[16,16]{1,0:T(8,128)S(1)} fusion(f32[16,24576]{1,0:T(8,128)S(1)} %reshape.12), kind=kOutput, calls=%fused_computation.33 | convolution fusion | flops 75497472 | bytes 1573888 | tf_op jit(solution)/shard_map/dot_general | solution.py:184
  81.6 10.7 %all_to_all.28 = f32[32,1,256]{2,1,0:T(1,128)S(1)} all-to-all(f32[32,1,256]{2,1,0:T(1,128)S(1)} %reshape.14), channel_id=1, replica_groups=mesh['pair'=4,'side'=2,'orb'=4] {'pair','side','orb'}, dimensions={0} | all-to-all | bytes 65536 | tf_op jit(solution)/shard_map/all_to_all | solution.py:185
  94.5 3.1 %shard_map.31 = f32[16,16]{1,0:T(8,128)} custom-call(f32[32,16,16]{2,1,0:T(8,128)} %reshape.15.copies), custom_call_target="tpu_custom_call" | custom-call | tf_op jit(solution)/shard_map/pallas_call | solution.py:186
  97.5 2.1 %fusion.6 = f32[16,24576]{1,0:T(8,128)S(1)} fusion(f32[16,16]{1,0:T(8,128)} %shard_map.31, f32[16,24576]{1,0:T(8,128)S(1)} %reshape.12), kind=kOutput, calls=%fused_computation.34 | convolution fusion | flops 75497472 | bytes 3146752 | tf_op jit(solution)/shard_map/dot_general | solution.py:192
  99.7 2.2 %fusion.7 = f32[16,16]{1,0:T(8,128)S(1)} fusion(f32[16,24576]{1,0:T(8,128)S(1)} %fusion.6), kind=kOutput, calls=%fused_computation.35 | convolution fusion | flops 75497472 | bytes 1573888 | tf_op jit(solution)/shard_map/dot_general | solution.py:184
  102.1 9.0 %all_to_all.29 = f32[32,1,256]{2,1,0:T(1,128)S(1)} all-to-all(f32[32,1,256]{2,1,0:T(1,128)S(1)} %reshape.16), channel_id=1, replica_groups=mesh['pair'=4,'side'=2,'orb'=4] {'pair','side','orb'}, dimensions={0} | all-to-all | bytes 65536 | tf_op jit(solution)/shard_map/all_to_all | solution.py:185
  112.7 3.1 %shard_map.32 = f32[16,16]{1,0:T(8,128)} custom-call(f32[32,16,16]{2,1,0:T(8,128)} %reshape.17.copies), custom_call_target="tpu_custom_call" | custom-call | tf_op jit(solution)/shard_map/pallas_call | solution.py:186
  115.7 2.1 %convolution_bitcast_fusion = f32[2,8,192,128]{3,1,2,0:T(8,128)S(1)} fusion(f32[16,16]{1,0:T(8,128)} %shard_map.32, f32[16,24576]{1,0:T(8,128)S(1)} %fusion.6), kind=kOutput, calls=%fused_computation | convolution fusion | flops 75497472 | bytes 3146752 | tf_op jit(solution)/shard_map/dot_general | solution.py:192
  118.2 22.5 %all_to_all.30 = f32[16,12,16,128]{3,2,1,0:T(8,128)S(1)} all-to-all(f32[16,12,16,128]{3,2,1,0:T(8,128)S(1)} %bitcast.32), channel_id=1, replica_groups=mesh['pair'=4,'side'=2,'orb'=4] {'orb'}, dimensions={0} | all-to-all | bytes 3145728 | tf_op jit(solution)/shard_map/all_to_all | solution.py:267
  (67 shorter events, 26.9 us)
Async XLA Ops:
  1.0 7.9 %collective-permute-start.3 = (f32[12,16,128]{2,1,0:T(8,128)S(1)}, f32[12,16,128]{2,1,0:T(8,128)S(1)}, u32[]{:S(2)}, u32[]{:S(2)}) collective-permute-start(f32[12,16,128]{2,1,0:T(8,128)S(1)} %constant_dynamic-slice_fusion.1), channel_id=1, source_target_pairs={{0,4},{4,0},{1,5},{5,1},{2,6},{6,2},{3,7},{7,3},{8,12},{12,8},{9,1... | collective-permute-start | bytes 294920 | tf_op jit(solution)/shard_map/ppermute | solution.py:211
  4.9 7.2 %collective-permute-start.4 = (f32[6,16,128]{2,1,0:T(8,128)S(1)}, f32[6,16,128]{2,1,0:T(8,128)S(1)}, u32[]{:S(2)}, u32[]{:S(2)}) collective-permute-start(f32[6,16,128]{2,1,0:T(8,128)S(1)} %constant_dynamic-slice_fusion), channel_id=1, source_target_pairs={{0,28},{4,8},{8,4},{12,16},{16,12},{20,24},{24,20},{28,0},{1,29},{... | collective-permute-start | bytes 147464 | tf_op jit(solution)/shard_map/ppermute | solution.py:212
  8.5 4.1 %collective-permute-start.5 = (f32[6,16,128]{2,1,0:T(8,128)S(1)}, f32[6,16,128]{2,1,0:T(8,128)S(1)}, u32[]{:S(2)}, u32[]{:S(2)}) collective-permute-start(f32[6,16,128]{2,1,0:T(8,128)S(1)} %constant_dynamic-slice_fusion), channel_id=1, source_target_pairs={{0,24},{4,12},{8,0},{12,20},{16,8},{20,28},{24,16},{28,4},{1,25},{... | collective-permute-start | bytes 147464 | tf_op jit(solution)/shard_map/ppermute | solution.py:213
  14.8 16.8 %collective-permute-start.7 = (f32[24,32,128]{2,1,0:T(8,128)}, f32[24,32,128]{2,1,0:T(8,128)}, u32[]{:S(2)}, u32[]{:S(2)}) collective-permute-start(f32[24,32,128]{2,1,0:T(8,128)} %pad_maximum_fusion.1), channel_id=1, source_target_pairs={{0,2},{1,3},{2,0},{3,1},{4,6},{5,7},{6,4},{7,5},{8,10},{9,11},{10,... | collective-permute-start | bytes 1179656 | tf_op jit(solution)/shard_map/ppermute | solution.py:218
  17.4 10.1 %collective-permute-start.10 = (f32[9,64,128]{2,1,0:T(8,128)}, f32[9,64,128]{2,1,0:T(8,128)S(1)}, u32[]{:S(2)}, u32[]{:S(2)}) collective-permute-start(f32[9,64,128]{2,1,0:T(8,128)} %get-tuple-element.37), channel_id=1, source_target_pairs={{0,24},{4,12},{8,0},{12,20},{16,8},{20,28},{24,16},{28,4},{1,25},{... | collective-permute-start | bytes 884744 | tf_op jit(solution)/shard_map/ppermute | solution.py:233
  19.7 16.7 %collective-permute-start.9 = (f32[9,64,128]{2,1,0:T(8,128)}, f32[9,64,128]{2,1,0:T(8,128)S(1)}, u32[]{:S(2)}, u32[]{:S(2)}) collective-permute-start(f32[9,64,128]{2,1,0:T(8,128)} %get-tuple-element.38), channel_id=1, source_target_pairs={{0,28},{4,8},{8,4},{12,16},{16,12},{20,24},{24,20},{28,0},{1,29},{... | collective-permute-start | bytes 884744 | tf_op jit(solution)/shard_map/ppermute | solution.py:232
  22.9 24.8 %collective-permute-start.8 = (f32[12,64,128]{2,1,0:T(8,128)}, f32[12,64,128]{2,1,0:T(8,128)S(1)}, u32[]{:S(2)}, u32[]{:S(2)}) collective-permute-start(f32[12,64,128]{2,1,0:T(8,128)} %get-tuple-element.41), channel_id=1, source_target_pairs={{0,4},{4,0},{1,5},{5,1},{2,6},{6,2},{3,7},{7,3},{8,12},{12,8},{9,1... | collective-permute-start | bytes 1179656 | tf_op jit(solution)/shard_map/ppermute | solution.py:231
  22.9 29.7 %collective-permute-start.1 = (f32[9,64,128]{2,1,0:T(8,128)}, f32[9,64,128]{2,1,0:T(8,128)S(1)}, u32[]{:S(2)}, u32[]{:S(2)}) collective-permute-start(f32[9,64,128]{2,1,0:T(8,128)} %get-tuple-element.40), channel_id=1, source_target_pairs={{0,28},{4,8},{8,4},{12,16},{16,12},{20,24},{24,20},{28,0},{1,29},{... | collective-permute-start | bytes 884744 | tf_op jit(solution)/shard_map/ppermute | solution.py:232
  27.5 27.2 %collective-permute-start.2 = (f32[9,64,128]{2,1,0:T(8,128)}, f32[9,64,128]{2,1,0:T(8,128)S(1)}, u32[]{:S(2)}, u32[]{:S(2)}) collective-permute-start(f32[9,64,128]{2,1,0:T(8,128)} %get-tuple-element.39), channel_id=1, source_target_pairs={{0,24},{4,12},{8,0},{12,20},{16,8},{20,28},{24,16},{28,4},{1,25},{... | collective-permute-start | bytes 884744 | tf_op jit(solution)/shard_map/ppermute | solution.py:233
  31.6 23.9 %collective-permute-start = (f32[12,64,128]{2,1,0:T(8,128)}, f32[12,64,128]{2,1,0:T(8,128)S(1)}, u32[]{:S(2)}, u32[]{:S(2)}) collective-permute-start(f32[12,64,128]{2,1,0:T(8,128)} %get-tuple-element.42), channel_id=1, source_target_pairs={{0,4},{4,0},{1,5},{5,1},{2,6},{6,2},{3,7},{7,3},{8,12},{12,8},{9,1... | collective-permute-start | bytes 1179656 | tf_op jit(solution)/shard_map/ppermute | solution.py:231
  52.4 8.4 %collective-permute-start.12 = (f32[12,16,128]{2,1,0:T(8,128)S(1)}, f32[12,16,128]{2,1,0:T(8,128)S(1)}, u32[]{:S(2)}, u32[]{:S(2)}) collective-permute-start(f32[12,16,128]{2,1,0:T(8,128)S(1)} %get-tuple-element.24), channel_id=1, source_target_pairs={{0,4},{4,0},{1,5},{5,1},{2,6},{6,2},{3,7},{7,3},{8,12},{12,8},{9,1... | collective-permute-start | bytes 294920 | tf_op jit(solution)/shard_map/ppermute | solution.py:250
  52.5 8.5 %collective-permute-start.14 = (f32[12,16,128]{2,1,0:T(8,128)S(1)}, f32[12,16,128]{2,1,0:T(8,128)S(1)}, u32[]{:S(2)}, u32[]{:S(2)}) collective-permute-start(f32[12,16,128]{2,1,0:T(8,128)S(1)} %get-tuple-element.26), channel_id=1, source_target_pairs={{0,1},{4,5},{1,0},{5,4},{2,3},{6,7},{3,2},{7,6},{8,9},{12,13},{9,8... | collective-permute-start | bytes 294920 | tf_op jit(solution)/shard_map/ppermute | solution.py:250
  52.6 11.5 %collective-permute-start.16 = (f32[12,16,128]{2,1,0:T(8,128)S(1)}, f32[12,16,128]{2,1,0:T(8,128)S(1)}, u32[]{:S(2)}, u32[]{:S(2)}) collective-permute-start(f32[12,16,128]{2,1,0:T(8,128)S(1)} %get-tuple-element.28), channel_id=1, source_target_pairs={{0,5},{4,1},{1,4},{5,0},{2,7},{6,3},{3,6},{7,2},{8,13},{12,9},{9,1... | collective-permute-start | bytes 294920 | tf_op jit(solution)/shard_map/ppermute | solution.py:250
  54.6 9.5 %collective-permute-start.18 = (f32[12,16,128]{2,1,0:T(8,128)S(1)}, f32[12,16,128]{2,1,0:T(8,128)S(1)}, u32[]{:S(2)}, u32[]{:S(2)}) collective-permute-start(f32[12,16,128]{2,1,0:T(8,128)S(1)} %get-tuple-element.30), channel_id=1, source_target_pairs={{0,2},{4,6},{1,3},{5,7},{2,0},{6,4},{3,1},{7,5},{8,10},{12,14},{9,... | collective-permute-start | bytes 294920 | tf_op jit(solution)/shard_map/ppermute | solution.py:250
  55.5 8.6 %collective-permute-start.20 = (f32[12,16,128]{2,1,0:T(8,128)S(1)}, f32[12,16,128]{2,1,0:T(8,128)S(1)}, u32[]{:S(2)}, u32[]{:S(2)}) collective-permute-start(f32[12,16,128]{2,1,0:T(8,128)S(1)} %get-tuple-element.32), channel_id=1, source_target_pairs={{0,6},{4,2},{1,7},{5,3},{2,4},{6,0},{3,5},{7,1},{8,14},{12,10},{9,... | collective-permute-start | bytes 294920 | tf_op jit(solution)/shard_map/ppermute | solution.py:250
  60.9 7.0 %collective-permute-start.22 = (f32[12,16,128]{2,1,0:T(8,128)S(1)}, f32[12,16,128]{2,1,0:T(8,128)S(1)}, u32[]{:S(2)}, u32[]{:S(2)}) collective-permute-start(f32[12,16,128]{2,1,0:T(8,128)S(1)} %get-tuple-element.34), channel_id=1, source_target_pairs={{0,3},{4,7},{1,2},{5,6},{2,1},{6,5},{3,0},{7,4},{8,11},{12,15},{9,... | collective-permute-start | bytes 294920 | tf_op jit(solution)/shard_map/ppermute | solution.py:250
  61.0 7.2 %collective-permute-start.24 = (f32[12,16,128]{2,1,0:T(8,128)S(1)}, f32[12,16,128]{2,1,0:T(8,128)S(1)}, u32[]{:S(2)}, u32[]{:S(2)}) collective-permute-start(f32[12,16,128]{2,1,0:T(8,128)S(1)} %get-tuple-element.36), channel_id=1, source_target_pairs={{0,7},{4,3},{1,6},{5,2},{2,5},{6,1},{3,4},{7,0},{8,15},{12,11},{9,... | collective-permute-start | bytes 294920 | tf_op jit(solution)/shard_map/ppermute | solution.py:250
  64.1 6.7 %collective-permute-start.11 = (f32[12,16,128]{2,1,0:T(8,128)S(1)}, f32[12,16,128]{2,1,0:T(8,128)S(1)}, u32[]{:S(2)}, u32[]{:S(2)}) collective-permute-start(f32[12,16,128]{2,1,0:T(8,128)S(1)} %get-tuple-element.23), channel_id=1, source_target_pairs={{0,4},{4,0},{1,5},{5,1},{2,6},{6,2},{3,7},{7,3},{8,12},{12,8},{9,1... | collective-permute-start | bytes 294920 | tf_op jit(solution)/shard_map/ppermute | solution.py:250
  64.2 6.7 %collective-permute-start.13 = (f32[12,16,128]{2,1,0:T(8,128)S(1)}, f32[12,16,128]{2,1,0:T(8,128)S(1)}, u32[]{:S(2)}, u32[]{:S(2)}) collective-permute-start(f32[12,16,128]{2,1,0:T(8,128)S(1)} %get-tuple-element.25), channel_id=1, source_target_pairs={{0,1},{4,5},{1,0},{5,4},{2,3},{6,7},{3,2},{7,6},{8,9},{12,13},{9,8... | collective-permute-start | bytes 294920 | tf_op jit(solution)/shard_map/ppermute | solution.py:250
  64.2 8.7 %collective-permute-start.15 = (f32[12,16,128]{2,1,0:T(8,128)S(1)}, f32[12,16,128]{2,1,0:T(8,128)S(1)}, u32[]{:S(2)}, u32[]{:S(2)}) collective-permute-start(f32[12,16,128]{2,1,0:T(8,128)S(1)} %get-tuple-element.27), channel_id=1, source_target_pairs={{0,5},{4,1},{1,4},{5,0},{2,7},{6,3},{3,6},{7,2},{8,13},{12,9},{9,1... | collective-permute-start | bytes 294920 | tf_op jit(solution)/shard_map/ppermute | solution.py:250
  67.9 9.9 %collective-permute-start.17 = (f32[12,16,128]{2,1,0:T(8,128)S(1)}, f32[12,16,128]{2,1,0:T(8,128)S(1)}, u32[]{:S(2)}, u32[]{:S(2)}) collective-permute-start(f32[12,16,128]{2,1,0:T(8,128)S(1)} %get-tuple-element.29), channel_id=1, source_target_pairs={{0,2},{4,6},{1,3},{5,7},{2,0},{6,4},{3,1},{7,5},{8,10},{12,14},{9,... | collective-permute-start | bytes 294920 | tf_op jit(solution)/shard_map/ppermute | solution.py:250
  68.1 9.6 %collective-permute-start.19 = (f32[12,16,128]{2,1,0:T(8,128)S(1)}, f32[12,16,128]{2,1,0:T(8,128)S(1)}, u32[]{:S(2)}, u32[]{:S(2)}) collective-permute-start(f32[12,16,128]{2,1,0:T(8,128)S(1)} %get-tuple-element.31), channel_id=1, source_target_pairs={{0,6},{4,2},{1,7},{5,3},{2,4},{6,0},{3,5},{7,1},{8,14},{12,10},{9,... | collective-permute-start | bytes 294920 | tf_op jit(solution)/shard_map/ppermute | solution.py:250
  70.8 7.4 %collective-permute-start.21 = (f32[12,16,128]{2,1,0:T(8,128)S(1)}, f32[12,16,128]{2,1,0:T(8,128)S(1)}, u32[]{:S(2)}, u32[]{:S(2)}) collective-permute-start(f32[12,16,128]{2,1,0:T(8,128)S(1)} %get-tuple-element.33), channel_id=1, source_target_pairs={{0,3},{4,7},{1,2},{5,6},{2,1},{6,5},{3,0},{7,4},{8,11},{12,15},{9,... | collective-permute-start | bytes 294920 | tf_op jit(solution)/shard_map/ppermute | solution.py:250
  70.8 7.4 %collective-permute-start.23 = (f32[12,16,128]{2,1,0:T(8,128)S(1)}, f32[12,16,128]{2,1,0:T(8,128)S(1)}, u32[]{:S(2)}, u32[]{:S(2)}) collective-permute-start(f32[12,16,128]{2,1,0:T(8,128)S(1)} %get-tuple-element.35), channel_id=1, source_target_pairs={{0,7},{4,3},{1,6},{5,2},{2,5},{6,1},{3,4},{7,0},{8,15},{12,11},{9,... | collective-permute-start | bytes 294920 | tf_op jit(solution)/shard_map/ppermute | solution.py:250
  (3 other events, 33.9 us)

commit v4 on v3

--- a/solution.py
+++ b/solution.py
@@ -23,6 +23,7 @@
 
 VMEM = pl.BlockSpec(memory_space=pltpu.VMEM)
 SMEM = pl.BlockSpec(memory_space=pltpu.SMEM)
+HBM = pl.BlockSpec(memory_space=pltpu.HBM)
 
 kinetic = -0.5 / (spacing * spacing)
 taps = tuple(kinetic * c / filter_half for c in coefficients)
@@ -30,6 +31,46 @@
 whole_taps = tuple(round(denominator * c) for c in coefficients)
 lane_scale = kinetic / filter_half / denominator
 shift = (kinetic * 2.0 * coefficients[0] - filter_centre) / filter_half
+
+
+def pack_kernel(place, orbitals, potential, *rest):
+    outs, sems = rest[:-1], rest[-1]
+    side, orb = place[0], place[2]
+    kept, rows = orbitals.shape[0] // 2, orbitals.shape[1]
+    part = outs[0].shape[1]
+    columns = pl.ds(pl.multiple_of(orb * part, part), part)
+    edge, shallow = pl.ds(side * (rows - DEEP), DEEP), pl.ds(side * (rows - WIDE), WIDE)
+    sources = [potential.at[:, columns], potential.at[shallow, columns]]
+    for at in range(kept):
+        given, stays = orbitals.at[(1 - side) * kept + at], orbitals.at[side * kept + at]
+        sources += [given.at[edge], given, stays.at[edge]]
+    copies = [pltpu.make_async_copy(a, b, sems.at[i]) for i, (a, b) in enumerate(zip(sources, outs))]
+    for copy in copies:
+        copy.start()
+    for copy in copies:
+        copy.wait()
+
+
+def packed(place, orbitals, potential, orb_count):
+    held, rows, cols, width = orbitals.shape
+    part = cols // orb_count
+    shapes = [(rows, part, width), (WIDE, part, width)]
+    shapes += [(DEEP, cols, width), (rows, cols, width), (DEEP, cols, width)] * (held // 2)
+    return pl.pallas_call(
+        pack_kernel,
+        out_shape=[jax.ShapeDtypeStruct(shape, jnp.float32) for shape in shapes],
+        in_specs=[SMEM, HBM, HBM],
+        out_specs=[VMEM] * len(shapes),
+        scratch_shapes=[pltpu.SemaphoreType.DMA((len(shapes),))],
+        compiler_params=pltpu.CompilerParams(vmem_limit_bytes=16 * 1024 * 1024),
+    )(place, orbitals, potential)
+
+
+def join_kernel(swapped, slanted, straight, out):
+    rows = swapped.shape[0]
+    out[pl.ds(0, rows)] = swapped[...]
+    out[pl.ds(rows, WIDE)] = slanted[...]
+    out[pl.ds(rows + WIDE, WIDE)] = straight[...]
 
 
 def split_dot(values, table):
@@ -44,9 +85,10 @@
     )
 
 
-def filter_kernel(at, place, own, swapped, slanted, straight, own_pot, pot_far, lane_table, *rest):
-    outs, (field, first, second, weight, sorted_pieces) = rest[:-5], rest[-5:]
-    side, me = place[0], place[1]
+def filter_kernel(at, shares, place, own, swapped, slanted, straight, own_pot, lane_table, *rest):
+    pot_far, outs = rest[:shares], rest[shares:-5]
+    field, first, second, weight, sorted_pieces = rest[-5:]
+    side, me, orb = place[0], place[1], place[2]
     rows, cols, _ = swapped.shape
     both = 2 * rows
     strips = cols // EIGHT
@@ -76,9 +118,12 @@
         return values * (1.0 / filter_half) + shift
 
     weight[pl.ds(WIDE + side * rows, rows)] = weigh(own_pot[...])
-    weight[pl.ds(WIDE + (1 - side) * rows, rows)] = weigh(pot_far[pl.ds(0, rows)])
-    weight[pl.ds(side * (both + WIDE), WIDE)] = weigh(pot_far[pl.ds(rows, WIDE)])
-    weight[pl.ds((1 - side) * (both + WIDE), WIDE)] = weigh(pot_far[pl.ds(rows + WIDE, WIDE)])
+    part = cols // shares
+    for apart, far in enumerate(pot_far):
+        columns = pl.ds(pl.multiple_of((orb ^ apart) * part, part), part)
+        weight[pl.ds(WIDE + (1 - side) * rows, rows), columns] = weigh(far[pl.ds(0, rows)])
+        weight[pl.ds(side * (both + WIDE), WIDE), columns] = weigh(far[pl.ds(rows, WIDE)])
+        weight[pl.ds((1 - side) * (both + WIDE), WIDE), columns] = weigh(far[pl.ds(rows + WIDE, WIDE)])
 
     def step(source, before, before_at, weight_at, total, store):
         width = source.shape[2]
@@ -124,8 +169,8 @@
         out[...] = sorted_pieces[me ^ apart]
 
 
-def filtered_pieces(at, place, own, swapped, slanted, straight, own_pot, pot_far, group):
-    rows, cols, width = swapped.shape
+def filtered_pieces(at, place, own, slanted_order, own_pot, pot_far, group):
+    rows, cols, width = own.shape[1:]
     both = 2 * rows
     apart = jnp.arange(width)[:, None] - jnp.arange(width)[None, :]
     lane_table = jnp.zeros((width, width), jnp.float32)
@@ -138,9 +183,9 @@
 
     piece = (rows, 2 * cols // group, width)
     return pl.pallas_call(
-        functools.partial(filter_kernel, at),
+        functools.partial(filter_kernel, at, len(pot_far)),
         out_shape=[jax.ShapeDtypeStruct(piece, jnp.float32)] * group,
-        in_specs=[SMEM] + [VMEM] * 7,
+        in_specs=[SMEM] + [VMEM] * (6 + len(pot_far)),
         out_specs=[VMEM] * group,
         scratch_shapes=[
             scratch(DEEP),
@@ -150,7 +195,7 @@
             pltpu.VMEM((group,) + piece, jnp.float32),
         ],
         compiler_params=pltpu.CompilerParams(vmem_limit_bytes=24 * 1024 * 1024),
-    )(place, own, swapped, slanted, straight, own_pot, pot_far, lane_table.astype(jnp.bfloat16))
+    )(place, own, slanted_order[1], slanted_order[0], slanted_order[2], own_pot, lane_table.astype(jnp.bfloat16), *pot_far)
 
 
 def sort_kernel(place, *refs):
@@ -205,50 +250,51 @@
     swap = [(0, 1), (1, 0)]
     slab_axes = ("pair", "side")
 
-    mine = lax.dynamic_slice_in_dim(potential, orb * part, part, axis=1)
-    edge = lax.dynamic_slice_in_dim(mine, side * (rows - WIDE), WIDE, axis=0)
-    pot_far = [
+    group = 2 * orb_count
+    me = 2 * orb + side
+
+    def flat_of(index):
+        return (index % 2) * orb_count + index // 2
+
+    place = jnp.stack([side, me, orb]).astype(jnp.int32)
+    mine, edge, *sent = packed(place, orbitals, potential, orb_count)
+
+    pieces = [
         lax.ppermute(mine, "side", swap),
         lax.ppermute(edge, slab_axes, slant),
         lax.ppermute(edge, slab_axes, ahead),
     ]
-    pot_far = jnp.concatenate(pot_far, axis=0)
-    reach = 1
-    while reach < orb_count:
-        other = lax.ppermute(pot_far, "orb", [(i, i ^ reach) for i in range(orb_count)])
-        low = (orb // reach) % 2 == 0
-        pot_far = jnp.concatenate([jnp.where(low, pot_far, other), jnp.where(low, other, pot_far)], axis=1)
-        reach *= 2
+    joined = pl.pallas_call(
+        join_kernel,
+        out_shape=jax.ShapeDtypeStruct((rows + 2 * WIDE, part, width), jnp.float32),
+        in_specs=[VMEM] * 3,
+        out_specs=VMEM,
+        compiler_params=pltpu.CompilerParams(vmem_limit_bytes=16 * 1024 * 1024),
+    )(*pieces)
+    pot_far = [joined] + [
+        lax.ppermute(joined, "orb", [(i, i ^ m) for i in range(orb_count)]) for m in range(1, orb_count)
+    ]
 
     fetched = []
     for at in range(kept):
-        given = lax.dynamic_index_in_dim(orbitals, (1 - side) * kept + at, 0, keepdims=False)
-        given_edge = lax.dynamic_slice_in_dim(given, side * (rows - DEEP), DEEP, axis=0)
-        stays = lax.dynamic_index_in_dim(orbitals, side * kept + at, 0, keepdims=False)
-        stays_edge = lax.dynamic_slice_in_dim(stays, side * (rows - DEEP), DEEP, axis=0)
         fetched.append(
             (
-                lax.ppermute(given, "side", swap),
-                lax.ppermute(given_edge, slab_axes, slant),
-                lax.ppermute(stays_edge, slab_axes, ahead),
+                lax.ppermute(sent[3 * at], slab_axes, slant),
+                lax.ppermute(sent[3 * at + 1], "side", swap),
+                lax.ppermute(sent[3 * at + 2], slab_axes, ahead),
             )
         )
 
-    group = 2 * orb_count
-    me = 2 * orb + side
-
-    def flat_of(index):
-        return (index % 2) * orb_count + index // 2
-
-    place = jnp.stack([side, me]).astype(jnp.int32)
     returned = []
+    order = sorted(range(1, group), key=lambda m: (-(m // 4 > 0) - m % 2, m))
+    spot = {m: 1 + index for index, m in enumerate(order)} | {0: 0}
     for at in range(kept):
-        pieces = filtered_pieces(at, place, orbitals, *fetched[at], potential, pot_far, group)
+        pieces = filtered_pieces(at, place, orbitals, fetched[at], potential, pot_far, group)
         returned.append(
             [pieces[0]]
             + [
                 lax.ppermute(pieces[m], ("side", "orb"), [(flat_of(i), flat_of(i ^ m)) for i in range(group)])
-                for m in range(1, group)
+                for m in order
             ]
         )
     grouped = pl.pallas_call(
@@ -257,7 +303,7 @@
         in_specs=[SMEM] + [VMEM] * (group * kept),
         out_specs=VMEM,
         compiler_params=pltpu.CompilerParams(vmem_limit_bytes=16 * 1024 * 1024),
-    )(place, *[returned[at][m] for m in range(group) for at in range(kept)])
+    )(place, *[returned[at][spot[m]] for m in range(group) for at in range(kept)])
     total = held * orb_count
     devices = slabs * orb_count
     flat = grouped.reshape(total, -1)

time: 142 us -> 139 us (0.979)
  Pallas kernels: 16.1 us -> 18.5 us
  other arithmetic: 3.7 us -> 1.68 us
  waiting for transfers between devices: 29.3 us -> 27.5 us
  local copies, waits for them, and re-layouts: 8.53 us -> 6.99 us
    ppermute x8 -> x9, waiting for transfers between devices: 18.6 us -> 11.4 us  [the longest x2 4.36 us: whole(): lax.ppermute(sent[3 * at + 2], slab_axes, ahead)]
    ppermute x1, waiting for transfers between devices: 3.16 us -> 6.22 us  [whole(): lax.ppermute(edge, slab_axes, slant)]
    dynamic_slice x3 -> x0, local copies, waits for them, and re-layouts: 2.96 us -> none  [the longest x1 1.04 us: whole(): lax.dynamic_slice_in_dim(stays, side * (rows - DEEP), DEEP, axis=0)]
    ppermute x14, waiting for transfers between devices: 7.03 us -> 9.87 us  [whole(): lax.ppermute(pieces[m], ('side', 'orb'), [(flat_of(i), flat_of(i ^ m)) fo...]
    ppermute x1, starting transfers between devices: 3.57 us -> 1.15 us  [whole(): lax.ppermute(edge, slab_axes, slant)]
    unnamed x11 -> x13, local copies, waits for them, and re-layouts: 2.28 us -> 4.67 us
    pallas_call x2 -> x4, Pallas kernels: 9.36 us -> 11.7 us  [the longest x2 10.4 us: filtered_pieces(): pl.pallas_call(functools.partial(filter_kernel, at, len(pot_far)), out_sh...]
    ppermute x14, starting transfers between devices: 13.6 us -> 11.7 us  [whole(): lax.ppermute(pieces[m], ('side', 'orb'), [(flat_of(i), flat_of(i ^ m)) fo...]
  transfers between devices with their start and end apart: 25 -> 26, of which waited for: 10 -> 9; matrix products, arithmetic and copies ran while one was open for 3% -> 0% of each run, Pallas kernels for 7% -> 8%
where the time goes in v4:
time: 139 us; the launch traced here: 138 us
  blocking collectives  43 us (31%)
  starting transfers between devices  32 us (23%)
  waiting for transfers between devices  27.5 us (20%)
  Pallas kernels  18.5 us (13%)
  matrix products  8.51 us (6%)
  local copies, waits for them, and re-layouts  6.99 us (5%)
  other arithmetic  1.68 us (1%)
    all_to_all x1, blocking collectives, whole(): return lax.all_to_all(basis, 'orb', split_axis=0, concat_axis=2, tiled=True)  22.5 us
    all_to_all x2, blocking collectives, orthonormal(): lax.all_to_all(jnp.broadcast_to(local_gram[None], (devices, total, total)...  20.5 us
    ppermute x14, starting transfers between devices, whole(): lax.ppermute(pieces[m], ('side', 'orb'), [(flat_of(i), flat_of(i ^ m)) fo...  11.7 us
    pallas_call x2, Pallas kernels, filtered_pieces(): pl.pallas_call(functools.partial(filter_kernel, at, len(pot_far)), out_sh...  10.4 us
    ppermute x14, waiting for transfers between devices, whole(): lax.ppermute(pieces[m], ('side', 'orb'), [(flat_of(i), flat_of(i ^ m)) fo...  9.87 us
    ppermute x2, starting transfers between devices, whole(): lax.ppermute(sent[3 * at], slab_axes, slant)  7.15 us
    ppermute x1, waiting for transfers between devices, whole(): lax.ppermute(edge, slab_axes, slant)  6.22 us
    pallas_call x2, Pallas kernels, orthonormal(): pl.pallas_call(functools.partial(factor_kernel, cell_total), out_shape=ja...  6.13 us
  transfers between devices with their start and end apart: 26, of which 9 were waited for; matrix products, arithmetic and copies ran while one was open for 0% of the time, Pallas kernels for 8%

profile of v4, /device:TPU:0, one launch (start us, length us, event | category | flops | bytes accessed | tf_op | source)
XLA Modules:
  0.0 138.3 jit_solution(18109069986319772780)
XLA Ops:
  3.8 3.0 %collective-permute-start.3 = (f32[12,16,128]{2,1,0:T(8,128)S(1)}, f32[12,16,128]{2,1,0:T(8,128)S(1)}, u32[]{:S(2)}, u32[]{:S(2)}) collective-permute-start(f32[12,16,128]{2,1,0:T(8,128)S(1)} %get-tuple-element.32), channel_id=1, source_target_pairs={{0,4},{4,0},{1,5},{5,1},{2,6},{6,2},{3,7},{7,3},{8,12},{12,8},{9,1... | collective-permute-start | bytes 294920 | tf_op jit(solution)/shard_map/ppermute | solution.py:263
  6.8 3.6 %collective-permute-start.10 = (f32[9,64,128]{2,1,0:T(8,128)S(1)}, f32[9,64,128]{2,1,0:T(8,128)S(1)}, u32[]{:S(2)}, u32[]{:S(2)}) collective-permute-start(f32[9,64,128]{2,1,0:T(8,128)S(1)} %get-tuple-element.36), channel_id=1, source_target_pairs={{0,28},{4,8},{8,4},{12,16},{16,12},{20,24},{24,20},{28,0},{1,29},{... | collective-permute-start | bytes 884744 | tf_op jit(solution)/shard_map/ppermute | solution.py:282
  13.3 6.2 %collective-permute-done.4.slanted = f32[6,16,128]{2,1,0:T(8,128)S(1)} collective-permute-done((f32[6,16,128]{2,1,0:T(8,128)S(1)}, f32[6,16,128]{2,1,0:T(8,128)S(1)}, u32[]{:S(2)}, u32[]{:S(2)}) %collective-permute-start.4) | collective-permute-done | bytes 49184 | tf_op jit(solution)/shard_map/ppermute | solution.py:264
  22.6 3.1 %collective-permute-start.11 = (f32[9,64,128]{2,1,0:T(8,128)S(1)}, f32[9,64,128]{2,1,0:T(8,128)S(1)}, u32[]{:S(2)}, u32[]{:S(2)}) collective-permute-start(f32[9,64,128]{2,1,0:T(8,128)S(1)} %get-tuple-element.37), channel_id=1, source_target_pairs={{0,24},{4,12},{8,0},{12,20},{16,8},{20,28},{24,16},{28,4},{1,25},{... | collective-permute-start | bytes 884744 | tf_op jit(solution)/shard_map/ppermute | solution.py:284
  28.6 2.0 %collective-permute-done.8.rest_3_ = f32[24,16,128]{2,1,0:T(8,128)S(1)} collective-permute-done((f32[24,16,128]{2,1,0:T(8,128)S(1)}, f32[24,16,128]{2,1,0:T(8,128)S(1)}, u32[]{:S(2)}, u32[]{:S(2)}) %collective-permute-start.8) | collective-permute-done | bytes 196640 | tf_op jit(solution)/shard_map/ppermute | solution.py:275
  30.6 3.6 %collective-permute-start.1 = (f32[9,64,128]{2,1,0:T(8,128)S(1)}, f32[9,64,128]{2,1,0:T(8,128)S(1)}, u32[]{:S(2)}, u32[]{:S(2)}) collective-permute-start(f32[9,64,128]{2,1,0:T(8,128)S(1)} %get-tuple-element.30), channel_id=1, source_target_pairs={{0,28},{4,8},{8,4},{12,16},{16,12},{20,24},{24,20},{28,0},{1,29},{... | collective-permute-start | bytes 884744 | tf_op jit(solution)/shard_map/ppermute | solution.py:282
  34.3 5.2 %shard_map.31 = (f32[12,16,128]{2,1,0:T(8,128)S(1)}, f32[12,16,128]{2,1,0:T(8,128)S(1)}, f32[12,16,128]{2,1,0:T(8,128)S(1)}, f32[12,16,128]{2,1,0:T(8,128)S(1)},...) custom-call(s32[3]{0:T(128)S(1)} %pad_add_fusion.place, ...), custom_call_target="tpu_custom_call" | custom-call | tf_op jit(solution)/shard_map/pallas_call | solution.py:185
  40.1 3.2 %collective-permute-done.1.slanted = f32[9,64,128]{2,1,0:T(8,128)S(1)} collective-permute-done((f32[9,64,128]{2,1,0:T(8,128)S(1)}, f32[9,64,128]{2,1,0:T(8,128)S(1)}, u32[]{:S(2)}, u32[]{:S(2)}) %collective-permute-start.1) | collective-permute-done | bytes 294944 | tf_op jit(solution)/shard_map/ppermute | solution.py:282
  43.2 4.4 %collective-permute-done.2.straight = f32[9,64,128]{2,1,0:T(8,128)S(1)} collective-permute-done((f32[9,64,128]{2,1,0:T(8,128)S(1)}, f32[9,64,128]{2,1,0:T(8,128)S(1)}, u32[]{:S(2)}, u32[]{:S(2)}) %collective-permute-start.2) | collective-permute-done | bytes 294944 | tf_op jit(solution)/shard_map/ppermute | solution.py:284
  49.1 2.2 %collective-permute-start.21 = (f32[12,16,128]{2,1,0:T(8,128)S(1)}, f32[12,16,128]{2,1,0:T(8,128)S(1)}, u32[]{:S(2)}, u32[]{:S(2)}) collective-permute-start(f32[12,16,128]{2,1,0:T(8,128)S(1)} %get-tuple-element.48), channel_id=1, source_target_pairs={{0,6},{4,2},{1,7},{5,3},{2,4},{6,0},{3,5},{7,1},{8,14},{12,10},{9,... | collective-permute-start | bytes 294920 | tf_op jit(solution)/shard_map/ppermute | solution.py:296
  51.3 5.2 %shard_map.30 = (f32[12,16,128]{2,1,0:T(8,128)S(1)}, f32[12,16,128]{2,1,0:T(8,128)S(1)}, f32[12,16,128]{2,1,0:T(8,128)S(1)}, f32[12,16,128]{2,1,0:T(8,128)S(1)},...) custom-call(s32[3]{0:T(128)S(1)} %pad_add_fusion.place, ...), custom_call_target="tpu_custom_call" | custom-call | tf_op jit(solution)/shard_map/pallas_call | solution.py:185
  57.8 2.0 %collective-permute-start.12 = (f32[12,16,128]{2,1,0:T(8,128)S(1)}, f32[12,16,128]{2,1,0:T(8,128)S(1)}, u32[]{:S(2)}, u32[]{:S(2)}) collective-permute-start(f32[12,16,128]{2,1,0:T(8,128)S(1)} %get-tuple-element.39), channel_id=1, source_target_pairs={{0,4},{4,0},{1,5},{5,1},{2,6},{6,2},{3,7},{7,3},{8,12},{12,8},{9,1... | collective-permute-start | bytes 294920 | tf_op jit(solution)/shard_map/ppermute | solution.py:296
  60.0 3.0 %collective-permute-done.23.refs_13_ = f32[12,16,128]{2,1,0:T(8,128)S(1)} collective-permute-done((f32[12,16,128]{2,1,0:T(8,128)S(1)}, f32[12,16,128]{2,1,0:T(8,128)S(1)}, u32[]{:S(2)}, u32[]{:S(2)}) %collective-permute-start.23) | collective-permute-done | bytes 98336 | tf_op jit(solution)/shard_map/ppermute | solution.py:296
  65.6 2.1 %collective-permute-start.24 = (f32[12,16,128]{2,1,0:T(8,128)S(1)}, f32[12,16,128]{2,1,0:T(8,128)S(1)}, u32[]{:S(2)}, u32[]{:S(2)}) collective-permute-start(f32[12,16,128]{2,1,0:T(8,128)S(1)} %get-tuple-element.51), channel_id=1, source_target_pairs={{0,7},{4,3},{1,6},{5,2},{2,5},{6,1},{3,4},{7,0},{8,15},{12,11},{9,... | collective-permute-start | bytes 294920 | tf_op jit(solution)/shard_map/ppermute | solution.py:296
  67.7 4.6 %collective-permute-done.18.refs_8_ = f32[12,16,128]{2,1,0:T(8,128)S(1)} collective-permute-done((f32[12,16,128]{2,1,0:T(8,128)S(1)}, f32[12,16,128]{2,1,0:T(8,128)S(1)}, u32[]{:S(2)}, u32[]{:S(2)}) %collective-permute-start.18) | collective-permute-done | bytes 98336 | tf_op jit(solution)/shard_map/ppermute | solution.py:296
  74.8 2.1 %fusion.5 = f32[16,16]{1,0:T(8,128)S(1)} fusion(f32[16,24576]{1,0:T(8,128)S(1)} %reshape.8), kind=kOutput, calls=%fused_computation.16 | convolution fusion | flops 75497472 | bytes 1573888 | tf_op jit(solution)/shard_map/dot_general | solution.py:229
  77.2 11.5 %all_to_all.28 = f32[32,1,256]{2,1,0:T(1,128)S(1)} all-to-all(f32[32,1,256]{2,1,0:T(1,128)S(1)} %reshape.10), channel_id=1, replica_groups=mesh['pair'=4,'side'=2,'orb'=4] {'pair','side','orb'}, dimensions={0} | all-to-all | bytes 65536 | tf_op jit(solution)/shard_map/all_to_all | solution.py:230
  90.9 3.1 %shard_map.33 = f32[16,16]{1,0:T(8,128)} custom-call(f32[32,16,16]{2,1,0:T(8,128)} %reshape.11.copies), custom_call_target="tpu_custom_call" | custom-call | tf_op jit(solution)/shard_map/pallas_call | solution.py:231
  93.9 2.1 %fusion.6 = f32[16,24576]{1,0:T(8,128)S(1)} fusion(f32[16,16]{1,0:T(8,128)} %shard_map.33, f32[16,24576]{1,0:T(8,128)S(1)} %reshape.8), kind=kOutput, calls=%fused_computation.17 | convolution fusion | flops 75497472 | bytes 3146752 | tf_op jit(solution)/shard_map/dot_general | solution.py:237
  96.1 2.1 %fusion.7 = f32[16,16]{1,0:T(8,128)S(1)} fusion(f32[16,24576]{1,0:T(8,128)S(1)} %fusion.6), kind=kOutput, calls=%fused_computation.18 | convolution fusion | flops 75497472 | bytes 1573888 | tf_op jit(solution)/shard_map/dot_general | solution.py:229
  98.4 9.0 %all_to_all.29 = f32[32,1,256]{2,1,0:T(1,128)S(1)} all-to-all(f32[32,1,256]{2,1,0:T(1,128)S(1)} %reshape.12), channel_id=1, replica_groups=mesh['pair'=4,'side'=2,'orb'=4] {'pair','side','orb'}, dimensions={0} | all-to-all | bytes 65536 | tf_op jit(solution)/shard_map/all_to_all | solution.py:230
  108.9 3.1 %shard_map.34 = f32[16,16]{1,0:T(8,128)} custom-call(f32[32,16,16]{2,1,0:T(8,128)} %reshape.13.copies), custom_call_target="tpu_custom_call" | custom-call | tf_op jit(solution)/shard_map/pallas_call | solution.py:231
  112.0 2.1 %convolution_bitcast_fusion = f32[2,8,192,128]{3,1,2,0:T(8,128)S(1)} fusion(f32[16,16]{1,0:T(8,128)} %shard_map.34, f32[16,24576]{1,0:T(8,128)S(1)} %fusion.6), kind=kOutput, calls=%fused_computation | convolution fusion | flops 75497472 | bytes 3146752 | tf_op jit(solution)/shard_map/dot_general | solution.py:237
  114.5 22.5 %all_to_all.30 = f32[16,12,16,128]{3,2,1,0:T(8,128)S(1)} all-to-all(f32[16,12,16,128]{3,2,1,0:T(8,128)S(1)} %bitcast.21), channel_id=1, replica_groups=mesh['pair'=4,'side'=2,'orb'=4] {'orb'}, dimensions={0} | all-to-all | bytes 3145728 | tf_op jit(solution)/shard_map/all_to_all | solution.py:313
  (64 shorter events, 27.2 us)
Async XLA Ops:
  3.8 15.8 %collective-permute-start.3 = (f32[12,16,128]{2,1,0:T(8,128)S(1)}, f32[12,16,128]{2,1,0:T(8,128)S(1)}, u32[]{:S(2)}, u32[]{:S(2)}) collective-permute-start(f32[12,16,128]{2,1,0:T(8,128)S(1)} %get-tuple-element.32), channel_id=1, source_target_pairs={{0,4},{4,0},{1,5},{5,1},{2,6},{6,2},{3,7},{7,3},{8,12},{12,8},{9,1... | collective-permute-start | bytes 294920 | tf_op jit(solution)/shard_map/ppermute | solution.py:263
  6.8 27.4 %collective-permute-start.10 = (f32[9,64,128]{2,1,0:T(8,128)S(1)}, f32[9,64,128]{2,1,0:T(8,128)S(1)}, u32[]{:S(2)}, u32[]{:S(2)}) collective-permute-start(f32[9,64,128]{2,1,0:T(8,128)S(1)} %get-tuple-element.36), channel_id=1, source_target_pairs={{0,28},{4,8},{8,4},{12,16},{16,12},{20,24},{24,20},{28,0},{1,29},{... | collective-permute-start | bytes 884744 | tf_op jit(solution)/shard_map/ppermute | solution.py:282
  10.4 9.2 %collective-permute-start.4 = (f32[6,16,128]{2,1,0:T(8,128)S(1)}, f32[6,16,128]{2,1,0:T(8,128)S(1)}, u32[]{:S(2)}, u32[]{:S(2)}) collective-permute-start(f32[6,16,128]{2,1,0:T(8,128)S(1)} %get-tuple-element.33), channel_id=1, source_target_pairs={{0,28},{4,8},{8,4},{12,16},{16,12},{20,24},{24,20},{28,0},{1,29},{... | collective-permute-start | bytes 147464 | tf_op jit(solution)/shard_map/ppermute | solution.py:264
  11.5 8.0 %collective-permute-start.5 = (f32[6,16,128]{2,1,0:T(8,128)S(1)}, f32[6,16,128]{2,1,0:T(8,128)S(1)}, u32[]{:S(2)}, u32[]{:S(2)}) collective-permute-start(f32[6,16,128]{2,1,0:T(8,128)S(1)} %get-tuple-element.33), channel_id=1, source_target_pairs={{0,24},{4,12},{8,0},{12,20},{16,8},{20,28},{24,16},{28,4},{1,25},{... | collective-permute-start | bytes 147464 | tf_op jit(solution)/shard_map/ppermute | solution.py:265
  19.6 7.8 %collective-permute-start.7 = (f32[24,16,128]{2,1,0:T(8,128)S(1)}, f32[24,16,128]{2,1,0:T(8,128)S(1)}, u32[]{:S(2)}, u32[]{:S(2)}) collective-permute-start(f32[24,16,128]{2,1,0:T(8,128)S(1)} %shard_map.29.rest_0_), channel_id=1, source_target_pairs={{0,2},{1,3},{2,0},{3,1},{4,6},{5,7},{6,4},{7,5},{8,10},{9,11},{10,... | collective-permute-start | bytes 589832 | tf_op jit(solution)/shard_map/ppermute | solution.py:275
  21.2 9.4 %collective-permute-start.8 = (f32[24,16,128]{2,1,0:T(8,128)S(1)}, f32[24,16,128]{2,1,0:T(8,128)S(1)}, u32[]{:S(2)}, u32[]{:S(2)}) collective-permute-start(f32[24,16,128]{2,1,0:T(8,128)S(1)} %shard_map.29.rest_0_), channel_id=1, source_target_pairs={{0,3},{1,2},{2,1},{3,0},{4,7},{5,6},{6,5},{7,4},{8,11},{9,10},{10,... | collective-permute-start | bytes 589832 | tf_op jit(solution)/shard_map/ppermute | solution.py:275
  21.5 12.8 %collective-permute-start.9 = (f32[12,64,128]{2,1,0:T(8,128)S(1)}, f32[12,64,128]{2,1,0:T(8,128)S(1)}, u32[]{:S(2)}, u32[]{:S(2)}) collective-permute-start(f32[12,64,128]{2,1,0:T(8,128)S(1)} %get-tuple-element.35), channel_id=1, source_target_pairs={{0,4},{4,0},{1,5},{5,1},{2,6},{6,2},{3,7},{7,3},{8,12},{12,8},{9,1... | collective-permute-start | bytes 1179656 | tf_op jit(solution)/shard_map/ppermute | solution.py:283
  22.6 11.7 %collective-permute-start.11 = (f32[9,64,128]{2,1,0:T(8,128)S(1)}, f32[9,64,128]{2,1,0:T(8,128)S(1)}, u32[]{:S(2)}, u32[]{:S(2)}) collective-permute-start(f32[9,64,128]{2,1,0:T(8,128)S(1)} %get-tuple-element.37), channel_id=1, source_target_pairs={{0,24},{4,12},{8,0},{12,20},{16,8},{20,28},{24,16},{28,4},{1,25},{... | collective-permute-start | bytes 884744 | tf_op jit(solution)/shard_map/ppermute | solution.py:284
  27.5 21.6 %collective-permute-start = (f32[12,64,128]{2,1,0:T(8,128)S(1)}, f32[12,64,128]{2,1,0:T(8,128)S(1)}, u32[]{:S(2)}, u32[]{:S(2)}) collective-permute-start(f32[12,64,128]{2,1,0:T(8,128)S(1)} %get-tuple-element.29), channel_id=1, source_target_pairs={{0,4},{4,0},{1,5},{5,1},{2,6},{6,2},{3,7},{7,3},{8,12},{12,8},{9,1... | collective-permute-start | bytes 1179656 | tf_op jit(solution)/shard_map/ppermute | solution.py:283
  30.6 12.6 %collective-permute-start.1 = (f32[9,64,128]{2,1,0:T(8,128)S(1)}, f32[9,64,128]{2,1,0:T(8,128)S(1)}, u32[]{:S(2)}, u32[]{:S(2)}) collective-permute-start(f32[9,64,128]{2,1,0:T(8,128)S(1)} %get-tuple-element.30), channel_id=1, source_target_pairs={{0,28},{4,8},{8,4},{12,16},{16,12},{20,24},{24,20},{28,0},{1,29},{... | collective-permute-start | bytes 884744 | tf_op jit(solution)/shard_map/ppermute | solution.py:282
  34.2 13.4 %collective-permute-start.2 = (f32[9,64,128]{2,1,0:T(8,128)S(1)}, f32[9,64,128]{2,1,0:T(8,128)S(1)}, u32[]{:S(2)}, u32[]{:S(2)}) collective-permute-start(f32[9,64,128]{2,1,0:T(8,128)S(1)} %get-tuple-element.31), channel_id=1, source_target_pairs={{0,24},{4,12},{8,0},{12,20},{16,8},{20,28},{24,16},{28,4},{1,25},{... | collective-permute-start | bytes 884744 | tf_op jit(solution)/shard_map/ppermute | solution.py:284
  39.6 17.0 %collective-permute-start.13 = (f32[12,16,128]{2,1,0:T(8,128)S(1)}, f32[12,16,128]{2,1,0:T(8,128)S(1)}, u32[]{:S(2)}, u32[]{:S(2)}) collective-permute-start(f32[12,16,128]{2,1,0:T(8,128)S(1)} %get-tuple-element.40), channel_id=1, source_target_pairs={{0,4},{4,0},{1,5},{5,1},{2,6},{6,2},{3,7},{7,3},{8,12},{12,8},{9,1... | collective-permute-start | bytes 294920 | tf_op jit(solution)/shard_map/ppermute | solution.py:296
  39.9 17.0 %collective-permute-start.15 = (f32[12,16,128]{2,1,0:T(8,128)S(1)}, f32[12,16,128]{2,1,0:T(8,128)S(1)}, u32[]{:S(2)}, u32[]{:S(2)}) collective-permute-start(f32[12,16,128]{2,1,0:T(8,128)S(1)} %get-tuple-element.42), channel_id=1, source_target_pairs={{0,1},{4,5},{1,0},{5,4},{2,3},{6,7},{3,2},{7,6},{8,9},{12,13},{9,8... | collective-permute-start | bytes 294920 | tf_op jit(solution)/shard_map/ppermute | solution.py:296
  43.2 14.6 %collective-permute-start.17 = (f32[12,16,128]{2,1,0:T(8,128)S(1)}, f32[12,16,128]{2,1,0:T(8,128)S(1)}, u32[]{:S(2)}, u32[]{:S(2)}) collective-permute-start(f32[12,16,128]{2,1,0:T(8,128)S(1)} %get-tuple-element.44), channel_id=1, source_target_pairs={{0,5},{4,1},{1,4},{5,0},{2,7},{6,3},{3,6},{7,2},{8,13},{12,9},{9,1... | collective-permute-start | bytes 294920 | tf_op jit(solution)/shard_map/ppermute | solution.py:296
  47.6 12.2 %collective-permute-start.19 = (f32[12,16,128]{2,1,0:T(8,128)S(1)}, f32[12,16,128]{2,1,0:T(8,128)S(1)}, u32[]{:S(2)}, u32[]{:S(2)}) collective-permute-start(f32[12,16,128]{2,1,0:T(8,128)S(1)} %get-tuple-element.46), channel_id=1, source_target_pairs={{0,2},{4,6},{1,3},{5,7},{2,0},{6,4},{3,1},{7,5},{8,10},{12,14},{9,... | collective-permute-start | bytes 294920 | tf_op jit(solution)/shard_map/ppermute | solution.py:296
  49.1 10.7 %collective-permute-start.21 = (f32[12,16,128]{2,1,0:T(8,128)S(1)}, f32[12,16,128]{2,1,0:T(8,128)S(1)}, u32[]{:S(2)}, u32[]{:S(2)}) collective-permute-start(f32[12,16,128]{2,1,0:T(8,128)S(1)} %get-tuple-element.48), channel_id=1, source_target_pairs={{0,6},{4,2},{1,7},{5,3},{2,4},{6,0},{3,5},{7,1},{8,14},{12,10},{9,... | collective-permute-start | bytes 294920 | tf_op jit(solution)/shard_map/ppermute | solution.py:296
  56.5 6.5 %collective-permute-start.23 = (f32[12,16,128]{2,1,0:T(8,128)S(1)}, f32[12,16,128]{2,1,0:T(8,128)S(1)}, u32[]{:S(2)}, u32[]{:S(2)}) collective-permute-start(f32[12,16,128]{2,1,0:T(8,128)S(1)} %get-tuple-element.50), channel_id=1, source_target_pairs={{0,3},{4,7},{1,2},{5,6},{2,1},{6,5},{3,0},{7,4},{8,11},{12,15},{9,... | collective-permute-start | bytes 294920 | tf_op jit(solution)/shard_map/ppermute | solution.py:296
  56.9 7.5 %collective-permute-start.25 = (f32[12,16,128]{2,1,0:T(8,128)S(1)}, f32[12,16,128]{2,1,0:T(8,128)S(1)}, u32[]{:S(2)}, u32[]{:S(2)}) collective-permute-start(f32[12,16,128]{2,1,0:T(8,128)S(1)} %get-tuple-element.52), channel_id=1, source_target_pairs={{0,7},{4,3},{1,6},{5,2},{2,5},{6,1},{3,4},{7,0},{8,15},{12,11},{9,... | collective-permute-start | bytes 294920 | tf_op jit(solution)/shard_map/ppermute | solution.py:296
  57.8 7.8 %collective-permute-start.12 = (f32[12,16,128]{2,1,0:T(8,128)S(1)}, f32[12,16,128]{2,1,0:T(8,128)S(1)}, u32[]{:S(2)}, u32[]{:S(2)}) collective-permute-start(f32[12,16,128]{2,1,0:T(8,128)S(1)} %get-tuple-element.39), channel_id=1, source_target_pairs={{0,4},{4,0},{1,5},{5,1},{2,6},{6,2},{3,7},{7,3},{8,12},{12,8},{9,1... | collective-permute-start | bytes 294920 | tf_op jit(solution)/shard_map/ppermute | solution.py:296
  59.8 7.9 %collective-permute-start.16 = (f32[12,16,128]{2,1,0:T(8,128)S(1)}, f32[12,16,128]{2,1,0:T(8,128)S(1)}, u32[]{:S(2)}, u32[]{:S(2)}) collective-permute-start(f32[12,16,128]{2,1,0:T(8,128)S(1)} %get-tuple-element.43), channel_id=1, source_target_pairs={{0,5},{4,1},{1,4},{5,0},{2,7},{6,3},{3,6},{7,2},{8,13},{12,9},{9,1... | collective-permute-start | bytes 294920 | tf_op jit(solution)/shard_map/ppermute | solution.py:296
  63.0 9.3 %collective-permute-start.18 = (f32[12,16,128]{2,1,0:T(8,128)S(1)}, f32[12,16,128]{2,1,0:T(8,128)S(1)}, u32[]{:S(2)}, u32[]{:S(2)}) collective-permute-start(f32[12,16,128]{2,1,0:T(8,128)S(1)} %get-tuple-element.45), channel_id=1, source_target_pairs={{0,2},{4,6},{1,3},{5,7},{2,0},{6,4},{3,1},{7,5},{8,10},{12,14},{9,... | collective-permute-start | bytes 294920 | tf_op jit(solution)/shard_map/ppermute | solution.py:296
  64.4 7.9 %collective-permute-start.20 = (f32[12,16,128]{2,1,0:T(8,128)S(1)}, f32[12,16,128]{2,1,0:T(8,128)S(1)}, u32[]{:S(2)}, u32[]{:S(2)}) collective-permute-start(f32[12,16,128]{2,1,0:T(8,128)S(1)} %get-tuple-element.47), channel_id=1, source_target_pairs={{0,6},{4,2},{1,7},{5,3},{2,4},{6,0},{3,5},{7,1},{8,14},{12,10},{9,... | collective-permute-start | bytes 294920 | tf_op jit(solution)/shard_map/ppermute | solution.py:296
  65.6 8.3 %collective-permute-start.22 = (f32[12,16,128]{2,1,0:T(8,128)S(1)}, f32[12,16,128]{2,1,0:T(8,128)S(1)}, u32[]{:S(2)}, u32[]{:S(2)}) collective-permute-start(f32[12,16,128]{2,1,0:T(8,128)S(1)} %get-tuple-element.49), channel_id=1, source_target_pairs={{0,3},{4,7},{1,2},{5,6},{2,1},{6,5},{3,0},{7,4},{8,11},{12,15},{9,... | collective-permute-start | bytes 294920 | tf_op jit(solution)/shard_map/ppermute | solution.py:296
  65.6 8.3 %collective-permute-start.24 = (f32[12,16,128]{2,1,0:T(8,128)S(1)}, f32[12,16,128]{2,1,0:T(8,128)S(1)}, u32[]{:S(2)}, u32[]{:S(2)}) collective-permute-start(f32[12,16,128]{2,1,0:T(8,128)S(1)} %get-tuple-element.51), channel_id=1, source_target_pairs={{0,7},{4,3},{1,6},{5,2},{2,5},{6,1},{3,4},{7,0},{8,15},{12,11},{9,... | collective-permute-start | bytes 294920 | tf_op jit(solution)/shard_map/ppermute | solution.py:296
  (6 other events, 74.9 us)

commit v5 on v4

--- a/solution.py
+++ b/solution.py
@@ -198,43 +198,119 @@
     )(place, own, slanted_order[1], slanted_order[0], slanted_order[2], own_pot, lane_table.astype(jnp.bfloat16), *pot_far)
 
 
-def sort_kernel(place, *refs):
-    given, out = refs[:-1], refs[-1]
-    kept = out.shape[1]
-    for index, ref in enumerate(given):
-        out[place[1] ^ (index // kept), index % kept] = ref[...]
-
-
-def factor_kernel(cell_total, copies, inverse):
-    total = inverse.shape[0]
-    gram = jnp.sum(copies[...], axis=0) * (1.0 / cell_total)
-    lanes = 128
-    row = lax.broadcasted_iota(jnp.int32, (total, total), 0)
-    column = lax.broadcasted_iota(jnp.int32, (total, total), 1)
-    unit = jnp.where(row == column, 1.0, 0.0).astype(jnp.float32)
-    table = jnp.concatenate([gram, unit, jnp.zeros((total, lanes - 2 * total), jnp.float32)], axis=1)
-    index = lax.broadcasted_iota(jnp.int32, (total, lanes), 0)
+LANES = 128
+
+
+def exact_dot(a, b, contract=((1,), (0,))):
+    return lax.dot_general(
+        a, b, (contract, ((), ())), precision=lax.Precision.HIGHEST, preferred_element_type=jnp.float32
+    )
+
+
+def table_of(shape, test):
+    rows = lax.broadcasted_iota(jnp.int32, shape, 0)
+    columns = lax.broadcasted_iota(jnp.int32, shape, 1)
+    return jnp.where(test(rows, columns), 1.0, 0.0).astype(jnp.float32)
+
+
+def gram_message(read, total, tiles, chunk):
+    tall = total * EIGHT
+
+    def body(index, sums):
+        wide = jnp.concatenate([read(index * chunk + t) for t in range(chunk)], axis=1)
+        return sums + exact_dot(wide, wide, ((1,), (1,)))
+
+    sums = lax.fori_loop(0, tiles // chunk, body, jnp.zeros((tall, tall), jnp.float32))
+    sums = sums * table_of((tall, tall), lambda r, c: r % EIGHT == c % EIGHT)
+    partial = exact_dot(table_of((total, tall), lambda r, c: c // EIGHT == r), sums)
+    spread = exact_dot(partial, table_of((tall, LANES), lambda r, c: r // EIGHT == c % total))
+    per = LANES // total
+    spread = spread * table_of((total, LANES), lambda r, c: c // total == r % per)
+    return jnp.concatenate(
+        [jnp.sum(spread[i * per : (i + 1) * per], axis=0, keepdims=True) for i in range(total // per)], axis=1
+    )
+
+
+def inverse_factor(copies, total, cell_total):
+    row = jnp.sum(copies[...], axis=0) * (1.0 / cell_total)
+    per = LANES // total
+    wide = jnp.concatenate(
+        [jnp.broadcast_to(row[:, i * LANES : (i + 1) * LANES], (per, LANES)) for i in range(total // per)], axis=0
+    )
+    wide = wide * table_of((total, LANES), lambda r, c: c // total == r % per)
+    table = exact_dot(wide, table_of((LANES, LANES), lambda r, c: r % total == c))
+    table = table + table_of((total, LANES), lambda r, c: c - total == r)
+    index = lax.broadcasted_iota(jnp.int32, (total, LANES), 0)
     for j in range(total):
-        pivot = table[j : j + 1, :]
-        scale = lax.rsqrt(table[j : j + 1, j : j + 1])
-        scale = scale * (1.5 - 0.5 * table[j : j + 1, j : j + 1] * scale * scale)
-        scaled = pivot * scale
+        value = table[j : j + 1, j : j + 1]
+        scale = lax.rsqrt(value)
+        scale = scale * (1.5 - 0.5 * value * scale * scale)
+        scaled = table[j : j + 1, :] * scale
         factor = table[:, j : j + 1] * scale
         table = jnp.where(index == j, scaled, jnp.where(index > j, table - factor * scaled, table))
-    inverse[...] = table[:, total : 2 * total]
-
-
-def orthonormal(flat, cell_total, devices):
-    total = flat.shape[0]
-    local_gram = jnp.dot(flat, flat.T, precision=lax.Precision.HIGHEST, preferred_element_type=jnp.float32)
-    copies = lax.all_to_all(jnp.broadcast_to(local_gram[None], (devices, total, total)), ALL, 0, 0)
-    inverse = pl.pallas_call(
-        functools.partial(factor_kernel, cell_total),
-        out_shape=jax.ShapeDtypeStruct((total, total), jnp.float32),
-        in_specs=[VMEM],
-        out_specs=VMEM,
-    )(copies)
-    return jnp.dot(inverse, flat, precision=lax.Precision.HIGHEST, preferred_element_type=jnp.float32)
+    return table
+
+
+def by_tiles(table, total):
+    tall = total * EIGHT
+    wide = exact_dot(table, table_of((LANES, tall), lambda r, c: r - total == c // EIGHT))
+    both = exact_dot(table_of((tall, total), lambda r, c: r // EIGHT == c), wide)
+    return both * table_of((tall, tall), lambda r, c: r % EIGHT == c % EIGHT)
+
+
+def tile_reader(ref):
+    total, width = ref.shape[0], ref.shape[2]
+    return lambda t: ref[:, pl.ds(pl.multiple_of(EIGHT * t, EIGHT), EIGHT), :].reshape(total * EIGHT, width)
+
+
+def chunk_of(tiles):
+    return next(c for c in (6, 4, 3, 2, 1) if tiles % c == 0)
+
+
+def first_kernel(kept, place, *refs):
+    given, (block, message) = refs[:-2], refs[-2:]
+    for index, ref in enumerate(given):
+        block[(place[1] ^ (index // kept)) * kept + index % kept] = ref[...].reshape(block.shape[1:])
+    total, tiles = block.shape[0], block.shape[1] // EIGHT
+    row = gram_message(tile_reader(block), total, tiles, chunk_of(tiles))
+    message[...] = jnp.broadcast_to(row[None], message.shape)
+
+
+def second_kernel(cell_total, copies, block, basis, message):
+    total, tiles = block.shape[0], block.shape[1] // EIGHT
+    apply_all(inverse_factor(copies, total, cell_total), block, basis)
+    row = gram_message(tile_reader(basis), total, tiles, chunk_of(tiles))
+    message[...] = jnp.broadcast_to(row[None], message.shape)
+
+
+def third_kernel(cell_total, copies, block, basis):
+    apply_all(inverse_factor(copies, block.shape[0], cell_total), block, basis)
+
+
+def apply_all(table, block, basis):
+    total, tiles, width = block.shape[0], block.shape[1] // EIGHT, block.shape[2]
+    matrix = by_tiles(table, total)
+    read, chunk = tile_reader(block), chunk_of(tiles)
+
+    def body(index, carry):
+        wide = jnp.concatenate([read(index * chunk + t) for t in range(chunk)], axis=1)
+        result = exact_dot(matrix, wide)
+        for t in range(chunk):
+            piece = result[:, t * width : (t + 1) * width].reshape(total, EIGHT, width)
+            basis[:, pl.ds(pl.multiple_of(EIGHT * (index * chunk + t), EIGHT), EIGHT), :] = piece
+        return carry
+
+    lax.fori_loop(0, tiles // chunk, body, 0)
+
+
+def small_call(kernel, out_shape, specs, *args):
+    return pl.pallas_call(
+        kernel,
+        out_shape=out_shape,
+        in_specs=specs,
+        out_specs=jax.tree.map(lambda _: VMEM, out_shape),
+        compiler_params=pltpu.CompilerParams(vmem_limit_bytes=24 * 1024 * 1024),
+    )(*args)
 
 
 def whole(orbitals, potential):
@@ -297,18 +373,24 @@
                 for m in order
             ]
         )
-    grouped = pl.pallas_call(
-        sort_kernel,
-        out_shape=jax.ShapeDtypeStruct((group, kept, rows, part, width), jnp.float32),
-        in_specs=[SMEM] + [VMEM] * (group * kept),
-        out_specs=VMEM,
-        compiler_params=pltpu.CompilerParams(vmem_limit_bytes=16 * 1024 * 1024),
-    )(place, *[returned[at][spot[m]] for m in range(group) for at in range(kept)])
-    total = held * orb_count
-    devices = slabs * orb_count
-    flat = grouped.reshape(total, -1)
-    cell_total = flat.shape[1] * devices
-    basis = orthonormal(orthonormal(flat, cell_total, devices), cell_total, devices)
+    total, devices = held * orb_count, slabs * orb_count
+    cell_total = rows * part * width * devices
+    block_shape = jax.ShapeDtypeStruct((total, rows * part, width), jnp.float32)
+    message_shape = jax.ShapeDtypeStruct((devices, 1, total * total), jnp.float32)
+
+    def exchanged(message):
+        return lax.all_to_all(message, ALL, 0, 0)
+
+    parts = [returned[at][spot[m]] for m in range(group) for at in range(kept)]
+    block, message = small_call(
+        functools.partial(first_kernel, kept), [block_shape, message_shape], [SMEM] + [VMEM] * len(parts), place, *parts
+    )
+    basis, message = small_call(
+        functools.partial(second_kernel, cell_total), [block_shape, message_shape], [VMEM] * 2, exchanged(message), block
+    )
+    basis = small_call(
+        functools.partial(third_kernel, cell_total), block_shape, [VMEM] * 2, exchanged(message), basis
+    )
     basis = basis.reshape(total, rows, part, width)
     return lax.all_to_all(basis, "orb", split_axis=0, concat_axis=2, tiled=True)
 

time: 139 us -> 131 us (0.942)
  matrix products: 8.51 us -> 0 us
  Pallas kernels: 18.5 us -> 23.8 us
  waiting for transfers between devices: 27.5 us -> 31.8 us
  local copies, waits for them, and re-layouts: 6.99 us -> 3.78 us
  starting transfers between devices: 32 us -> 29.4 us
  other arithmetic: 1.68 us -> 0.16 us
    dot_general x4 -> x0, matrix products: 8.51 us -> none  [the longest x2 4.29 us: orthonormal(): jnp.dot(inverse, flat, precision=lax.Precision.HIGHEST, preferred_element...]
    pallas_call x3, Pallas kernels: 6.78 us -> 13.1 us  [small_call(): pl.pallas_call(kernel, out_shape=out_shape, in_specs=specs, out_specs=jax...]
    ppermute x1, waiting for transfers between devices: 0.01 us -> 4.84 us  [whole(): lax.ppermute(edge, slab_axes, ahead)]
    ppermute x1, waiting for transfers between devices: 6.22 us -> 2.13 us  [whole(): lax.ppermute(edge, slab_axes, slant)]
    ppermute x3, waiting for transfers between devices: 3.9 us -> 7.36 us  [whole(): lax.ppermute(joined, 'orb', [(i, i ^ m) for i in range(orb_count)])]
    unnamed x13 -> x8, local copies, waits for them, and re-layouts: 4.67 us -> 2.41 us
    ppermute x2, waiting for transfers between devices: 3.17 us -> 1.01 us  [whole(): lax.ppermute(sent[3 * at], slab_axes, slant)]
    ppermute x2, starting transfers between devices: 2.17 us -> 0.08 us  [whole(): lax.ppermute(sent[3 * at + 1], 'side', swap)]
  transfers between devices with their start and end apart: 26 -> 26, of which waited for: 9 -> 12; matrix products, arithmetic and copies ran while one was open for 0% -> 0% of each run, Pallas kernels for 8% -> 7%
where the time goes in v5:
time: 131 us
  blocking collectives  41.8 us (32%)
  waiting for transfers between devices  31.8 us (24%)
  starting transfers between devices  29.4 us (22%)
  Pallas kernels  23.8 us (18%)
  local copies, waits for them, and re-layouts  3.78 us (3%)
    all_to_all x1, blocking collectives, whole(): return lax.all_to_all(basis, 'orb', split_axis=0, concat_axis=2, tiled=True)  22.5 us
    all_to_all x2, blocking collectives, exchanged(): return lax.all_to_all(message, ALL, 0, 0)  19.3 us
    pallas_call x3, Pallas kernels, small_call(): pl.pallas_call(kernel, out_shape=out_shape, in_specs=specs, out_specs=jax...  13.1 us
    ppermute x14, starting transfers between devices, whole(): lax.ppermute(pieces[m], ('side', 'orb'), [(flat_of(i), flat_of(i ^ m)) fo...  11.8 us
    ppermute x14, waiting for transfers between devices, whole(): lax.ppermute(pieces[m], ('side', 'orb'), [(flat_of(i), flat_of(i ^ m)) fo...  10.3 us
    pallas_call x2, Pallas kernels, filtered_pieces(): pl.pallas_call(functools.partial(filter_kernel, at, len(pot_far)), out_sh...  9.39 us
    ppermute x3, waiting for transfers between devices, whole(): lax.ppermute(joined, 'orb', [(i, i ^ m) for i in range(orb_count)])  7.36 us
    ppermute x2, starting transfers between devices, whole(): lax.ppermute(sent[3 * at], slab_axes, slant)  7.15 us
  transfers between devices with their start and end apart: 26, of which 12 were waited for; matrix products, arithmetic and copies ran while one was open for 0% of the time, Pallas kernels for 7%

profile of v5, /device:TPU:0, one launch (start us, length us, event | category | flops | bytes accessed | tf_op | source)
XLA Modules:
  0.0 130.9 jit_solution(8675453899976530797)
XLA Ops:
  3.8 3.0 %collective-permute-start.3 = (f32[12,16,128]{2,1,0:T(8,128)S(1)}, f32[12,16,128]{2,1,0:T(8,128)S(1)}, u32[]{:S(2)}, u32[]{:S(2)}) collective-permute-start(f32[12,16,128]{2,1,0:T(8,128)S(1)} %get-tuple-element.36), channel_id=1, source_target_pairs={{0,4},{4,0},{1,5},{5,1},{2,6},{6,2},{3,7},{7,3},{8,12},{12,8},{9,1... | collective-permute-start | bytes 294920 | tf_op jit(solution)/shard_map/ppermute | solution.py:339
  6.8 3.6 %collective-permute-start.1 = (f32[9,64,128]{2,1,0:T(8,128)S(1)}, f32[9,64,128]{2,1,0:T(8,128)S(1)}, u32[]{:S(2)}, u32[]{:S(2)}) collective-permute-start(f32[9,64,128]{2,1,0:T(8,128)S(1)} %get-tuple-element.34), channel_id=1, source_target_pairs={{0,28},{4,8},{8,4},{12,16},{16,12},{20,24},{24,20},{28,0},{1,29},{... | collective-permute-start | bytes 884744 | tf_op jit(solution)/shard_map/ppermute | solution.py:358
  10.8 2.3 %collective-permute-start.4 = (f32[6,16,128]{2,1,0:T(8,128)S(1)}, f32[6,16,128]{2,1,0:T(8,128)S(1)}, u32[]{:S(2)}, u32[]{:S(2)}) collective-permute-start(f32[6,16,128]{2,1,0:T(8,128)S(1)} %get-tuple-element.37), channel_id=1, source_target_pairs={{0,28},{4,8},{8,4},{12,16},{16,12},{20,24},{24,20},{28,0},{1,29},{... | collective-permute-start | bytes 147464 | tf_op jit(solution)/shard_map/ppermute | solution.py:340
  13.1 4.8 %collective-permute-done.5.straight = f32[6,16,128]{2,1,0:T(8,128)S(1)} collective-permute-done((f32[6,16,128]{2,1,0:T(8,128)S(1)}, f32[6,16,128]{2,1,0:T(8,128)S(1)}, u32[]{:S(2)}, u32[]{:S(2)}) %collective-permute-start.5) | collective-permute-done | bytes 49184 | tf_op jit(solution)/shard_map/ppermute | solution.py:341
  17.9 2.1 %collective-permute-done.4.slanted = f32[6,16,128]{2,1,0:T(8,128)S(1)} collective-permute-done((f32[6,16,128]{2,1,0:T(8,128)S(1)}, f32[6,16,128]{2,1,0:T(8,128)S(1)}, u32[]{:S(2)}, u32[]{:S(2)}) %collective-permute-start.4) | collective-permute-done | bytes 49184 | tf_op jit(solution)/shard_map/ppermute | solution.py:340
  22.1 5.2 %collective-permute-done.8.rest_3_ = f32[24,16,128]{2,1,0:T(8,128)S(1)} collective-permute-done((f32[24,16,128]{2,1,0:T(8,128)S(1)}, f32[24,16,128]{2,1,0:T(8,128)S(1)}, u32[]{:S(2)}, u32[]{:S(2)}) %collective-permute-start.8) | collective-permute-done | bytes 196640 | tf_op jit(solution)/shard_map/ppermute | solution.py:351
  27.3 2.2 %collective-permute-start.2 = (f32[9,64,128]{2,1,0:T(8,128)S(1)}, f32[9,64,128]{2,1,0:T(8,128)S(1)}, u32[]{:S(2)}, u32[]{:S(2)}) collective-permute-start(f32[9,64,128]{2,1,0:T(8,128)S(1)} %get-tuple-element.35), channel_id=1, source_target_pairs={{0,24},{4,12},{8,0},{12,20},{16,8},{20,28},{24,16},{28,4},{1,25},{... | collective-permute-start | bytes 884744 | tf_op jit(solution)/shard_map/ppermute | solution.py:360
  29.4 2.1 %collective-permute-done.7.rest_2_ = f32[24,16,128]{2,1,0:T(8,128)S(1)} collective-permute-done((f32[24,16,128]{2,1,0:T(8,128)S(1)}, f32[24,16,128]{2,1,0:T(8,128)S(1)}, u32[]{:S(2)}, u32[]{:S(2)}) %collective-permute-start.7) | collective-permute-done | bytes 196640 | tf_op jit(solution)/shard_map/ppermute | solution.py:351
  31.6 3.6 %collective-permute-start.10 = (f32[9,64,128]{2,1,0:T(8,128)S(1)}, f32[9,64,128]{2,1,0:T(8,128)S(1)}, u32[]{:S(2)}, u32[]{:S(2)}) collective-permute-start(f32[9,64,128]{2,1,0:T(8,128)S(1)} %get-tuple-element.40), channel_id=1, source_target_pairs={{0,28},{4,8},{8,4},{12,16},{16,12},{20,24},{24,20},{28,0},{1,29},{... | collective-permute-start | bytes 884744 | tf_op jit(solution)/shard_map/ppermute | solution.py:358
  37.2 4.7 %shard_map.30 = (f32[12,16,128]{2,1,0:T(8,128)S(1)}, f32[12,16,128]{2,1,0:T(8,128)S(1)}, f32[12,16,128]{2,1,0:T(8,128)S(1)}, f32[12,16,128]{2,1,0:T(8,128)S(1)},...) custom-call(s32[3]{0:T(128)S(1)} %pad_add_fusion.place, ...), custom_call_target="tpu_custom_call" | custom-call | tf_op jit(solution)/shard_map/pallas_call | solution.py:185
  41.9 2.2 %collective-permute-start.12 = (f32[12,16,128]{2,1,0:T(8,128)S(1)}, f32[12,16,128]{2,1,0:T(8,128)S(1)}, u32[]{:S(2)}, u32[]{:S(2)}) collective-permute-start(f32[12,16,128]{2,1,0:T(8,128)S(1)} %get-tuple-element.43), channel_id=1, source_target_pairs={{0,4},{4,0},{1,5},{5,1},{2,6},{6,2},{3,7},{7,3},{8,12},{12,8},{9,1... | collective-permute-start | bytes 294920 | tf_op jit(solution)/shard_map/ppermute | solution.py:372
  45.1 4.1 %collective-permute-done.11.straight = f32[9,64,128]{2,1,0:T(8,128)S(1)} collective-permute-done((f32[9,64,128]{2,1,0:T(8,128)S(1)}, f32[9,64,128]{2,1,0:T(8,128)S(1)}, u32[]{:S(2)}, u32[]{:S(2)}) %collective-permute-start.11) | collective-permute-done | bytes 294944 | tf_op jit(solution)/shard_map/ppermute | solution.py:360
  49.9 3.1 %collective-permute-start.20 = (f32[12,16,128]{2,1,0:T(8,128)S(1)}, f32[12,16,128]{2,1,0:T(8,128)S(1)}, u32[]{:S(2)}, u32[]{:S(2)}) collective-permute-start(f32[12,16,128]{2,1,0:T(8,128)S(1)} %get-tuple-element.51), channel_id=1, source_target_pairs={{0,6},{4,2},{1,7},{5,3},{2,4},{6,0},{3,5},{7,1},{8,14},{12,10},{9,... | collective-permute-start | bytes 294920 | tf_op jit(solution)/shard_map/ppermute | solution.py:372
  53.0 4.7 %shard_map.31 = (f32[12,16,128]{2,1,0:T(8,128)S(1)}, f32[12,16,128]{2,1,0:T(8,128)S(1)}, f32[12,16,128]{2,1,0:T(8,128)S(1)}, f32[12,16,128]{2,1,0:T(8,128)S(1)},...) custom-call(s32[3]{0:T(128)S(1)} %pad_add_fusion.place, ...), custom_call_target="tpu_custom_call" | custom-call | tf_op jit(solution)/shard_map/pallas_call | solution.py:185
  58.6 2.4 %collective-permute-start.13 = (f32[12,16,128]{2,1,0:T(8,128)S(1)}, f32[12,16,128]{2,1,0:T(8,128)S(1)}, u32[]{:S(2)}, u32[]{:S(2)}) collective-permute-start(f32[12,16,128]{2,1,0:T(8,128)S(1)} %get-tuple-element.44), channel_id=1, source_target_pairs={{0,4},{4,0},{1,5},{5,1},{2,6},{6,2},{3,7},{7,3},{8,12},{12,8},{9,1... | collective-permute-start | bytes 294920 | tf_op jit(solution)/shard_map/ppermute | solution.py:372
  61.2 3.1 %collective-permute-done.22.refs_12_ = f32[12,16,128]{2,1,0:T(8,128)S(1)} collective-permute-done((f32[12,16,128]{2,1,0:T(8,128)S(1)}, f32[12,16,128]{2,1,0:T(8,128)S(1)}, u32[]{:S(2)}, u32[]{:S(2)}) %collective-permute-start.22) | collective-permute-done | bytes 98336 | tf_op jit(solution)/shard_map/ppermute | solution.py:372
  66.2 2.7 %collective-permute-start.25 = (f32[12,16,128]{2,1,0:T(8,128)S(1)}, f32[12,16,128]{2,1,0:T(8,128)S(1)}, u32[]{:S(2)}, u32[]{:S(2)}) collective-permute-start(f32[12,16,128]{2,1,0:T(8,128)S(1)} %get-tuple-element.56), channel_id=1, source_target_pairs={{0,7},{4,3},{1,6},{5,2},{2,5},{6,1},{3,4},{7,0},{8,15},{12,11},{9,... | collective-permute-start | bytes 294920 | tf_op jit(solution)/shard_map/ppermute | solution.py:372
  68.9 4.8 %collective-permute-done.19.refs_9_ = f32[12,16,128]{2,1,0:T(8,128)S(1)} collective-permute-done((f32[12,16,128]{2,1,0:T(8,128)S(1)}, f32[12,16,128]{2,1,0:T(8,128)S(1)}, u32[]{:S(2)}, u32[]{:S(2)}) %collective-permute-start.19) | collective-permute-done | bytes 98336 | tf_op jit(solution)/shard_map/ppermute | solution.py:372
  74.5 3.0 %shard_map.32 = (f32[16,192,128]{2,1,0:T(8,128)S(1)}, f32[32,1,256]{2,1,0:T(1,128)S(1)}) custom-call(s32[3]{0:T(128)S(1)} %pad_add_fusion.place, f32[12,16,128]{2,1,0:T(8,128)S(1)} %get-tuple-element.38.refs_0_, f32[12,16,128]{2,1,0:T(8,128)S(1)} %get-tuple-element.42.refs_1_, f32[12,16,128]{2,1,0:T(8,128)S(1)} %collective-permute-done.12.refs_2_, ...), custom_call_target="tpu_custom_call" | custom-call | tf_op jit(solution)/shard_map/pallas_call | solution.py:307
  77.6 10.3 %all_to_all.28.copies = f32[32,1,256]{2,1,0:T(1,128)S(1)} all-to-all(f32[32,1,256]{2,1,0:T(1,128)S(1)} %get-tuple-element.57), channel_id=1, replica_groups=mesh['pair'=4,'side'=2,'orb'=4] {'pair','side','orb'}, dimensions={0} | all-to-all | bytes 65536 | tf_op jit(solution)/shard_map/all_to_all | solution.py:382
  87.9 6.3 %shard_map.33 = (f32[16,192,128]{2,1,0:T(8,128)S(1)}, f32[32,1,256]{2,1,0:T(1,128)S(1)}) custom-call(f32[32,1,256]{2,1,0:T(1,128)S(1)} %all_to_all.28.copies, f32[16,192,128]{2,1,0:T(8,128)S(1)} %get-tuple-element.58.block), custom_call_target="tpu_custom_call" | custom-call | tf_op jit(solution)/shard_map/pallas_call | solution.py:307
  94.2 9.0 %all_to_all.29.copies = f32[32,1,256]{2,1,0:T(1,128)S(1)} all-to-all(f32[32,1,256]{2,1,0:T(1,128)S(1)} %get-tuple-element.59), channel_id=1, replica_groups=mesh['pair'=4,'side'=2,'orb'=4] {'pair','side','orb'}, dimensions={0} | all-to-all | bytes 65536 | tf_op jit(solution)/shard_map/all_to_all | solution.py:382
  103.1 3.8 %shard_map.34 = f32[16,192,128]{2,1,0:T(8,128)S(1)} custom-call(f32[32,1,256]{2,1,0:T(1,128)S(1)} %all_to_all.29.copies, f32[16,192,128]{2,1,0:T(8,128)S(1)} %get-tuple-element.60.block), custom_call_target="tpu_custom_call" | custom-call | tf_op jit(solution)/shard_map/pallas_call | solution.py:307
  107.0 22.5 %all_to_all.30 = f32[16,12,16,128]{3,2,1,0:T(8,128)S(1)} all-to-all(f32[16,12,16,128]{3,2,1,0:T(8,128)S(1)} %bitcast.8), channel_id=1, replica_groups=mesh['pair'=4,'side'=2,'orb'=4] {'orb'}, dimensions={0} | all-to-all | bytes 3145728 | tf_op jit(solution)/shard_map/all_to_all | solution.py:395
  (49 shorter events, 15.2 us)
Async XLA Ops:
  3.8 16.3 %collective-permute-start.3 = (f32[12,16,128]{2,1,0:T(8,128)S(1)}, f32[12,16,128]{2,1,0:T(8,128)S(1)}, u32[]{:S(2)}, u32[]{:S(2)}) collective-permute-start(f32[12,16,128]{2,1,0:T(8,128)S(1)} %get-tuple-element.36), channel_id=1, source_target_pairs={{0,4},{4,0},{1,5},{5,1},{2,6},{6,2},{3,7},{7,3},{8,12},{12,8},{9,1... | collective-permute-start | bytes 294920 | tf_op jit(solution)/shard_map/ppermute | solution.py:339
  6.8 28.4 %collective-permute-start.1 = (f32[9,64,128]{2,1,0:T(8,128)S(1)}, f32[9,64,128]{2,1,0:T(8,128)S(1)}, u32[]{:S(2)}, u32[]{:S(2)}) collective-permute-start(f32[9,64,128]{2,1,0:T(8,128)S(1)} %get-tuple-element.34), channel_id=1, source_target_pairs={{0,28},{4,8},{8,4},{12,16},{16,12},{20,24},{24,20},{28,0},{1,29},{... | collective-permute-start | bytes 884744 | tf_op jit(solution)/shard_map/ppermute | solution.py:358
  10.4 7.6 %collective-permute-start.5 = (f32[6,16,128]{2,1,0:T(8,128)S(1)}, f32[6,16,128]{2,1,0:T(8,128)S(1)}, u32[]{:S(2)}, u32[]{:S(2)}) collective-permute-start(f32[6,16,128]{2,1,0:T(8,128)S(1)} %get-tuple-element.37), channel_id=1, source_target_pairs={{0,24},{4,12},{8,0},{12,20},{16,8},{20,28},{24,16},{28,4},{1,25},{... | collective-permute-start | bytes 147464 | tf_op jit(solution)/shard_map/ppermute | solution.py:341
  10.8 9.2 %collective-permute-start.4 = (f32[6,16,128]{2,1,0:T(8,128)S(1)}, f32[6,16,128]{2,1,0:T(8,128)S(1)}, u32[]{:S(2)}, u32[]{:S(2)}) collective-permute-start(f32[6,16,128]{2,1,0:T(8,128)S(1)} %get-tuple-element.37), channel_id=1, source_target_pairs={{0,28},{4,8},{8,4},{12,16},{16,12},{20,24},{24,20},{28,0},{1,29},{... | collective-permute-start | bytes 147464 | tf_op jit(solution)/shard_map/ppermute | solution.py:340
  20.1 7.2 %collective-permute-start.8 = (f32[24,16,128]{2,1,0:T(8,128)S(1)}, f32[24,16,128]{2,1,0:T(8,128)S(1)}, u32[]{:S(2)}, u32[]{:S(2)}) collective-permute-start(f32[24,16,128]{2,1,0:T(8,128)S(1)} %shard_map.29.rest_0_), channel_id=1, source_target_pairs={{0,3},{1,2},{2,1},{3,0},{4,7},{5,6},{6,5},{7,4},{8,11},{9,10},{10,... | collective-permute-start | bytes 589832 | tf_op jit(solution)/shard_map/ppermute | solution.py:351
  20.2 11.4 %collective-permute-start.7 = (f32[24,16,128]{2,1,0:T(8,128)S(1)}, f32[24,16,128]{2,1,0:T(8,128)S(1)}, u32[]{:S(2)}, u32[]{:S(2)}) collective-permute-start(f32[24,16,128]{2,1,0:T(8,128)S(1)} %shard_map.29.rest_0_), channel_id=1, source_target_pairs={{0,2},{1,3},{2,0},{3,1},{4,6},{5,7},{6,4},{7,5},{8,10},{9,11},{10,... | collective-permute-start | bytes 589832 | tf_op jit(solution)/shard_map/ppermute | solution.py:351
  21.8 9.9 %collective-permute-start.6 = (f32[24,16,128]{2,1,0:T(8,128)S(1)}, f32[24,16,128]{2,1,0:T(8,128)S(1)}, u32[]{:S(2)}, u32[]{:S(2)}) collective-permute-start(f32[24,16,128]{2,1,0:T(8,128)S(1)} %shard_map.29.rest_0_), channel_id=1, source_target_pairs={{0,1},{1,0},{2,3},{3,2},{4,5},{5,4},{6,7},{7,6},{8,9},{9,8},{10,11... | collective-permute-start | bytes 589832 | tf_op jit(solution)/shard_map/ppermute | solution.py:351
  22.0 15.1 %collective-permute-start = (f32[12,64,128]{2,1,0:T(8,128)S(1)}, f32[12,64,128]{2,1,0:T(8,128)S(1)}, u32[]{:S(2)}, u32[]{:S(2)}) collective-permute-start(f32[12,64,128]{2,1,0:T(8,128)S(1)} %get-tuple-element.33), channel_id=1, source_target_pairs={{0,4},{4,0},{1,5},{5,1},{2,6},{6,2},{3,7},{7,3},{8,12},{12,8},{9,1... | collective-permute-start | bytes 1179656 | tf_op jit(solution)/shard_map/ppermute | solution.py:359
  27.3 9.9 %collective-permute-start.2 = (f32[9,64,128]{2,1,0:T(8,128)S(1)}, f32[9,64,128]{2,1,0:T(8,128)S(1)}, u32[]{:S(2)}, u32[]{:S(2)}) collective-permute-start(f32[9,64,128]{2,1,0:T(8,128)S(1)} %get-tuple-element.35), channel_id=1, source_target_pairs={{0,24},{4,12},{8,0},{12,20},{16,8},{20,28},{24,16},{28,4},{1,25},{... | collective-permute-start | bytes 884744 | tf_op jit(solution)/shard_map/ppermute | solution.py:360
  31.6 18.3 %collective-permute-start.9 = (f32[12,64,128]{2,1,0:T(8,128)S(1)}, f32[12,64,128]{2,1,0:T(8,128)S(1)}, u32[]{:S(2)}, u32[]{:S(2)}) collective-permute-start(f32[12,64,128]{2,1,0:T(8,128)S(1)} %get-tuple-element.39), channel_id=1, source_target_pairs={{0,4},{4,0},{1,5},{5,1},{2,6},{6,2},{3,7},{7,3},{8,12},{12,8},{9,1... | collective-permute-start | bytes 1179656 | tf_op jit(solution)/shard_map/ppermute | solution.py:359
  31.6 13.5 %collective-permute-start.10 = (f32[9,64,128]{2,1,0:T(8,128)S(1)}, f32[9,64,128]{2,1,0:T(8,128)S(1)}, u32[]{:S(2)}, u32[]{:S(2)}) collective-permute-start(f32[9,64,128]{2,1,0:T(8,128)S(1)} %get-tuple-element.40), channel_id=1, source_target_pairs={{0,28},{4,8},{8,4},{12,16},{16,12},{20,24},{24,20},{28,0},{1,29},{... | collective-permute-start | bytes 884744 | tf_op jit(solution)/shard_map/ppermute | solution.py:358
  35.2 13.9 %collective-permute-start.11 = (f32[9,64,128]{2,1,0:T(8,128)S(1)}, f32[9,64,128]{2,1,0:T(8,128)S(1)}, u32[]{:S(2)}, u32[]{:S(2)}) collective-permute-start(f32[9,64,128]{2,1,0:T(8,128)S(1)} %get-tuple-element.41), channel_id=1, source_target_pairs={{0,24},{4,12},{8,0},{12,20},{16,8},{20,28},{24,16},{28,4},{1,25},{... | collective-permute-start | bytes 884744 | tf_op jit(solution)/shard_map/ppermute | solution.py:360
  41.9 15.8 %collective-permute-start.12 = (f32[12,16,128]{2,1,0:T(8,128)S(1)}, f32[12,16,128]{2,1,0:T(8,128)S(1)}, u32[]{:S(2)}, u32[]{:S(2)}) collective-permute-start(f32[12,16,128]{2,1,0:T(8,128)S(1)} %get-tuple-element.43), channel_id=1, source_target_pairs={{0,4},{4,0},{1,5},{5,1},{2,6},{6,2},{3,7},{7,3},{8,12},{12,8},{9,1... | collective-permute-start | bytes 294920 | tf_op jit(solution)/shard_map/ppermute | solution.py:372
  44.1 13.7 %collective-permute-start.14 = (f32[12,16,128]{2,1,0:T(8,128)S(1)}, f32[12,16,128]{2,1,0:T(8,128)S(1)}, u32[]{:S(2)}, u32[]{:S(2)}) collective-permute-start(f32[12,16,128]{2,1,0:T(8,128)S(1)} %get-tuple-element.45), channel_id=1, source_target_pairs={{0,1},{4,5},{1,0},{5,4},{2,3},{6,7},{3,2},{7,6},{8,9},{12,13},{9,8... | collective-permute-start | bytes 294920 | tf_op jit(solution)/shard_map/ppermute | solution.py:372
  45.1 13.5 %collective-permute-start.16 = (f32[12,16,128]{2,1,0:T(8,128)S(1)}, f32[12,16,128]{2,1,0:T(8,128)S(1)}, u32[]{:S(2)}, u32[]{:S(2)}) collective-permute-start(f32[12,16,128]{2,1,0:T(8,128)S(1)} %get-tuple-element.47), channel_id=1, source_target_pairs={{0,5},{4,1},{1,4},{5,0},{2,7},{6,3},{3,6},{7,2},{8,13},{12,9},{9,1... | collective-permute-start | bytes 294920 | tf_op jit(solution)/shard_map/ppermute | solution.py:372
  49.1 11.9 %collective-permute-start.18 = (f32[12,16,128]{2,1,0:T(8,128)S(1)}, f32[12,16,128]{2,1,0:T(8,128)S(1)}, u32[]{:S(2)}, u32[]{:S(2)}) collective-permute-start(f32[12,16,128]{2,1,0:T(8,128)S(1)} %get-tuple-element.49), channel_id=1, source_target_pairs={{0,2},{4,6},{1,3},{5,7},{2,0},{6,4},{3,1},{7,5},{8,10},{12,14},{9,... | collective-permute-start | bytes 294920 | tf_op jit(solution)/shard_map/ppermute | solution.py:372
  49.9 11.1 %collective-permute-start.20 = (f32[12,16,128]{2,1,0:T(8,128)S(1)}, f32[12,16,128]{2,1,0:T(8,128)S(1)}, u32[]{:S(2)}, u32[]{:S(2)}) collective-permute-start(f32[12,16,128]{2,1,0:T(8,128)S(1)} %get-tuple-element.51), channel_id=1, source_target_pairs={{0,6},{4,2},{1,7},{5,3},{2,4},{6,0},{3,5},{7,1},{8,14},{12,10},{9,... | collective-permute-start | bytes 294920 | tf_op jit(solution)/shard_map/ppermute | solution.py:372
  57.7 6.5 %collective-permute-start.22 = (f32[12,16,128]{2,1,0:T(8,128)S(1)}, f32[12,16,128]{2,1,0:T(8,128)S(1)}, u32[]{:S(2)}, u32[]{:S(2)}) collective-permute-start(f32[12,16,128]{2,1,0:T(8,128)S(1)} %get-tuple-element.53), channel_id=1, source_target_pairs={{0,3},{4,7},{1,2},{5,6},{2,1},{6,5},{3,0},{7,4},{8,11},{12,15},{9,... | collective-permute-start | bytes 294920 | tf_op jit(solution)/shard_map/ppermute | solution.py:372
  58.6 7.6 %collective-permute-start.13 = (f32[12,16,128]{2,1,0:T(8,128)S(1)}, f32[12,16,128]{2,1,0:T(8,128)S(1)}, u32[]{:S(2)}, u32[]{:S(2)}) collective-permute-start(f32[12,16,128]{2,1,0:T(8,128)S(1)} %get-tuple-element.44), channel_id=1, source_target_pairs={{0,4},{4,0},{1,5},{5,1},{2,6},{6,2},{3,7},{7,3},{8,12},{12,8},{9,1... | collective-permute-start | bytes 294920 | tf_op jit(solution)/shard_map/ppermute | solution.py:372
  61.0 7.9 %collective-permute-start.17 = (f32[12,16,128]{2,1,0:T(8,128)S(1)}, f32[12,16,128]{2,1,0:T(8,128)S(1)}, u32[]{:S(2)}, u32[]{:S(2)}) collective-permute-start(f32[12,16,128]{2,1,0:T(8,128)S(1)} %get-tuple-element.48), channel_id=1, source_target_pairs={{0,5},{4,1},{1,4},{5,0},{2,7},{6,3},{3,6},{7,2},{8,13},{12,9},{9,1... | collective-permute-start | bytes 294920 | tf_op jit(solution)/shard_map/ppermute | solution.py:372
  64.2 9.5 %collective-permute-start.19 = (f32[12,16,128]{2,1,0:T(8,128)S(1)}, f32[12,16,128]{2,1,0:T(8,128)S(1)}, u32[]{:S(2)}, u32[]{:S(2)}) collective-permute-start(f32[12,16,128]{2,1,0:T(8,128)S(1)} %get-tuple-element.50), channel_id=1, source_target_pairs={{0,2},{4,6},{1,3},{5,7},{2,0},{6,4},{3,1},{7,5},{8,10},{12,14},{9,... | collective-permute-start | bytes 294920 | tf_op jit(solution)/shard_map/ppermute | solution.py:372
  64.3 9.5 %collective-permute-start.21 = (f32[12,16,128]{2,1,0:T(8,128)S(1)}, f32[12,16,128]{2,1,0:T(8,128)S(1)}, u32[]{:S(2)}, u32[]{:S(2)}) collective-permute-start(f32[12,16,128]{2,1,0:T(8,128)S(1)} %get-tuple-element.52), channel_id=1, source_target_pairs={{0,6},{4,2},{1,7},{5,3},{2,4},{6,0},{3,5},{7,1},{8,14},{12,10},{9,... | collective-permute-start | bytes 294920 | tf_op jit(solution)/shard_map/ppermute | solution.py:372
  66.2 8.3 %collective-permute-start.23 = (f32[12,16,128]{2,1,0:T(8,128)S(1)}, f32[12,16,128]{2,1,0:T(8,128)S(1)}, u32[]{:S(2)}, u32[]{:S(2)}) collective-permute-start(f32[12,16,128]{2,1,0:T(8,128)S(1)} %get-tuple-element.54), channel_id=1, source_target_pairs={{0,3},{4,7},{1,2},{5,6},{2,1},{6,5},{3,0},{7,4},{8,11},{12,15},{9,... | collective-permute-start | bytes 294920 | tf_op jit(solution)/shard_map/ppermute | solution.py:372
  66.2 8.3 %collective-permute-start.25 = (f32[12,16,128]{2,1,0:T(8,128)S(1)}, f32[12,16,128]{2,1,0:T(8,128)S(1)}, u32[]{:S(2)}, u32[]{:S(2)}) collective-permute-start(f32[12,16,128]{2,1,0:T(8,128)S(1)} %get-tuple-element.56), channel_id=1, source_target_pairs={{0,7},{4,3},{1,6},{5,2},{2,5},{6,1},{3,4},{7,0},{8,15},{12,11},{9,... | collective-permute-start | bytes 294920 | tf_op jit(solution)/shard_map/ppermute | solution.py:372
  (6 other events, 83.5 us)

commit v6 on v5

--- a/solution.py
+++ b/solution.py
@@ -18,6 +18,7 @@
 DEEP = REACH * STEPS
 WIDE = REACH * (STEPS - 1)
 EIGHT = 8
+CORES = 2
 BLOCKS = 3
 ALL = ("pair", "side", "orb")
 
@@ -165,11 +166,17 @@
         sorted_pieces[2 * to + half, row - half * rows, pl.ds(EIGHT * strip - to * piece, EIGHT), :] = value
 
     step(second, first, 2 * REACH, 2 * REACH, both, store_out)
-    for apart, out in enumerate(outs):
+    group = sorted_pieces.shape[0]
+    for apart, out in enumerate(outs[:group]):
         out[...] = sorted_pieces[me ^ apart]
-
-
-def filtered_pieces(at, place, own, slanted_order, own_pot, pot_far, group):
+    for index, out in enumerate(outs[group:]):
+        chip = orb // CORES ^ (1 if index < 2 else 0)
+        slab = side ^ (index % 2)
+        for core in range(CORES):
+            out[core] = sorted_pieces[2 * (CORES * chip + core) + slab]
+
+
+def filtered_pieces(at, place, own, slanted_order, own_pot, pot_far, group, spares):
     rows, cols, width = own.shape[1:]
     both = 2 * rows
     apart = jnp.arange(width)[:, None] - jnp.arange(width)[None, :]
@@ -184,9 +191,10 @@
     piece = (rows, 2 * cols // group, width)
     return pl.pallas_call(
         functools.partial(filter_kernel, at, len(pot_far)),
-        out_shape=[jax.ShapeDtypeStruct(piece, jnp.float32)] * group,
+        out_shape=[jax.ShapeDtypeStruct(piece, jnp.float32)] * group
+        + [jax.ShapeDtypeStruct((CORES,) + piece, jnp.float32)] * spares,
         in_specs=[SMEM] + [VMEM] * (6 + len(pot_far)),
-        out_specs=[VMEM] * group,
+        out_specs=[VMEM] * (group + spares),
         scratch_shapes=[
             scratch(DEEP),
             scratch(WIDE),
@@ -285,6 +293,75 @@
 
 def third_kernel(cell_total, copies, block, basis):
     apply_all(inverse_factor(copies, block.shape[0], cell_total), block, basis)
+
+
+def second_and_bundle_kernel(cell_total, place, copies, block, *refs):
+    given, (table_out, message, bundle, basis) = refs[:-4], refs[-4:]
+    total, tiles = block.shape[0], block.shape[1] // EIGHT
+    table = inverse_factor(copies, total, cell_total)
+    table_out[...] = table
+    apply_all(table, block, basis)
+    row = gram_message(tile_reader(basis), total, tiles, chunk_of(tiles))
+    message[...] = jnp.broadcast_to(row[None], message.shape)
+    kept = len(given) // 4
+    side = place[0]
+    for index, ref in enumerate(given):
+        kind, at = index // kept, index % kept
+        slot = (kind // 2) * 2 * kept + (side ^ (kind % 2)) * kept + at
+        bundle[slot] = ref[...].reshape(bundle.shape[1:])
+
+
+def last_kernel(cell_total, place, copies, table, block, block_near, bundle, bundle_near, out):
+    total, width = block.shape[0], block.shape[2]
+    held, rows, _ = out.shape[:3]
+    orb = place[2]
+    core, chip = orb % CORES, orb // CORES
+    tall, short = total * EIGHT, held * EIGHT
+    second = inverse_factor(copies, total, cell_total)
+    pick = table_of((LANES, total), lambda r, c: r - total == c)
+    product = exact_dot(exact_dot(second, pick), exact_dot(table[...], pick))
+
+    def matrix_for(orbital_of):
+        wide = exact_dot(product, table_of((total, tall), lambda r, c: orbital_of(c // EIGHT) == r))
+        own = exact_dot(table_of((short, total), lambda r, c: orb * held + r // EIGHT == c), wide)
+        return own * table_of((short, tall), lambda r, c: r % EIGHT == c % EIGHT)
+
+    def write(matrix, read, tiles, first_column):
+        chunk, strips = chunk_of(tiles), tiles // rows
+
+        def body(index, carry):
+            wide = jnp.concatenate([read(index * chunk + t) for t in range(chunk)], axis=1)
+            result = exact_dot(matrix, wide)
+            for t in range(chunk):
+                tile = index * chunk + t
+                piece = result[:, t * width : (t + 1) * width].reshape(held, EIGHT, width)
+                column = pl.multiple_of(first_column + (tile % strips) * EIGHT, EIGHT)
+                out[:, tile // strips, pl.ds(column, EIGHT), :] = piece
+            return carry
+
+        lax.fori_loop(0, tiles // chunk, body, 0)
+
+    tiles = block.shape[1] // EIGHT
+    part = block.shape[1] // rows
+    natural = matrix_for(lambda index: index)
+    write(natural, tile_reader(block), tiles, orb * part)
+    write(natural, tile_reader(block_near), tiles, (orb ^ 1) * part)
+
+    def orbital_of(index):
+        kind, local = index // held, index % held
+        flip = kind // 2
+        quad = jnp.where(kind % 2 == 0, orb ^ flip, core ^ flip)
+        return quad * held + local
+
+    mixed = matrix_for(orbital_of)
+    for share in range(CORES):
+
+        def read(t, share=share):
+            span = pl.ds(pl.multiple_of(share * block.shape[1] + EIGHT * t, EIGHT), EIGHT)
+            both = jnp.concatenate([bundle[:, span, :], bundle_near[:, span, :]], axis=0)
+            return both.reshape(tall, width)
+
+        write(mixed, read, tiles, ((1 - chip) * CORES + share) * part)
 
 
 def apply_all(table, block, basis):
@@ -361,11 +438,13 @@
             )
         )
 
-    returned = []
+    spares = 4 if orb_count == 2 * CORES and kept == 2 else 0
+    returned, spare = [], []
     order = sorted(range(1, group), key=lambda m: (-(m // 4 > 0) - m % 2, m))
     spot = {m: 1 + index for index, m in enumerate(order)} | {0: 0}
     for at in range(kept):
-        pieces = filtered_pieces(at, place, orbitals, fetched[at], potential, pot_far, group)
+        pieces = filtered_pieces(at, place, orbitals, fetched[at], potential, pot_far, group, spares)
+        spare.append(pieces[group:])
         returned.append(
             [pieces[0]]
             + [
@@ -385,6 +464,32 @@
     block, message = small_call(
         functools.partial(first_kernel, kept), [block_shape, message_shape], [SMEM] + [VMEM] * len(parts), place, *parts
     )
+    if spares:
+        up = [(i, i + CORES) for i in range(CORES)]
+        slanted_up = [(s * orb_count + i, (1 - s) * orb_count + i + CORES) for s in range(2) for i in range(CORES)]
+        cores = [(i, i ^ 1) for i in range(orb_count)]
+        given = [spare[at][0] for at in range(kept)]
+        given += [lax.ppermute(spare[at][1], "side", swap) for at in range(kept)]
+        given += [lax.ppermute(spare[at][2], "orb", up) for at in range(kept)]
+        given += [lax.ppermute(spare[at][3], ("side", "orb"), slanted_up) for at in range(kept)]
+        block_near = lax.ppermute(block, "orb", cores)
+        bundle_shape = jax.ShapeDtypeStruct((2 * held, CORES * rows * part, width), jnp.float32)
+        table_shape = jax.ShapeDtypeStruct((total, LANES), jnp.float32)
+        table, message, bundle = pl.pallas_call(
+            functools.partial(second_and_bundle_kernel, cell_total),
+            out_shape=[table_shape, message_shape, bundle_shape],
+            in_specs=[SMEM] + [VMEM] * (2 + len(given)),
+            out_specs=[VMEM] * 3,
+            scratch_shapes=[pltpu.VMEM(block_shape.shape, jnp.float32)],
+            compiler_params=pltpu.CompilerParams(vmem_limit_bytes=24 * 1024 * 1024),
+        )(place, exchanged(message), block, *given)
+        bundle_near = lax.ppermute(bundle, "orb", cores)
+        return small_call(
+            functools.partial(last_kernel, cell_total),
+            jax.ShapeDtypeStruct((held, rows, cols, width), jnp.float32),
+            [SMEM] + [VMEM] * 6,
+            *(place, exchanged(message), table, block, block_near, bundle, bundle_near),
+        )
     basis, message = small_call(
         functools.partial(second_kernel, cell_total), [block_shape, message_shape], [VMEM] * 2, exchanged(message), block
     )

time: 131 us -> 127 us (0.969)
  blocking collectives: 41.8 us -> 8.93 us
  starting transfers between devices: 29.4 us -> 44.5 us
  Pallas kernels: 23.8 us -> 32.3 us
  waiting for transfers between devices: 31.8 us -> 35.1 us
  local copies, waits for them, and re-layouts: 3.78 us -> 5.61 us
    all_to_all x1 -> x0, blocking collectives: 22.5 us -> none  [whole(): return lax.all_to_all(basis, 'orb', split_axis=0, concat_axis=2, tiled=True)]
    ppermute x0 -> x8, starting transfers between devices: none -> 12.6 us  [the longest x2 6.5 us: whole(): lax.ppermute(spare[at][3], ('side', 'orb'), slanted_up)]
    all_to_all x2 -> x1, blocking collectives: 19.3 us -> 8.93 us  [exchanged(): return lax.all_to_all(message, ALL, 0, 0)]
    pallas_call x0 -> x1, Pallas kernels: none -> 7.49 us  [whole(): pl.pallas_call(functools.partial(second_and_bundle_kernel, cell_total), o...]
    ppermute x2, waiting for transfers between devices: 5.36 us -> 11.9 us  [whole(): lax.ppermute(sent[3 * at + 2], slab_axes, ahead)]
    all_to_all x0 -> x1, waiting for transfers between devices: none -> 6.23 us  [exchanged(): return lax.all_to_all(message, ALL, 0, 0)]
    ppermute x14, waiting for transfers between devices: 10.3 us -> 4.83 us  [whole(): lax.ppermute(pieces[m], ('side', 'orb'), [(flat_of(i), flat_of(i ^ m)) fo...]
    ppermute x1, waiting for transfers between devices: 4.84 us -> 0.01 us  [whole(): lax.ppermute(edge, slab_axes, ahead)]
  transfers between devices with their start and end apart: 26 -> 35, of which waited for: 12 -> 9; matrix products, arithmetic and copies ran while one was open for 0% -> 0% of each run, Pallas kernels for 7% -> 17%
where the time goes in v6:
time: 127 us
  starting transfers between devices  44.5 us (35%)
  waiting for transfers between devices  35.1 us (28%)
  Pallas kernels  32.3 us (25%)
  blocking collectives  8.93 us (7%)
  local copies, waits for them, and re-layouts  5.61 us (4%)
    ppermute x14, starting transfers between devices, whole(): lax.ppermute(pieces[m], ('side', 'orb'), [(flat_of(i), flat_of(i ^ m)) fo...  13.2 us
    pallas_call x2, Pallas kernels, small_call(): pl.pallas_call(kernel, out_shape=out_shape, in_specs=specs, out_specs=jax...  12.6 us
    ppermute x2, waiting for transfers between devices, whole(): lax.ppermute(sent[3 * at + 2], slab_axes, ahead)  11.9 us
    pallas_call x2, Pallas kernels, filtered_pieces(): pl.pallas_call(functools.partial(filter_kernel, at, len(pot_far)), out_sh...  10.9 us
    ppermute x3, waiting for transfers between devices, whole(): lax.ppermute(joined, 'orb', [(i, i ^ m) for i in range(orb_count)])  9.55 us
    all_to_all x1, blocking collectives, exchanged(): return lax.all_to_all(message, ALL, 0, 0)  8.93 us
    pallas_call x1, Pallas kernels, whole(): pl.pallas_call(functools.partial(second_and_bundle_kernel, cell_total), o...  7.49 us
    ppermute x2, starting transfers between devices, whole(): lax.ppermute(spare[at][3], ('side', 'orb'), slanted_up)  6.5 us
  transfers between devices with their start and end apart: 35, of which 9 were waited for; matrix products, arithmetic and copies ran while one was open for 0% of the time, Pallas kernels for 17%

profile of v6, /device:TPU:0, one launch (start us, length us, event | category | flops | bytes accessed | tf_op | source)
XLA Modules:
  0.0 126.7 jit_solution(13510288973537408011)
XLA Ops:
  3.8 3.0 %collective-permute-start.3 = (f32[12,16,128]{2,1,0:T(8,128)S(1)}, f32[12,16,128]{2,1,0:T(8,128)S(1)}, u32[]{:S(2)}, u32[]{:S(2)}) collective-permute-start(f32[12,16,128]{2,1,0:T(8,128)S(1)} %get-tuple-element.45), channel_id=1, source_target_pairs={{0,4},{4,0},{1,5},{5,1},{2,6},{6,2},{3,7},{7,3},{8,12},{12,8},{9,1... | collective-permute-start | bytes 294920 | tf_op jit(solution)/shard_map/ppermute | solution.py:416
  6.8 3.6 %collective-permute-start.5 = (f32[6,16,128]{2,1,0:T(8,128)S(1)}, f32[6,16,128]{2,1,0:T(8,128)S(1)}, u32[]{:S(2)}, u32[]{:S(2)}) collective-permute-start(f32[6,16,128]{2,1,0:T(8,128)S(1)} %get-tuple-element.46), channel_id=1, source_target_pairs={{0,24},{4,12},{8,0},{12,20},{16,8},{20,28},{24,16},{28,4},{1,25},{... | collective-permute-start | bytes 147464 | tf_op jit(solution)/shard_map/ppermute | solution.py:418
  10.4 4.7 %collective-permute-start.10 = (f32[9,64,128]{2,1,0:T(8,128)S(1)}, f32[9,64,128]{2,1,0:T(8,128)S(1)}, u32[]{:S(2)}, u32[]{:S(2)}) collective-permute-start(f32[9,64,128]{2,1,0:T(8,128)S(1)} %get-tuple-element.49), channel_id=1, source_target_pairs={{0,28},{4,8},{8,4},{12,16},{16,12},{20,24},{24,20},{28,0},{1,29},{... | collective-permute-start | bytes 884744 | tf_op jit(solution)/shard_map/ppermute | solution.py:435
  15.1 2.6 %collective-permute-done.4.slanted = f32[6,16,128]{2,1,0:T(8,128)S(1)} collective-permute-done((f32[6,16,128]{2,1,0:T(8,128)S(1)}, f32[6,16,128]{2,1,0:T(8,128)S(1)}, u32[]{:S(2)}, u32[]{:S(2)}) %collective-permute-start.4) | collective-permute-done | bytes 49184 | tf_op jit(solution)/shard_map/ppermute | solution.py:417
  19.7 5.3 %collective-permute-done.8.rest_3_ = f32[24,16,128]{2,1,0:T(8,128)S(1)} collective-permute-done((f32[24,16,128]{2,1,0:T(8,128)S(1)}, f32[24,16,128]{2,1,0:T(8,128)S(1)}, u32[]{:S(2)}, u32[]{:S(2)}) %collective-permute-start.8) | collective-permute-done | bytes 196640 | tf_op jit(solution)/shard_map/ppermute | solution.py:428
  24.9 4.3 %collective-permute-done.7.rest_2_ = f32[24,16,128]{2,1,0:T(8,128)S(1)} collective-permute-done((f32[24,16,128]{2,1,0:T(8,128)S(1)}, f32[24,16,128]{2,1,0:T(8,128)S(1)}, u32[]{:S(2)}, u32[]{:S(2)}) %collective-permute-start.7) | collective-permute-done | bytes 196640 | tf_op jit(solution)/shard_map/ppermute | solution.py:428
  31.3 7.8 %collective-permute-done.11.straight = f32[9,64,128]{2,1,0:T(8,128)S(1)} collective-permute-done((f32[9,64,128]{2,1,0:T(8,128)S(1)}, f32[9,64,128]{2,1,0:T(8,128)S(1)}, u32[]{:S(2)}, u32[]{:S(2)}) %collective-permute-start.11) | collective-permute-done | bytes 294944 | tf_op jit(solution)/shard_map/ppermute | solution.py:437
  39.1 5.4 %shard_map.31 = (f32[12,16,128]{2,1,0:T(8,128)S(1)}, f32[12,16,128]{2,1,0:T(8,128)S(1)}, f32[12,16,128]{2,1,0:T(8,128)S(1)}, f32[12,16,128]{2,1,0:T(8,128)S(1)},...) custom-call(s32[3]{0:T(128)S(1)} %pad_add_fusion.place, ...), custom_call_target="tpu_custom_call" | custom-call | tf_op jit(solution)/shard_map/pallas_call | solution.py:192
  44.6 2.1 %collective-permute-start.17 = (f32[12,16,128]{2,1,0:T(8,128)S(1)}, f32[12,16,128]{2,1,0:T(8,128)S(1)}, u32[]{:S(2)}, u32[]{:S(2)}) collective-permute-start(f32[12,16,128]{2,1,0:T(8,128)S(1)} %get-tuple-element.57), channel_id=1, source_target_pairs={{0,5},{4,1},{1,4},{5,0},{2,7},{6,3},{3,6},{7,2},{8,13},{12,9},{9,1... | collective-permute-start | bytes 294920 | tf_op jit(solution)/shard_map/ppermute | solution.py:451
  46.7 4.1 %collective-permute-done.2.straight = f32[9,64,128]{2,1,0:T(8,128)S(1)} collective-permute-done((f32[9,64,128]{2,1,0:T(8,128)S(1)}, f32[9,64,128]{2,1,0:T(8,128)S(1)}, u32[]{:S(2)}, u32[]{:S(2)}) %collective-permute-start.2) | collective-permute-done | bytes 294944 | tf_op jit(solution)/shard_map/ppermute | solution.py:437
  51.8 5.5 %shard_map.30 = (f32[12,16,128]{2,1,0:T(8,128)S(1)}, f32[12,16,128]{2,1,0:T(8,128)S(1)}, f32[12,16,128]{2,1,0:T(8,128)S(1)}, f32[12,16,128]{2,1,0:T(8,128)S(1)},...) custom-call(s32[3]{0:T(128)S(1)} %pad_add_fusion.place, ...), custom_call_target="tpu_custom_call" | custom-call | tf_op jit(solution)/shard_map/pallas_call | solution.py:192
  57.3 3.7 %collective-permute-start.25 = (f32[12,16,128]{2,1,0:T(8,128)S(1)}, f32[12,16,128]{2,1,0:T(8,128)S(1)}, u32[]{:S(2)}, u32[]{:S(2)}) collective-permute-start(f32[12,16,128]{2,1,0:T(8,128)S(1)} %get-tuple-element.65), channel_id=1, source_target_pairs={{0,7},{4,3},{1,6},{5,2},{2,5},{6,1},{3,4},{7,0},{8,15},{12,11},{9,... | collective-permute-start | bytes 294920 | tf_op jit(solution)/shard_map/ppermute | solution.py:451
  61.1 2.1 %collective-permute-start.16 = (f32[12,16,128]{2,1,0:T(8,128)S(1)}, f32[12,16,128]{2,1,0:T(8,128)S(1)}, u32[]{:S(2)}, u32[]{:S(2)}) collective-permute-start(f32[12,16,128]{2,1,0:T(8,128)S(1)} %get-tuple-element.56), channel_id=1, source_target_pairs={{0,5},{4,1},{1,4},{5,0},{2,7},{6,3},{3,6},{7,2},{8,13},{12,9},{9,1... | collective-permute-start | bytes 294920 | tf_op jit(solution)/shard_map/ppermute | solution.py:451
  66.6 2.1 %collective-permute-start.20 = (f32[12,16,128]{2,1,0:T(8,128)S(1)}, f32[12,16,128]{2,1,0:T(8,128)S(1)}, u32[]{:S(2)}, u32[]{:S(2)}) collective-permute-start(f32[12,16,128]{2,1,0:T(8,128)S(1)} %get-tuple-element.60), channel_id=1, source_target_pairs={{0,6},{4,2},{1,7},{5,3},{2,4},{6,0},{3,5},{7,1},{8,14},{12,10},{9,... | collective-permute-start | bytes 294920 | tf_op jit(solution)/shard_map/ppermute | solution.py:451
  70.2 3.0 %collective-permute-start.29 = (f32[2,12,16,128]{3,2,1,0:T(8,128)S(1)}, f32[2,12,16,128]{3,2,1,0:T(8,128)S(1)}, u32[]{:S(2)}, u32[]{:S(2)}) collective-permute-start(f32[2,12,16,128]{3,2,1,0:T(8,128)S(1)} %get-tuple-element.73), channel_id=1, source_target_pairs={{0,2},{1,3},{4,6},{5,7},{8,10},{9,11},{12,14},{13,15},{16,18},{17,... | collective-permute-start | bytes 589832 | tf_op jit(solution)/shard_map/ppermute | solution.py:473
  73.2 2.1 %collective-permute-done.20.refs_10_ = f32[12,16,128]{2,1,0:T(8,128)S(1)} collective-permute-done((f32[12,16,128]{2,1,0:T(8,128)S(1)}, f32[12,16,128]{2,1,0:T(8,128)S(1)}, u32[]{:S(2)}, u32[]{:S(2)}) %collective-permute-start.20) | collective-permute-done | bytes 98336 | tf_op jit(solution)/shard_map/ppermute | solution.py:451
  75.3 4.5 %collective-permute-start.31 = (f32[2,12,16,128]{3,2,1,0:T(8,128)}, f32[2,12,16,128]{3,2,1,0:T(8,128)}, u32[]{:S(2)}, u32[]{:S(2)}) collective-permute-start(f32[2,12,16,128]{3,2,1,0:T(8,128)} %get-tuple-element.75), channel_id=1, source_target_pairs={{0,6},{1,7},{4,2},{5,3},{8,14},{9,15},{12,10},{13,11},{16,22},{17,... | collective-permute-start | bytes 589832 | tf_op jit(solution)/shard_map/ppermute | solution.py:474
  83.2 2.0 %collective-permute-start.30 = (f32[2,12,16,128]{3,2,1,0:T(8,128)}, f32[2,12,16,128]{3,2,1,0:T(8,128)}, u32[]{:S(2)}, u32[]{:S(2)}) collective-permute-start(f32[2,12,16,128]{3,2,1,0:T(8,128)} %get-tuple-element.74), channel_id=1, source_target_pairs={{0,6},{1,7},{4,2},{5,3},{8,14},{9,15},{12,10},{13,11},{16,22},{17,... | collective-permute-start | bytes 589832 | tf_op jit(solution)/shard_map/ppermute | solution.py:474
  85.2 3.6 %shard_map.32 = (f32[16,192,128]{2,1,0:T(8,128)S(1)}, f32[32,1,256]{2,1,0:T(1,128)}) custom-call(s32[3]{0:T(128)S(1)} %pad_add_fusion.place, f32[12,16,128]{2,1,0:T(8,128)S(1)} %get-tuple-element.47.refs_0_, f32[12,16,128]{2,1,0:T(8,128)S(1)} %get-tuple-element.51.refs_1_, f32[12,16,128]{2,1,0:T(8,128)S(1)} %collective-permute-done.12.refs_2_, ...), custom_call_target="tpu_custom_call" | custom-call | tf_op jit(solution)/shard_map/pallas_call | solution.py:384
  88.9 3.3 %all-to-all-start = ((f32[32,1,256]{2,1,0:T(1,128)}), f32[32,1,256]{2,1,0:T(1,128)}, u32[]{:S(2)}, u32[]{:S(2)}) async-start(f32[32,1,256]{2,1,0:T(1,128)} %get-tuple-element.66), calls=%async_computation | async-start | bytes 65536 | tf_op jit(solution)/shard_map/all_to_all | solution.py:461
  93.0 6.2 %all-to-all-done.copies = f32[32,1,256]{2,1,0:T(1,128)} async-done(((f32[32,1,256]{2,1,0:T(1,128)}), f32[32,1,256]{2,1,0:T(1,128)}, u32[]{:S(2)}, u32[]{:S(2)}) %all-to-all-start) | async-done | bytes 32800 | tf_op jit(solution)/shard_map/all_to_all | solution.py:461
  101.1 7.5 %shard_map.33 = (f32[16,128]{1,0:T(8,128)S(1)}, f32[32,1,256]{2,1,0:T(1,128)S(1)}, f32[8,384,128]{2,1,0:T(8,128)S(1)}) custom-call(s32[3]{0:T(128)S(1)} %pad_add_fusion.place, f32[32,1,256]{2,1,0:T(1,128)} %all-to-all-done.copies, f32[16,192,128]{2,1,0:T(8,128)S(1)} %get-tuple-element.67.block, f32[2,12,16,128]{3,2,1,0:T(8,128)S(1)} %get-tuple-element.68.refs_0_, ...), custom_call_target="tpu_custom_call" | custom-call | tf_op jit(solution)/shard_map/pallas_call | solution.py:478
  108.8 8.9 %all_to_all.10.copies = f32[32,1,256]{2,1,0:T(1,128)S(1)} all-to-all(f32[32,1,256]{2,1,0:T(1,128)S(1)} %get-tuple-element.76), channel_id=1, replica_groups=mesh['pair'=4,'side'=2,'orb'=4] {'pair','side','orb'}, dimensions={0} | all-to-all | bytes 65536 | tf_op jit(solution)/shard_map/all_to_all | solution.py:461
  117.8 9.0 %shard_map.34 = f32[4,12,64,128]{3,2,1,0:T(8,128)} custom-call(s32[3]{0:T(128)S(1)} %pad_add_fusion.place, f32[32,1,256]{2,1,0:T(1,128)S(1)} %all_to_all.10.copies, f32[16,128]{1,0:T(8,128)S(1)} %get-tuple-element.77.table, f32[16,192,128]{2,1,0:T(8,128)S(1)} %get-tuple-element.67.block, f32[16,192,128]{2,1,0:T(8,128)S(1)} %collective-permute-done.32.block_near, ...), custom_call_target="tpu_custom_call" | custom-call | tf_op jit(solution)/shard_map/pallas_call | solution.py:384
  (72 shorter events, 20.3 us)
Async XLA Ops:
  3.8 14.0 %collective-permute-start.3 = (f32[12,16,128]{2,1,0:T(8,128)S(1)}, f32[12,16,128]{2,1,0:T(8,128)S(1)}, u32[]{:S(2)}, u32[]{:S(2)}) collective-permute-start(f32[12,16,128]{2,1,0:T(8,128)S(1)} %get-tuple-element.45), channel_id=1, source_target_pairs={{0,4},{4,0},{1,5},{5,1},{2,6},{6,2},{3,7},{7,3},{8,12},{12,8},{9,1... | collective-permute-start | bytes 294920 | tf_op jit(solution)/shard_map/ppermute | solution.py:416
  10.4 19.8 %collective-permute-start.10 = (f32[9,64,128]{2,1,0:T(8,128)S(1)}, f32[9,64,128]{2,1,0:T(8,128)S(1)}, u32[]{:S(2)}, u32[]{:S(2)}) collective-permute-start(f32[9,64,128]{2,1,0:T(8,128)S(1)} %get-tuple-element.49), channel_id=1, source_target_pairs={{0,28},{4,8},{8,4},{12,16},{16,12},{20,24},{24,20},{28,0},{1,29},{... | collective-permute-start | bytes 884744 | tf_op jit(solution)/shard_map/ppermute | solution.py:435
  17.8 11.4 %collective-permute-start.7 = (f32[24,16,128]{2,1,0:T(8,128)S(1)}, f32[24,16,128]{2,1,0:T(8,128)S(1)}, u32[]{:S(2)}, u32[]{:S(2)}) collective-permute-start(f32[24,16,128]{2,1,0:T(8,128)S(1)} %shard_map.29.rest_0_), channel_id=1, source_target_pairs={{0,2},{1,3},{2,0},{3,1},{4,6},{5,7},{6,4},{7,5},{8,10},{9,11},{10,... | collective-permute-start | bytes 589832 | tf_op jit(solution)/shard_map/ppermute | solution.py:428
  19.4 9.8 %collective-permute-start.6 = (f32[24,16,128]{2,1,0:T(8,128)S(1)}, f32[24,16,128]{2,1,0:T(8,128)S(1)}, u32[]{:S(2)}, u32[]{:S(2)}) collective-permute-start(f32[24,16,128]{2,1,0:T(8,128)S(1)} %shard_map.29.rest_0_), channel_id=1, source_target_pairs={{0,1},{1,0},{2,3},{3,2},{4,5},{5,4},{6,7},{7,6},{8,9},{9,8},{10,11... | collective-permute-start | bytes 589832 | tf_op jit(solution)/shard_map/ppermute | solution.py:428
  19.7 19.4 %collective-permute-start.9 = (f32[12,64,128]{2,1,0:T(8,128)S(1)}, f32[12,64,128]{2,1,0:T(8,128)S(1)}, u32[]{:S(2)}, u32[]{:S(2)}) collective-permute-start(f32[12,64,128]{2,1,0:T(8,128)S(1)} %get-tuple-element.48), channel_id=1, source_target_pairs={{0,4},{4,0},{1,5},{5,1},{2,6},{6,2},{3,7},{7,3},{8,12},{12,8},{9,1... | collective-permute-start | bytes 1179656 | tf_op jit(solution)/shard_map/ppermute | solution.py:436
  24.9 26.4 %collective-permute-start = (f32[12,64,128]{2,1,0:T(8,128)S(1)}, f32[12,64,128]{2,1,0:T(8,128)S(1)}, u32[]{:S(2)}, u32[]{:S(2)}) collective-permute-start(f32[12,64,128]{2,1,0:T(8,128)S(1)} %get-tuple-element.42), channel_id=1, source_target_pairs={{0,4},{4,0},{1,5},{5,1},{2,6},{6,2},{3,7},{7,3},{8,12},{12,8},{9,1... | collective-permute-start | bytes 1179656 | tf_op jit(solution)/shard_map/ppermute | solution.py:436
  29.2 9.9 %collective-permute-start.11 = (f32[9,64,128]{2,1,0:T(8,128)S(1)}, f32[9,64,128]{2,1,0:T(8,128)S(1)}, u32[]{:S(2)}, u32[]{:S(2)}) collective-permute-start(f32[9,64,128]{2,1,0:T(8,128)S(1)} %get-tuple-element.50), channel_id=1, source_target_pairs={{0,24},{4,12},{8,0},{12,20},{16,8},{20,28},{24,16},{28,4},{1,25},{... | collective-permute-start | bytes 884744 | tf_op jit(solution)/shard_map/ppermute | solution.py:437
  29.2 15.3 %collective-permute-start.1 = (f32[9,64,128]{2,1,0:T(8,128)S(1)}, f32[9,64,128]{2,1,0:T(8,128)S(1)}, u32[]{:S(2)}, u32[]{:S(2)}) collective-permute-start(f32[9,64,128]{2,1,0:T(8,128)S(1)} %get-tuple-element.43), channel_id=1, source_target_pairs={{0,28},{4,8},{8,4},{12,16},{16,12},{20,24},{24,20},{28,0},{1,29},{... | collective-permute-start | bytes 884744 | tf_op jit(solution)/shard_map/ppermute | solution.py:435
  30.2 20.6 %collective-permute-start.2 = (f32[9,64,128]{2,1,0:T(8,128)S(1)}, f32[9,64,128]{2,1,0:T(8,128)S(1)}, u32[]{:S(2)}, u32[]{:S(2)}) collective-permute-start(f32[9,64,128]{2,1,0:T(8,128)S(1)} %get-tuple-element.44), channel_id=1, source_target_pairs={{0,24},{4,12},{8,0},{12,20},{16,8},{20,28},{24,16},{28,4},{1,25},{... | collective-permute-start | bytes 884744 | tf_op jit(solution)/shard_map/ppermute | solution.py:437
  44.5 12.8 %collective-permute-start.15 = (f32[12,16,128]{2,1,0:T(8,128)S(1)}, f32[12,16,128]{2,1,0:T(8,128)S(1)}, u32[]{:S(2)}, u32[]{:S(2)}) collective-permute-start(f32[12,16,128]{2,1,0:T(8,128)S(1)} %get-tuple-element.55), channel_id=1, source_target_pairs={{0,1},{4,5},{1,0},{5,4},{2,3},{6,7},{3,2},{7,6},{8,9},{12,13},{9,8... | collective-permute-start | bytes 294920 | tf_op jit(solution)/shard_map/ppermute | solution.py:451
  44.6 16.4 %collective-permute-start.17 = (f32[12,16,128]{2,1,0:T(8,128)S(1)}, f32[12,16,128]{2,1,0:T(8,128)S(1)}, u32[]{:S(2)}, u32[]{:S(2)}) collective-permute-start(f32[12,16,128]{2,1,0:T(8,128)S(1)} %get-tuple-element.57), channel_id=1, source_target_pairs={{0,5},{4,1},{1,4},{5,0},{2,7},{6,3},{3,6},{7,2},{8,13},{12,9},{9,1... | collective-permute-start | bytes 294920 | tf_op jit(solution)/shard_map/ppermute | solution.py:451
  50.8 10.2 %collective-permute-start.19 = (f32[12,16,128]{2,1,0:T(8,128)S(1)}, f32[12,16,128]{2,1,0:T(8,128)S(1)}, u32[]{:S(2)}, u32[]{:S(2)}) collective-permute-start(f32[12,16,128]{2,1,0:T(8,128)S(1)} %get-tuple-element.59), channel_id=1, source_target_pairs={{0,2},{4,6},{1,3},{5,7},{2,0},{6,4},{3,1},{7,5},{8,10},{12,14},{9,... | collective-permute-start | bytes 294920 | tf_op jit(solution)/shard_map/ppermute | solution.py:451
  51.3 9.7 %collective-permute-start.21 = (f32[12,16,128]{2,1,0:T(8,128)S(1)}, f32[12,16,128]{2,1,0:T(8,128)S(1)}, u32[]{:S(2)}, u32[]{:S(2)}) collective-permute-start(f32[12,16,128]{2,1,0:T(8,128)S(1)} %get-tuple-element.61), channel_id=1, source_target_pairs={{0,6},{4,2},{1,7},{5,3},{2,4},{6,0},{3,5},{7,1},{8,14},{12,10},{9,... | collective-permute-start | bytes 294920 | tf_op jit(solution)/shard_map/ppermute | solution.py:451
  51.8 11.3 %collective-permute-start.23 = (f32[12,16,128]{2,1,0:T(8,128)S(1)}, f32[12,16,128]{2,1,0:T(8,128)S(1)}, u32[]{:S(2)}, u32[]{:S(2)}) collective-permute-start(f32[12,16,128]{2,1,0:T(8,128)S(1)} %get-tuple-element.63), channel_id=1, source_target_pairs={{0,3},{4,7},{1,2},{5,6},{2,1},{6,5},{3,0},{7,4},{8,11},{12,15},{9,... | collective-permute-start | bytes 294920 | tf_op jit(solution)/shard_map/ppermute | solution.py:451
  63.1 19.4 %collective-permute-start.27 = (f32[2,12,16,128]{3,2,1,0:T(8,128)S(1)}, f32[2,12,16,128]{3,2,1,0:T(8,128)S(1)}, u32[]{:S(2)}, u32[]{:S(2)}) collective-permute-start(f32[2,12,16,128]{3,2,1,0:T(8,128)S(1)} %get-tuple-element.71), channel_id=1, source_target_pairs={{0,4},{4,0},{1,5},{5,1},{2,6},{6,2},{3,7},{7,3},{8,12},{12,8},{9,1... | collective-permute-start | bytes 589832 | tf_op jit(solution)/shard_map/ppermute | solution.py:472
  68.7 11.1 %collective-permute-start.22 = (f32[12,16,128]{2,1,0:T(8,128)S(1)}, f32[12,16,128]{2,1,0:T(8,128)S(1)}, u32[]{:S(2)}, u32[]{:S(2)}) collective-permute-start(f32[12,16,128]{2,1,0:T(8,128)S(1)} %get-tuple-element.62), channel_id=1, source_target_pairs={{0,3},{4,7},{1,2},{5,6},{2,1},{6,5},{3,0},{7,4},{8,11},{12,15},{9,... | collective-permute-start | bytes 294920 | tf_op jit(solution)/shard_map/ppermute | solution.py:451
  68.7 11.9 %collective-permute-start.24 = (f32[12,16,128]{2,1,0:T(8,128)S(1)}, f32[12,16,128]{2,1,0:T(8,128)S(1)}, u32[]{:S(2)}, u32[]{:S(2)}) collective-permute-start(f32[12,16,128]{2,1,0:T(8,128)S(1)} %get-tuple-element.64), channel_id=1, source_target_pairs={{0,7},{4,3},{1,6},{5,2},{2,5},{6,1},{3,4},{7,0},{8,15},{12,11},{9,... | collective-permute-start | bytes 294920 | tf_op jit(solution)/shard_map/ppermute | solution.py:451
  70.2 21.9 %collective-permute-start.29 = (f32[2,12,16,128]{3,2,1,0:T(8,128)S(1)}, f32[2,12,16,128]{3,2,1,0:T(8,128)S(1)}, u32[]{:S(2)}, u32[]{:S(2)}) collective-permute-start(f32[2,12,16,128]{3,2,1,0:T(8,128)S(1)} %get-tuple-element.73), channel_id=1, source_target_pairs={{0,2},{1,3},{4,6},{5,7},{8,10},{9,11},{12,14},{13,15},{16,18},{17,... | collective-permute-start | bytes 589832 | tf_op jit(solution)/shard_map/ppermute | solution.py:473
  75.3 23.9 %collective-permute-start.31 = (f32[2,12,16,128]{3,2,1,0:T(8,128)}, f32[2,12,16,128]{3,2,1,0:T(8,128)}, u32[]{:S(2)}, u32[]{:S(2)}) collective-permute-start(f32[2,12,16,128]{3,2,1,0:T(8,128)} %get-tuple-element.75), channel_id=1, source_target_pairs={{0,6},{1,7},{4,2},{5,3},{8,14},{9,15},{12,10},{13,11},{16,22},{17,... | collective-permute-start | bytes 589832 | tf_op jit(solution)/shard_map/ppermute | solution.py:474
  79.8 19.4 %collective-permute-start.26 = (f32[2,12,16,128]{3,2,1,0:T(8,128)}, f32[2,12,16,128]{3,2,1,0:T(8,128)}, u32[]{:S(2)}, u32[]{:S(2)}) collective-permute-start(f32[2,12,16,128]{3,2,1,0:T(8,128)} %get-tuple-element.70), channel_id=1, source_target_pairs={{0,4},{4,0},{1,5},{5,1},{2,6},{6,2},{3,7},{7,3},{8,12},{12,8},{9,1... | collective-permute-start | bytes 589832 | tf_op jit(solution)/shard_map/ppermute | solution.py:472
  80.6 18.7 %collective-permute-start.28 = (f32[2,12,16,128]{3,2,1,0:T(8,128)}, f32[2,12,16,128]{3,2,1,0:T(8,128)}, u32[]{:S(2)}, u32[]{:S(2)}) collective-permute-start(f32[2,12,16,128]{3,2,1,0:T(8,128)} %get-tuple-element.72), channel_id=1, source_target_pairs={{0,2},{1,3},{4,6},{5,7},{8,10},{9,11},{12,14},{13,15},{16,18},{17,... | collective-permute-start | bytes 589832 | tf_op jit(solution)/shard_map/ppermute | solution.py:473
  83.2 16.0 %collective-permute-start.30 = (f32[2,12,16,128]{3,2,1,0:T(8,128)}, f32[2,12,16,128]{3,2,1,0:T(8,128)}, u32[]{:S(2)}, u32[]{:S(2)}) collective-permute-start(f32[2,12,16,128]{3,2,1,0:T(8,128)} %get-tuple-element.74), channel_id=1, source_target_pairs={{0,6},{1,7},{4,2},{5,3},{8,14},{9,15},{12,10},{13,11},{16,22},{17,... | collective-permute-start | bytes 589832 | tf_op jit(solution)/shard_map/ppermute | solution.py:474
  88.9 10.4 %all-to-all-start = ((f32[32,1,256]{2,1,0:T(1,128)}), f32[32,1,256]{2,1,0:T(1,128)}, u32[]{:S(2)}, u32[]{:S(2)}) async-start(f32[32,1,256]{2,1,0:T(1,128)} %get-tuple-element.66), calls=%async_computation | async-start | bytes 65536 | tf_op jit(solution)/shard_map/all_to_all | solution.py:461
  92.8 24.9 %collective-permute-start.32 = (f32[16,192,128]{2,1,0:T(8,128)S(1)}, f32[16,192,128]{2,1,0:T(8,128)S(1)}, u32[]{:S(2)}, u32[]{:S(2)}) collective-permute-start(f32[16,192,128]{2,1,0:T(8,128)S(1)} %get-tuple-element.67.block), channel_id=1, source_target_pairs={{0,1},{1,0},{2,3},{3,2},{4,5},{5,4},{6,7},{7,6},{8,9},{9,8},{10,11... | collective-permute-start | bytes 4718600 | tf_op jit(solution)/shard_map/ppermute | solution.py:475
  (19 other events, 160.8 us)

commit v7 on v5

--- a/solution.py
+++ b/solution.py
@@ -18,6 +18,7 @@
 DEEP = REACH * STEPS
 WIDE = REACH * (STEPS - 1)
 EIGHT = 8
+CORES = 2
 BLOCKS = 3
 ALL = ("pair", "side", "orb")
 
@@ -85,9 +86,10 @@
     )
 
 
-def filter_kernel(at, shares, place, own, swapped, slanted, straight, own_pot, lane_table, *rest):
-    pot_far, outs = rest[:shares], rest[shares:-5]
-    field, first, second, weight, sorted_pieces = rest[-5:]
+def filter_kernel(at, shares, early, late, place, own, swapped, slanted, straight, own_pot, lane_table, *rest):
+    pot_far, before, outs = rest[:shares], rest[shares : shares + at], rest[shares + at : -4]
+    field, first, second, weight = rest[-4:]
+    outs, sorted_pieces = outs[:-1], outs[-1]
     side, me, orb = place[0], place[1], place[2]
     rows, cols, _ = swapped.shape
     both = 2 * rows
@@ -165,11 +167,22 @@
         sorted_pieces[2 * to + half, row - half * rows, pl.ds(EIGHT * strip - to * piece, EIGHT), :] = value
 
     step(second, first, 2 * REACH, 2 * REACH, both, store_out)
-    for apart, out in enumerate(outs):
+    for apart, out in zip(early, outs):
         out[...] = sorted_pieces[me ^ apart]
-
-
-def filtered_pieces(at, place, own, slanted_order, own_pot, pot_far, group):
+    stages = (*before, sorted_pieces)
+    for apart, out in zip(late, outs[len(early) :]):
+        for stage, pieces in enumerate(stages):
+            out[stage] = pieces[me ^ apart]
+    for index, out in enumerate(outs[len(early) + len(late) :]):
+        chip = orb // CORES ^ (1 if index < 2 else 0)
+        slab = side ^ (index % 2)
+        for stage, pieces in enumerate(stages):
+            for core in range(CORES):
+                out[stage, core] = pieces[2 * (CORES * chip + core) + slab]
+
+
+def filtered_pieces(at, place, own, fetched, own_pot, pot_far, group, before, early, late, spares):
+    slanted, swapped, straight = fetched
     rows, cols, width = own.shape[1:]
     both = 2 * rows
     apart = jnp.arange(width)[:, None] - jnp.arange(width)[None, :]
@@ -182,20 +195,20 @@
         return pltpu.VMEM((both + 2 * margin, cols + 2 * EIGHT, width), jnp.float32)
 
     piece = (rows, 2 * cols // group, width)
+    shapes = [piece] * len(early) + [(at + 1, *piece)] * len(late) + [(at + 1, CORES, *piece)] * spares + [(group, *piece)]
     return pl.pallas_call(
-        functools.partial(filter_kernel, at, len(pot_far)),
-        out_shape=[jax.ShapeDtypeStruct(piece, jnp.float32)] * group,
-        in_specs=[SMEM] + [VMEM] * (6 + len(pot_far)),
-        out_specs=[VMEM] * group,
+        functools.partial(filter_kernel, at, len(pot_far), early, late),
+        out_shape=[jax.ShapeDtypeStruct(shape, jnp.float32) for shape in shapes],
+        in_specs=[SMEM] + [VMEM] * (6 + len(pot_far) + at),
+        out_specs=[VMEM] * len(shapes),
         scratch_shapes=[
             scratch(DEEP),
             scratch(WIDE),
             scratch(REACH),
             pltpu.VMEM((both + 2 * WIDE, cols, width), jnp.float32),
-            pltpu.VMEM((group,) + piece, jnp.float32),
         ],
         compiler_params=pltpu.CompilerParams(vmem_limit_bytes=24 * 1024 * 1024),
-    )(place, own, slanted_order[1], slanted_order[0], slanted_order[2], own_pot, lane_table.astype(jnp.bfloat16), *pot_far)
+    )(place, own, swapped, slanted, straight, own_pot, lane_table.astype(jnp.bfloat16), *pot_far, *before)
 
 
 LANES = 128
@@ -267,10 +280,14 @@
     return next(c for c in (6, 4, 3, 2, 1) if tiles % c == 0)
 
 
-def first_kernel(kept, place, *refs):
+def first_kernel(early, late, kept, place, *refs):
     given, (block, message) = refs[:-2], refs[-2:]
-    for index, ref in enumerate(given):
-        block[(place[1] ^ (index // kept)) * kept + index % kept] = ref[...].reshape(block.shape[1:])
+    me, shape = place[1], block.shape[1:]
+    for at in range(kept):
+        for index, apart in enumerate(early):
+            block[(me ^ apart) * kept + at] = given[at * len(early) + index][...].reshape(shape)
+        for index, apart in enumerate(late):
+            block[(me ^ apart) * kept + at] = given[kept * len(early) + index][at].reshape(shape)
     total, tiles = block.shape[0], block.shape[1] // EIGHT
     row = gram_message(tile_reader(block), total, tiles, chunk_of(tiles))
     message[...] = jnp.broadcast_to(row[None], message.shape)
@@ -285,6 +302,68 @@
 
 def third_kernel(cell_total, copies, block, basis):
     apply_all(inverse_factor(copies, block.shape[0], cell_total), block, basis)
+
+
+def second_and_bundle_kernel(cell_total, place, copies, block, *refs):
+    given, (table_out, message, bundle, basis) = refs[:-4], refs[-4:]
+    total, tiles = block.shape[0], block.shape[1] // EIGHT
+    table = inverse_factor(copies, total, cell_total)
+    table_out[...] = table
+    apply_all(table, block, basis)
+    row = gram_message(tile_reader(basis), total, tiles, chunk_of(tiles))
+    message[...] = jnp.broadcast_to(row[None], message.shape)
+    side, kept = place[0], given[0].shape[0]
+    for kind, ref in enumerate(given):
+        for at in range(kept):
+            slot = (kind // 2) * 2 * kept + (side ^ (kind % 2)) * kept + at
+            bundle[slot] = ref[at].reshape(bundle.shape[1:])
+
+
+def last_kernel(cell_total, place, copies, table, block, block_near, bundle, bundle_near, out, splats):
+    total, length, width = block.shape
+    held, rows = out.shape[:2]
+    part = length // rows
+    orb = place[2]
+    core, chip = orb % CORES, orb // CORES
+    second = inverse_factor(copies, total, cell_total)
+    pick = table_of((LANES, total), lambda r, c: r - total == c)
+    product = exact_dot(exact_dot(second, pick), exact_dot(table[...], pick))
+    own = exact_dot(table_of((held * EIGHT, total), lambda r, c: orb * held + r // EIGHT == c), product)
+    wide = exact_dot(own, table_of((total, total * width), lambda r, c: c // width == r))
+    for orbital in range(total):
+        splats[orbital] = wide[:, orbital * width : (orbital + 1) * width].reshape(held, EIGHT, width)
+
+    def write(sources, first_column):
+        def body(row, carry):
+            for strip in range(part // EIGHT):
+                sums = None
+                for orbital, load in sources:
+                    values = load(row, strip)
+                    terms = [splats[orbital, i] * values for i in range(held)]
+                    sums = terms if sums is None else [a + b for a, b in zip(sums, terms)]
+                column = pl.multiple_of(first_column + strip * EIGHT, EIGHT)
+                for i in range(held):
+                    out[i, row, pl.ds(column, EIGHT), :] = sums[i]
+            return carry
+
+        lax.fori_loop(0, rows, body, 0, unroll=2)
+
+    def at(ref, index, offset=0):
+        def load(row, strip):
+            start = pl.multiple_of(offset + row * part + strip * EIGHT, EIGHT)
+            return ref[index, pl.ds(start, EIGHT), :]
+
+        return load
+
+    write([(j, at(block, j)) for j in range(total)], orb * part)
+    write([(j, at(block_near, j)) for j in range(total)], (orb ^ 1) * part)
+    for share in range(CORES):
+        sources = []
+        for flip, ref in enumerate((bundle, bundle_near)):
+            for j in range(2 * held):
+                quad = (core if j // held else orb) ^ flip
+                sources.append((quad * held + j % held, at(ref, j, share * length)))
+        write(sources, ((1 - chip) * CORES + share) * part)
 
 
 def apply_all(table, block, basis):
@@ -361,18 +440,35 @@
             )
         )
 
-    returned = []
-    order = sorted(range(1, group), key=lambda m: (-(m // 4 > 0) - m % 2, m))
-    spot = {m: 1 + index for index, m in enumerate(order)} | {0: 0}
+    early = tuple(sorted((m for m in range(1, group) if m >= 2 * CORES), key=lambda m: (-(m % 2), m)))
+    late = tuple(m for m in range(group) if m < 2 * CORES)
+    spares = 4 if orb_count == 2 * CORES and kept == 2 else 0
+
+    def to_partner(piece, m):
+        if m == 0:
+            return piece
+        return lax.ppermute(piece, ("side", "orb"), [(flat_of(i), flat_of(i ^ m)) for i in range(group)])
+
+    parts, before = [], []
     for at in range(kept):
-        pieces = filtered_pieces(at, place, orbitals, fetched[at], potential, pot_far, group)
-        returned.append(
-            [pieces[0]]
-            + [
-                lax.ppermute(pieces[m], ("side", "orb"), [(flat_of(i), flat_of(i ^ m)) for i in range(group)])
-                for m in order
-            ]
+        final = at == kept - 1
+        outs = filtered_pieces(
+            at,
+            place,
+            orbitals,
+            fetched[at],
+            potential,
+            pot_far,
+            group,
+            before,
+            early,
+            late if final else (),
+            spares if final else 0,
         )
+        parts += [to_partner(piece, m) for piece, m in zip(outs, early)]
+        before.append(outs[-1])
+    parts += [to_partner(piece, m) for piece, m in zip(outs[len(early) :], late)]
+    spare = outs[len(early) + len(late) : -1]
     total, devices = held * orb_count, slabs * orb_count
     cell_total = rows * part * width * devices
     block_shape = jax.ShapeDtypeStruct((total, rows * part, width), jnp.float32)
@@ -381,10 +477,39 @@
     def exchanged(message):
         return lax.all_to_all(message, ALL, 0, 0)
 
-    parts = [returned[at][spot[m]] for m in range(group) for at in range(kept)]
     block, message = small_call(
-        functools.partial(first_kernel, kept), [block_shape, message_shape], [SMEM] + [VMEM] * len(parts), place, *parts
-    )
+        functools.partial(first_kernel, early, late, kept), [block_shape, message_shape], [SMEM] + [VMEM] * len(parts), place, *parts
+    )
+    if spares:
+        up = [(i, i + CORES) for i in range(CORES)]
+        slanted_up = [(s * orb_count + i, (1 - s) * orb_count + i + CORES) for s in range(2) for i in range(CORES)]
+        cores = [(i, i ^ 1) for i in range(orb_count)]
+        given = [
+            spare[0],
+            lax.ppermute(spare[1], "side", swap),
+            lax.ppermute(spare[2], "orb", up),
+            lax.ppermute(spare[3], ("side", "orb"), slanted_up),
+        ]
+        block_near = lax.ppermute(block, "orb", cores)
+        bundle_shape = jax.ShapeDtypeStruct((2 * held, CORES * rows * part, width), jnp.float32)
+        table_shape = jax.ShapeDtypeStruct((total, LANES), jnp.float32)
+        table, message, bundle = pl.pallas_call(
+            functools.partial(second_and_bundle_kernel, cell_total),
+            out_shape=[table_shape, message_shape, bundle_shape],
+            in_specs=[SMEM] + [VMEM] * (2 + len(given)),
+            out_specs=[VMEM] * 3,
+            scratch_shapes=[pltpu.VMEM(block_shape.shape, jnp.float32)],
+            compiler_params=pltpu.CompilerParams(vmem_limit_bytes=24 * 1024 * 1024),
+        )(place, exchanged(message), block, *given)
+        bundle_near = lax.ppermute(bundle, "orb", cores)
+        return pl.pallas_call(
+            functools.partial(last_kernel, cell_total),
+            out_shape=jax.ShapeDtypeStruct((held, rows, cols, width), jnp.float32),
+            in_specs=[SMEM] + [VMEM] * 6,
+            out_specs=VMEM,
+            scratch_shapes=[pltpu.VMEM((total, held, EIGHT, width), jnp.float32)],
+            compiler_params=pltpu.CompilerParams(vmem_limit_bytes=24 * 1024 * 1024),
+        )(place, exchanged(message), table, block, block_near, bundle, bundle_near)
     basis, message = small_call(
         functools.partial(second_kernel, cell_total), [block_shape, message_shape], [VMEM] * 2, exchanged(message), block
     )

time: 131 us -> 131 us (level)
  blocking collectives: 41.8 us -> 8.93 us
  waiting for transfers between devices: 31.8 us -> 56 us
  Pallas kernels: 23.8 us -> 29.4 us
  starting transfers between devices: 29.4 us -> 33.8 us
  local copies, waits for them, and re-layouts: 3.78 us -> 2.41 us
    all_to_all x1 -> x0, blocking collectives: 22.5 us -> none  [whole(): return lax.all_to_all(basis, 'orb', split_axis=0, concat_axis=2, tiled=True)]
    pallas_call x2 -> x4, Pallas kernels: 9.39 us -> 24.5 us  [the longest x2 10.6 us: filtered_pieces(): pl.pallas_call(functools.partial(filter_kernel, at, len(pot_far), early,...]
    ppermute x14 -> x16, waiting for transfers between devices: 10.3 us -> 24.2 us  [the longest x11 24.2 us: to_partner(): lax.ppermute(piece, ('side', 'orb'), [(flat_of(i), flat_of(i ^ m)) for i...]
    all_to_all x2 -> x1, blocking collectives: 19.3 us -> 8.93 us  [exchanged(): return lax.all_to_all(message, ALL, 0, 0)]
    pallas_call x3 -> x1, Pallas kernels: 13.1 us -> 3.66 us  [small_call(): pl.pallas_call(kernel, out_shape=out_shape, in_specs=specs, out_specs=jax...]
    ppermute x2, waiting for transfers between devices: 5.36 us -> 12.6 us  [whole(): lax.ppermute(sent[3 * at + 2], slab_axes, ahead)]
    all_to_all x0 -> x1, waiting for transfers between devices: none -> 6.99 us  [exchanged(): return lax.all_to_all(message, ALL, 0, 0)]
    ppermute x1, waiting for transfers between devices: 4.84 us -> 0.01 us  [whole(): lax.ppermute(edge, slab_axes, ahead)]
  transfers between devices with their start and end apart: 26 -> 29, of which waited for: 12 -> 11; matrix products, arithmetic and copies ran while one was open for 0% -> 0% of each run, Pallas kernels for 7% -> 17%
where the time goes in v7:
time: 131 us
  waiting for transfers between devices  56 us (43%)
  starting transfers between devices  33.8 us (26%)
  Pallas kernels  29.4 us (22%)
  blocking collectives  8.93 us (7%)
  local copies, waits for them, and re-layouts  2.41 us (2%)
    ppermute x11, waiting for transfers between devices, to_partner(): lax.ppermute(piece, ('side', 'orb'), [(flat_of(i), flat_of(i ^ m)) for i...  24.2 us
    ppermute x2, waiting for transfers between devices, whole(): lax.ppermute(sent[3 * at + 2], slab_axes, ahead)  12.6 us
    pallas_call x2, Pallas kernels, filtered_pieces(): pl.pallas_call(functools.partial(filter_kernel, at, len(pot_far), early,...  10.6 us
    ppermute x3, waiting for transfers between devices, whole(): lax.ppermute(joined, 'orb', [(i, i ^ m) for i in range(orb_count)])  9.55 us
    all_to_all x1, blocking collectives, exchanged(): return lax.all_to_all(message, ALL, 0, 0)  8.93 us
    pallas_call x1, Pallas kernels, whole(): pl.pallas_call(functools.partial(second_and_bundle_kernel, cell_total), o...  7.47 us
    all_to_all x1, waiting for transfers between devices, exchanged(): return lax.all_to_all(message, ALL, 0, 0)  6.99 us
    ppermute x11, starting transfers between devices, to_partner(): lax.ppermute(piece, ('side', 'orb'), [(flat_of(i), flat_of(i ^ m)) for i...  6.47 us
  transfers between devices with their start and end apart: 29, of which 11 were waited for; matrix products, arithmetic and copies ran while one was open for 0% of the time, Pallas kernels for 17%

profile of v7, /device:TPU:0, one launch (start us, length us, event | category | flops | bytes accessed | tf_op | source)
XLA Modules:
  0.0 130.9 jit_solution(17578068117983187212)
XLA Ops:
  3.8 3.0 %collective-permute-start.3 = (f32[12,16,128]{2,1,0:T(8,128)S(1)}, f32[12,16,128]{2,1,0:T(8,128)S(1)}, u32[]{:S(2)}, u32[]{:S(2)}) collective-permute-start(f32[12,16,128]{2,1,0:T(8,128)S(1)} %get-tuple-element.38), channel_id=1, source_target_pairs={{0,4},{4,0},{1,5},{5,1},{2,6},{6,2},{3,7},{7,3},{8,12},{12,8},{9,1... | collective-permute-start | bytes 294920 | tf_op jit(solution)/shard_map/ppermute | solution.py:418
  6.8 3.6 %collective-permute-start.5 = (f32[6,16,128]{2,1,0:T(8,128)S(1)}, f32[6,16,128]{2,1,0:T(8,128)S(1)}, u32[]{:S(2)}, u32[]{:S(2)}) collective-permute-start(f32[6,16,128]{2,1,0:T(8,128)S(1)} %get-tuple-element.39), channel_id=1, source_target_pairs={{0,24},{4,12},{8,0},{12,20},{16,8},{20,28},{24,16},{28,4},{1,25},{... | collective-permute-start | bytes 147464 | tf_op jit(solution)/shard_map/ppermute | solution.py:420
  10.4 4.7 %collective-permute-start.1 = (f32[9,64,128]{2,1,0:T(8,128)S(1)}, f32[9,64,128]{2,1,0:T(8,128)S(1)}, u32[]{:S(2)}, u32[]{:S(2)}) collective-permute-start(f32[9,64,128]{2,1,0:T(8,128)S(1)} %get-tuple-element.36), channel_id=1, source_target_pairs={{0,28},{4,8},{8,4},{12,16},{16,12},{20,24},{24,20},{28,0},{1,29},{... | collective-permute-start | bytes 884744 | tf_op jit(solution)/shard_map/ppermute | solution.py:437
  15.1 2.6 %collective-permute-done.4.slanted = f32[6,16,128]{2,1,0:T(8,128)S(1)} collective-permute-done((f32[6,16,128]{2,1,0:T(8,128)S(1)}, f32[6,16,128]{2,1,0:T(8,128)S(1)}, u32[]{:S(2)}, u32[]{:S(2)}) %collective-permute-start.4) | collective-permute-done | bytes 49184 | tf_op jit(solution)/shard_map/ppermute | solution.py:419
  17.8 1.6 %collective-permute-start.7 = (f32[24,16,128]{2,1,0:T(8,128)S(1)}, f32[24,16,128]{2,1,0:T(8,128)S(1)}, u32[]{:S(2)}, u32[]{:S(2)}) collective-permute-start(f32[24,16,128]{2,1,0:T(8,128)S(1)} %shard_map.29.rest_0_), channel_id=1, source_target_pairs={{0,2},{1,3},{2,0},{3,1},{4,6},{5,7},{6,4},{7,5},{8,10},{9,11},{10,... | collective-permute-start | bytes 589832 | tf_op jit(solution)/shard_map/ppermute | solution.py:430
  19.7 5.3 %collective-permute-done.8.rest_3_ = f32[24,16,128]{2,1,0:T(8,128)S(1)} collective-permute-done((f32[24,16,128]{2,1,0:T(8,128)S(1)}, f32[24,16,128]{2,1,0:T(8,128)S(1)}, u32[]{:S(2)}, u32[]{:S(2)}) %collective-permute-start.8) | collective-permute-done | bytes 196640 | tf_op jit(solution)/shard_map/ppermute | solution.py:430
  24.9 4.3 %collective-permute-done.7.rest_2_ = f32[24,16,128]{2,1,0:T(8,128)S(1)} collective-permute-done((f32[24,16,128]{2,1,0:T(8,128)S(1)}, f32[24,16,128]{2,1,0:T(8,128)S(1)}, u32[]{:S(2)}, u32[]{:S(2)}) %collective-permute-start.7) | collective-permute-done | bytes 196640 | tf_op jit(solution)/shard_map/ppermute | solution.py:430
  31.3 7.8 %collective-permute-done.2.straight = f32[9,64,128]{2,1,0:T(8,128)S(1)} collective-permute-done((f32[9,64,128]{2,1,0:T(8,128)S(1)}, f32[9,64,128]{2,1,0:T(8,128)S(1)}, u32[]{:S(2)}, u32[]{:S(2)}) %collective-permute-start.2) | collective-permute-done | bytes 294944 | tf_op jit(solution)/shard_map/ppermute | solution.py:439
  39.1 4.7 %shard_map.30 = (f32[12,16,128]{2,1,0:T(8,128)S(1)}, f32[12,16,128]{2,1,0:T(8,128)S(1)}, f32[12,16,128]{2,1,0:T(8,128)S(1)}, f32[12,16,128]{2,1,0:T(8,128)S(1)}, f32[8,12,16,128]{3,2,1,0:T(8,128)S(1)}) custom-call(s32[3]{0:T(128)S(1)} %pad_add_fusion.place, f32[4,12,64,128]{3,2,1,0:T(8,128)S(1)} %copy-done.1, ...), custom_call_target="tpu_custom_call" | custom-call | tf_op jit(solution)/shard_map/pallas_call | solution.py:199
  45.9 4.9 %collective-permute-done.15.straight = f32[9,64,128]{2,1,0:T(8,128)S(1)} collective-permute-done((f32[9,64,128]{2,1,0:T(8,128)S(1)}, f32[9,64,128]{2,1,0:T(8,128)S(1)}, u32[]{:S(2)}, u32[]{:S(2)}) %collective-permute-start.15) | collective-permute-done | bytes 294944 | tf_op jit(solution)/shard_map/ppermute | solution.py:439
  51.1 6.0 %shard_map.31 = (f32[12,16,128]{2,1,0:T(8,128)S(1)}, f32[12,16,128]{2,1,0:T(8,128)S(1)}, f32[12,16,128]{2,1,0:T(8,128)S(1)}, f32[12,16,128]{2,1,0:T(8,128)S(1)},...) custom-call(s32[3]{0:T(128)S(1)} %pad_add_fusion.place, ...), custom_call_target="tpu_custom_call" | custom-call | tf_op jit(solution)/shard_map/pallas_call | solution.py:199
  57.1 2.6 %collective-permute-start.17 = (f32[12,16,128]{2,1,0:T(8,128)S(1)}, f32[12,16,128]{2,1,0:T(8,128)S(1)}, u32[]{:S(2)}, u32[]{:S(2)}) collective-permute-start(f32[12,16,128]{2,1,0:T(8,128)S(1)} %get-tuple-element.49), channel_id=1, source_target_pairs={{0,7},{4,3},{1,6},{5,2},{2,5},{6,1},{3,4},{7,0},{8,15},{12,11},{9,... | collective-permute-start | bytes 294920 | tf_op jit(solution)/shard_map/ppermute | solution.py:450
  59.7 1.5 %collective-permute-start.18 = (f32[12,16,128]{2,1,0:T(8,128)S(1)}, f32[12,16,128]{2,1,0:T(8,128)S(1)}, u32[]{:S(2)}, u32[]{:S(2)}) collective-permute-start(f32[12,16,128]{2,1,0:T(8,128)S(1)} %get-tuple-element.50), channel_id=1, source_target_pairs={{0,2},{4,6},{1,3},{5,7},{2,0},{6,4},{3,1},{7,5},{8,10},{12,14},{9,... | collective-permute-start | bytes 294920 | tf_op jit(solution)/shard_map/ppermute | solution.py:450
  61.2 2.0 %collective-permute-start.23 = (f32[2,2,12,16,128]{4,3,2,1,0:T(8,128)}, f32[2,2,12,16,128]{4,3,2,1,0:T(8,128)}, u32[]{:S(2)}, u32[]{:S(2)}) collective-permute-start(f32[2,2,12,16,128]{4,3,2,1,0:T(8,128)} %get-tuple-element.59), channel_id=1, source_target_pairs={{0,4},{4,0},{1,5},{5,1},{2,6},{6,2},{3,7},{7,3},{8,12},{12,8},{9,1... | collective-permute-start | bytes 1179656 | tf_op jit(solution)/shard_map/ppermute | solution.py:489
  63.8 2.7 %collective-permute-start.24 = (f32[2,2,12,16,128]{4,3,2,1,0:T(8,128)}, f32[2,2,12,16,128]{4,3,2,1,0:T(8,128)}, u32[]{:S(2)}, u32[]{:S(2)}) collective-permute-start(f32[2,2,12,16,128]{4,3,2,1,0:T(8,128)} %get-tuple-element.60), channel_id=1, source_target_pairs={{0,2},{1,3},{4,6},{5,7},{8,10},{9,11},{12,14},{13,15},{16,18},{17,... | collective-permute-start | bytes 1179656 | tf_op jit(solution)/shard_map/ppermute | solution.py:490
  66.5 2.0 %collective-permute-start.25 = (f32[2,2,12,16,128]{4,3,2,1,0:T(8,128)}, f32[2,2,12,16,128]{4,3,2,1,0:T(8,128)}, u32[]{:S(2)}, u32[]{:S(2)}) collective-permute-start(f32[2,2,12,16,128]{4,3,2,1,0:T(8,128)} %get-tuple-element.61), channel_id=1, source_target_pairs={{0,6},{1,7},{4,2},{5,3},{8,14},{9,15},{12,10},{13,11},{16,22},{17,... | collective-permute-start | bytes 1179656 | tf_op jit(solution)/shard_map/ppermute | solution.py:491
  68.6 17.1 %collective-permute-done.19.refs_7_ = f32[12,16,128]{2,1,0:T(8,128)S(1)} collective-permute-done((f32[12,16,128]{2,1,0:T(8,128)S(1)}, f32[12,16,128]{2,1,0:T(8,128)S(1)}, u32[]{:S(2)}, u32[]{:S(2)}) %collective-permute-start.19) | collective-permute-done | bytes 98336 | tf_op jit(solution)/shard_map/ppermute | solution.py:450
  87.1 5.1 %collective-permute-done.22.refs_11_ = f32[2,12,16,128]{3,2,1,0:T(8,128)S(1)} collective-permute-done((f32[2,12,16,128]{3,2,1,0:T(8,128)S(1)}, f32[2,12,16,128]{3,2,1,0:T(8,128)S(1)}, u32[]{:S(2)}, u32[]{:S(2)}) %collective-permute-start.22) | collective-permute-done | bytes 196640 | tf_op jit(solution)/shard_map/ppermute | solution.py:450
  92.2 3.7 %shard_map.32 = (f32[16,192,128]{2,1,0:T(8,128)S(1)}, f32[32,1,256]{2,1,0:T(1,128)}) custom-call(s32[3]{0:T(128)S(1)} %pad_add_fusion.place, f32[12,16,128]{2,1,0:T(8,128)S(1)} %collective-permute-done.9.refs_0_, f32[12,16,128]{2,1,0:T(8,128)S(1)} %collective-permute-done.10.refs_1_, f32[12,16,128]{2,1,0:T(8,128)S(1)} %collective-permute-done.11.refs_2_, ...), custom_call_target="tpu_custom_call" | custom-call | tf_op jit(solution)/shard_map/pallas_call | solution.py:386
  95.8 4.8 %all-to-all-start = ((f32[32,1,256]{2,1,0:T(1,128)}), f32[32,1,256]{2,1,0:T(1,128)}, u32[]{:S(2)}, u32[]{:S(2)}) async-start(f32[32,1,256]{2,1,0:T(1,128)} %get-tuple-element.56), calls=%async_computation | async-start | bytes 65536 | tf_op jit(solution)/shard_map/all_to_all | solution.py:478
  100.9 7.0 %all-to-all-done.copies = f32[32,1,256]{2,1,0:T(1,128)} async-done(((f32[32,1,256]{2,1,0:T(1,128)}), f32[32,1,256]{2,1,0:T(1,128)}, u32[]{:S(2)}, u32[]{:S(2)}) %all-to-all-start) | async-done | bytes 32800 | tf_op jit(solution)/shard_map/all_to_all | solution.py:478
  107.9 7.5 %shard_map.33 = (f32[16,128]{1,0:T(8,128)S(1)}, f32[32,1,256]{2,1,0:T(1,128)S(1)}, f32[8,384,128]{2,1,0:T(8,128)S(1)}) custom-call(s32[3]{0:T(128)S(1)} %pad_add_fusion.place, f32[32,1,256]{2,1,0:T(1,128)} %all-to-all-done.copies, f32[16,192,128]{2,1,0:T(8,128)S(1)} %get-tuple-element.57.block, f32[2,2,12,16,128]{4,3,2,1,0:T(8,128)S(1)} %get-tuple-element.58.refs_0_, ...), custom_call_target="tpu_custom_call" | custom-call | tf_op jit(solution)/shard_map/pallas_call | solution.py:496
  115.6 8.9 %all_to_all.10.copies = f32[32,1,256]{2,1,0:T(1,128)S(1)} all-to-all(f32[32,1,256]{2,1,0:T(1,128)S(1)} %get-tuple-element.62), channel_id=1, replica_groups=mesh['pair'=4,'side'=2,'orb'=4] {'pair','side','orb'}, dimensions={0} | all-to-all | bytes 65536 | tf_op jit(solution)/shard_map/all_to_all | solution.py:478
  124.5 6.4 %shard_map.34 = f32[4,12,64,128]{3,2,1,0:T(8,128)} custom-call(s32[3]{0:T(128)S(1)} %pad_add_fusion.place, f32[32,1,256]{2,1,0:T(1,128)S(1)} %all_to_all.10.copies, f32[16,128]{1,0:T(8,128)S(1)} %get-tuple-element.63.table, f32[16,192,128]{2,1,0:T(8,128)S(1)} %get-tuple-element.57.block, f32[16,192,128]{2,1,0:T(8,128)S(1)} %collective-permute-done.26.block_near, ...), custom_call_target="tpu_custom_call" | custom-call | tf_op jit(solution)/shard_map/pallas_call | solution.py:505
  (52 shorter events, 11.2 us)
Async XLA Ops:
  3.8 14.0 %collective-permute-start.3 = (f32[12,16,128]{2,1,0:T(8,128)S(1)}, f32[12,16,128]{2,1,0:T(8,128)S(1)}, u32[]{:S(2)}, u32[]{:S(2)}) collective-permute-start(f32[12,16,128]{2,1,0:T(8,128)S(1)} %get-tuple-element.38), channel_id=1, source_target_pairs={{0,4},{4,0},{1,5},{5,1},{2,6},{6,2},{3,7},{7,3},{8,12},{12,8},{9,1... | collective-permute-start | bytes 294920 | tf_op jit(solution)/shard_map/ppermute | solution.py:418
  6.8 8.3 %collective-permute-start.5 = (f32[6,16,128]{2,1,0:T(8,128)S(1)}, f32[6,16,128]{2,1,0:T(8,128)S(1)}, u32[]{:S(2)}, u32[]{:S(2)}) collective-permute-start(f32[6,16,128]{2,1,0:T(8,128)S(1)} %get-tuple-element.39), channel_id=1, source_target_pairs={{0,24},{4,12},{8,0},{12,20},{16,8},{20,28},{24,16},{28,4},{1,25},{... | collective-permute-start | bytes 147464 | tf_op jit(solution)/shard_map/ppermute | solution.py:420
  10.4 19.8 %collective-permute-start.1 = (f32[9,64,128]{2,1,0:T(8,128)S(1)}, f32[9,64,128]{2,1,0:T(8,128)S(1)}, u32[]{:S(2)}, u32[]{:S(2)}) collective-permute-start(f32[9,64,128]{2,1,0:T(8,128)S(1)} %get-tuple-element.36), channel_id=1, source_target_pairs={{0,28},{4,8},{8,4},{12,16},{16,12},{20,24},{24,20},{28,0},{1,29},{... | collective-permute-start | bytes 884744 | tf_op jit(solution)/shard_map/ppermute | solution.py:437
  17.8 11.4 %collective-permute-start.7 = (f32[24,16,128]{2,1,0:T(8,128)S(1)}, f32[24,16,128]{2,1,0:T(8,128)S(1)}, u32[]{:S(2)}, u32[]{:S(2)}) collective-permute-start(f32[24,16,128]{2,1,0:T(8,128)S(1)} %shard_map.29.rest_0_), channel_id=1, source_target_pairs={{0,2},{1,3},{2,0},{3,1},{4,6},{5,7},{6,4},{7,5},{8,10},{9,11},{10,... | collective-permute-start | bytes 589832 | tf_op jit(solution)/shard_map/ppermute | solution.py:430
  19.4 9.8 %collective-permute-start.6 = (f32[24,16,128]{2,1,0:T(8,128)S(1)}, f32[24,16,128]{2,1,0:T(8,128)S(1)}, u32[]{:S(2)}, u32[]{:S(2)}) collective-permute-start(f32[24,16,128]{2,1,0:T(8,128)S(1)} %shard_map.29.rest_0_), channel_id=1, source_target_pairs={{0,1},{1,0},{2,3},{3,2},{4,5},{5,4},{6,7},{7,6},{8,9},{9,8},{10,11... | collective-permute-start | bytes 589832 | tf_op jit(solution)/shard_map/ppermute | solution.py:430
  19.7 19.4 %collective-permute-start = (f32[12,64,128]{2,1,0:T(8,128)S(1)}, f32[12,64,128]{2,1,0:T(8,128)S(1)}, u32[]{:S(2)}, u32[]{:S(2)}) collective-permute-start(f32[12,64,128]{2,1,0:T(8,128)S(1)} %get-tuple-element.35), channel_id=1, source_target_pairs={{0,4},{4,0},{1,5},{5,1},{2,6},{6,2},{3,7},{7,3},{8,12},{12,8},{9,1... | collective-permute-start | bytes 1179656 | tf_op jit(solution)/shard_map/ppermute | solution.py:438
  24.9 26.2 %collective-permute-start.13 = (f32[12,64,128]{2,1,0:T(8,128)S(1)}, f32[12,64,128]{2,1,0:T(8,128)S(1)}, u32[]{:S(2)}, u32[]{:S(2)}) collective-permute-start(f32[12,64,128]{2,1,0:T(8,128)S(1)} %get-tuple-element.44), channel_id=1, source_target_pairs={{0,4},{4,0},{1,5},{5,1},{2,6},{6,2},{3,7},{7,3},{8,12},{12,8},{9,1... | collective-permute-start | bytes 1179656 | tf_op jit(solution)/shard_map/ppermute | solution.py:438
  29.2 9.9 %collective-permute-start.2 = (f32[9,64,128]{2,1,0:T(8,128)S(1)}, f32[9,64,128]{2,1,0:T(8,128)S(1)}, u32[]{:S(2)}, u32[]{:S(2)}) collective-permute-start(f32[9,64,128]{2,1,0:T(8,128)S(1)} %get-tuple-element.37), channel_id=1, source_target_pairs={{0,24},{4,12},{8,0},{12,20},{16,8},{20,28},{24,16},{28,4},{1,25},{... | collective-permute-start | bytes 884744 | tf_op jit(solution)/shard_map/ppermute | solution.py:439
  29.2 15.2 %collective-permute-start.14 = (f32[9,64,128]{2,1,0:T(8,128)S(1)}, f32[9,64,128]{2,1,0:T(8,128)S(1)}, u32[]{:S(2)}, u32[]{:S(2)}) collective-permute-start(f32[9,64,128]{2,1,0:T(8,128)S(1)} %get-tuple-element.45), channel_id=1, source_target_pairs={{0,28},{4,8},{8,4},{12,16},{16,12},{20,24},{24,20},{28,0},{1,29},{... | collective-permute-start | bytes 884744 | tf_op jit(solution)/shard_map/ppermute | solution.py:437
  30.2 20.6 %collective-permute-start.15 = (f32[9,64,128]{2,1,0:T(8,128)S(1)}, f32[9,64,128]{2,1,0:T(8,128)S(1)}, u32[]{:S(2)}, u32[]{:S(2)}) collective-permute-start(f32[9,64,128]{2,1,0:T(8,128)S(1)} %get-tuple-element.46), channel_id=1, source_target_pairs={{0,24},{4,12},{8,0},{12,20},{16,8},{20,28},{24,16},{28,4},{1,25},{... | collective-permute-start | bytes 884744 | tf_op jit(solution)/shard_map/ppermute | solution.py:439
  43.8 13.4 %collective-permute-start.9 = (f32[12,16,128]{2,1,0:T(8,128)S(1)}, f32[12,16,128]{2,1,0:T(8,128)S(1)}, u32[]{:S(2)}, u32[]{:S(2)}) collective-permute-start(f32[12,16,128]{2,1,0:T(8,128)S(1)} %get-tuple-element.40), channel_id=1, source_target_pairs={{0,6},{4,2},{1,7},{5,3},{2,4},{6,0},{3,5},{7,1},{8,14},{12,10},{9,... | collective-permute-start | bytes 294920 | tf_op jit(solution)/shard_map/ppermute | solution.py:450
  43.9 15.8 %collective-permute-start.10 = (f32[12,16,128]{2,1,0:T(8,128)S(1)}, f32[12,16,128]{2,1,0:T(8,128)S(1)}, u32[]{:S(2)}, u32[]{:S(2)}) collective-permute-start(f32[12,16,128]{2,1,0:T(8,128)S(1)} %get-tuple-element.41), channel_id=1, source_target_pairs={{0,7},{4,3},{1,6},{5,2},{2,5},{6,1},{3,4},{7,0},{8,15},{12,11},{9,... | collective-permute-start | bytes 294920 | tf_op jit(solution)/shard_map/ppermute | solution.py:450
  44.4 16.8 %collective-permute-start.11 = (f32[12,16,128]{2,1,0:T(8,128)S(1)}, f32[12,16,128]{2,1,0:T(8,128)S(1)}, u32[]{:S(2)}, u32[]{:S(2)}) collective-permute-start(f32[12,16,128]{2,1,0:T(8,128)S(1)} %get-tuple-element.42), channel_id=1, source_target_pairs={{0,2},{4,6},{1,3},{5,7},{2,0},{6,4},{3,1},{7,5},{8,10},{12,14},{9,... | collective-permute-start | bytes 294920 | tf_op jit(solution)/shard_map/ppermute | solution.py:450
  50.8 10.4 %collective-permute-start.12 = (f32[12,16,128]{2,1,0:T(8,128)S(1)}, f32[12,16,128]{2,1,0:T(8,128)S(1)}, u32[]{:S(2)}, u32[]{:S(2)}) collective-permute-start(f32[12,16,128]{2,1,0:T(8,128)S(1)} %get-tuple-element.43), channel_id=1, source_target_pairs={{0,3},{4,7},{1,2},{5,6},{2,1},{6,5},{3,0},{7,4},{8,11},{12,15},{9,... | collective-permute-start | bytes 294920 | tf_op jit(solution)/shard_map/ppermute | solution.py:450
  57.1 9.4 %collective-permute-start.17 = (f32[12,16,128]{2,1,0:T(8,128)S(1)}, f32[12,16,128]{2,1,0:T(8,128)S(1)}, u32[]{:S(2)}, u32[]{:S(2)}) collective-permute-start(f32[12,16,128]{2,1,0:T(8,128)S(1)} %get-tuple-element.49), channel_id=1, source_target_pairs={{0,7},{4,3},{1,6},{5,2},{2,5},{6,1},{3,4},{7,0},{8,15},{12,11},{9,... | collective-permute-start | bytes 294920 | tf_op jit(solution)/shard_map/ppermute | solution.py:450
  59.7 8.9 %collective-permute-start.18 = (f32[12,16,128]{2,1,0:T(8,128)S(1)}, f32[12,16,128]{2,1,0:T(8,128)S(1)}, u32[]{:S(2)}, u32[]{:S(2)}) collective-permute-start(f32[12,16,128]{2,1,0:T(8,128)S(1)} %get-tuple-element.50), channel_id=1, source_target_pairs={{0,2},{4,6},{1,3},{5,7},{2,0},{6,4},{3,1},{7,5},{8,10},{12,14},{9,... | collective-permute-start | bytes 294920 | tf_op jit(solution)/shard_map/ppermute | solution.py:450
  61.2 24.5 %collective-permute-start.20 = (f32[2,12,16,128]{3,2,1,0:T(8,128)S(1)}, f32[2,12,16,128]{3,2,1,0:T(8,128)S(1)}, u32[]{:S(2)}, u32[]{:S(2)}) collective-permute-start(f32[2,12,16,128]{3,2,1,0:T(8,128)S(1)} %get-tuple-element.53), channel_id=1, source_target_pairs={{0,4},{4,0},{1,5},{5,1},{2,6},{6,2},{3,7},{7,3},{8,12},{12,8},{9,1... | collective-permute-start | bytes 589832 | tf_op jit(solution)/shard_map/ppermute | solution.py:450
  61.2 46.7 %collective-permute-start.23 = (f32[2,2,12,16,128]{4,3,2,1,0:T(8,128)}, f32[2,2,12,16,128]{4,3,2,1,0:T(8,128)}, u32[]{:S(2)}, u32[]{:S(2)}) collective-permute-start(f32[2,2,12,16,128]{4,3,2,1,0:T(8,128)} %get-tuple-element.59), channel_id=1, source_target_pairs={{0,4},{4,0},{1,5},{5,1},{2,6},{6,2},{3,7},{7,3},{8,12},{12,8},{9,1... | collective-permute-start | bytes 1179656 | tf_op jit(solution)/shard_map/ppermute | solution.py:489
  63.8 44.1 %collective-permute-start.24 = (f32[2,2,12,16,128]{4,3,2,1,0:T(8,128)}, f32[2,2,12,16,128]{4,3,2,1,0:T(8,128)}, u32[]{:S(2)}, u32[]{:S(2)}) collective-permute-start(f32[2,2,12,16,128]{4,3,2,1,0:T(8,128)} %get-tuple-element.60), channel_id=1, source_target_pairs={{0,2},{1,3},{4,6},{5,7},{8,10},{9,11},{12,14},{13,15},{16,18},{17,... | collective-permute-start | bytes 1179656 | tf_op jit(solution)/shard_map/ppermute | solution.py:490
  66.5 41.4 %collective-permute-start.25 = (f32[2,2,12,16,128]{4,3,2,1,0:T(8,128)}, f32[2,2,12,16,128]{4,3,2,1,0:T(8,128)}, u32[]{:S(2)}, u32[]{:S(2)}) collective-permute-start(f32[2,2,12,16,128]{4,3,2,1,0:T(8,128)} %get-tuple-element.61), channel_id=1, source_target_pairs={{0,6},{1,7},{4,2},{5,3},{8,14},{9,15},{12,10},{13,11},{16,22},{17,... | collective-permute-start | bytes 1179656 | tf_op jit(solution)/shard_map/ppermute | solution.py:491
  68.6 17.1 %collective-permute-start.19 = (f32[12,16,128]{2,1,0:T(8,128)S(1)}, f32[12,16,128]{2,1,0:T(8,128)S(1)}, u32[]{:S(2)}, u32[]{:S(2)}) collective-permute-start(f32[12,16,128]{2,1,0:T(8,128)S(1)} %get-tuple-element.51), channel_id=1, source_target_pairs={{0,3},{4,7},{1,2},{5,6},{2,1},{6,5},{3,0},{7,4},{8,11},{12,15},{9,... | collective-permute-start | bytes 294920 | tf_op jit(solution)/shard_map/ppermute | solution.py:450
  95.8 12.1 %all-to-all-start = ((f32[32,1,256]{2,1,0:T(1,128)}), f32[32,1,256]{2,1,0:T(1,128)}, u32[]{:S(2)}, u32[]{:S(2)}) async-start(f32[32,1,256]{2,1,0:T(1,128)} %get-tuple-element.56), calls=%async_computation | async-start | bytes 65536 | tf_op jit(solution)/shard_map/all_to_all | solution.py:478
  100.7 23.9 %collective-permute-start.26 = (f32[16,192,128]{2,1,0:T(8,128)S(1)}, f32[16,192,128]{2,1,0:T(8,128)S(1)}, u32[]{:S(2)}, u32[]{:S(2)}) collective-permute-start(f32[16,192,128]{2,1,0:T(8,128)S(1)} %get-tuple-element.57.block), channel_id=1, source_target_pairs={{0,1},{1,0},{2,3},{3,2},{4,5},{5,4},{6,7},{7,6},{8,9},{9,8},{10,11... | collective-permute-start | bytes 4718600 | tf_op jit(solution)/shard_map/ppermute | solution.py:493
  115.4 9.1 %collective-permute-start.27 = (f32[8,384,128]{2,1,0:T(8,128)S(1)}, f32[8,384,128]{2,1,0:T(8,128)S(1)}, u32[]{:S(2)}, u32[]{:S(2)}) collective-permute-start(f32[8,384,128]{2,1,0:T(8,128)S(1)} %get-tuple-element.64.bundle), channel_id=1, source_target_pairs={{0,1},{1,0},{2,3},{3,2},{4,5},{5,4},{6,7},{7,6},{8,9},{9,8},{10,11... | collective-permute-start | bytes 4718600 | tf_op jit(solution)/shard_map/ppermute | solution.py:504
  (9 other events, 104.8 us)

commit v8 on v7

--- a/solution.py
+++ b/solution.py
@@ -19,6 +19,7 @@
 WIDE = REACH * (STEPS - 1)
 EIGHT = 8
 CORES = 2
+WIDTH = 4
 BLOCKS = 3
 ALL = ("pair", "side", "orb")
 
@@ -64,7 +65,7 @@
         out_specs=[VMEM] * len(shapes),
         scratch_shapes=[pltpu.SemaphoreType.DMA((len(shapes),))],
         compiler_params=pltpu.CompilerParams(vmem_limit_bytes=16 * 1024 * 1024),
-    )(place, orbitals, potential)
+    )(place, *(pltpu.with_memory_space_constraint(array, pltpu.HBM) for array in (orbitals, potential)))
 
 
 def join_kernel(swapped, slanted, straight, out):
@@ -254,13 +255,25 @@
     table = exact_dot(wide, table_of((LANES, LANES), lambda r, c: r % total == c))
     table = table + table_of((total, LANES), lambda r, c: c - total == r)
     index = lax.broadcasted_iota(jnp.int32, (total, LANES), 0)
-    for j in range(total):
-        value = table[j : j + 1, j : j + 1]
-        scale = lax.rsqrt(value)
-        scale = scale * (1.5 - 0.5 * value * scale * scale)
-        scaled = table[j : j + 1, :] * scale
-        factor = table[:, j : j + 1] * scale
-        table = jnp.where(index == j, scaled, jnp.where(index > j, table - factor * scaled, table))
+    for start in range(0, total, WIDTH):
+        block = range(start, min(start + WIDTH, total))
+        columns = {j: jnp.broadcast_to(table[:, j : j + 1], (total, LANES)) for j in block}
+        rows = {j: table[j : j + 1, :] for j in block}
+        reduced = table
+        for j in block:
+            value = columns[j][j : j + 1, :]
+            scale = lax.rsqrt(value)
+            scale = scale * (1.5 - 0.5 * value * scale * scale)
+            factor, rows[j] = columns[j] * scale, rows[j] * scale
+            for later in block:
+                if later > j:
+                    share = factor[later : later + 1, :]
+                    columns[later] = columns[later] - factor * share
+                    rows[later] = rows[later] - share * rows[j]
+            reduced = reduced - factor * rows[j]
+        for j in block:
+            table = jnp.where(index == j, rows[j], table)
+        table = jnp.where(index > block[-1], reduced, table)
     return table
 
 
@@ -304,14 +317,17 @@
     apply_all(inverse_factor(copies, block.shape[0], cell_total), block, basis)
 
 
-def second_and_bundle_kernel(cell_total, place, copies, block, *refs):
-    given, (table_out, message, bundle, basis) = refs[:-4], refs[-4:]
+def table_kernel(cell_total, copies, block, table_out, message, basis):
     total, tiles = block.shape[0], block.shape[1] // EIGHT
     table = inverse_factor(copies, total, cell_total)
     table_out[...] = table
     apply_all(table, block, basis)
     row = gram_message(tile_reader(basis), total, tiles, chunk_of(tiles))
     message[...] = jnp.broadcast_to(row[None], message.shape)
+
+
+def bundle_kernel(place, *refs):
+    given, bundle = refs[:-1], refs[-1]
     side, kept = place[0], given[0].shape[0]
     for kind, ref in enumerate(given):
         for at in range(kept):
@@ -440,8 +456,8 @@
             )
         )
 
-    early = tuple(sorted((m for m in range(1, group) if m >= 2 * CORES), key=lambda m: (-(m % 2), m)))
-    late = tuple(m for m in range(group) if m < 2 * CORES)
+    early = tuple(sorted((m for m in range(1, group) if m != CORES), key=lambda m: (m < 2 * CORES, -(m % 2), m)))
+    late = (0, CORES)
     spares = 4 if orb_count == 2 * CORES and kept == 2 else 0
 
     def to_partner(piece, m):
@@ -493,15 +509,16 @@
         block_near = lax.ppermute(block, "orb", cores)
         bundle_shape = jax.ShapeDtypeStruct((2 * held, CORES * rows * part, width), jnp.float32)
         table_shape = jax.ShapeDtypeStruct((total, LANES), jnp.float32)
-        table, message, bundle = pl.pallas_call(
-            functools.partial(second_and_bundle_kernel, cell_total),
-            out_shape=[table_shape, message_shape, bundle_shape],
-            in_specs=[SMEM] + [VMEM] * (2 + len(given)),
-            out_specs=[VMEM] * 3,
+        bundle = small_call(bundle_kernel, bundle_shape, [SMEM] + [VMEM] * len(given), place, *given)
+        bundle_near = lax.ppermute(bundle, "orb", cores)
+        table, message = pl.pallas_call(
+            functools.partial(table_kernel, cell_total),
+            out_shape=[table_shape, message_shape],
+            in_specs=[VMEM] * 2,
+            out_specs=[VMEM] * 2,
             scratch_shapes=[pltpu.VMEM(block_shape.shape, jnp.float32)],
             compiler_params=pltpu.CompilerParams(vmem_limit_bytes=24 * 1024 * 1024),
-        )(place, exchanged(message), block, *given)
-        bundle_near = lax.ppermute(bundle, "orb", cores)
+        )(exchanged(message), block)
         return pl.pallas_call(
             functools.partial(last_kernel, cell_total),
             out_shape=jax.ShapeDtypeStruct((held, rows, cols, width), jnp.float32),
@@ -513,9 +530,7 @@
     basis, message = small_call(
         functools.partial(second_kernel, cell_total), [block_shape, message_shape], [VMEM] * 2, exchanged(message), block
     )
-    basis = small_call(
-        functools.partial(third_kernel, cell_total), block_shape, [VMEM] * 2, exchanged(message), basis
-    )
+    basis = small_call(functools.partial(third_kernel, cell_total), block_shape, [VMEM] * 2, exchanged(message), basis)
     basis = basis.reshape(total, rows, part, width)
     return lax.all_to_all(basis, "orb", split_axis=0, concat_axis=2, tiled=True)
 

time: 131 us -> 131 us (level)
  blocking collectives: 8.93 us -> 19.6 us
  starting transfers between devices: 33.8 us -> 26 us
  local copies, waits for them, and re-layouts: 2.41 us -> 0.01 us
  Pallas kernels: 29.4 us -> 27.3 us
  waiting for transfers between devices: 56 us -> 57.4 us
    all_to_all x1 -> x2, blocking collectives: 8.93 us -> 19.6 us  [exchanged(): return lax.all_to_all(message, ALL, 0, 0)]
    ppermute x2, waiting for transfers between devices: 0.01 us -> 9.68 us  [whole(): lax.ppermute(sent[3 * at + 1], 'side', swap)]
    ppermute x2, waiting for transfers between devices: 12.6 us -> 4.02 us  [whole(): lax.ppermute(sent[3 * at + 2], slab_axes, ahead)]
    all_to_all x1 -> x0, waiting for transfers between devices: 6.99 us -> none  [exchanged(): return lax.all_to_all(message, ALL, 0, 0)]
    all_to_all x1 -> x0, starting transfers between devices: 4.82 us -> none  [exchanged(): return lax.all_to_all(message, ALL, 0, 0)]
    ppermute x2, starting transfers between devices: 5.72 us -> 1.5 us  [whole(): lax.ppermute(sent[3 * at], slab_axes, slant)]
    ppermute x11 -> x13, waiting for transfers between devices: 24.2 us -> 27.6 us  [to_partner(): lax.ppermute(piece, ('side', 'orb'), [(flat_of(i), flat_of(i ^ m)) for i...]
    ppermute x1, waiting for transfers between devices: 2.59 us -> 5.03 us  [whole(): lax.ppermute(edge, slab_axes, slant)]
  transfers between devices with their start and end apart: 29 -> 30, of which waited for: 11 -> 11; matrix products, arithmetic and copies ran while one was open for 0% -> 0% of each run, Pallas kernels for 17% -> 15%
where the time goes in v8:
time: 131 us
  waiting for transfers between devices  57.4 us (44%)
  Pallas kernels  27.3 us (21%)
  starting transfers between devices  26 us (20%)
  blocking collectives  19.6 us (15%)
    ppermute x13, waiting for transfers between devices, to_partner(): lax.ppermute(piece, ('side', 'orb'), [(flat_of(i), flat_of(i ^ m)) for i...  27.6 us
    all_to_all x2, blocking collectives, exchanged(): return lax.all_to_all(message, ALL, 0, 0)  19.6 us
    pallas_call x2, Pallas kernels, filtered_pieces(): pl.pallas_call(functools.partial(filter_kernel, at, len(pot_far), early,...  10.4 us
    ppermute x2, waiting for transfers between devices, whole(): lax.ppermute(sent[3 * at + 1], 'side', swap)  9.68 us
    ppermute x3, waiting for transfers between devices, whole(): lax.ppermute(joined, 'orb', [(i, i ^ m) for i in range(orb_count)])  9.3 us
    ppermute x13, starting transfers between devices, to_partner(): lax.ppermute(piece, ('side', 'orb'), [(flat_of(i), flat_of(i ^ m)) for i...  8.55 us
    pallas_call x1, Pallas kernels, whole(): pl.pallas_call(functools.partial(last_kernel, cell_total), out_shape=jax....  5.65 us
    pallas_call x1, Pallas kernels, whole(): pl.pallas_call(functools.partial(table_kernel, cell_total), out_shape=[ta...  5.46 us
  transfers between devices with their start and end apart: 30, of which 11 were waited for; matrix products, arithmetic and copies ran while one was open for 0% of the time, Pallas kernels for 15%

profile of v8, /device:TPU:0, one launch (start us, length us, event | category | flops | bytes accessed | tf_op | source)
XLA Modules:
  0.0 130.6 jit_solution(3724219576559300140)
XLA Ops:
  0.1 2.2 %shard_map.28 = (f32[12,16,128]{2,1,0:T(8,128)S(1)}, f32[6,16,128]{2,1,0:T(8,128)S(1)}, f32[9,64,128]{2,1,0:T(8,128)S(1)}, f32[12,64,128]{2,1,0:T(8,128)S(1)}, f...) custom-call(s32[3]{0:T(128)S(1)} %pad_add_fusion.place, ...), custom_call_target="tpu_custom_call" | custom-call | tf_op jit(solution)/shard_map/pallas_call | solution.py:61
  2.3 3.1 %collective-permute-start.3 = (f32[12,16,128]{2,1,0:T(8,128)S(1)}, f32[12,16,128]{2,1,0:T(8,128)S(1)}, u32[]{:S(2)}, u32[]{:S(2)}) collective-permute-start(f32[12,16,128]{2,1,0:T(8,128)S(1)} %get-tuple-element.39), channel_id=1, source_target_pairs={{0,4},{4,0},{1,5},{5,1},{2,6},{6,2},{3,7},{7,3},{8,12},{12,8},{9,1... | collective-permute-start | bytes 294920 | tf_op jit(solution)/shard_map/ppermute | solution.py:434
  5.4 3.6 %collective-permute-start.5 = (f32[6,16,128]{2,1,0:T(8,128)S(1)}, f32[6,16,128]{2,1,0:T(8,128)S(1)}, u32[]{:S(2)}, u32[]{:S(2)}) collective-permute-start(f32[6,16,128]{2,1,0:T(8,128)S(1)} %get-tuple-element.40), channel_id=1, source_target_pairs={{0,24},{4,12},{8,0},{12,20},{16,8},{20,28},{24,16},{28,4},{1,25},{... | collective-permute-start | bytes 147464 | tf_op jit(solution)/shard_map/ppermute | solution.py:436
  9.0 1.7 %collective-permute-done.5.straight = f32[6,16,128]{2,1,0:T(8,128)S(1)} collective-permute-done((f32[6,16,128]{2,1,0:T(8,128)S(1)}, f32[6,16,128]{2,1,0:T(8,128)S(1)}, u32[]{:S(2)}, u32[]{:S(2)}) %collective-permute-start.5) | collective-permute-done | bytes 49184 | tf_op jit(solution)/shard_map/ppermute | solution.py:436
  10.7 5.0 %collective-permute-done.4.slanted = f32[6,16,128]{2,1,0:T(8,128)S(1)} collective-permute-done((f32[6,16,128]{2,1,0:T(8,128)S(1)}, f32[6,16,128]{2,1,0:T(8,128)S(1)}, u32[]{:S(2)}, u32[]{:S(2)}) %collective-permute-start.4) | collective-permute-done | bytes 49184 | tf_op jit(solution)/shard_map/ppermute | solution.py:435
  18.0 5.1 %collective-permute-done.8.rest_3_ = f32[24,16,128]{2,1,0:T(8,128)S(1)} collective-permute-done((f32[24,16,128]{2,1,0:T(8,128)S(1)}, f32[24,16,128]{2,1,0:T(8,128)S(1)}, u32[]{:S(2)}, u32[]{:S(2)}) %collective-permute-start.8) | collective-permute-done | bytes 196640 | tf_op jit(solution)/shard_map/ppermute | solution.py:446
  23.0 4.2 %collective-permute-done.7.rest_2_ = f32[24,16,128]{2,1,0:T(8,128)S(1)} collective-permute-done((f32[24,16,128]{2,1,0:T(8,128)S(1)}, f32[24,16,128]{2,1,0:T(8,128)S(1)}, u32[]{:S(2)}, u32[]{:S(2)}) %collective-permute-start.7) | collective-permute-done | bytes 196640 | tf_op jit(solution)/shard_map/ppermute | solution.py:446
  28.9 4.0 %collective-permute-done.2.straight = f32[9,64,128]{2,1,0:T(8,128)S(1)} collective-permute-done((f32[9,64,128]{2,1,0:T(8,128)S(1)}, f32[9,64,128]{2,1,0:T(8,128)S(1)}, u32[]{:S(2)}, u32[]{:S(2)}) %collective-permute-start.2) | collective-permute-done | bytes 294944 | tf_op jit(solution)/shard_map/ppermute | solution.py:455
  32.9 9.7 %collective-permute-done.swapped = f32[12,64,128]{2,1,0:T(8,128)S(1)} collective-permute-done((f32[12,64,128]{2,1,0:T(8,128)S(1)}, f32[12,64,128]{2,1,0:T(8,128)S(1)}, u32[]{:S(2)}, u32[]{:S(2)}) %collective-permute-start) | collective-permute-done | bytes 393248 | tf_op jit(solution)/shard_map/ppermute | solution.py:454
  42.6 4.7 %shard_map.30 = (f32[12,16,128]{2,1,0:T(8,128)S(1)}, f32[12,16,128]{2,1,0:T(8,128)S(1)}, f32[12,16,128]{2,1,0:T(8,128)S(1)}, f32[12,16,128]{2,1,0:T(8,128)S(1)},...) custom-call(s32[3]{0:T(128)S(1)} %pad_add_fusion.place, ...), custom_call_target="tpu_custom_call" | custom-call | tf_op jit(solution)/shard_map/pallas_call | solution.py:200
  49.0 2.8 %collective-permute-start.12 = (f32[12,16,128]{2,1,0:T(8,128)S(1)}, f32[12,16,128]{2,1,0:T(8,128)S(1)}, u32[]{:S(2)}, u32[]{:S(2)}) collective-permute-start(f32[12,16,128]{2,1,0:T(8,128)S(1)} %get-tuple-element.44), channel_id=1, source_target_pairs={{0,3},{4,7},{1,2},{5,6},{2,1},{6,5},{3,0},{7,4},{8,11},{12,15},{9,... | collective-permute-start | bytes 294920 | tf_op jit(solution)/shard_map/ppermute | solution.py:466
  51.8 2.3 %collective-permute-done.9.refs_0_ = f32[12,16,128]{2,1,0:T(8,128)S(1)} collective-permute-done((f32[12,16,128]{2,1,0:T(8,128)S(1)}, f32[12,16,128]{2,1,0:T(8,128)S(1)}, u32[]{:S(2)}, u32[]{:S(2)}) %collective-permute-start.9) | collective-permute-done | bytes 98336 | tf_op jit(solution)/shard_map/ppermute | solution.py:466
  54.1 5.7 %shard_map.31 = (f32[12,16,128]{2,1,0:T(8,128)S(1)}, f32[12,16,128]{2,1,0:T(8,128)S(1)}, f32[12,16,128]{2,1,0:T(8,128)S(1)}, f32[12,16,128]{2,1,0:T(8,128)S(1)},...) custom-call(s32[3]{0:T(128)S(1)} %pad_add_fusion.place, ...), custom_call_target="tpu_custom_call" | custom-call | tf_op jit(solution)/shard_map/pallas_call | solution.py:200
  60.4 1.8 %collective-permute-start.19 = (f32[12,16,128]{2,1,0:T(8,128)S(1)}, f32[12,16,128]{2,1,0:T(8,128)S(1)}, u32[]{:S(2)}, u32[]{:S(2)}) collective-permute-start(f32[12,16,128]{2,1,0:T(8,128)S(1)} %get-tuple-element.52), channel_id=1, source_target_pairs={{0,7},{4,3},{1,6},{5,2},{2,5},{6,1},{3,4},{7,0},{8,15},{12,11},{9,... | collective-permute-start | bytes 294920 | tf_op jit(solution)/shard_map/ppermute | solution.py:466
  62.2 2.0 %collective-permute-start.26 = (f32[2,2,12,16,128]{4,3,2,1,0:T(8,128)S(1)}, f32[2,2,12,16,128]{4,3,2,1,0:T(8,128)S(1)}, u32[]{:S(2)}, u32[]{:S(2)}) collective-permute-start(f32[2,2,12,16,128]{4,3,2,1,0:T(8,128)S(1)} %get-tuple-element.64), channel_id=1, source_target_pairs={{0,4},{4,0},{1,5},{5,1},{2,6},{6,2},{3,7},{7,3},{8,12},{12,8},{9,1... | collective-permute-start | bytes 1179656 | tf_op jit(solution)/shard_map/ppermute | solution.py:505
  64.2 3.0 %collective-permute-start.27 = (f32[2,2,12,16,128]{4,3,2,1,0:T(8,128)S(1)}, f32[2,2,12,16,128]{4,3,2,1,0:T(8,128)S(1)}, u32[]{:S(2)}, u32[]{:S(2)}) collective-permute-start(f32[2,2,12,16,128]{4,3,2,1,0:T(8,128)S(1)} %get-tuple-element.65), channel_id=1, source_target_pairs={{0,2},{1,3},{4,6},{5,7},{8,10},{9,11},{12,14},{13,15},{16,18},{17,... | collective-permute-start | bytes 1179656 | tf_op jit(solution)/shard_map/ppermute | solution.py:506
  69.6 17.0 %collective-permute-done.20.refs_8_ = f32[12,16,128]{2,1,0:T(8,128)S(1)} collective-permute-done((f32[12,16,128]{2,1,0:T(8,128)S(1)}, f32[12,16,128]{2,1,0:T(8,128)S(1)}, u32[]{:S(2)}, u32[]{:S(2)}) %collective-permute-start.20) | collective-permute-done | bytes 98336 | tf_op jit(solution)/shard_map/ppermute | solution.py:466
  87.6 3.6 %collective-permute-done.22.refs_10_ = f32[12,16,128]{2,1,0:T(8,128)S(1)} collective-permute-done((f32[12,16,128]{2,1,0:T(8,128)S(1)}, f32[12,16,128]{2,1,0:T(8,128)S(1)}, u32[]{:S(2)}, u32[]{:S(2)}) %collective-permute-start.22) | collective-permute-done | bytes 98336 | tf_op jit(solution)/shard_map/ppermute | solution.py:466
  91.2 4.3 %collective-permute-done.23.refs_11_ = f32[12,16,128]{2,1,0:T(8,128)S(1)} collective-permute-done((f32[12,16,128]{2,1,0:T(8,128)S(1)}, f32[12,16,128]{2,1,0:T(8,128)S(1)}, u32[]{:S(2)}, u32[]{:S(2)}) %collective-permute-start.23) | collective-permute-done | bytes 98336 | tf_op jit(solution)/shard_map/ppermute | solution.py:466
  95.5 3.0 %shard_map.32 = (f32[16,192,128]{2,1,0:T(8,128)S(1)}, f32[32,1,256]{2,1,0:T(1,128)S(1)}) custom-call(s32[3]{0:T(128)S(1)} %pad_add_fusion.place, f32[12,16,128]{2,1,0:T(8,128)S(1)} %collective-permute-done.9.refs_0_, f32[12,16,128]{2,1,0:T(8,128)S(1)} %collective-permute-done.10.refs_1_, f32[12,16,128]{2,1,0:T(8,128)S(1)} %collective-permute-done.11.refs_2_, ...), custom_call_target="tpu_custom_call" | custom-call | tf_op jit(solution)/shard_map/pallas_call | solution.py:402
  99.9 10.7 %all_to_all.10.copies = f32[32,1,256]{2,1,0:T(1,128)S(1)} all-to-all(f32[32,1,256]{2,1,0:T(1,128)S(1)} %get-tuple-element.59), channel_id=1, replica_groups=mesh['pair'=4,'side'=2,'orb'=4] {'pair','side','orb'}, dimensions={0} | all-to-all | bytes 65536 | tf_op jit(solution)/shard_map/all_to_all | solution.py:494
  110.6 5.5 %shard_map.33 = (f32[16,128]{1,0:T(8,128)S(1)}, f32[32,1,256]{2,1,0:T(1,128)S(1)}) custom-call(f32[32,1,256]{2,1,0:T(1,128)S(1)} %all_to_all.10.copies, f32[16,192,128]{2,1,0:T(8,128)S(1)} %get-tuple-element.60.block), custom_call_target="tpu_custom_call" | custom-call | tf_op jit(solution)/shard_map/pallas_call | solution.py:514
  116.0 9.0 %all_to_all.11.copies = f32[32,1,256]{2,1,0:T(1,128)S(1)} all-to-all(f32[32,1,256]{2,1,0:T(1,128)S(1)} %get-tuple-element.61), channel_id=1, replica_groups=mesh['pair'=4,'side'=2,'orb'=4] {'pair','side','orb'}, dimensions={0} | all-to-all | bytes 65536 | tf_op jit(solution)/shard_map/all_to_all | solution.py:494
  125.0 5.6 %shard_map.35 = f32[4,12,64,128]{3,2,1,0:T(8,128)} custom-call(s32[3]{0:T(128)S(1)} %pad_add_fusion.place, f32[32,1,256]{2,1,0:T(1,128)S(1)} %all_to_all.11.copies, f32[16,128]{1,0:T(8,128)S(1)} %get-tuple-element.62.table, f32[16,192,128]{2,1,0:T(8,128)S(1)} %get-tuple-element.60.block, f32[16,192,128]{2,1,0:T(8,128)S(1)} %collective-permute-done.25.block_near, ...), custom_call_target="tpu_custom_call" | custom-call | tf_op jit(solution)/shard_map/pallas_call | solution.py:522
  (52 shorter events, 10.8 us)
Async XLA Ops:
  2.3 13.5 %collective-permute-start.3 = (f32[12,16,128]{2,1,0:T(8,128)S(1)}, f32[12,16,128]{2,1,0:T(8,128)S(1)}, u32[]{:S(2)}, u32[]{:S(2)}) collective-permute-start(f32[12,16,128]{2,1,0:T(8,128)S(1)} %get-tuple-element.39), channel_id=1, source_target_pairs={{0,4},{4,0},{1,5},{5,1},{2,6},{6,2},{3,7},{7,3},{8,12},{12,8},{9,1... | collective-permute-start | bytes 294920 | tf_op jit(solution)/shard_map/ppermute | solution.py:434
  15.9 12.3 %collective-permute-start.1 = (f32[9,64,128]{2,1,0:T(8,128)S(1)}, f32[9,64,128]{2,1,0:T(8,128)S(1)}, u32[]{:S(2)}, u32[]{:S(2)}) collective-permute-start(f32[9,64,128]{2,1,0:T(8,128)S(1)} %get-tuple-element.37), channel_id=1, source_target_pairs={{0,28},{4,8},{8,4},{12,16},{16,12},{20,24},{24,20},{28,0},{1,29},{... | collective-permute-start | bytes 884744 | tf_op jit(solution)/shard_map/ppermute | solution.py:453
  16.5 10.8 %collective-permute-start.7 = (f32[24,16,128]{2,1,0:T(8,128)S(1)}, f32[24,16,128]{2,1,0:T(8,128)S(1)}, u32[]{:S(2)}, u32[]{:S(2)}) collective-permute-start(f32[24,16,128]{2,1,0:T(8,128)S(1)} %shard_map.29.rest_0_), channel_id=1, source_target_pairs={{0,2},{1,3},{2,0},{3,1},{4,6},{5,7},{6,4},{7,5},{8,10},{9,11},{10,... | collective-permute-start | bytes 589832 | tf_op jit(solution)/shard_map/ppermute | solution.py:446
  17.9 9.3 %collective-permute-start.6 = (f32[24,16,128]{2,1,0:T(8,128)S(1)}, f32[24,16,128]{2,1,0:T(8,128)S(1)}, u32[]{:S(2)}, u32[]{:S(2)}) collective-permute-start(f32[24,16,128]{2,1,0:T(8,128)S(1)} %shard_map.29.rest_0_), channel_id=1, source_target_pairs={{0,1},{1,0},{2,3},{3,2},{4,5},{5,4},{6,7},{7,6},{8,9},{9,8},{10,11... | collective-permute-start | bytes 589832 | tf_op jit(solution)/shard_map/ppermute | solution.py:446
  18.0 24.6 %collective-permute-start = (f32[12,64,128]{2,1,0:T(8,128)S(1)}, f32[12,64,128]{2,1,0:T(8,128)S(1)}, u32[]{:S(2)}, u32[]{:S(2)}) collective-permute-start(f32[12,64,128]{2,1,0:T(8,128)S(1)} %get-tuple-element.36), channel_id=1, source_target_pairs={{0,4},{4,0},{1,5},{5,1},{2,6},{6,2},{3,7},{7,3},{8,12},{12,8},{9,1... | collective-permute-start | bytes 1179656 | tf_op jit(solution)/shard_map/ppermute | solution.py:454
  23.0 9.9 %collective-permute-start.2 = (f32[9,64,128]{2,1,0:T(8,128)S(1)}, f32[9,64,128]{2,1,0:T(8,128)S(1)}, u32[]{:S(2)}, u32[]{:S(2)}) collective-permute-start(f32[9,64,128]{2,1,0:T(8,128)S(1)} %get-tuple-element.38), channel_id=1, source_target_pairs={{0,24},{4,12},{8,0},{12,20},{16,8},{20,28},{24,16},{28,4},{1,25},{... | collective-permute-start | bytes 884744 | tf_op jit(solution)/shard_map/ppermute | solution.py:455
  27.3 24.5 %collective-permute-start.15 = (f32[12,64,128]{2,1,0:T(8,128)S(1)}, f32[12,64,128]{2,1,0:T(8,128)S(1)}, u32[]{:S(2)}, u32[]{:S(2)}) collective-permute-start(f32[12,64,128]{2,1,0:T(8,128)S(1)} %get-tuple-element.47), channel_id=1, source_target_pairs={{0,4},{4,0},{1,5},{5,1},{2,6},{6,2},{3,7},{7,3},{8,12},{12,8},{9,1... | collective-permute-start | bytes 1179656 | tf_op jit(solution)/shard_map/ppermute | solution.py:454
  27.3 21.3 %collective-permute-start.16 = (f32[9,64,128]{2,1,0:T(8,128)S(1)}, f32[9,64,128]{2,1,0:T(8,128)S(1)}, u32[]{:S(2)}, u32[]{:S(2)}) collective-permute-start(f32[9,64,128]{2,1,0:T(8,128)S(1)} %get-tuple-element.48), channel_id=1, source_target_pairs={{0,28},{4,8},{8,4},{12,16},{16,12},{20,24},{24,20},{28,0},{1,29},{... | collective-permute-start | bytes 884744 | tf_op jit(solution)/shard_map/ppermute | solution.py:453
  28.2 20.8 %collective-permute-start.17 = (f32[9,64,128]{2,1,0:T(8,128)S(1)}, f32[9,64,128]{2,1,0:T(8,128)S(1)}, u32[]{:S(2)}, u32[]{:S(2)}) collective-permute-start(f32[9,64,128]{2,1,0:T(8,128)S(1)} %get-tuple-element.49), channel_id=1, source_target_pairs={{0,24},{4,12},{8,0},{12,20},{16,8},{20,28},{24,16},{28,4},{1,25},{... | collective-permute-start | bytes 884744 | tf_op jit(solution)/shard_map/ppermute | solution.py:455
  47.8 12.0 %collective-permute-start.10 = (f32[12,16,128]{2,1,0:T(8,128)S(1)}, f32[12,16,128]{2,1,0:T(8,128)S(1)}, u32[]{:S(2)}, u32[]{:S(2)}) collective-permute-start(f32[12,16,128]{2,1,0:T(8,128)S(1)} %get-tuple-element.42), channel_id=1, source_target_pairs={{0,7},{4,3},{1,6},{5,2},{2,5},{6,1},{3,4},{7,0},{8,15},{12,11},{9,... | collective-permute-start | bytes 294920 | tf_op jit(solution)/shard_map/ppermute | solution.py:466
  48.5 11.8 %collective-permute-start.11 = (f32[12,16,128]{2,1,0:T(8,128)S(1)}, f32[12,16,128]{2,1,0:T(8,128)S(1)}, u32[]{:S(2)}, u32[]{:S(2)}) collective-permute-start(f32[12,16,128]{2,1,0:T(8,128)S(1)} %get-tuple-element.43), channel_id=1, source_target_pairs={{0,2},{4,6},{1,3},{5,7},{2,0},{6,4},{3,1},{7,5},{8,10},{12,14},{9,... | collective-permute-start | bytes 294920 | tf_op jit(solution)/shard_map/ppermute | solution.py:466
  49.0 13.2 %collective-permute-start.12 = (f32[12,16,128]{2,1,0:T(8,128)S(1)}, f32[12,16,128]{2,1,0:T(8,128)S(1)}, u32[]{:S(2)}, u32[]{:S(2)}) collective-permute-start(f32[12,16,128]{2,1,0:T(8,128)S(1)} %get-tuple-element.44), channel_id=1, source_target_pairs={{0,3},{4,7},{1,2},{5,6},{2,1},{6,5},{3,0},{7,4},{8,11},{12,15},{9,... | collective-permute-start | bytes 294920 | tf_op jit(solution)/shard_map/ppermute | solution.py:466
  51.7 12.5 %collective-permute-start.13 = (f32[12,16,128]{2,1,0:T(8,128)S(1)}, f32[12,16,128]{2,1,0:T(8,128)S(1)}, u32[]{:S(2)}, u32[]{:S(2)}) collective-permute-start(f32[12,16,128]{2,1,0:T(8,128)S(1)} %get-tuple-element.45), channel_id=1, source_target_pairs={{0,4},{4,0},{1,5},{5,1},{2,6},{6,2},{3,7},{7,3},{8,12},{12,8},{9,1... | collective-permute-start | bytes 294920 | tf_op jit(solution)/shard_map/ppermute | solution.py:466
  54.1 13.1 %collective-permute-start.14 = (f32[12,16,128]{2,1,0:T(8,128)S(1)}, f32[12,16,128]{2,1,0:T(8,128)S(1)}, u32[]{:S(2)}, u32[]{:S(2)}) collective-permute-start(f32[12,16,128]{2,1,0:T(8,128)S(1)} %get-tuple-element.46), channel_id=1, source_target_pairs={{0,5},{4,1},{1,4},{5,0},{2,7},{6,3},{3,6},{7,2},{8,13},{12,9},{9,1... | collective-permute-start | bytes 294920 | tf_op jit(solution)/shard_map/ppermute | solution.py:466
  59.8 8.8 %collective-permute-start.18 = (f32[12,16,128]{2,1,0:T(8,128)S(1)}, f32[12,16,128]{2,1,0:T(8,128)S(1)}, u32[]{:S(2)}, u32[]{:S(2)}) collective-permute-start(f32[12,16,128]{2,1,0:T(8,128)S(1)} %get-tuple-element.51), channel_id=1, source_target_pairs={{0,6},{4,2},{1,7},{5,3},{2,4},{6,0},{3,5},{7,1},{8,14},{12,10},{9,... | collective-permute-start | bytes 294920 | tf_op jit(solution)/shard_map/ppermute | solution.py:466
  60.4 8.3 %collective-permute-start.19 = (f32[12,16,128]{2,1,0:T(8,128)S(1)}, f32[12,16,128]{2,1,0:T(8,128)S(1)}, u32[]{:S(2)}, u32[]{:S(2)}) collective-permute-start(f32[12,16,128]{2,1,0:T(8,128)S(1)} %get-tuple-element.52), channel_id=1, source_target_pairs={{0,7},{4,3},{1,6},{5,2},{2,5},{6,1},{3,4},{7,0},{8,15},{12,11},{9,... | collective-permute-start | bytes 294920 | tf_op jit(solution)/shard_map/ppermute | solution.py:466
  62.2 36.5 %collective-permute-start.26 = (f32[2,2,12,16,128]{4,3,2,1,0:T(8,128)S(1)}, f32[2,2,12,16,128]{4,3,2,1,0:T(8,128)S(1)}, u32[]{:S(2)}, u32[]{:S(2)}) collective-permute-start(f32[2,2,12,16,128]{4,3,2,1,0:T(8,128)S(1)} %get-tuple-element.64), channel_id=1, source_target_pairs={{0,4},{4,0},{1,5},{5,1},{2,6},{6,2},{3,7},{7,3},{8,12},{12,8},{9,1... | collective-permute-start | bytes 1179656 | tf_op jit(solution)/shard_map/ppermute | solution.py:505
  64.2 34.5 %collective-permute-start.27 = (f32[2,2,12,16,128]{4,3,2,1,0:T(8,128)S(1)}, f32[2,2,12,16,128]{4,3,2,1,0:T(8,128)S(1)}, u32[]{:S(2)}, u32[]{:S(2)}) collective-permute-start(f32[2,2,12,16,128]{4,3,2,1,0:T(8,128)S(1)} %get-tuple-element.65), channel_id=1, source_target_pairs={{0,2},{1,3},{4,6},{5,7},{8,10},{9,11},{12,14},{13,15},{16,18},{17,... | collective-permute-start | bytes 1179656 | tf_op jit(solution)/shard_map/ppermute | solution.py:506
  67.3 31.4 %collective-permute-start.28 = (f32[2,2,12,16,128]{4,3,2,1,0:T(8,128)S(1)}, f32[2,2,12,16,128]{4,3,2,1,0:T(8,128)S(1)}, u32[]{:S(2)}, u32[]{:S(2)}) collective-permute-start(f32[2,2,12,16,128]{4,3,2,1,0:T(8,128)S(1)} %get-tuple-element.66), channel_id=1, source_target_pairs={{0,6},{1,7},{4,2},{5,3},{8,14},{9,15},{12,10},{13,11},{16,22},{17,... | collective-permute-start | bytes 1179656 | tf_op jit(solution)/shard_map/ppermute | solution.py:507
  68.6 18.0 %collective-permute-start.20 = (f32[12,16,128]{2,1,0:T(8,128)S(1)}, f32[12,16,128]{2,1,0:T(8,128)S(1)}, u32[]{:S(2)}, u32[]{:S(2)}) collective-permute-start(f32[12,16,128]{2,1,0:T(8,128)S(1)} %get-tuple-element.53), channel_id=1, source_target_pairs={{0,2},{4,6},{1,3},{5,7},{2,0},{6,4},{3,1},{7,5},{8,10},{12,14},{9,... | collective-permute-start | bytes 294920 | tf_op jit(solution)/shard_map/ppermute | solution.py:466
  68.7 18.9 %collective-permute-start.21 = (f32[12,16,128]{2,1,0:T(8,128)S(1)}, f32[12,16,128]{2,1,0:T(8,128)S(1)}, u32[]{:S(2)}, u32[]{:S(2)}) collective-permute-start(f32[12,16,128]{2,1,0:T(8,128)S(1)} %get-tuple-element.54), channel_id=1, source_target_pairs={{0,3},{4,7},{1,2},{5,6},{2,1},{6,5},{3,0},{7,4},{8,11},{12,15},{9,... | collective-permute-start | bytes 294920 | tf_op jit(solution)/shard_map/ppermute | solution.py:466
  87.6 7.9 %collective-permute-start.24 = (f32[2,12,16,128]{3,2,1,0:T(8,128)S(1)}, f32[2,12,16,128]{3,2,1,0:T(8,128)S(1)}, u32[]{:S(2)}, u32[]{:S(2)}) collective-permute-start(f32[2,12,16,128]{3,2,1,0:T(8,128)S(1)} %get-tuple-element.58), channel_id=1, source_target_pairs={{0,1},{4,5},{1,0},{5,4},{2,3},{6,7},{3,2},{7,6},{8,9},{12,13},{9,8... | collective-permute-start | bytes 589832 | tf_op jit(solution)/shard_map/ppermute | solution.py:466
  98.6 26.4 %collective-permute-start.25 = (f32[16,192,128]{2,1,0:T(8,128)S(1)}, f32[16,192,128]{2,1,0:T(8,128)S(1)}, u32[]{:S(2)}, u32[]{:S(2)}) collective-permute-start(f32[16,192,128]{2,1,0:T(8,128)S(1)} %get-tuple-element.60.block), channel_id=1, source_target_pairs={{0,1},{1,0},{2,3},{3,2},{4,5},{5,4},{6,7},{7,6},{8,9},{9,8},{10,11... | collective-permute-start | bytes 4718600 | tf_op jit(solution)/shard_map/ppermute | solution.py:509
  99.4 25.6 %collective-permute-start.29 = (f32[8,384,128]{2,1,0:T(8,128)S(1)}, f32[8,384,128]{2,1,0:T(8,128)S(1)}, u32[]{:S(2)}, u32[]{:S(2)}) collective-permute-start(f32[8,384,128]{2,1,0:T(8,128)S(1)} %shard_map.34.bundle), channel_id=1, source_target_pairs={{0,1},{1,0},{2,3},{3,2},{4,5},{5,4},{6,7},{7,6},{8,9},{9,8},{10,11... | collective-permute-start | bytes 4718600 | tf_op jit(solution)/shard_map/ppermute | solution.py:513
  (8 other events, 120.4 us)

commit v9 on v8

--- a/solution.py
+++ b/solution.py
@@ -227,14 +227,23 @@
     return jnp.where(test(rows, columns), 1.0, 0.0).astype(jnp.float32)
 
 
-def gram_message(read, total, tiles, chunk):
+def split(values):
+    high = values.astype(jnp.bfloat16)
+    rest = values - high.astype(jnp.float32)
+    middle = rest.astype(jnp.bfloat16)
+    return high, middle, (rest - middle.astype(jnp.float32)).astype(jnp.bfloat16)
+
+
+def product(a, b, contract=((1,), (0,))):
+    return lax.dot_general(a, b, (contract, ((), ())), preferred_element_type=jnp.float32)
+
+
+def gram_message(wide, total):
     tall = total * EIGHT
-
-    def body(index, sums):
-        wide = jnp.concatenate([read(index * chunk + t) for t in range(chunk)], axis=1)
-        return sums + exact_dot(wide, wide, ((1,), (1,)))
-
-    sums = lax.fori_loop(0, tiles // chunk, body, jnp.zeros((tall, tall), jnp.float32))
+    high, middle, low = split(wide)
+    joined, doubled = jnp.concatenate([high, middle], axis=1), jnp.concatenate([high, high], axis=1)
+    mixed = product(doubled, jnp.concatenate([middle, low], axis=1), ((1,), (1,)))
+    sums = product(joined, joined, ((1,), (1,))) + (mixed + mixed.T)
     sums = sums * table_of((tall, tall), lambda r, c: r % EIGHT == c % EIGHT)
     partial = exact_dot(table_of((total, tall), lambda r, c: c // EIGHT == r), sums)
     spread = exact_dot(partial, table_of((tall, LANES), lambda r, c: r // EIGHT == c % total))
@@ -284,13 +293,10 @@
     return both * table_of((tall, tall), lambda r, c: r % EIGHT == c % EIGHT)
 
 
-def tile_reader(ref):
-    total, width = ref.shape[0], ref.shape[2]
-    return lambda t: ref[:, pl.ds(pl.multiple_of(EIGHT * t, EIGHT), EIGHT), :].reshape(total * EIGHT, width)
-
-
-def chunk_of(tiles):
-    return next(c for c in (6, 4, 3, 2, 1) if tiles % c == 0)
+def side_by_side(ref):
+    total, length, width = ref.shape
+    tiles = [ref[:, start : start + EIGHT, :].reshape(total * EIGHT, width) for start in range(0, length, EIGHT)]
+    return jnp.concatenate(tiles, axis=1)
 
 
 def first_kernel(early, late, kept, place, *refs):
@@ -301,45 +307,53 @@
             block[(me ^ apart) * kept + at] = given[at * len(early) + index][...].reshape(shape)
         for index, apart in enumerate(late):
             block[(me ^ apart) * kept + at] = given[kept * len(early) + index][at].reshape(shape)
-    total, tiles = block.shape[0], block.shape[1] // EIGHT
-    row = gram_message(tile_reader(block), total, tiles, chunk_of(tiles))
-    message[...] = jnp.broadcast_to(row[None], message.shape)
+    message[...] = jnp.broadcast_to(gram_message(side_by_side(block), block.shape[0])[None], message.shape)
+
+
+def applied(table, block):
+    total = block.shape[0]
+    tall = total * EIGHT
+    high, middle, low = split(by_tiles(table, total))
+    values_high, values_middle, values_low = split(side_by_side(block))
+    left = jnp.concatenate(
+        [jnp.concatenate([high, high], axis=1), jnp.concatenate([middle, middle], axis=1)], axis=0
+    )
+    main = product(left, jnp.concatenate([values_high, values_middle], axis=0))
+    rest = product(jnp.concatenate([low, high], axis=1), jnp.concatenate([values_high, values_low], axis=0))
+    return main[:tall] + (main[tall:] + rest)
+
+
+def put(wide, basis):
+    total, length, width = basis.shape
+    for t in range(length // EIGHT):
+        piece = wide[:, t * width : (t + 1) * width].reshape(total, EIGHT, width)
+        basis[:, EIGHT * t : EIGHT * (t + 1), :] = piece
 
 
 def second_kernel(cell_total, copies, block, basis, message):
-    total, tiles = block.shape[0], block.shape[1] // EIGHT
-    apply_all(inverse_factor(copies, total, cell_total), block, basis)
-    row = gram_message(tile_reader(basis), total, tiles, chunk_of(tiles))
-    message[...] = jnp.broadcast_to(row[None], message.shape)
+    total = block.shape[0]
+    wide = applied(inverse_factor(copies, total, cell_total), block)
+    put(wide, basis)
+    message[...] = jnp.broadcast_to(gram_message(wide, total)[None], message.shape)
 
 
 def third_kernel(cell_total, copies, block, basis):
-    apply_all(inverse_factor(copies, block.shape[0], cell_total), block, basis)
-
-
-def table_kernel(cell_total, copies, block, table_out, message, basis):
-    total, tiles = block.shape[0], block.shape[1] // EIGHT
+    put(applied(inverse_factor(copies, block.shape[0], cell_total), block), basis)
+
+
+def table_kernel(cell_total, copies, block, table_out, message):
+    total = block.shape[0]
     table = inverse_factor(copies, total, cell_total)
     table_out[...] = table
-    apply_all(table, block, basis)
-    row = gram_message(tile_reader(basis), total, tiles, chunk_of(tiles))
-    message[...] = jnp.broadcast_to(row[None], message.shape)
-
-
-def bundle_kernel(place, *refs):
-    given, bundle = refs[:-1], refs[-1]
-    side, kept = place[0], given[0].shape[0]
-    for kind, ref in enumerate(given):
-        for at in range(kept):
-            slot = (kind // 2) * 2 * kept + (side ^ (kind % 2)) * kept + at
-            bundle[slot] = ref[at].reshape(bundle.shape[1:])
-
-
-def last_kernel(cell_total, place, copies, table, block, block_near, bundle, bundle_near, out, splats):
+    message[...] = jnp.broadcast_to(gram_message(applied(table, block), total)[None], message.shape)
+
+
+def last_kernel(cell_total, place, copies, table, block, block_near, *refs):
+    spares, (out, splats) = refs[:-2], refs[-2:]
     total, length, width = block.shape
     held, rows = out.shape[:2]
     part = length // rows
-    orb = place[2]
+    side, orb = place[0], place[2]
     core, chip = orb % CORES, orb // CORES
     second = inverse_factor(copies, total, cell_total)
     pick = table_of((LANES, total), lambda r, c: r - total == c)
@@ -364,38 +378,28 @@
 
         lax.fori_loop(0, rows, body, 0, unroll=2)
 
-    def at(ref, index, offset=0):
+    def at(ref, index):
         def load(row, strip):
-            start = pl.multiple_of(offset + row * part + strip * EIGHT, EIGHT)
-            return ref[index, pl.ds(start, EIGHT), :]
+            return ref[index, pl.ds(pl.multiple_of(row * part + strip * EIGHT, EIGHT), EIGHT), :]
 
         return load
 
     write([(j, at(block, j)) for j in range(total)], orb * part)
     write([(j, at(block_near, j)) for j in range(total)], (orb ^ 1) * part)
+
+    def spare_at(ref, stage, share):
+        return lambda row, strip: ref[stage, share, row, pl.ds(strip * EIGHT, EIGHT), :]
+
+    kinds = len(spares) // 2
     for share in range(CORES):
         sources = []
-        for flip, ref in enumerate((bundle, bundle_near)):
-            for j in range(2 * held):
-                quad = (core if j // held else orb) ^ flip
-                sources.append((quad * held + j % held, at(ref, j, share * length)))
+        for index, ref in enumerate(spares):
+            flip, kind = index // kinds, index % kinds
+            quad = (core if kind // 2 else orb) ^ flip
+            for stage in range(ref.shape[0]):
+                orbital = quad * held + (side ^ (kind % 2)) * ref.shape[0] + stage
+                sources.append((orbital, spare_at(ref, stage, share)))
         write(sources, ((1 - chip) * CORES + share) * part)
-
-
-def apply_all(table, block, basis):
-    total, tiles, width = block.shape[0], block.shape[1] // EIGHT, block.shape[2]
-    matrix = by_tiles(table, total)
-    read, chunk = tile_reader(block), chunk_of(tiles)
-
-    def body(index, carry):
-        wide = jnp.concatenate([read(index * chunk + t) for t in range(chunk)], axis=1)
-        result = exact_dot(matrix, wide)
-        for t in range(chunk):
-            piece = result[:, t * width : (t + 1) * width].reshape(total, EIGHT, width)
-            basis[:, pl.ds(pl.multiple_of(EIGHT * (index * chunk + t), EIGHT), EIGHT), :] = piece
-        return carry
-
-    lax.fori_loop(0, tiles // chunk, body, 0)
 
 
 def small_call(kernel, out_shape, specs, *args):
@@ -494,7 +498,10 @@
         return lax.all_to_all(message, ALL, 0, 0)
 
     block, message = small_call(
-        functools.partial(first_kernel, early, late, kept), [block_shape, message_shape], [SMEM] + [VMEM] * len(parts), place, *parts
+        functools.partial(first_kernel, early, late, kept),
+        [block_shape, message_shape],
+        [SMEM] + [VMEM] * len(parts),
+        *(place, *parts),
     )
     if spares:
         up = [(i, i + CORES) for i in range(CORES)]
@@ -507,26 +514,23 @@
             lax.ppermute(spare[3], ("side", "orb"), slanted_up),
         ]
         block_near = lax.ppermute(block, "orb", cores)
-        bundle_shape = jax.ShapeDtypeStruct((2 * held, CORES * rows * part, width), jnp.float32)
         table_shape = jax.ShapeDtypeStruct((total, LANES), jnp.float32)
-        bundle = small_call(bundle_kernel, bundle_shape, [SMEM] + [VMEM] * len(given), place, *given)
-        bundle_near = lax.ppermute(bundle, "orb", cores)
+        given += [lax.ppermute(piece, "orb", cores) for piece in given]
         table, message = pl.pallas_call(
             functools.partial(table_kernel, cell_total),
             out_shape=[table_shape, message_shape],
             in_specs=[VMEM] * 2,
             out_specs=[VMEM] * 2,
-            scratch_shapes=[pltpu.VMEM(block_shape.shape, jnp.float32)],
             compiler_params=pltpu.CompilerParams(vmem_limit_bytes=24 * 1024 * 1024),
         )(exchanged(message), block)
         return pl.pallas_call(
             functools.partial(last_kernel, cell_total),
             out_shape=jax.ShapeDtypeStruct((held, rows, cols, width), jnp.float32),
-            in_specs=[SMEM] + [VMEM] * 6,
+            in_specs=[SMEM] + [VMEM] * (4 + len(given)),
             out_specs=VMEM,
             scratch_shapes=[pltpu.VMEM((total, held, EIGHT, width), jnp.float32)],
             compiler_params=pltpu.CompilerParams(vmem_limit_bytes=24 * 1024 * 1024),
-        )(place, exchanged(message), table, block, block_near, bundle, bundle_near)
+        )(place, exchanged(message), table, block, block_near, *given)
     basis, message = small_call(
         functools.partial(second_kernel, cell_total), [block_shape, message_shape], [VMEM] * 2, exchanged(message), block
     )

time: 131 us -> 129 us (0.985)
  waiting for transfers between devices: 57.4 us -> 47 us
  starting transfers between devices: 26 us -> 35.7 us
  Pallas kernels: 27.3 us -> 23.7 us
  blocking collectives: 19.6 us -> 21.7 us
    ppermute x13, waiting for transfers between devices: 27.6 us -> 6.32 us  [to_partner(): lax.ppermute(piece, ('side', 'orb'), [(flat_of(i), flat_of(i ^ m)) for i...]
    ppermute x2, waiting for transfers between devices: 9.68 us -> 0.01 us  [whole(): lax.ppermute(sent[3 * at + 1], 'side', swap)]
    ppermute x1, waiting for transfers between devices: 0.01 us -> 8.13 us  [whole(): lax.ppermute(spare[2], 'orb', up)]
    ppermute x1, waiting for transfers between devices: 0.01 us -> 6.4 us  [whole(): lax.ppermute(spare[1], 'side', swap)]
    ppermute x2, waiting for transfers between devices: 4.02 us -> 7.66 us  [whole(): lax.ppermute(sent[3 * at + 2], slab_axes, ahead)]
    ppermute x2, starting transfers between devices: 0.62 us -> 4.13 us  [whole(): lax.ppermute(sent[3 * at + 2], slab_axes, ahead)]
    ppermute x2, starting transfers between devices: 1.5 us -> 4.9 us  [whole(): lax.ppermute(sent[3 * at], slab_axes, slant)]
    ppermute x13, starting transfers between devices: 8.55 us -> 11.7 us  [to_partner(): lax.ppermute(piece, ('side', 'orb'), [(flat_of(i), flat_of(i ^ m)) for i...]
  transfers between devices with their start and end apart: 30 -> 33, of which waited for: 11 -> 14; matrix products, arithmetic and copies ran while one was open for 0% -> 0% of each run, Pallas kernels for 15% -> 11%
where the time goes in v9:
time: 129 us; the launch traced here: 128 us
  waiting for transfers between devices  47 us (36%)
  starting transfers between devices  35.7 us (28%)
  Pallas kernels  23.7 us (18%)
  blocking collectives  21.7 us (17%)
    all_to_all x2, blocking collectives, exchanged(): return lax.all_to_all(message, ALL, 0, 0)  21.7 us
    ppermute x13, starting transfers between devices, to_partner(): lax.ppermute(piece, ('side', 'orb'), [(flat_of(i), flat_of(i ^ m)) for i...  11.7 us
    pallas_call x2, Pallas kernels, filtered_pieces(): pl.pallas_call(functools.partial(filter_kernel, at, len(pot_far), early,...  10.4 us
    ppermute x3, waiting for transfers between devices, whole(): lax.ppermute(joined, 'orb', [(i, i ^ m) for i in range(orb_count)])  9.47 us
    ppermute x1, waiting for transfers between devices, whole(): lax.ppermute(spare[2], 'orb', up)  8.13 us
    ppermute x2, waiting for transfers between devices, whole(): lax.ppermute(sent[3 * at + 2], slab_axes, ahead)  7.66 us
    ppermute x1, waiting for transfers between devices, whole(): lax.ppermute(spare[1], 'side', swap)  6.4 us
    ppermute x13, waiting for transfers between devices, to_partner(): lax.ppermute(piece, ('side', 'orb'), [(flat_of(i), flat_of(i ^ m)) for i...  6.32 us
  transfers between devices with their start and end apart: 33, of which 14 were waited for; matrix products, arithmetic and copies ran while one was open for 0% of the time, Pallas kernels for 11%

profile of v9, /device:TPU:0, one launch (start us, length us, event | category | flops | bytes accessed | tf_op | source)
XLA Modules:
  0.0 128.4 jit_solution(18354129063151230250)
XLA Ops:
  0.1 2.2 %shard_map.28 = (f32[12,16,128]{2,1,0:T(8,128)S(1)}, f32[6,16,128]{2,1,0:T(8,128)S(1)}, f32[9,64,128]{2,1,0:T(8,128)S(1)}, f32[12,64,128]{2,1,0:T(8,128)S(1)}, f...) custom-call(s32[3]{0:T(128)S(1)} %pad_add_fusion.place, ...), custom_call_target="tpu_custom_call" | custom-call | tf_op jit(solution)/shard_map/pallas_call | solution.py:61
  2.3 3.1 %collective-permute-start.3 = (f32[12,16,128]{2,1,0:T(8,128)S(1)}, f32[12,16,128]{2,1,0:T(8,128)S(1)}, u32[]{:S(2)}, u32[]{:S(2)}) collective-permute-start(f32[12,16,128]{2,1,0:T(8,128)S(1)} %get-tuple-element.39), channel_id=1, source_target_pairs={{0,4},{4,0},{1,5},{5,1},{2,6},{6,2},{3,7},{7,3},{8,12},{12,8},{9,1... | collective-permute-start | bytes 294920 | tf_op jit(solution)/shard_map/ppermute | solution.py:438
  5.4 3.5 %collective-permute-start.1 = (f32[9,64,128]{2,1,0:T(8,128)S(1)}, f32[9,64,128]{2,1,0:T(8,128)S(1)}, u32[]{:S(2)}, u32[]{:S(2)}) collective-permute-start(f32[9,64,128]{2,1,0:T(8,128)S(1)} %get-tuple-element.37), channel_id=1, source_target_pairs={{0,28},{4,8},{8,4},{12,16},{16,12},{20,24},{24,20},{28,0},{1,29},{... | collective-permute-start | bytes 884744 | tf_op jit(solution)/shard_map/ppermute | solution.py:457
  9.3 2.4 %collective-permute-start.4 = (f32[6,16,128]{2,1,0:T(8,128)S(1)}, f32[6,16,128]{2,1,0:T(8,128)S(1)}, u32[]{:S(2)}, u32[]{:S(2)}) collective-permute-start(f32[6,16,128]{2,1,0:T(8,128)S(1)} %get-tuple-element.40), channel_id=1, source_target_pairs={{0,28},{4,8},{8,4},{12,16},{16,12},{20,24},{24,20},{28,0},{1,29},{... | collective-permute-start | bytes 147464 | tf_op jit(solution)/shard_map/ppermute | solution.py:439
  11.7 4.7 %collective-permute-done.5.straight = f32[6,16,128]{2,1,0:T(8,128)S(1)} collective-permute-done((f32[6,16,128]{2,1,0:T(8,128)S(1)}, f32[6,16,128]{2,1,0:T(8,128)S(1)}, u32[]{:S(2)}, u32[]{:S(2)}) %collective-permute-start.5) | collective-permute-done | bytes 49184 | tf_op jit(solution)/shard_map/ppermute | solution.py:440
  16.4 2.2 %collective-permute-done.4.slanted = f32[6,16,128]{2,1,0:T(8,128)S(1)} collective-permute-done((f32[6,16,128]{2,1,0:T(8,128)S(1)}, f32[6,16,128]{2,1,0:T(8,128)S(1)}, u32[]{:S(2)}, u32[]{:S(2)}) %collective-permute-start.4) | collective-permute-done | bytes 49184 | tf_op jit(solution)/shard_map/ppermute | solution.py:439
  20.6 5.2 %collective-permute-done.8.rest_3_ = f32[24,16,128]{2,1,0:T(8,128)S(1)} collective-permute-done((f32[24,16,128]{2,1,0:T(8,128)S(1)}, f32[24,16,128]{2,1,0:T(8,128)S(1)}, u32[]{:S(2)}, u32[]{:S(2)}) %collective-permute-start.8) | collective-permute-done | bytes 196640 | tf_op jit(solution)/shard_map/ppermute | solution.py:450
  25.9 4.2 %collective-permute-done.7.rest_2_ = f32[24,16,128]{2,1,0:T(8,128)S(1)} collective-permute-done((f32[24,16,128]{2,1,0:T(8,128)S(1)}, f32[24,16,128]{2,1,0:T(8,128)S(1)}, u32[]{:S(2)}, u32[]{:S(2)}) %collective-permute-start.7) | collective-permute-done | bytes 196640 | tf_op jit(solution)/shard_map/ppermute | solution.py:450
  30.1 2.1 %collective-permute-start.2 = (f32[9,64,128]{2,1,0:T(8,128)S(1)}, f32[9,64,128]{2,1,0:T(8,128)S(1)}, u32[]{:S(2)}, u32[]{:S(2)}) collective-permute-start(f32[9,64,128]{2,1,0:T(8,128)S(1)} %get-tuple-element.38), channel_id=1, source_target_pairs={{0,24},{4,12},{8,0},{12,20},{16,8},{20,28},{24,16},{28,4},{1,25},{... | collective-permute-start | bytes 884744 | tf_op jit(solution)/shard_map/ppermute | solution.py:459
  35.8 4.2 %collective-permute-done.2.straight = f32[9,64,128]{2,1,0:T(8,128)S(1)} collective-permute-done((f32[9,64,128]{2,1,0:T(8,128)S(1)}, f32[9,64,128]{2,1,0:T(8,128)S(1)}, u32[]{:S(2)}, u32[]{:S(2)}) %collective-permute-start.2) | collective-permute-done | bytes 294944 | tf_op jit(solution)/shard_map/ppermute | solution.py:459
  40.0 4.7 %shard_map.30 = (f32[12,16,128]{2,1,0:T(8,128)S(1)}, f32[12,16,128]{2,1,0:T(8,128)S(1)}, f32[12,16,128]{2,1,0:T(8,128)S(1)}, f32[12,16,128]{2,1,0:T(8,128)S(1)},...) custom-call(s32[3]{0:T(128)S(1)} %pad_add_fusion.place, ...), custom_call_target="tpu_custom_call" | custom-call | tf_op jit(solution)/shard_map/pallas_call | solution.py:200
  45.8 2.0 %collective-permute-done.16.slanted = f32[9,64,128]{2,1,0:T(8,128)S(1)} collective-permute-done((f32[9,64,128]{2,1,0:T(8,128)S(1)}, f32[9,64,128]{2,1,0:T(8,128)S(1)}, u32[]{:S(2)}, u32[]{:S(2)}) %collective-permute-start.16) | collective-permute-done | bytes 294944 | tf_op jit(solution)/shard_map/ppermute | solution.py:457
  48.3 3.4 %collective-permute-done.17.straight = f32[9,64,128]{2,1,0:T(8,128)S(1)} collective-permute-done((f32[9,64,128]{2,1,0:T(8,128)S(1)}, f32[9,64,128]{2,1,0:T(8,128)S(1)}, u32[]{:S(2)}, u32[]{:S(2)}) %collective-permute-start.17) | collective-permute-done | bytes 294944 | tf_op jit(solution)/shard_map/ppermute | solution.py:459
  54.1 5.7 %shard_map.31 = (f32[12,16,128]{2,1,0:T(8,128)S(1)}, f32[12,16,128]{2,1,0:T(8,128)S(1)}, f32[12,16,128]{2,1,0:T(8,128)S(1)}, f32[12,16,128]{2,1,0:T(8,128)S(1)},...) custom-call(s32[3]{0:T(128)S(1)} %pad_add_fusion.place, ...), custom_call_target="tpu_custom_call" | custom-call | tf_op jit(solution)/shard_map/pallas_call | solution.py:200
  59.8 2.9 %collective-permute-start.18 = (f32[12,16,128]{2,1,0:T(8,128)S(1)}, f32[12,16,128]{2,1,0:T(8,128)S(1)}, u32[]{:S(2)}, u32[]{:S(2)}) collective-permute-start(f32[12,16,128]{2,1,0:T(8,128)S(1)} %get-tuple-element.51), channel_id=1, source_target_pairs={{0,6},{4,2},{1,7},{5,3},{2,4},{6,0},{3,5},{7,1},{8,14},{12,10},{9,... | collective-permute-start | bytes 294920 | tf_op jit(solution)/shard_map/ppermute | solution.py:470
  73.9 2.1 %shard_map.32 = (f32[16,192,128]{2,1,0:T(8,128)S(1)}, f32[32,1,256]{2,1,0:T(1,128)S(1)}) custom-call(s32[3]{0:T(128)S(1)} %pad_add_fusion.place, f32[12,16,128]{2,1,0:T(8,128)S(1)} %collective-permute-done.9.refs_0_, f32[12,16,128]{2,1,0:T(8,128)S(1)} %collective-permute-done.10.refs_1_, f32[12,16,128]{2,1,0:T(8,128)S(1)} %collective-permute-done.11.refs_2_, ...), custom_call_target="tpu_custom_call" | custom-call | tf_op jit(solution)/shard_map/pallas_call | solution.py:406
  77.8 2.6 %collective-permute-start.27 = (f32[2,2,12,16,128]{4,3,2,1,0:T(8,128)S(1)}, f32[2,2,12,16,128]{4,3,2,1,0:T(8,128)S(1)}, u32[]{:S(2)}, u32[]{:S(2)}) collective-permute-start(f32[2,2,12,16,128]{4,3,2,1,0:T(8,128)S(1)} %get-tuple-element.65), channel_id=1, source_target_pairs={{0,2},{1,3},{4,6},{5,7},{8,10},{9,11},{12,14},{13,15},{16,18},{17,... | collective-permute-start | bytes 1179656 | tf_op jit(solution)/shard_map/ppermute | solution.py:513
  80.4 2.1 %collective-permute-start.28 = (f32[2,2,12,16,128]{4,3,2,1,0:T(8,128)S(1)}, f32[2,2,12,16,128]{4,3,2,1,0:T(8,128)S(1)}, u32[]{:S(2)}, u32[]{:S(2)}) collective-permute-start(f32[2,2,12,16,128]{4,3,2,1,0:T(8,128)S(1)} %get-tuple-element.66), channel_id=1, source_target_pairs={{0,6},{1,7},{4,2},{5,3},{8,14},{9,15},{12,10},{13,11},{16,22},{17,... | collective-permute-start | bytes 1179656 | tf_op jit(solution)/shard_map/ppermute | solution.py:514
  82.6 6.4 %collective-permute-done.26.refs_1_ = f32[2,2,12,16,128]{4,3,2,1,0:T(8,128)S(1)} collective-permute-done((f32[2,2,12,16,128]{4,3,2,1,0:T(8,128)S(1)}, f32[2,2,12,16,128]{4,3,2,1,0:T(8,128)S(1)}, u32[]{:S(2)}, u32[]{:S(2)}) %collective-permute-start.26) | collective-permute-done | bytes 393248 | tf_op jit(solution)/shard_map/ppermute | solution.py:512
  89.0 8.1 %collective-permute-done.27.refs_2_ = f32[2,2,12,16,128]{4,3,2,1,0:T(8,128)S(1)} collective-permute-done((f32[2,2,12,16,128]{4,3,2,1,0:T(8,128)S(1)}, f32[2,2,12,16,128]{4,3,2,1,0:T(8,128)S(1)}, u32[]{:S(2)}, u32[]{:S(2)}) %collective-permute-start.27) | collective-permute-done | bytes 393248 | tf_op jit(solution)/shard_map/ppermute | solution.py:513
  97.6 12.7 %all_to_all.10.copies = f32[32,1,256]{2,1,0:T(1,128)S(1)} all-to-all(f32[32,1,256]{2,1,0:T(1,128)S(1)} %get-tuple-element.59), channel_id=1, replica_groups=mesh['pair'=4,'side'=2,'orb'=4] {'pair','side','orb'}, dimensions={0} | all-to-all | bytes 65536 | tf_op jit(solution)/shard_map/all_to_all | solution.py:498
  110.3 3.3 %shard_map.33 = (f32[16,128]{1,0:T(8,128)S(1)}, f32[32,1,256]{2,1,0:T(1,128)S(1)}) custom-call(f32[32,1,256]{2,1,0:T(1,128)S(1)} %all_to_all.10.copies, f32[16,192,128]{2,1,0:T(8,128)S(1)} %get-tuple-element.60.block), custom_call_target="tpu_custom_call" | custom-call | tf_op jit(solution)/shard_map/pallas_call | solution.py:519
  113.7 9.0 %all_to_all.11.copies = f32[32,1,256]{2,1,0:T(1,128)S(1)} all-to-all(f32[32,1,256]{2,1,0:T(1,128)S(1)} %get-tuple-element.61), channel_id=1, replica_groups=mesh['pair'=4,'side'=2,'orb'=4] {'pair','side','orb'}, dimensions={0} | all-to-all | bytes 65536 | tf_op jit(solution)/shard_map/all_to_all | solution.py:498
  122.6 5.7 %shard_map.34 = f32[4,12,64,128]{3,2,1,0:T(8,128)} custom-call(s32[3]{0:T(128)S(1)} %pad_add_fusion.place, f32[32,1,256]{2,1,0:T(1,128)S(1)} %all_to_all.11.copies, f32[16,128]{1,0:T(8,128)S(1)} %get-tuple-element.62.table, f32[16,192,128]{2,1,0:T(8,128)S(1)} %get-tuple-element.60.block, f32[16,192,128]{2,1,0:T(8,128)S(1)} %collective-permute-done.25.block_near, ...), custom_call_target="tpu_custom_call" | custom-call | tf_op jit(solution)/shard_map/pallas_call | solution.py:526
  (57 shorter events, 23.6 us)
Async XLA Ops:
  2.3 16.3 %collective-permute-start.3 = (f32[12,16,128]{2,1,0:T(8,128)S(1)}, f32[12,16,128]{2,1,0:T(8,128)S(1)}, u32[]{:S(2)}, u32[]{:S(2)}) collective-permute-start(f32[12,16,128]{2,1,0:T(8,128)S(1)} %get-tuple-element.39), channel_id=1, source_target_pairs={{0,4},{4,0},{1,5},{5,1},{2,6},{6,2},{3,7},{7,3},{8,12},{12,8},{9,1... | collective-permute-start | bytes 294920 | tf_op jit(solution)/shard_map/ppermute | solution.py:438
  5.4 28.3 %collective-permute-start.1 = (f32[9,64,128]{2,1,0:T(8,128)S(1)}, f32[9,64,128]{2,1,0:T(8,128)S(1)}, u32[]{:S(2)}, u32[]{:S(2)}) collective-permute-start(f32[9,64,128]{2,1,0:T(8,128)S(1)} %get-tuple-element.37), channel_id=1, source_target_pairs={{0,28},{4,8},{8,4},{12,16},{16,12},{20,24},{24,20},{28,0},{1,29},{... | collective-permute-start | bytes 884744 | tf_op jit(solution)/shard_map/ppermute | solution.py:457
  9.3 9.3 %collective-permute-start.4 = (f32[6,16,128]{2,1,0:T(8,128)S(1)}, f32[6,16,128]{2,1,0:T(8,128)S(1)}, u32[]{:S(2)}, u32[]{:S(2)}) collective-permute-start(f32[6,16,128]{2,1,0:T(8,128)S(1)} %get-tuple-element.40), channel_id=1, source_target_pairs={{0,28},{4,8},{8,4},{12,16},{16,12},{20,24},{24,20},{28,0},{1,29},{... | collective-permute-start | bytes 147464 | tf_op jit(solution)/shard_map/ppermute | solution.py:439
  18.7 11.4 %collective-permute-start.7 = (f32[24,16,128]{2,1,0:T(8,128)S(1)}, f32[24,16,128]{2,1,0:T(8,128)S(1)}, u32[]{:S(2)}, u32[]{:S(2)}) collective-permute-start(f32[24,16,128]{2,1,0:T(8,128)S(1)} %shard_map.29.rest_0_), channel_id=1, source_target_pairs={{0,2},{1,3},{2,0},{3,1},{4,6},{5,7},{6,4},{7,5},{8,10},{9,11},{10,... | collective-permute-start | bytes 589832 | tf_op jit(solution)/shard_map/ppermute | solution.py:450
  20.3 11.9 %collective-permute-start.6 = (f32[24,16,128]{2,1,0:T(8,128)S(1)}, f32[24,16,128]{2,1,0:T(8,128)S(1)}, u32[]{:S(2)}, u32[]{:S(2)}) collective-permute-start(f32[24,16,128]{2,1,0:T(8,128)S(1)} %shard_map.29.rest_0_), channel_id=1, source_target_pairs={{0,1},{1,0},{2,3},{3,2},{4,5},{5,4},{6,7},{7,6},{8,9},{9,8},{10,11... | collective-permute-start | bytes 589832 | tf_op jit(solution)/shard_map/ppermute | solution.py:450
  20.5 19.4 %collective-permute-start = (f32[12,64,128]{2,1,0:T(8,128)S(1)}, f32[12,64,128]{2,1,0:T(8,128)S(1)}, u32[]{:S(2)}, u32[]{:S(2)}) collective-permute-start(f32[12,64,128]{2,1,0:T(8,128)S(1)} %get-tuple-element.36), channel_id=1, source_target_pairs={{0,4},{4,0},{1,5},{5,1},{2,6},{6,2},{3,7},{7,3},{8,12},{12,8},{9,1... | collective-permute-start | bytes 1179656 | tf_op jit(solution)/shard_map/ppermute | solution.py:458
  25.8 26.2 %collective-permute-start.15 = (f32[12,64,128]{2,1,0:T(8,128)S(1)}, f32[12,64,128]{2,1,0:T(8,128)S(1)}, u32[]{:S(2)}, u32[]{:S(2)}) collective-permute-start(f32[12,64,128]{2,1,0:T(8,128)S(1)} %get-tuple-element.47), channel_id=1, source_target_pairs={{0,4},{4,0},{1,5},{5,1},{2,6},{6,2},{3,7},{7,3},{8,12},{12,8},{9,1... | collective-permute-start | bytes 1179656 | tf_op jit(solution)/shard_map/ppermute | solution.py:458
  30.1 9.9 %collective-permute-start.2 = (f32[9,64,128]{2,1,0:T(8,128)S(1)}, f32[9,64,128]{2,1,0:T(8,128)S(1)}, u32[]{:S(2)}, u32[]{:S(2)}) collective-permute-start(f32[9,64,128]{2,1,0:T(8,128)S(1)} %get-tuple-element.38), channel_id=1, source_target_pairs={{0,24},{4,12},{8,0},{12,20},{16,8},{20,28},{24,16},{28,4},{1,25},{... | collective-permute-start | bytes 884744 | tf_op jit(solution)/shard_map/ppermute | solution.py:459
  32.2 15.6 %collective-permute-start.16 = (f32[9,64,128]{2,1,0:T(8,128)S(1)}, f32[9,64,128]{2,1,0:T(8,128)S(1)}, u32[]{:S(2)}, u32[]{:S(2)}) collective-permute-start(f32[9,64,128]{2,1,0:T(8,128)S(1)} %get-tuple-element.48), channel_id=1, source_target_pairs={{0,28},{4,8},{8,4},{12,16},{16,12},{20,24},{24,20},{28,0},{1,29},{... | collective-permute-start | bytes 884744 | tf_op jit(solution)/shard_map/ppermute | solution.py:457
  33.6 18.1 %collective-permute-start.17 = (f32[9,64,128]{2,1,0:T(8,128)S(1)}, f32[9,64,128]{2,1,0:T(8,128)S(1)}, u32[]{:S(2)}, u32[]{:S(2)}) collective-permute-start(f32[9,64,128]{2,1,0:T(8,128)S(1)} %get-tuple-element.49), channel_id=1, source_target_pairs={{0,24},{4,12},{8,0},{12,20},{16,8},{20,28},{24,16},{28,4},{1,25},{... | collective-permute-start | bytes 884744 | tf_op jit(solution)/shard_map/ppermute | solution.py:459
  44.7 15.1 %collective-permute-start.9 = (f32[12,16,128]{2,1,0:T(8,128)S(1)}, f32[12,16,128]{2,1,0:T(8,128)S(1)}, u32[]{:S(2)}, u32[]{:S(2)}) collective-permute-start(f32[12,16,128]{2,1,0:T(8,128)S(1)} %get-tuple-element.41), channel_id=1, source_target_pairs={{0,6},{4,2},{1,7},{5,3},{2,4},{6,0},{3,5},{7,1},{8,14},{12,10},{9,... | collective-permute-start | bytes 294920 | tf_op jit(solution)/shard_map/ppermute | solution.py:470
  45.5 14.2 %collective-permute-start.10 = (f32[12,16,128]{2,1,0:T(8,128)S(1)}, f32[12,16,128]{2,1,0:T(8,128)S(1)}, u32[]{:S(2)}, u32[]{:S(2)}) collective-permute-start(f32[12,16,128]{2,1,0:T(8,128)S(1)} %get-tuple-element.42), channel_id=1, source_target_pairs={{0,7},{4,3},{1,6},{5,2},{2,5},{6,1},{3,4},{7,0},{8,15},{12,11},{9,... | collective-permute-start | bytes 294920 | tf_op jit(solution)/shard_map/ppermute | solution.py:470
  47.8 14.9 %collective-permute-start.11 = (f32[12,16,128]{2,1,0:T(8,128)S(1)}, f32[12,16,128]{2,1,0:T(8,128)S(1)}, u32[]{:S(2)}, u32[]{:S(2)}) collective-permute-start(f32[12,16,128]{2,1,0:T(8,128)S(1)} %get-tuple-element.43), channel_id=1, source_target_pairs={{0,2},{4,6},{1,3},{5,7},{2,0},{6,4},{3,1},{7,5},{8,10},{12,14},{9,... | collective-permute-start | bytes 294920 | tf_op jit(solution)/shard_map/ppermute | solution.py:470
  51.7 11.0 %collective-permute-start.12 = (f32[12,16,128]{2,1,0:T(8,128)S(1)}, f32[12,16,128]{2,1,0:T(8,128)S(1)}, u32[]{:S(2)}, u32[]{:S(2)}) collective-permute-start(f32[12,16,128]{2,1,0:T(8,128)S(1)} %get-tuple-element.44), channel_id=1, source_target_pairs={{0,3},{4,7},{1,2},{5,6},{2,1},{6,5},{3,0},{7,4},{8,11},{12,15},{9,... | collective-permute-start | bytes 294920 | tf_op jit(solution)/shard_map/ppermute | solution.py:470
  52.1 10.8 %collective-permute-start.13 = (f32[12,16,128]{2,1,0:T(8,128)S(1)}, f32[12,16,128]{2,1,0:T(8,128)S(1)}, u32[]{:S(2)}, u32[]{:S(2)}) collective-permute-start(f32[12,16,128]{2,1,0:T(8,128)S(1)} %get-tuple-element.45), channel_id=1, source_target_pairs={{0,4},{4,0},{1,5},{5,1},{2,6},{6,2},{3,7},{7,3},{8,12},{12,8},{9,1... | collective-permute-start | bytes 294920 | tf_op jit(solution)/shard_map/ppermute | solution.py:470
  62.7 11.2 %collective-permute-start.24 = (f32[2,12,16,128]{3,2,1,0:T(8,128)S(1)}, f32[2,12,16,128]{3,2,1,0:T(8,128)S(1)}, u32[]{:S(2)}, u32[]{:S(2)}) collective-permute-start(f32[2,12,16,128]{3,2,1,0:T(8,128)S(1)} %get-tuple-element.58), channel_id=1, source_target_pairs={{0,1},{4,5},{1,0},{5,4},{2,3},{6,7},{3,2},{7,6},{8,9},{12,13},{9,8... | collective-permute-start | bytes 589832 | tf_op jit(solution)/shard_map/ppermute | solution.py:470
  76.0 46.6 %collective-permute-start.25 = (f32[16,192,128]{2,1,0:T(8,128)S(1)}, f32[16,192,128]{2,1,0:T(8,128)S(1)}, u32[]{:S(2)}, u32[]{:S(2)}) collective-permute-start(f32[16,192,128]{2,1,0:T(8,128)S(1)} %get-tuple-element.60.block), channel_id=1, source_target_pairs={{0,1},{1,0},{2,3},{3,2},{4,5},{5,4},{6,7},{7,6},{8,9},{9,8},{10,11... | collective-permute-start | bytes 4718600 | tf_op jit(solution)/shard_map/ppermute | solution.py:516
  77.0 12.0 %collective-permute-start.26 = (f32[2,2,12,16,128]{4,3,2,1,0:T(8,128)S(1)}, f32[2,2,12,16,128]{4,3,2,1,0:T(8,128)S(1)}, u32[]{:S(2)}, u32[]{:S(2)}) collective-permute-start(f32[2,2,12,16,128]{4,3,2,1,0:T(8,128)S(1)} %get-tuple-element.64), channel_id=1, source_target_pairs={{0,4},{4,0},{1,5},{5,1},{2,6},{6,2},{3,7},{7,3},{8,12},{12,8},{9,1... | collective-permute-start | bytes 1179656 | tf_op jit(solution)/shard_map/ppermute | solution.py:512
  77.8 19.3 %collective-permute-start.27 = (f32[2,2,12,16,128]{4,3,2,1,0:T(8,128)S(1)}, f32[2,2,12,16,128]{4,3,2,1,0:T(8,128)S(1)}, u32[]{:S(2)}, u32[]{:S(2)}) collective-permute-start(f32[2,2,12,16,128]{4,3,2,1,0:T(8,128)S(1)} %get-tuple-element.65), channel_id=1, source_target_pairs={{0,2},{1,3},{4,6},{5,7},{8,10},{9,11},{12,14},{13,15},{16,18},{17,... | collective-permute-start | bytes 1179656 | tf_op jit(solution)/shard_map/ppermute | solution.py:513
  80.4 16.7 %collective-permute-start.28 = (f32[2,2,12,16,128]{4,3,2,1,0:T(8,128)S(1)}, f32[2,2,12,16,128]{4,3,2,1,0:T(8,128)S(1)}, u32[]{:S(2)}, u32[]{:S(2)}) collective-permute-start(f32[2,2,12,16,128]{4,3,2,1,0:T(8,128)S(1)} %get-tuple-element.66), channel_id=1, source_target_pairs={{0,6},{1,7},{4,2},{5,3},{8,14},{9,15},{12,10},{13,11},{16,22},{17,... | collective-permute-start | bytes 1179656 | tf_op jit(solution)/shard_map/ppermute | solution.py:514
  82.5 40.1 %collective-permute-start.29 = (f32[2,2,12,16,128]{4,3,2,1,0:T(8,128)S(1)}, f32[2,2,12,16,128]{4,3,2,1,0:T(8,128)S(1)}, u32[]{:S(2)}, u32[]{:S(2)}) collective-permute-start(f32[2,2,12,16,128]{4,3,2,1,0:T(8,128)S(1)} %get-tuple-element.63.refs_0_), channel_id=1, source_target_pairs={{0,1},{1,0},{2,3},{3,2},{4,5},{5,4},{6,7},{7,6},{8,9},{9,8},{10,11... | collective-permute-start | bytes 1179656 | tf_op jit(solution)/shard_map/ppermute | solution.py:518
  89.0 33.7 %collective-permute-start.30 = (f32[2,2,12,16,128]{4,3,2,1,0:T(8,128)S(1)}, f32[2,2,12,16,128]{4,3,2,1,0:T(8,128)S(1)}, u32[]{:S(2)}, u32[]{:S(2)}) collective-permute-start(f32[2,2,12,16,128]{4,3,2,1,0:T(8,128)S(1)} %collective-permute-done.26.refs_1_), channel_id=1, source_target_pairs={{0,1},{1,0},{2,3},{3,2},{4,5},{5,4},{6,7},{7,6},{8,9},{9,8},{10,11... | collective-permute-start | bytes 1179656 | tf_op jit(solution)/shard_map/ppermute | solution.py:518
  97.1 25.5 %collective-permute-start.31 = (f32[2,2,12,16,128]{4,3,2,1,0:T(8,128)S(1)}, f32[2,2,12,16,128]{4,3,2,1,0:T(8,128)S(1)}, u32[]{:S(2)}, u32[]{:S(2)}) collective-permute-start(f32[2,2,12,16,128]{4,3,2,1,0:T(8,128)S(1)} %collective-permute-done.27.refs_2_), channel_id=1, source_target_pairs={{0,1},{1,0},{2,3},{3,2},{4,5},{5,4},{6,7},{7,6},{8,9},{9,8},{10,11... | collective-permute-start | bytes 1179656 | tf_op jit(solution)/shard_map/ppermute | solution.py:518
  97.1 25.5 %collective-permute-start.32 = (f32[2,2,12,16,128]{4,3,2,1,0:T(8,128)S(1)}, f32[2,2,12,16,128]{4,3,2,1,0:T(8,128)S(1)}, u32[]{:S(2)}, u32[]{:S(2)}) collective-permute-start(f32[2,2,12,16,128]{4,3,2,1,0:T(8,128)S(1)} %collective-permute-done.28.refs_3_), channel_id=1, source_target_pairs={{0,1},{1,0},{2,3},{3,2},{4,5},{5,4},{6,7},{7,6},{8,9},{9,8},{10,11... | collective-permute-start | bytes 1179656 | tf_op jit(solution)/shard_map/ppermute | solution.py:518
  (11 other events, 142.5 us)

commit v10 on v9

--- a/solution.py
+++ b/solution.py
@@ -511,18 +511,16 @@
             spare[0],
             lax.ppermute(spare[1], "side", swap),
             lax.ppermute(spare[2], "orb", up),
-            lax.ppermute(spare[3], ("side", "orb"), slanted_up),
         ]
+        given.append(lax.ppermute(spare[3], ("side", "orb"), slanted_up))
         block_near = lax.ppermute(block, "orb", cores)
         table_shape = jax.ShapeDtypeStruct((total, LANES), jnp.float32)
-        given += [lax.ppermute(piece, "orb", cores) for piece in given]
-        table, message = pl.pallas_call(
-            functools.partial(table_kernel, cell_total),
-            out_shape=[table_shape, message_shape],
-            in_specs=[VMEM] * 2,
-            out_specs=[VMEM] * 2,
-            compiler_params=pltpu.CompilerParams(vmem_limit_bytes=24 * 1024 * 1024),
-        )(exchanged(message), block)
+        near = [lax.ppermute(piece, "orb", cores) for piece in given[:-1]]
+        given = given + near + [lax.ppermute(given[-1], "orb", cores)]
+        copies = exchanged(message)
+        table, message = small_call(
+            functools.partial(table_kernel, cell_total), [table_shape, message_shape], [VMEM] * 2, copies, block
+        )
         return pl.pallas_call(
             functools.partial(last_kernel, cell_total),
             out_shape=jax.ShapeDtypeStruct((held, rows, cols, width), jnp.float32),

time: 129 us -> 129 us (level)
    pallas_call x1 -> x2, Pallas kernels: 2.13 us -> 5.47 us  [small_call(): pl.pallas_call(kernel, out_shape=out_shape, in_specs=specs, out_specs=jax...]
    pallas_call x1 -> x0, Pallas kernels: 3.34 us -> none  [whole(): pl.pallas_call(functools.partial(table_kernel, cell_total), out_shape=[ta...]
where the time goes in v10:
time: 129 us; the launch traced here: 128 us
  waiting for transfers between devices  47 us (36%)
  starting transfers between devices  35.7 us (28%)
  Pallas kernels  23.7 us (18%)
  blocking collectives  21.7 us (17%)
    all_to_all x2, blocking collectives, exchanged(): return lax.all_to_all(message, ALL, 0, 0)  21.7 us
    ppermute x13, starting transfers between devices, to_partner(): lax.ppermute(piece, ('side', 'orb'), [(flat_of(i), flat_of(i ^ m)) for i...  11.7 us
    pallas_call x2, Pallas kernels, filtered_pieces(): pl.pallas_call(functools.partial(filter_kernel, at, len(pot_far), early,...  10.4 us
    ppermute x3, waiting for transfers between devices, whole(): lax.ppermute(joined, 'orb', [(i, i ^ m) for i in range(orb_count)])  9.47 us
    ppermute x1, waiting for transfers between devices, whole(): lax.ppermute(spare[2], 'orb', up)  8.13 us
    ppermute x2, waiting for transfers between devices, whole(): lax.ppermute(sent[3 * at + 2], slab_axes, ahead)  7.66 us
    ppermute x1, waiting for transfers between devices, whole(): lax.ppermute(spare[1], 'side', swap)  6.4 us
    ppermute x13, waiting for transfers between devices, to_partner(): lax.ppermute(piece, ('side', 'orb'), [(flat_of(i), flat_of(i ^ m)) for i...  6.32 us
  transfers between devices with their start and end apart: 33, of which 14 were waited for; matrix products, arithmetic and copies ran while one was open for 0% of the time, Pallas kernels for 11%

profile of v10, /device:TPU:0, one launch (start us, length us, event | category | flops | bytes accessed | tf_op | source)
XLA Modules:
  0.0 128.4 jit_solution(18354129063151230250)
XLA Ops:
  0.1 2.2 %shard_map.28 = (f32[12,16,128]{2,1,0:T(8,128)S(1)}, f32[6,16,128]{2,1,0:T(8,128)S(1)}, f32[9,64,128]{2,1,0:T(8,128)S(1)}, f32[12,64,128]{2,1,0:T(8,128)S(1)}, f...) custom-call(s32[3]{0:T(128)S(1)} %pad_add_fusion.place, ...), custom_call_target="tpu_custom_call" | custom-call | tf_op jit(solution)/shard_map/pallas_call | solution.py:61
  2.3 3.1 %collective-permute-start.3 = (f32[12,16,128]{2,1,0:T(8,128)S(1)}, f32[12,16,128]{2,1,0:T(8,128)S(1)}, u32[]{:S(2)}, u32[]{:S(2)}) collective-permute-start(f32[12,16,128]{2,1,0:T(8,128)S(1)} %get-tuple-element.39), channel_id=1, source_target_pairs={{0,4},{4,0},{1,5},{5,1},{2,6},{6,2},{3,7},{7,3},{8,12},{12,8},{9,1... | collective-permute-start | bytes 294920 | tf_op jit(solution)/shard_map/ppermute | solution.py:438
  5.4 3.5 %collective-permute-start.1 = (f32[9,64,128]{2,1,0:T(8,128)S(1)}, f32[9,64,128]{2,1,0:T(8,128)S(1)}, u32[]{:S(2)}, u32[]{:S(2)}) collective-permute-start(f32[9,64,128]{2,1,0:T(8,128)S(1)} %get-tuple-element.37), channel_id=1, source_target_pairs={{0,28},{4,8},{8,4},{12,16},{16,12},{20,24},{24,20},{28,0},{1,29},{... | collective-permute-start | bytes 884744 | tf_op jit(solution)/shard_map/ppermute | solution.py:457
  9.3 2.4 %collective-permute-start.4 = (f32[6,16,128]{2,1,0:T(8,128)S(1)}, f32[6,16,128]{2,1,0:T(8,128)S(1)}, u32[]{:S(2)}, u32[]{:S(2)}) collective-permute-start(f32[6,16,128]{2,1,0:T(8,128)S(1)} %get-tuple-element.40), channel_id=1, source_target_pairs={{0,28},{4,8},{8,4},{12,16},{16,12},{20,24},{24,20},{28,0},{1,29},{... | collective-permute-start | bytes 147464 | tf_op jit(solution)/shard_map/ppermute | solution.py:439
  11.7 4.7 %collective-permute-done.5.straight = f32[6,16,128]{2,1,0:T(8,128)S(1)} collective-permute-done((f32[6,16,128]{2,1,0:T(8,128)S(1)}, f32[6,16,128]{2,1,0:T(8,128)S(1)}, u32[]{:S(2)}, u32[]{:S(2)}) %collective-permute-start.5) | collective-permute-done | bytes 49184 | tf_op jit(solution)/shard_map/ppermute | solution.py:440
  16.4 2.2 %collective-permute-done.4.slanted = f32[6,16,128]{2,1,0:T(8,128)S(1)} collective-permute-done((f32[6,16,128]{2,1,0:T(8,128)S(1)}, f32[6,16,128]{2,1,0:T(8,128)S(1)}, u32[]{:S(2)}, u32[]{:S(2)}) %collective-permute-start.4) | collective-permute-done | bytes 49184 | tf_op jit(solution)/shard_map/ppermute | solution.py:439
  20.6 5.2 %collective-permute-done.8.rest_3_ = f32[24,16,128]{2,1,0:T(8,128)S(1)} collective-permute-done((f32[24,16,128]{2,1,0:T(8,128)S(1)}, f32[24,16,128]{2,1,0:T(8,128)S(1)}, u32[]{:S(2)}, u32[]{:S(2)}) %collective-permute-start.8) | collective-permute-done | bytes 196640 | tf_op jit(solution)/shard_map/ppermute | solution.py:450
  25.9 4.2 %collective-permute-done.7.rest_2_ = f32[24,16,128]{2,1,0:T(8,128)S(1)} collective-permute-done((f32[24,16,128]{2,1,0:T(8,128)S(1)}, f32[24,16,128]{2,1,0:T(8,128)S(1)}, u32[]{:S(2)}, u32[]{:S(2)}) %collective-permute-start.7) | collective-permute-done | bytes 196640 | tf_op jit(solution)/shard_map/ppermute | solution.py:450
  30.1 2.1 %collective-permute-start.2 = (f32[9,64,128]{2,1,0:T(8,128)S(1)}, f32[9,64,128]{2,1,0:T(8,128)S(1)}, u32[]{:S(2)}, u32[]{:S(2)}) collective-permute-start(f32[9,64,128]{2,1,0:T(8,128)S(1)} %get-tuple-element.38), channel_id=1, source_target_pairs={{0,24},{4,12},{8,0},{12,20},{16,8},{20,28},{24,16},{28,4},{1,25},{... | collective-permute-start | bytes 884744 | tf_op jit(solution)/shard_map/ppermute | solution.py:459
  35.8 4.2 %collective-permute-done.2.straight = f32[9,64,128]{2,1,0:T(8,128)S(1)} collective-permute-done((f32[9,64,128]{2,1,0:T(8,128)S(1)}, f32[9,64,128]{2,1,0:T(8,128)S(1)}, u32[]{:S(2)}, u32[]{:S(2)}) %collective-permute-start.2) | collective-permute-done | bytes 294944 | tf_op jit(solution)/shard_map/ppermute | solution.py:459
  40.0 4.7 %shard_map.30 = (f32[12,16,128]{2,1,0:T(8,128)S(1)}, f32[12,16,128]{2,1,0:T(8,128)S(1)}, f32[12,16,128]{2,1,0:T(8,128)S(1)}, f32[12,16,128]{2,1,0:T(8,128)S(1)},...) custom-call(s32[3]{0:T(128)S(1)} %pad_add_fusion.place, ...), custom_call_target="tpu_custom_call" | custom-call | tf_op jit(solution)/shard_map/pallas_call | solution.py:200
  45.8 2.0 %collective-permute-done.16.slanted = f32[9,64,128]{2,1,0:T(8,128)S(1)} collective-permute-done((f32[9,64,128]{2,1,0:T(8,128)S(1)}, f32[9,64,128]{2,1,0:T(8,128)S(1)}, u32[]{:S(2)}, u32[]{:S(2)}) %collective-permute-start.16) | collective-permute-done | bytes 294944 | tf_op jit(solution)/shard_map/ppermute | solution.py:457
  48.3 3.4 %collective-permute-done.17.straight = f32[9,64,128]{2,1,0:T(8,128)S(1)} collective-permute-done((f32[9,64,128]{2,1,0:T(8,128)S(1)}, f32[9,64,128]{2,1,0:T(8,128)S(1)}, u32[]{:S(2)}, u32[]{:S(2)}) %collective-permute-start.17) | collective-permute-done | bytes 294944 | tf_op jit(solution)/shard_map/ppermute | solution.py:459
  54.1 5.7 %shard_map.31 = (f32[12,16,128]{2,1,0:T(8,128)S(1)}, f32[12,16,128]{2,1,0:T(8,128)S(1)}, f32[12,16,128]{2,1,0:T(8,128)S(1)}, f32[12,16,128]{2,1,0:T(8,128)S(1)},...) custom-call(s32[3]{0:T(128)S(1)} %pad_add_fusion.place, ...), custom_call_target="tpu_custom_call" | custom-call | tf_op jit(solution)/shard_map/pallas_call | solution.py:200
  59.8 2.9 %collective-permute-start.18 = (f32[12,16,128]{2,1,0:T(8,128)S(1)}, f32[12,16,128]{2,1,0:T(8,128)S(1)}, u32[]{:S(2)}, u32[]{:S(2)}) collective-permute-start(f32[12,16,128]{2,1,0:T(8,128)S(1)} %get-tuple-element.51), channel_id=1, source_target_pairs={{0,6},{4,2},{1,7},{5,3},{2,4},{6,0},{3,5},{7,1},{8,14},{12,10},{9,... | collective-permute-start | bytes 294920 | tf_op jit(solution)/shard_map/ppermute | solution.py:470
  73.9 2.1 %shard_map.32 = (f32[16,192,128]{2,1,0:T(8,128)S(1)}, f32[32,1,256]{2,1,0:T(1,128)S(1)}) custom-call(s32[3]{0:T(128)S(1)} %pad_add_fusion.place, f32[12,16,128]{2,1,0:T(8,128)S(1)} %collective-permute-done.9.refs_0_, f32[12,16,128]{2,1,0:T(8,128)S(1)} %collective-permute-done.10.refs_1_, f32[12,16,128]{2,1,0:T(8,128)S(1)} %collective-permute-done.11.refs_2_, ...), custom_call_target="tpu_custom_call" | custom-call | tf_op jit(solution)/shard_map/pallas_call | solution.py:406
  77.8 2.6 %collective-permute-start.27 = (f32[2,2,12,16,128]{4,3,2,1,0:T(8,128)S(1)}, f32[2,2,12,16,128]{4,3,2,1,0:T(8,128)S(1)}, u32[]{:S(2)}, u32[]{:S(2)}) collective-permute-start(f32[2,2,12,16,128]{4,3,2,1,0:T(8,128)S(1)} %get-tuple-element.65), channel_id=1, source_target_pairs={{0,2},{1,3},{4,6},{5,7},{8,10},{9,11},{12,14},{13,15},{16,18},{17,... | collective-permute-start | bytes 1179656 | tf_op jit(solution)/shard_map/ppermute | solution.py:513
  80.4 2.1 %collective-permute-start.28 = (f32[2,2,12,16,128]{4,3,2,1,0:T(8,128)S(1)}, f32[2,2,12,16,128]{4,3,2,1,0:T(8,128)S(1)}, u32[]{:S(2)}, u32[]{:S(2)}) collective-permute-start(f32[2,2,12,16,128]{4,3,2,1,0:T(8,128)S(1)} %get-tuple-element.66), channel_id=1, source_target_pairs={{0,6},{1,7},{4,2},{5,3},{8,14},{9,15},{12,10},{13,11},{16,22},{17,... | collective-permute-start | bytes 1179656 | tf_op jit(solution)/shard_map/ppermute | solution.py:515
  82.6 6.4 %collective-permute-done.26.refs_1_ = f32[2,2,12,16,128]{4,3,2,1,0:T(8,128)S(1)} collective-permute-done((f32[2,2,12,16,128]{4,3,2,1,0:T(8,128)S(1)}, f32[2,2,12,16,128]{4,3,2,1,0:T(8,128)S(1)}, u32[]{:S(2)}, u32[]{:S(2)}) %collective-permute-start.26) | collective-permute-done | bytes 393248 | tf_op jit(solution)/shard_map/ppermute | solution.py:512
  89.0 8.1 %collective-permute-done.27.refs_2_ = f32[2,2,12,16,128]{4,3,2,1,0:T(8,128)S(1)} collective-permute-done((f32[2,2,12,16,128]{4,3,2,1,0:T(8,128)S(1)}, f32[2,2,12,16,128]{4,3,2,1,0:T(8,128)S(1)}, u32[]{:S(2)}, u32[]{:S(2)}) %collective-permute-start.27) | collective-permute-done | bytes 393248 | tf_op jit(solution)/shard_map/ppermute | solution.py:513
  97.6 12.7 %all_to_all.10.copies = f32[32,1,256]{2,1,0:T(1,128)S(1)} all-to-all(f32[32,1,256]{2,1,0:T(1,128)S(1)} %get-tuple-element.59), channel_id=1, replica_groups=mesh['pair'=4,'side'=2,'orb'=4] {'pair','side','orb'}, dimensions={0} | all-to-all | bytes 65536 | tf_op jit(solution)/shard_map/all_to_all | solution.py:498
  110.3 3.3 %shard_map.33 = (f32[16,128]{1,0:T(8,128)S(1)}, f32[32,1,256]{2,1,0:T(1,128)S(1)}) custom-call(f32[32,1,256]{2,1,0:T(1,128)S(1)} %all_to_all.10.copies, f32[16,192,128]{2,1,0:T(8,128)S(1)} %get-tuple-element.60.block), custom_call_target="tpu_custom_call" | custom-call | tf_op jit(solution)/shard_map/pallas_call | solution.py:406
  113.7 9.0 %all_to_all.11.copies = f32[32,1,256]{2,1,0:T(1,128)S(1)} all-to-all(f32[32,1,256]{2,1,0:T(1,128)S(1)} %get-tuple-element.61), channel_id=1, replica_groups=mesh['pair'=4,'side'=2,'orb'=4] {'pair','side','orb'}, dimensions={0} | all-to-all | bytes 65536 | tf_op jit(solution)/shard_map/all_to_all | solution.py:498
  122.6 5.7 %shard_map.34 = f32[4,12,64,128]{3,2,1,0:T(8,128)} custom-call(s32[3]{0:T(128)S(1)} %pad_add_fusion.place, f32[32,1,256]{2,1,0:T(1,128)S(1)} %all_to_all.11.copies, f32[16,128]{1,0:T(8,128)S(1)} %get-tuple-element.62.table, f32[16,192,128]{2,1,0:T(8,128)S(1)} %get-tuple-element.60.block, f32[16,192,128]{2,1,0:T(8,128)S(1)} %collective-permute-done.25.block_near, ...), custom_call_target="tpu_custom_call" | custom-call | tf_op jit(solution)/shard_map/pallas_call | solution.py:524
  (57 shorter events, 23.6 us)
Async XLA Ops:
  2.3 16.3 %collective-permute-start.3 = (f32[12,16,128]{2,1,0:T(8,128)S(1)}, f32[12,16,128]{2,1,0:T(8,128)S(1)}, u32[]{:S(2)}, u32[]{:S(2)}) collective-permute-start(f32[12,16,128]{2,1,0:T(8,128)S(1)} %get-tuple-element.39), channel_id=1, source_target_pairs={{0,4},{4,0},{1,5},{5,1},{2,6},{6,2},{3,7},{7,3},{8,12},{12,8},{9,1... | collective-permute-start | bytes 294920 | tf_op jit(solution)/shard_map/ppermute | solution.py:438
  5.4 28.3 %collective-permute-start.1 = (f32[9,64,128]{2,1,0:T(8,128)S(1)}, f32[9,64,128]{2,1,0:T(8,128)S(1)}, u32[]{:S(2)}, u32[]{:S(2)}) collective-permute-start(f32[9,64,128]{2,1,0:T(8,128)S(1)} %get-tuple-element.37), channel_id=1, source_target_pairs={{0,28},{4,8},{8,4},{12,16},{16,12},{20,24},{24,20},{28,0},{1,29},{... | collective-permute-start | bytes 884744 | tf_op jit(solution)/shard_map/ppermute | solution.py:457
  9.3 9.3 %collective-permute-start.4 = (f32[6,16,128]{2,1,0:T(8,128)S(1)}, f32[6,16,128]{2,1,0:T(8,128)S(1)}, u32[]{:S(2)}, u32[]{:S(2)}) collective-permute-start(f32[6,16,128]{2,1,0:T(8,128)S(1)} %get-tuple-element.40), channel_id=1, source_target_pairs={{0,28},{4,8},{8,4},{12,16},{16,12},{20,24},{24,20},{28,0},{1,29},{... | collective-permute-start | bytes 147464 | tf_op jit(solution)/shard_map/ppermute | solution.py:439
  18.7 11.4 %collective-permute-start.7 = (f32[24,16,128]{2,1,0:T(8,128)S(1)}, f32[24,16,128]{2,1,0:T(8,128)S(1)}, u32[]{:S(2)}, u32[]{:S(2)}) collective-permute-start(f32[24,16,128]{2,1,0:T(8,128)S(1)} %shard_map.29.rest_0_), channel_id=1, source_target_pairs={{0,2},{1,3},{2,0},{3,1},{4,6},{5,7},{6,4},{7,5},{8,10},{9,11},{10,... | collective-permute-start | bytes 589832 | tf_op jit(solution)/shard_map/ppermute | solution.py:450
  20.3 11.9 %collective-permute-start.6 = (f32[24,16,128]{2,1,0:T(8,128)S(1)}, f32[24,16,128]{2,1,0:T(8,128)S(1)}, u32[]{:S(2)}, u32[]{:S(2)}) collective-permute-start(f32[24,16,128]{2,1,0:T(8,128)S(1)} %shard_map.29.rest_0_), channel_id=1, source_target_pairs={{0,1},{1,0},{2,3},{3,2},{4,5},{5,4},{6,7},{7,6},{8,9},{9,8},{10,11... | collective-permute-start | bytes 589832 | tf_op jit(solution)/shard_map/ppermute | solution.py:450
  20.5 19.4 %collective-permute-start = (f32[12,64,128]{2,1,0:T(8,128)S(1)}, f32[12,64,128]{2,1,0:T(8,128)S(1)}, u32[]{:S(2)}, u32[]{:S(2)}) collective-permute-start(f32[12,64,128]{2,1,0:T(8,128)S(1)} %get-tuple-element.36), channel_id=1, source_target_pairs={{0,4},{4,0},{1,5},{5,1},{2,6},{6,2},{3,7},{7,3},{8,12},{12,8},{9,1... | collective-permute-start | bytes 1179656 | tf_op jit(solution)/shard_map/ppermute | solution.py:458
  25.8 26.2 %collective-permute-start.15 = (f32[12,64,128]{2,1,0:T(8,128)S(1)}, f32[12,64,128]{2,1,0:T(8,128)S(1)}, u32[]{:S(2)}, u32[]{:S(2)}) collective-permute-start(f32[12,64,128]{2,1,0:T(8,128)S(1)} %get-tuple-element.47), channel_id=1, source_target_pairs={{0,4},{4,0},{1,5},{5,1},{2,6},{6,2},{3,7},{7,3},{8,12},{12,8},{9,1... | collective-permute-start | bytes 1179656 | tf_op jit(solution)/shard_map/ppermute | solution.py:458
  30.1 9.9 %collective-permute-start.2 = (f32[9,64,128]{2,1,0:T(8,128)S(1)}, f32[9,64,128]{2,1,0:T(8,128)S(1)}, u32[]{:S(2)}, u32[]{:S(2)}) collective-permute-start(f32[9,64,128]{2,1,0:T(8,128)S(1)} %get-tuple-element.38), channel_id=1, source_target_pairs={{0,24},{4,12},{8,0},{12,20},{16,8},{20,28},{24,16},{28,4},{1,25},{... | collective-permute-start | bytes 884744 | tf_op jit(solution)/shard_map/ppermute | solution.py:459
  32.2 15.6 %collective-permute-start.16 = (f32[9,64,128]{2,1,0:T(8,128)S(1)}, f32[9,64,128]{2,1,0:T(8,128)S(1)}, u32[]{:S(2)}, u32[]{:S(2)}) collective-permute-start(f32[9,64,128]{2,1,0:T(8,128)S(1)} %get-tuple-element.48), channel_id=1, source_target_pairs={{0,28},{4,8},{8,4},{12,16},{16,12},{20,24},{24,20},{28,0},{1,29},{... | collective-permute-start | bytes 884744 | tf_op jit(solution)/shard_map/ppermute | solution.py:457
  33.6 18.1 %collective-permute-start.17 = (f32[9,64,128]{2,1,0:T(8,128)S(1)}, f32[9,64,128]{2,1,0:T(8,128)S(1)}, u32[]{:S(2)}, u32[]{:S(2)}) collective-permute-start(f32[9,64,128]{2,1,0:T(8,128)S(1)} %get-tuple-element.49), channel_id=1, source_target_pairs={{0,24},{4,12},{8,0},{12,20},{16,8},{20,28},{24,16},{28,4},{1,25},{... | collective-permute-start | bytes 884744 | tf_op jit(solution)/shard_map/ppermute | solution.py:459
  44.7 15.1 %collective-permute-start.9 = (f32[12,16,128]{2,1,0:T(8,128)S(1)}, f32[12,16,128]{2,1,0:T(8,128)S(1)}, u32[]{:S(2)}, u32[]{:S(2)}) collective-permute-start(f32[12,16,128]{2,1,0:T(8,128)S(1)} %get-tuple-element.41), channel_id=1, source_target_pairs={{0,6},{4,2},{1,7},{5,3},{2,4},{6,0},{3,5},{7,1},{8,14},{12,10},{9,... | collective-permute-start | bytes 294920 | tf_op jit(solution)/shard_map/ppermute | solution.py:470
  45.5 14.2 %collective-permute-start.10 = (f32[12,16,128]{2,1,0:T(8,128)S(1)}, f32[12,16,128]{2,1,0:T(8,128)S(1)}, u32[]{:S(2)}, u32[]{:S(2)}) collective-permute-start(f32[12,16,128]{2,1,0:T(8,128)S(1)} %get-tuple-element.42), channel_id=1, source_target_pairs={{0,7},{4,3},{1,6},{5,2},{2,5},{6,1},{3,4},{7,0},{8,15},{12,11},{9,... | collective-permute-start | bytes 294920 | tf_op jit(solution)/shard_map/ppermute | solution.py:470
  47.8 14.9 %collective-permute-start.11 = (f32[12,16,128]{2,1,0:T(8,128)S(1)}, f32[12,16,128]{2,1,0:T(8,128)S(1)}, u32[]{:S(2)}, u32[]{:S(2)}) collective-permute-start(f32[12,16,128]{2,1,0:T(8,128)S(1)} %get-tuple-element.43), channel_id=1, source_target_pairs={{0,2},{4,6},{1,3},{5,7},{2,0},{6,4},{3,1},{7,5},{8,10},{12,14},{9,... | collective-permute-start | bytes 294920 | tf_op jit(solution)/shard_map/ppermute | solution.py:470
  51.7 11.0 %collective-permute-start.12 = (f32[12,16,128]{2,1,0:T(8,128)S(1)}, f32[12,16,128]{2,1,0:T(8,128)S(1)}, u32[]{:S(2)}, u32[]{:S(2)}) collective-permute-start(f32[12,16,128]{2,1,0:T(8,128)S(1)} %get-tuple-element.44), channel_id=1, source_target_pairs={{0,3},{4,7},{1,2},{5,6},{2,1},{6,5},{3,0},{7,4},{8,11},{12,15},{9,... | collective-permute-start | bytes 294920 | tf_op jit(solution)/shard_map/ppermute | solution.py:470
  52.1 10.8 %collective-permute-start.13 = (f32[12,16,128]{2,1,0:T(8,128)S(1)}, f32[12,16,128]{2,1,0:T(8,128)S(1)}, u32[]{:S(2)}, u32[]{:S(2)}) collective-permute-start(f32[12,16,128]{2,1,0:T(8,128)S(1)} %get-tuple-element.45), channel_id=1, source_target_pairs={{0,4},{4,0},{1,5},{5,1},{2,6},{6,2},{3,7},{7,3},{8,12},{12,8},{9,1... | collective-permute-start | bytes 294920 | tf_op jit(solution)/shard_map/ppermute | solution.py:470
  62.7 11.2 %collective-permute-start.24 = (f32[2,12,16,128]{3,2,1,0:T(8,128)S(1)}, f32[2,12,16,128]{3,2,1,0:T(8,128)S(1)}, u32[]{:S(2)}, u32[]{:S(2)}) collective-permute-start(f32[2,12,16,128]{3,2,1,0:T(8,128)S(1)} %get-tuple-element.58), channel_id=1, source_target_pairs={{0,1},{4,5},{1,0},{5,4},{2,3},{6,7},{3,2},{7,6},{8,9},{12,13},{9,8... | collective-permute-start | bytes 589832 | tf_op jit(solution)/shard_map/ppermute | solution.py:470
  76.0 46.6 %collective-permute-start.25 = (f32[16,192,128]{2,1,0:T(8,128)S(1)}, f32[16,192,128]{2,1,0:T(8,128)S(1)}, u32[]{:S(2)}, u32[]{:S(2)}) collective-permute-start(f32[16,192,128]{2,1,0:T(8,128)S(1)} %get-tuple-element.60.block), channel_id=1, source_target_pairs={{0,1},{1,0},{2,3},{3,2},{4,5},{5,4},{6,7},{7,6},{8,9},{9,8},{10,11... | collective-permute-start | bytes 4718600 | tf_op jit(solution)/shard_map/ppermute | solution.py:516
  77.0 12.0 %collective-permute-start.26 = (f32[2,2,12,16,128]{4,3,2,1,0:T(8,128)S(1)}, f32[2,2,12,16,128]{4,3,2,1,0:T(8,128)S(1)}, u32[]{:S(2)}, u32[]{:S(2)}) collective-permute-start(f32[2,2,12,16,128]{4,3,2,1,0:T(8,128)S(1)} %get-tuple-element.64), channel_id=1, source_target_pairs={{0,4},{4,0},{1,5},{5,1},{2,6},{6,2},{3,7},{7,3},{8,12},{12,8},{9,1... | collective-permute-start | bytes 1179656 | tf_op jit(solution)/shard_map/ppermute | solution.py:512
  77.8 19.3 %collective-permute-start.27 = (f32[2,2,12,16,128]{4,3,2,1,0:T(8,128)S(1)}, f32[2,2,12,16,128]{4,3,2,1,0:T(8,128)S(1)}, u32[]{:S(2)}, u32[]{:S(2)}) collective-permute-start(f32[2,2,12,16,128]{4,3,2,1,0:T(8,128)S(1)} %get-tuple-element.65), channel_id=1, source_target_pairs={{0,2},{1,3},{4,6},{5,7},{8,10},{9,11},{12,14},{13,15},{16,18},{17,... | collective-permute-start | bytes 1179656 | tf_op jit(solution)/shard_map/ppermute | solution.py:513
  80.4 16.7 %collective-permute-start.28 = (f32[2,2,12,16,128]{4,3,2,1,0:T(8,128)S(1)}, f32[2,2,12,16,128]{4,3,2,1,0:T(8,128)S(1)}, u32[]{:S(2)}, u32[]{:S(2)}) collective-permute-start(f32[2,2,12,16,128]{4,3,2,1,0:T(8,128)S(1)} %get-tuple-element.66), channel_id=1, source_target_pairs={{0,6},{1,7},{4,2},{5,3},{8,14},{9,15},{12,10},{13,11},{16,22},{17,... | collective-permute-start | bytes 1179656 | tf_op jit(solution)/shard_map/ppermute | solution.py:515
  82.5 40.1 %collective-permute-start.29 = (f32[2,2,12,16,128]{4,3,2,1,0:T(8,128)S(1)}, f32[2,2,12,16,128]{4,3,2,1,0:T(8,128)S(1)}, u32[]{:S(2)}, u32[]{:S(2)}) collective-permute-start(f32[2,2,12,16,128]{4,3,2,1,0:T(8,128)S(1)} %get-tuple-element.63.refs_0_), channel_id=1, source_target_pairs={{0,1},{1,0},{2,3},{3,2},{4,5},{5,4},{6,7},{7,6},{8,9},{9,8},{10,11... | collective-permute-start | bytes 1179656 | tf_op jit(solution)/shard_map/ppermute | solution.py:518
  89.0 33.7 %collective-permute-start.30 = (f32[2,2,12,16,128]{4,3,2,1,0:T(8,128)S(1)}, f32[2,2,12,16,128]{4,3,2,1,0:T(8,128)S(1)}, u32[]{:S(2)}, u32[]{:S(2)}) collective-permute-start(f32[2,2,12,16,128]{4,3,2,1,0:T(8,128)S(1)} %collective-permute-done.26.refs_1_), channel_id=1, source_target_pairs={{0,1},{1,0},{2,3},{3,2},{4,5},{5,4},{6,7},{7,6},{8,9},{9,8},{10,11... | collective-permute-start | bytes 1179656 | tf_op jit(solution)/shard_map/ppermute | solution.py:518
  97.1 25.5 %collective-permute-start.31 = (f32[2,2,12,16,128]{4,3,2,1,0:T(8,128)S(1)}, f32[2,2,12,16,128]{4,3,2,1,0:T(8,128)S(1)}, u32[]{:S(2)}, u32[]{:S(2)}) collective-permute-start(f32[2,2,12,16,128]{4,3,2,1,0:T(8,128)S(1)} %collective-permute-done.27.refs_2_), channel_id=1, source_target_pairs={{0,1},{1,0},{2,3},{3,2},{4,5},{5,4},{6,7},{7,6},{8,9},{9,8},{10,11... | collective-permute-start | bytes 1179656 | tf_op jit(solution)/shard_map/ppermute | solution.py:518
  97.1 25.5 %collective-permute-start.32 = (f32[2,2,12,16,128]{4,3,2,1,0:T(8,128)S(1)}, f32[2,2,12,16,128]{4,3,2,1,0:T(8,128)S(1)}, u32[]{:S(2)}, u32[]{:S(2)}) collective-permute-start(f32[2,2,12,16,128]{4,3,2,1,0:T(8,128)S(1)} %collective-permute-done.28.refs_3_), channel_id=1, source_target_pairs={{0,1},{1,0},{2,3},{3,2},{4,5},{5,4},{6,7},{7,6},{8,9},{9,8},{10,11... | collective-permute-start | bytes 1179656 | tf_op jit(solution)/shard_map/ppermute | solution.py:519
  (11 other events, 142.5 us)

commit v11 on v9

--- a/solution.py
+++ b/solution.py
@@ -341,20 +341,28 @@
     put(applied(inverse_factor(copies, block.shape[0], cell_total), block), basis)
 
 
-def table_kernel(cell_total, copies, block, table_out, message):
+def table_kernel(cell_total, copies, block, table_out, message_far, message, sem):
     total = block.shape[0]
     table = inverse_factor(copies, total, cell_total)
     table_out[...] = table
     message[...] = jnp.broadcast_to(gram_message(applied(table, block), total)[None], message.shape)
+    leave = pltpu.make_async_copy(message, message_far, sem)
+    leave.start()
+    leave.wait()
 
 
 def last_kernel(cell_total, place, copies, table, block, block_near, *refs):
-    spares, (out, splats) = refs[:-2], refs[-2:]
+    count = (len(refs) - 5) // 2
+    far, (out_far, splats, out), spares = refs[:count], refs[count : count + 3], refs[count + 3 : 2 * count + 3]
+    sems, sems_out = refs[2 * count + 3 :]
     total, length, width = block.shape
     held, rows = out.shape[:2]
     part = length // rows
     side, orb = place[0], place[2]
-    core, chip = orb % CORES, orb // CORES
+    chip = orb // CORES
+    fetches = [pltpu.make_async_copy(a, b, sems.at[i]) for i, (a, b) in enumerate(zip(far, spares))]
+    for fetch in fetches:
+        fetch.start()
     second = inverse_factor(copies, total, cell_total)
     pick = table_of((LANES, total), lambda r, c: r - total == c)
     product = exact_dot(exact_dot(second, pick), exact_dot(table[...], pick))
@@ -387,6 +395,14 @@
     write([(j, at(block, j)) for j in range(total)], orb * part)
     write([(j, at(block_near, j)) for j in range(total)], (orb ^ 1) * part)
 
+    def leave(which, index):
+        columns = pl.ds(pl.multiple_of(which * CORES * part, EIGHT), CORES * part)
+        return pltpu.make_async_copy(out.at[:, :, columns], out_far.at[:, :, columns], sems_out.at[index])
+
+    leave(chip, 0).start()
+    for fetch in fetches:
+        fetch.wait()
+
     def spare_at(ref, stage, share):
         return lambda row, strip: ref[stage, share, row, pl.ds(strip * EIGHT, EIGHT), :]
 
@@ -395,11 +411,14 @@
         sources = []
         for index, ref in enumerate(spares):
             flip, kind = index // kinds, index % kinds
-            quad = (core if kind // 2 else orb) ^ flip
+            quad = (orb ^ CORES if kind // 2 else orb) ^ flip
             for stage in range(ref.shape[0]):
                 orbital = quad * held + (side ^ (kind % 2)) * ref.shape[0] + stage
                 sources.append((orbital, spare_at(ref, stage, share)))
         write(sources, ((1 - chip) * CORES + share) * part)
+    leave(1 - chip, 1).start()
+    leave(chip, 0).wait()
+    leave(1 - chip, 1).wait()
 
 
 def small_call(kernel, out_shape, specs, *args):
@@ -504,31 +523,40 @@
         *(place, *parts),
     )
     if spares:
-        up = [(i, i + CORES) for i in range(CORES)]
-        slanted_up = [(s * orb_count + i, (1 - s) * orb_count + i + CORES) for s in range(2) for i in range(CORES)]
+        across = [(i, i ^ CORES) for i in range(orb_count)]
+        slanted_across = [(t * orb_count + i, (1 - t) * orb_count + (i ^ CORES)) for t in range(2) for i in range(orb_count)]
         cores = [(i, i ^ 1) for i in range(orb_count)]
         given = [
             spare[0],
             lax.ppermute(spare[1], "side", swap),
-            lax.ppermute(spare[2], "orb", up),
-            lax.ppermute(spare[3], ("side", "orb"), slanted_up),
+            lax.ppermute(spare[2], "orb", across),
         ]
+        given.append(lax.ppermute(spare[3], ("side", "orb"), slanted_across))
         block_near = lax.ppermute(block, "orb", cores)
         table_shape = jax.ShapeDtypeStruct((total, LANES), jnp.float32)
-        given += [lax.ppermute(piece, "orb", cores) for piece in given]
+        near = [lax.ppermute(piece, "orb", cores) for piece in given[:-1]]
+        given = given + near + [lax.ppermute(given[-1], "orb", cores)]
+        copies = exchanged(message)
         table, message = pl.pallas_call(
             functools.partial(table_kernel, cell_total),
             out_shape=[table_shape, message_shape],
             in_specs=[VMEM] * 2,
-            out_specs=[VMEM] * 2,
+            out_specs=[VMEM, HBM],
+            scratch_shapes=[pltpu.VMEM(message_shape.shape, jnp.float32), pltpu.SemaphoreType.DMA],
             compiler_params=pltpu.CompilerParams(vmem_limit_bytes=24 * 1024 * 1024),
-        )(exchanged(message), block)
+        )(copies, block)
         return pl.pallas_call(
             functools.partial(last_kernel, cell_total),
             out_shape=jax.ShapeDtypeStruct((held, rows, cols, width), jnp.float32),
-            in_specs=[SMEM] + [VMEM] * (4 + len(given)),
-            out_specs=VMEM,
-            scratch_shapes=[pltpu.VMEM((total, held, EIGHT, width), jnp.float32)],
+            in_specs=[SMEM] + [VMEM] * 4 + [HBM] * len(given),
+            out_specs=HBM,
+            scratch_shapes=[
+                pltpu.VMEM((total, held, EIGHT, width), jnp.float32),
+                pltpu.VMEM((held, rows, cols, width), jnp.float32),
+                *(pltpu.VMEM(piece.shape, jnp.float32) for piece in given),
+                pltpu.SemaphoreType.DMA((len(given),)),
+                pltpu.SemaphoreType.DMA((2,)),
+            ],
             compiler_params=pltpu.CompilerParams(vmem_limit_bytes=24 * 1024 * 1024),
         )(place, exchanged(message), table, block, block_near, *given)
     basis, message = small_call(

time: 129 us -> 128 us (level)
  waiting for transfers between devices: 47 us -> 49.4 us
  blocking collectives: 21.7 us -> 19.5 us
  starting transfers between devices: 35.7 us -> 33.6 us
    all_to_all x2, blocking collectives: 21.7 us -> 19.5 us  [exchanged(): return lax.all_to_all(message, ALL, 0, 0)]
    ppermute x1, waiting for transfers between devices: 6.4 us -> 8.49 us  [whole(): lax.ppermute(spare[1], 'side', swap)]
    ppermute x6, starting transfers between devices: 5.25 us -> 3.17 us  [the longest x1 2.01 us: whole(): given.append(lax.ppermute(spare[3], ('side', 'orb'), slanted_across))]
where the time goes in v11:
time: 128 us
  waiting for transfers between devices  49.4 us (39%)
  starting transfers between devices  33.6 us (26%)
  Pallas kernels  24.9 us (19%)
  blocking collectives  19.5 us (15%)
    all_to_all x2, blocking collectives, exchanged(): return lax.all_to_all(message, ALL, 0, 0)  19.5 us
    ppermute x13, starting transfers between devices, to_partner(): lax.ppermute(piece, ('side', 'orb'), [(flat_of(i), flat_of(i ^ m)) for i...  11.7 us
    pallas_call x2, Pallas kernels, filtered_pieces(): pl.pallas_call(functools.partial(filter_kernel, at, len(pot_far), early,...  10.4 us
    ppermute x3, waiting for transfers between devices, whole(): lax.ppermute(joined, 'orb', [(i, i ^ m) for i in range(orb_count)])  9.47 us
    ppermute x1, waiting for transfers between devices, whole(): lax.ppermute(spare[1], 'side', swap)  8.49 us
    ppermute x1, waiting for transfers between devices, whole(): lax.ppermute(spare[2], 'orb', across)  8.44 us
    ppermute x2, waiting for transfers between devices, whole(): lax.ppermute(sent[3 * at + 2], slab_axes, ahead)  7.66 us
    pallas_call x1, Pallas kernels, whole(): pl.pallas_call(functools.partial(last_kernel, cell_total), out_shape=jax....  6.88 us
  transfers between devices with their start and end apart: 33, of which 14 were waited for; matrix products, arithmetic and copies ran while one was open for 0% of the time, Pallas kernels for 11%

profile of v11, /device:TPU:0, one launch (start us, length us, event | category | flops | bytes accessed | tf_op | source)
XLA Modules:
  0.0 127.7 jit_solution(6120961900971582503)
XLA Ops:
  0.1 2.2 %shard_map.28 = (f32[12,16,128]{2,1,0:T(8,128)S(1)}, f32[6,16,128]{2,1,0:T(8,128)S(1)}, f32[9,64,128]{2,1,0:T(8,128)S(1)}, f32[12,64,128]{2,1,0:T(8,128)S(1)}, f...) custom-call(s32[3]{0:T(128)S(1)} %pad_add_fusion.place, ...), custom_call_target="tpu_custom_call" | custom-call | tf_op jit(solution)/shard_map/pallas_call | solution.py:61
  2.3 3.1 %collective-permute-start.3 = (f32[12,16,128]{2,1,0:T(8,128)S(1)}, f32[12,16,128]{2,1,0:T(8,128)S(1)}, u32[]{:S(2)}, u32[]{:S(2)}) collective-permute-start(f32[12,16,128]{2,1,0:T(8,128)S(1)} %get-tuple-element.39), channel_id=1, source_target_pairs={{0,4},{4,0},{1,5},{5,1},{2,6},{6,2},{3,7},{7,3},{8,12},{12,8},{9,1... | collective-permute-start | bytes 294920 | tf_op jit(solution)/shard_map/ppermute | solution.py:457
  5.4 3.5 %collective-permute-start.1 = (f32[9,64,128]{2,1,0:T(8,128)S(1)}, f32[9,64,128]{2,1,0:T(8,128)S(1)}, u32[]{:S(2)}, u32[]{:S(2)}) collective-permute-start(f32[9,64,128]{2,1,0:T(8,128)S(1)} %get-tuple-element.37), channel_id=1, source_target_pairs={{0,28},{4,8},{8,4},{12,16},{16,12},{20,24},{24,20},{28,0},{1,29},{... | collective-permute-start | bytes 884744 | tf_op jit(solution)/shard_map/ppermute | solution.py:476
  9.3 2.4 %collective-permute-start.4 = (f32[6,16,128]{2,1,0:T(8,128)S(1)}, f32[6,16,128]{2,1,0:T(8,128)S(1)}, u32[]{:S(2)}, u32[]{:S(2)}) collective-permute-start(f32[6,16,128]{2,1,0:T(8,128)S(1)} %get-tuple-element.40), channel_id=1, source_target_pairs={{0,28},{4,8},{8,4},{12,16},{16,12},{20,24},{24,20},{28,0},{1,29},{... | collective-permute-start | bytes 147464 | tf_op jit(solution)/shard_map/ppermute | solution.py:458
  11.7 4.7 %collective-permute-done.5.straight = f32[6,16,128]{2,1,0:T(8,128)S(1)} collective-permute-done((f32[6,16,128]{2,1,0:T(8,128)S(1)}, f32[6,16,128]{2,1,0:T(8,128)S(1)}, u32[]{:S(2)}, u32[]{:S(2)}) %collective-permute-start.5) | collective-permute-done | bytes 49184 | tf_op jit(solution)/shard_map/ppermute | solution.py:459
  16.4 2.2 %collective-permute-done.4.slanted = f32[6,16,128]{2,1,0:T(8,128)S(1)} collective-permute-done((f32[6,16,128]{2,1,0:T(8,128)S(1)}, f32[6,16,128]{2,1,0:T(8,128)S(1)}, u32[]{:S(2)}, u32[]{:S(2)}) %collective-permute-start.4) | collective-permute-done | bytes 49184 | tf_op jit(solution)/shard_map/ppermute | solution.py:458
  20.6 5.2 %collective-permute-done.8.rest_3_ = f32[24,16,128]{2,1,0:T(8,128)S(1)} collective-permute-done((f32[24,16,128]{2,1,0:T(8,128)S(1)}, f32[24,16,128]{2,1,0:T(8,128)S(1)}, u32[]{:S(2)}, u32[]{:S(2)}) %collective-permute-start.8) | collective-permute-done | bytes 196640 | tf_op jit(solution)/shard_map/ppermute | solution.py:469
  25.9 4.2 %collective-permute-done.7.rest_2_ = f32[24,16,128]{2,1,0:T(8,128)S(1)} collective-permute-done((f32[24,16,128]{2,1,0:T(8,128)S(1)}, f32[24,16,128]{2,1,0:T(8,128)S(1)}, u32[]{:S(2)}, u32[]{:S(2)}) %collective-permute-start.7) | collective-permute-done | bytes 196640 | tf_op jit(solution)/shard_map/ppermute | solution.py:469
  30.1 2.1 %collective-permute-start.2 = (f32[9,64,128]{2,1,0:T(8,128)S(1)}, f32[9,64,128]{2,1,0:T(8,128)S(1)}, u32[]{:S(2)}, u32[]{:S(2)}) collective-permute-start(f32[9,64,128]{2,1,0:T(8,128)S(1)} %get-tuple-element.38), channel_id=1, source_target_pairs={{0,24},{4,12},{8,0},{12,20},{16,8},{20,28},{24,16},{28,4},{1,25},{... | collective-permute-start | bytes 884744 | tf_op jit(solution)/shard_map/ppermute | solution.py:478
  33.6 2.0 %collective-permute-start.17 = (f32[9,64,128]{2,1,0:T(8,128)S(1)}, f32[9,64,128]{2,1,0:T(8,128)S(1)}, u32[]{:S(2)}, u32[]{:S(2)}) collective-permute-start(f32[9,64,128]{2,1,0:T(8,128)S(1)} %get-tuple-element.49), channel_id=1, source_target_pairs={{0,24},{4,12},{8,0},{12,20},{16,8},{20,28},{24,16},{28,4},{1,25},{... | collective-permute-start | bytes 884744 | tf_op jit(solution)/shard_map/ppermute | solution.py:478
  35.8 4.2 %collective-permute-done.2.straight = f32[9,64,128]{2,1,0:T(8,128)S(1)} collective-permute-done((f32[9,64,128]{2,1,0:T(8,128)S(1)}, f32[9,64,128]{2,1,0:T(8,128)S(1)}, u32[]{:S(2)}, u32[]{:S(2)}) %collective-permute-start.2) | collective-permute-done | bytes 294944 | tf_op jit(solution)/shard_map/ppermute | solution.py:478
  40.0 4.7 %shard_map.30 = (f32[12,16,128]{2,1,0:T(8,128)S(1)}, f32[12,16,128]{2,1,0:T(8,128)S(1)}, f32[12,16,128]{2,1,0:T(8,128)S(1)}, f32[12,16,128]{2,1,0:T(8,128)S(1)},...) custom-call(s32[3]{0:T(128)S(1)} %pad_add_fusion.place, ...), custom_call_target="tpu_custom_call" | custom-call | tf_op jit(solution)/shard_map/pallas_call | solution.py:200
  45.8 2.0 %collective-permute-done.16.slanted = f32[9,64,128]{2,1,0:T(8,128)S(1)} collective-permute-done((f32[9,64,128]{2,1,0:T(8,128)S(1)}, f32[9,64,128]{2,1,0:T(8,128)S(1)}, u32[]{:S(2)}, u32[]{:S(2)}) %collective-permute-start.16) | collective-permute-done | bytes 294944 | tf_op jit(solution)/shard_map/ppermute | solution.py:476
  48.3 3.4 %collective-permute-done.17.straight = f32[9,64,128]{2,1,0:T(8,128)S(1)} collective-permute-done((f32[9,64,128]{2,1,0:T(8,128)S(1)}, f32[9,64,128]{2,1,0:T(8,128)S(1)}, u32[]{:S(2)}, u32[]{:S(2)}) %collective-permute-start.17) | collective-permute-done | bytes 294944 | tf_op jit(solution)/shard_map/ppermute | solution.py:478
  54.1 5.7 %shard_map.31 = (f32[12,16,128]{2,1,0:T(8,128)S(1)}, f32[12,16,128]{2,1,0:T(8,128)S(1)}, f32[12,16,128]{2,1,0:T(8,128)S(1)}, f32[12,16,128]{2,1,0:T(8,128)S(1)},...) custom-call(s32[3]{0:T(128)S(1)} %pad_add_fusion.place, ...), custom_call_target="tpu_custom_call" | custom-call | tf_op jit(solution)/shard_map/pallas_call | solution.py:200
  59.8 2.9 %collective-permute-start.18 = (f32[12,16,128]{2,1,0:T(8,128)S(1)}, f32[12,16,128]{2,1,0:T(8,128)S(1)}, u32[]{:S(2)}, u32[]{:S(2)}) collective-permute-start(f32[12,16,128]{2,1,0:T(8,128)S(1)} %get-tuple-element.51), channel_id=1, source_target_pairs={{0,6},{4,2},{1,7},{5,3},{2,4},{6,0},{3,5},{7,1},{8,14},{12,10},{9,... | collective-permute-start | bytes 294920 | tf_op jit(solution)/shard_map/ppermute | solution.py:489
  69.8 2.0 %collective-permute-done.20.refs_8_ = f32[12,16,128]{2,1,0:T(8,128)S(1)} collective-permute-done((f32[12,16,128]{2,1,0:T(8,128)S(1)}, f32[12,16,128]{2,1,0:T(8,128)S(1)}, u32[]{:S(2)}, u32[]{:S(2)}) %collective-permute-start.20) | collective-permute-done | bytes 98336 | tf_op jit(solution)/shard_map/ppermute | solution.py:489
  73.9 2.1 %shard_map.32 = (f32[16,192,128]{2,1,0:T(8,128)S(1)}, f32[32,1,256]{2,1,0:T(1,128)S(1)}) custom-call(s32[3]{0:T(128)S(1)} %pad_add_fusion.place, f32[12,16,128]{2,1,0:T(8,128)S(1)} %collective-permute-done.9.refs_0_, f32[12,16,128]{2,1,0:T(8,128)S(1)} %collective-permute-done.10.refs_1_, f32[12,16,128]{2,1,0:T(8,128)S(1)} %collective-permute-done.11.refs_2_, ...), custom_call_target="tpu_custom_call" | custom-call | tf_op jit(solution)/shard_map/pallas_call | solution.py:425
  80.5 8.5 %collective-permute-done.26.refs_1_ = f32[2,2,12,16,128]{4,3,2,1,0:T(8,128)S(1)} collective-permute-done((f32[2,2,12,16,128]{4,3,2,1,0:T(8,128)S(1)}, f32[2,2,12,16,128]{4,3,2,1,0:T(8,128)S(1)}, u32[]{:S(2)}, u32[]{:S(2)}) %collective-permute-start.26) | collective-permute-done | bytes 393248 | tf_op jit(solution)/shard_map/ppermute | solution.py:531
  89.0 8.4 %collective-permute-done.27.refs_2_ = f32[2,2,12,16,128]{4,3,2,1,0:T(8,128)S(1)} collective-permute-done((f32[2,2,12,16,128]{4,3,2,1,0:T(8,128)S(1)}, f32[2,2,12,16,128]{4,3,2,1,0:T(8,128)S(1)}, u32[]{:S(2)}, u32[]{:S(2)}) %collective-permute-start.27) | collective-permute-done | bytes 393248 | tf_op jit(solution)/shard_map/ppermute | solution.py:532
  97.9 10.5 %all_to_all.10.copies = f32[32,1,256]{2,1,0:T(1,128)S(1)} all-to-all(f32[32,1,256]{2,1,0:T(1,128)S(1)} %get-tuple-element.59), channel_id=1, replica_groups=mesh['pair'=4,'side'=2,'orb'=4] {'pair','side','orb'}, dimensions={0} | all-to-all | bytes 65536 | tf_op jit(solution)/shard_map/all_to_all | solution.py:517
  108.4 3.4 %shard_map.33 = (f32[16,128]{1,0:T(8,128)S(1)}, f32[32,1,256]{2,1,0:T(1,128)S(1)}) custom-call(f32[32,1,256]{2,1,0:T(1,128)S(1)} %all_to_all.10.copies, f32[16,192,128]{2,1,0:T(8,128)S(1)} %get-tuple-element.60.block), custom_call_target="tpu_custom_call" | custom-call | tf_op jit(solution)/shard_map/pallas_call | solution.py:540
  111.8 9.0 %all_to_all.11.copies = f32[32,1,256]{2,1,0:T(1,128)S(1)} all-to-all(f32[32,1,256]{2,1,0:T(1,128)S(1)} %get-tuple-element.61), channel_id=1, replica_groups=mesh['pair'=4,'side'=2,'orb'=4] {'pair','side','orb'}, dimensions={0} | all-to-all | bytes 65536 | tf_op jit(solution)/shard_map/all_to_all | solution.py:517
  120.8 6.9 %shard_map.34 = f32[4,12,64,128]{3,2,1,0:T(8,128)} custom-call(s32[3]{0:T(128)S(1)} %pad_add_fusion.place, f32[32,1,256]{2,1,0:T(1,128)S(1)} %all_to_all.11.copies, f32[16,128]{1,0:T(8,128)S(1)} %get-tuple-element.62.table, f32[16,192,128]{2,1,0:T(8,128)S(1)} %get-tuple-element.60.block, f32[16,192,128]{2,1,0:T(8,128)S(1)} %collective-permute-done.25.block_near, ...), custom_call_target="tpu_custom_call" | custom-call | tf_op jit(solution)/shard_map/pallas_call | solution.py:548
  (57 shorter events, 22.1 us)
Async XLA Ops:
  2.3 16.3 %collective-permute-start.3 = (f32[12,16,128]{2,1,0:T(8,128)S(1)}, f32[12,16,128]{2,1,0:T(8,128)S(1)}, u32[]{:S(2)}, u32[]{:S(2)}) collective-permute-start(f32[12,16,128]{2,1,0:T(8,128)S(1)} %get-tuple-element.39), channel_id=1, source_target_pairs={{0,4},{4,0},{1,5},{5,1},{2,6},{6,2},{3,7},{7,3},{8,12},{12,8},{9,1... | collective-permute-start | bytes 294920 | tf_op jit(solution)/shard_map/ppermute | solution.py:457
  5.4 28.3 %collective-permute-start.1 = (f32[9,64,128]{2,1,0:T(8,128)S(1)}, f32[9,64,128]{2,1,0:T(8,128)S(1)}, u32[]{:S(2)}, u32[]{:S(2)}) collective-permute-start(f32[9,64,128]{2,1,0:T(8,128)S(1)} %get-tuple-element.37), channel_id=1, source_target_pairs={{0,28},{4,8},{8,4},{12,16},{16,12},{20,24},{24,20},{28,0},{1,29},{... | collective-permute-start | bytes 884744 | tf_op jit(solution)/shard_map/ppermute | solution.py:476
  9.3 9.3 %collective-permute-start.4 = (f32[6,16,128]{2,1,0:T(8,128)S(1)}, f32[6,16,128]{2,1,0:T(8,128)S(1)}, u32[]{:S(2)}, u32[]{:S(2)}) collective-permute-start(f32[6,16,128]{2,1,0:T(8,128)S(1)} %get-tuple-element.40), channel_id=1, source_target_pairs={{0,28},{4,8},{8,4},{12,16},{16,12},{20,24},{24,20},{28,0},{1,29},{... | collective-permute-start | bytes 147464 | tf_op jit(solution)/shard_map/ppermute | solution.py:458
  18.7 11.4 %collective-permute-start.7 = (f32[24,16,128]{2,1,0:T(8,128)S(1)}, f32[24,16,128]{2,1,0:T(8,128)S(1)}, u32[]{:S(2)}, u32[]{:S(2)}) collective-permute-start(f32[24,16,128]{2,1,0:T(8,128)S(1)} %shard_map.29.rest_0_), channel_id=1, source_target_pairs={{0,2},{1,3},{2,0},{3,1},{4,6},{5,7},{6,4},{7,5},{8,10},{9,11},{10,... | collective-permute-start | bytes 589832 | tf_op jit(solution)/shard_map/ppermute | solution.py:469
  20.3 11.9 %collective-permute-start.6 = (f32[24,16,128]{2,1,0:T(8,128)S(1)}, f32[24,16,128]{2,1,0:T(8,128)S(1)}, u32[]{:S(2)}, u32[]{:S(2)}) collective-permute-start(f32[24,16,128]{2,1,0:T(8,128)S(1)} %shard_map.29.rest_0_), channel_id=1, source_target_pairs={{0,1},{1,0},{2,3},{3,2},{4,5},{5,4},{6,7},{7,6},{8,9},{9,8},{10,11... | collective-permute-start | bytes 589832 | tf_op jit(solution)/shard_map/ppermute | solution.py:469
  20.5 19.4 %collective-permute-start = (f32[12,64,128]{2,1,0:T(8,128)S(1)}, f32[12,64,128]{2,1,0:T(8,128)S(1)}, u32[]{:S(2)}, u32[]{:S(2)}) collective-permute-start(f32[12,64,128]{2,1,0:T(8,128)S(1)} %get-tuple-element.36), channel_id=1, source_target_pairs={{0,4},{4,0},{1,5},{5,1},{2,6},{6,2},{3,7},{7,3},{8,12},{12,8},{9,1... | collective-permute-start | bytes 1179656 | tf_op jit(solution)/shard_map/ppermute | solution.py:477
  25.8 26.2 %collective-permute-start.15 = (f32[12,64,128]{2,1,0:T(8,128)S(1)}, f32[12,64,128]{2,1,0:T(8,128)S(1)}, u32[]{:S(2)}, u32[]{:S(2)}) collective-permute-start(f32[12,64,128]{2,1,0:T(8,128)S(1)} %get-tuple-element.47), channel_id=1, source_target_pairs={{0,4},{4,0},{1,5},{5,1},{2,6},{6,2},{3,7},{7,3},{8,12},{12,8},{9,1... | collective-permute-start | bytes 1179656 | tf_op jit(solution)/shard_map/ppermute | solution.py:477
  30.1 9.9 %collective-permute-start.2 = (f32[9,64,128]{2,1,0:T(8,128)S(1)}, f32[9,64,128]{2,1,0:T(8,128)S(1)}, u32[]{:S(2)}, u32[]{:S(2)}) collective-permute-start(f32[9,64,128]{2,1,0:T(8,128)S(1)} %get-tuple-element.38), channel_id=1, source_target_pairs={{0,24},{4,12},{8,0},{12,20},{16,8},{20,28},{24,16},{28,4},{1,25},{... | collective-permute-start | bytes 884744 | tf_op jit(solution)/shard_map/ppermute | solution.py:478
  32.2 15.6 %collective-permute-start.16 = (f32[9,64,128]{2,1,0:T(8,128)S(1)}, f32[9,64,128]{2,1,0:T(8,128)S(1)}, u32[]{:S(2)}, u32[]{:S(2)}) collective-permute-start(f32[9,64,128]{2,1,0:T(8,128)S(1)} %get-tuple-element.48), channel_id=1, source_target_pairs={{0,28},{4,8},{8,4},{12,16},{16,12},{20,24},{24,20},{28,0},{1,29},{... | collective-permute-start | bytes 884744 | tf_op jit(solution)/shard_map/ppermute | solution.py:476
  33.6 18.1 %collective-permute-start.17 = (f32[9,64,128]{2,1,0:T(8,128)S(1)}, f32[9,64,128]{2,1,0:T(8,128)S(1)}, u32[]{:S(2)}, u32[]{:S(2)}) collective-permute-start(f32[9,64,128]{2,1,0:T(8,128)S(1)} %get-tuple-element.49), channel_id=1, source_target_pairs={{0,24},{4,12},{8,0},{12,20},{16,8},{20,28},{24,16},{28,4},{1,25},{... | collective-permute-start | bytes 884744 | tf_op jit(solution)/shard_map/ppermute | solution.py:478
  44.7 15.1 %collective-permute-start.9 = (f32[12,16,128]{2,1,0:T(8,128)S(1)}, f32[12,16,128]{2,1,0:T(8,128)S(1)}, u32[]{:S(2)}, u32[]{:S(2)}) collective-permute-start(f32[12,16,128]{2,1,0:T(8,128)S(1)} %get-tuple-element.41), channel_id=1, source_target_pairs={{0,6},{4,2},{1,7},{5,3},{2,4},{6,0},{3,5},{7,1},{8,14},{12,10},{9,... | collective-permute-start | bytes 294920 | tf_op jit(solution)/shard_map/ppermute | solution.py:489
  45.5 14.2 %collective-permute-start.10 = (f32[12,16,128]{2,1,0:T(8,128)S(1)}, f32[12,16,128]{2,1,0:T(8,128)S(1)}, u32[]{:S(2)}, u32[]{:S(2)}) collective-permute-start(f32[12,16,128]{2,1,0:T(8,128)S(1)} %get-tuple-element.42), channel_id=1, source_target_pairs={{0,7},{4,3},{1,6},{5,2},{2,5},{6,1},{3,4},{7,0},{8,15},{12,11},{9,... | collective-permute-start | bytes 294920 | tf_op jit(solution)/shard_map/ppermute | solution.py:489
  47.8 14.9 %collective-permute-start.11 = (f32[12,16,128]{2,1,0:T(8,128)S(1)}, f32[12,16,128]{2,1,0:T(8,128)S(1)}, u32[]{:S(2)}, u32[]{:S(2)}) collective-permute-start(f32[12,16,128]{2,1,0:T(8,128)S(1)} %get-tuple-element.43), channel_id=1, source_target_pairs={{0,2},{4,6},{1,3},{5,7},{2,0},{6,4},{3,1},{7,5},{8,10},{12,14},{9,... | collective-permute-start | bytes 294920 | tf_op jit(solution)/shard_map/ppermute | solution.py:489
  51.7 11.0 %collective-permute-start.12 = (f32[12,16,128]{2,1,0:T(8,128)S(1)}, f32[12,16,128]{2,1,0:T(8,128)S(1)}, u32[]{:S(2)}, u32[]{:S(2)}) collective-permute-start(f32[12,16,128]{2,1,0:T(8,128)S(1)} %get-tuple-element.44), channel_id=1, source_target_pairs={{0,3},{4,7},{1,2},{5,6},{2,1},{6,5},{3,0},{7,4},{8,11},{12,15},{9,... | collective-permute-start | bytes 294920 | tf_op jit(solution)/shard_map/ppermute | solution.py:489
  52.1 10.8 %collective-permute-start.13 = (f32[12,16,128]{2,1,0:T(8,128)S(1)}, f32[12,16,128]{2,1,0:T(8,128)S(1)}, u32[]{:S(2)}, u32[]{:S(2)}) collective-permute-start(f32[12,16,128]{2,1,0:T(8,128)S(1)} %get-tuple-element.45), channel_id=1, source_target_pairs={{0,4},{4,0},{1,5},{5,1},{2,6},{6,2},{3,7},{7,3},{8,12},{12,8},{9,1... | collective-permute-start | bytes 294920 | tf_op jit(solution)/shard_map/ppermute | solution.py:489
  62.7 11.2 %collective-permute-start.24 = (f32[2,12,16,128]{3,2,1,0:T(8,128)S(1)}, f32[2,12,16,128]{3,2,1,0:T(8,128)S(1)}, u32[]{:S(2)}, u32[]{:S(2)}) collective-permute-start(f32[2,12,16,128]{3,2,1,0:T(8,128)S(1)} %get-tuple-element.58), channel_id=1, source_target_pairs={{0,1},{4,5},{1,0},{5,4},{2,3},{6,7},{3,2},{7,6},{8,9},{12,13},{9,8... | collective-permute-start | bytes 589832 | tf_op jit(solution)/shard_map/ppermute | solution.py:489
  76.0 44.8 %collective-permute-start.25 = (f32[16,192,128]{2,1,0:T(8,128)S(1)}, f32[16,192,128]{2,1,0:T(8,128)S(1)}, u32[]{:S(2)}, u32[]{:S(2)}) collective-permute-start(f32[16,192,128]{2,1,0:T(8,128)S(1)} %get-tuple-element.60.block), channel_id=1, source_target_pairs={{0,1},{1,0},{2,3},{3,2},{4,5},{5,4},{6,7},{7,6},{8,9},{9,8},{10,11... | collective-permute-start | bytes 4718600 | tf_op jit(solution)/shard_map/ppermute | solution.py:535
  77.0 12.0 %collective-permute-start.26 = (f32[2,2,12,16,128]{4,3,2,1,0:T(8,128)S(1)}, f32[2,2,12,16,128]{4,3,2,1,0:T(8,128)S(1)}, u32[]{:S(2)}, u32[]{:S(2)}) collective-permute-start(f32[2,2,12,16,128]{4,3,2,1,0:T(8,128)S(1)} %get-tuple-element.64), channel_id=1, source_target_pairs={{0,4},{4,0},{1,5},{5,1},{2,6},{6,2},{3,7},{7,3},{8,12},{12,8},{9,1... | collective-permute-start | bytes 1179656 | tf_op jit(solution)/shard_map/ppermute | solution.py:531
  77.8 19.6 %collective-permute-start.27 = (f32[2,2,12,16,128]{4,3,2,1,0:T(8,128)S(1)}, f32[2,2,12,16,128]{4,3,2,1,0:T(8,128)S(1)}, u32[]{:S(2)}, u32[]{:S(2)}) collective-permute-start(f32[2,2,12,16,128]{4,3,2,1,0:T(8,128)S(1)} %get-tuple-element.65), channel_id=1, source_target_pairs={{0,2},{1,3},{2,0},{3,1},{4,6},{5,7},{6,4},{7,5},{8,10},{9,11},{10,... | collective-permute-start | bytes 1179656 | tf_op jit(solution)/shard_map/ppermute | solution.py:532
  78.4 19.0 %collective-permute-start.28 = (f32[2,2,12,16,128]{4,3,2,1,0:T(8,128)S(1)}, f32[2,2,12,16,128]{4,3,2,1,0:T(8,128)S(1)}, u32[]{:S(2)}, u32[]{:S(2)}) collective-permute-start(f32[2,2,12,16,128]{4,3,2,1,0:T(8,128)S(1)} %get-tuple-element.66), channel_id=1, source_target_pairs={{0,6},{1,7},{2,4},{3,5},{4,2},{5,3},{6,0},{7,1},{8,14},{9,15},{10,... | collective-permute-start | bytes 1179656 | tf_op jit(solution)/shard_map/ppermute | solution.py:534
  80.5 40.3 %collective-permute-start.29 = (f32[2,2,12,16,128]{4,3,2,1,0:T(8,128)S(1)}, f32[2,2,12,16,128]{4,3,2,1,0:T(8,128)S(1)}, u32[]{:S(2)}, u32[]{:S(2)}) collective-permute-start(f32[2,2,12,16,128]{4,3,2,1,0:T(8,128)S(1)} %get-tuple-element.63.refs_0_), channel_id=1, source_target_pairs={{0,1},{1,0},{2,3},{3,2},{4,5},{5,4},{6,7},{7,6},{8,9},{9,8},{10,11... | collective-permute-start | bytes 1179656 | tf_op jit(solution)/shard_map/ppermute | solution.py:537
  89.0 31.8 %collective-permute-start.30 = (f32[2,2,12,16,128]{4,3,2,1,0:T(8,128)S(1)}, f32[2,2,12,16,128]{4,3,2,1,0:T(8,128)S(1)}, u32[]{:S(2)}, u32[]{:S(2)}) collective-permute-start(f32[2,2,12,16,128]{4,3,2,1,0:T(8,128)S(1)} %collective-permute-done.26.refs_1_), channel_id=1, source_target_pairs={{0,1},{1,0},{2,3},{3,2},{4,5},{5,4},{6,7},{7,6},{8,9},{9,8},{10,11... | collective-permute-start | bytes 1179656 | tf_op jit(solution)/shard_map/ppermute | solution.py:537
  97.4 23.4 %collective-permute-start.31 = (f32[2,2,12,16,128]{4,3,2,1,0:T(8,128)S(1)}, f32[2,2,12,16,128]{4,3,2,1,0:T(8,128)S(1)}, u32[]{:S(2)}, u32[]{:S(2)}) collective-permute-start(f32[2,2,12,16,128]{4,3,2,1,0:T(8,128)S(1)} %collective-permute-done.27.refs_2_), channel_id=1, source_target_pairs={{0,1},{1,0},{2,3},{3,2},{4,5},{5,4},{6,7},{7,6},{8,9},{9,8},{10,11... | collective-permute-start | bytes 1179656 | tf_op jit(solution)/shard_map/ppermute | solution.py:537
  97.4 23.4 %collective-permute-start.32 = (f32[2,2,12,16,128]{4,3,2,1,0:T(8,128)S(1)}, f32[2,2,12,16,128]{4,3,2,1,0:T(8,128)S(1)}, u32[]{:S(2)}, u32[]{:S(2)}) collective-permute-start(f32[2,2,12,16,128]{4,3,2,1,0:T(8,128)S(1)} %collective-permute-done.28.refs_3_), channel_id=1, source_target_pairs={{0,1},{1,0},{2,3},{3,2},{4,5},{5,4},{6,7},{7,6},{8,9},{9,8},{10,11... | collective-permute-start | bytes 1179656 | tf_op jit(solution)/shard_map/ppermute | solution.py:538
  (11 other events, 142.5 us)

commit v12 on v11

--- a/solution.py
+++ b/solution.py
@@ -299,8 +299,13 @@
     return jnp.concatenate(tiles, axis=1)
 
 
-def first_kernel(early, late, kept, place, *refs):
-    given, (block, message) = refs[:-2], refs[-2:]
+def first_kernel(early, late, kept, forwards, place, *refs):
+    outs = 2 + len(forwards[:1])
+    given, (block, message, *forward) = refs[:-outs], refs[-outs:]
+    if forward:
+        for slot, apart in enumerate(forwards):
+            for at in range(kept):
+                forward[0][slot, at] = given[at * len(early) + early.index(apart)][...]
     me, shape = place[1], block.shape[1:]
     for at in range(kept):
         for index, apart in enumerate(early):
@@ -403,18 +408,24 @@
     for fetch in fetches:
         fetch.wait()
 
-    def spare_at(ref, stage, share):
-        return lambda row, strip: ref[stage, share, row, pl.ds(strip * EIGHT, EIGHT), :]
-
-    kinds = len(spares) // 2
-    for share in range(CORES):
+    def piece_at(ref, first, second):
+        return lambda row, strip: ref[first, second, row, pl.ds(strip * EIGHT, EIGHT), :]
+
+    kinds, kept = count // 2, held // 2
+    core = orb % CORES
+    for turn in range(CORES):
+        share = core ^ turn
         sources = []
-        for index, ref in enumerate(spares):
-            flip, kind = index // kinds, index % kinds
-            quad = (orb ^ CORES if kind // 2 else orb) ^ flip
-            for stage in range(ref.shape[0]):
-                orbital = quad * held + (side ^ (kind % 2)) * ref.shape[0] + stage
-                sources.append((orbital, spare_at(ref, stage, share)))
+        for flip in range(2):
+            for kind in range(kinds - 1):
+                quad = (orb ^ CORES if kind // 2 else orb) ^ flip
+                for stage in range(kept):
+                    orbital = quad * held + (side ^ (kind % 2)) * kept + stage
+                    sources.append((orbital, piece_at(spares[flip * kinds + kind], stage, share)))
+            quad = orb ^ CORES ^ turn ^ flip
+            for stage in range(kept):
+                orbital = quad * held + (side ^ 1) * kept + stage
+                sources.append((orbital, piece_at(spares[turn * kinds + kinds - 1], flip, stage)))
         write(sources, ((1 - chip) * CORES + share) * part)
     leave(1 - chip, 1).start()
     leave(chip, 0).wait()
@@ -471,17 +482,14 @@
 
     fetched = []
     for at in range(kept):
-        fetched.append(
-            (
-                lax.ppermute(sent[3 * at], slab_axes, slant),
-                lax.ppermute(sent[3 * at + 1], "side", swap),
-                lax.ppermute(sent[3 * at + 2], slab_axes, ahead),
-            )
-        )
+        swapped = lax.ppermute(sent[3 * at + 1], "side", swap)
+        slanted = lax.ppermute(sent[3 * at], slab_axes, slant)
+        straight = lax.ppermute(sent[3 * at + 2], slab_axes, ahead)
+        fetched.append((slanted, swapped, straight))
 
     early = tuple(sorted((m for m in range(1, group) if m != CORES), key=lambda m: (m < 2 * CORES, -(m % 2), m)))
     late = (0, CORES)
-    spares = 4 if orb_count == 2 * CORES and kept == 2 else 0
+    spares = 3 if orb_count == 2 * CORES and kept == 2 else 0
 
     def to_partner(piece, m):
         if m == 0:
@@ -516,22 +524,23 @@
     def exchanged(message):
         return lax.all_to_all(message, ALL, 0, 0)
 
-    block, message = small_call(
-        functools.partial(first_kernel, early, late, kept),
-        [block_shape, message_shape],
+    forwards = (1, 1 + CORES) if spares else ()
+    forward_shape = jax.ShapeDtypeStruct((CORES, kept, rows, part, width), jnp.float32)
+    block, message, *forward = small_call(
+        functools.partial(first_kernel, early, late, kept, forwards),
+        [block_shape, message_shape] + [forward_shape] * len(forwards[:1]),
         [SMEM] + [VMEM] * len(parts),
         *(place, *parts),
     )
     if spares:
         across = [(i, i ^ CORES) for i in range(orb_count)]
-        slanted_across = [(t * orb_count + i, (1 - t) * orb_count + (i ^ CORES)) for t in range(2) for i in range(orb_count)]
         cores = [(i, i ^ 1) for i in range(orb_count)]
         given = [
             spare[0],
             lax.ppermute(spare[1], "side", swap),
             lax.ppermute(spare[2], "orb", across),
         ]
-        given.append(lax.ppermute(spare[3], ("side", "orb"), slanted_across))
+        given.append(lax.ppermute(forward[0], "orb", across))
         block_near = lax.ppermute(block, "orb", cores)
         table_shape = jax.ShapeDtypeStruct((total, LANES), jnp.float32)
         near = [lax.ppermute(piece, "orb", cores) for piece in given[:-1]]

time: 128 us -> 127 us (level)
    ppermute x7, waiting for transfers between devices: 9.71 us -> 17.3 us  [the longest x2 7.66 us: whole(): straight = lax.ppermute(sent[3 * at + 2], slab_axes, ahead)]
    ppermute x1, waiting for transfers between devices: 8.44 us -> 1.72 us  [whole(): lax.ppermute(spare[2], 'orb', across)]
  transfers between devices with their start and end apart: 33 -> 33, of which waited for: 14 -> 15; matrix products, arithmetic and copies ran while one was open for 0% -> 0% of each run, Pallas kernels for 11% -> 11%
where the time goes in v12:
time: 127 us
  waiting for transfers between devices  50 us (39%)
  starting transfers between devices  32.5 us (26%)
  Pallas kernels  25 us (20%)
  blocking collectives  19.6 us (15%)
    all_to_all x2, blocking collectives, exchanged(): return lax.all_to_all(message, ALL, 0, 0)  19.6 us
    ppermute x13, starting transfers between devices, to_partner(): lax.ppermute(piece, ('side', 'orb'), [(flat_of(i), flat_of(i ^ m)) for i...  11.7 us
    pallas_call x2, Pallas kernels, filtered_pieces(): pl.pallas_call(functools.partial(filter_kernel, at, len(pot_far), early,...  10.3 us
    ppermute x3, waiting for transfers between devices, whole(): lax.ppermute(joined, 'orb', [(i, i ^ m) for i in range(orb_count)])  9.47 us
    ppermute x1, waiting for transfers between devices, whole(): lax.ppermute(spare[1], 'side', swap)  8.23 us
    ppermute x2, waiting for transfers between devices, whole(): straight = lax.ppermute(sent[3 * at + 2], slab_axes, ahead)  7.66 us
    ppermute x1, waiting for transfers between devices, whole(): given.append(lax.ppermute(forward[0], 'orb', across))  7.61 us
    pallas_call x1, Pallas kernels, whole(): pl.pallas_call(functools.partial(last_kernel, cell_total), out_shape=jax....  6.91 us
  transfers between devices with their start and end apart: 33, of which 15 were waited for; matrix products, arithmetic and copies ran while one was open for 0% of the time, Pallas kernels for 11%

profile of v12, /device:TPU:0, one launch (start us, length us, event | category | flops | bytes accessed | tf_op | source)
XLA Modules:
  0.0 127.3 jit_solution(18035158015529171523)
XLA Ops:
  0.1 2.2 %shard_map.28 = (f32[12,16,128]{2,1,0:T(8,128)S(1)}, f32[6,16,128]{2,1,0:T(8,128)S(1)}, f32[9,64,128]{2,1,0:T(8,128)S(1)}, f32[12,64,128]{2,1,0:T(8,128)S(1)}, f...) custom-call(s32[3]{0:T(128)S(1)} %pad_add_fusion.place, ...), custom_call_target="tpu_custom_call" | custom-call | tf_op jit(solution)/shard_map/pallas_call | solution.py:61
  2.3 3.1 %collective-permute-start.3 = (f32[12,16,128]{2,1,0:T(8,128)S(1)}, f32[12,16,128]{2,1,0:T(8,128)S(1)}, u32[]{:S(2)}, u32[]{:S(2)}) collective-permute-start(f32[12,16,128]{2,1,0:T(8,128)S(1)} %get-tuple-element.39), channel_id=1, source_target_pairs={{0,4},{4,0},{1,5},{5,1},{2,6},{6,2},{3,7},{7,3},{8,12},{12,8},{9,1... | collective-permute-start | bytes 294920 | tf_op jit(solution)/shard_map/ppermute | solution.py:468
  5.4 3.5 %collective-permute-start.1 = (f32[9,64,128]{2,1,0:T(8,128)S(1)}, f32[9,64,128]{2,1,0:T(8,128)S(1)}, u32[]{:S(2)}, u32[]{:S(2)}) collective-permute-start(f32[9,64,128]{2,1,0:T(8,128)S(1)} %get-tuple-element.37), channel_id=1, source_target_pairs={{0,28},{4,8},{8,4},{12,16},{16,12},{20,24},{24,20},{28,0},{1,29},{... | collective-permute-start | bytes 884744 | tf_op jit(solution)/shard_map/ppermute | solution.py:486
  9.3 2.4 %collective-permute-start.4 = (f32[6,16,128]{2,1,0:T(8,128)S(1)}, f32[6,16,128]{2,1,0:T(8,128)S(1)}, u32[]{:S(2)}, u32[]{:S(2)}) collective-permute-start(f32[6,16,128]{2,1,0:T(8,128)S(1)} %get-tuple-element.40), channel_id=1, source_target_pairs={{0,28},{4,8},{8,4},{12,16},{16,12},{20,24},{24,20},{28,0},{1,29},{... | collective-permute-start | bytes 147464 | tf_op jit(solution)/shard_map/ppermute | solution.py:469
  11.7 4.7 %collective-permute-done.5.straight = f32[6,16,128]{2,1,0:T(8,128)S(1)} collective-permute-done((f32[6,16,128]{2,1,0:T(8,128)S(1)}, f32[6,16,128]{2,1,0:T(8,128)S(1)}, u32[]{:S(2)}, u32[]{:S(2)}) %collective-permute-start.5) | collective-permute-done | bytes 49184 | tf_op jit(solution)/shard_map/ppermute | solution.py:470
  16.4 2.2 %collective-permute-done.4.slanted = f32[6,16,128]{2,1,0:T(8,128)S(1)} collective-permute-done((f32[6,16,128]{2,1,0:T(8,128)S(1)}, f32[6,16,128]{2,1,0:T(8,128)S(1)}, u32[]{:S(2)}, u32[]{:S(2)}) %collective-permute-start.4) | collective-permute-done | bytes 49184 | tf_op jit(solution)/shard_map/ppermute | solution.py:469
  20.6 5.2 %collective-permute-done.8.rest_3_ = f32[24,16,128]{2,1,0:T(8,128)S(1)} collective-permute-done((f32[24,16,128]{2,1,0:T(8,128)S(1)}, f32[24,16,128]{2,1,0:T(8,128)S(1)}, u32[]{:S(2)}, u32[]{:S(2)}) %collective-permute-start.8) | collective-permute-done | bytes 196640 | tf_op jit(solution)/shard_map/ppermute | solution.py:480
  25.9 4.2 %collective-permute-done.7.rest_2_ = f32[24,16,128]{2,1,0:T(8,128)S(1)} collective-permute-done((f32[24,16,128]{2,1,0:T(8,128)S(1)}, f32[24,16,128]{2,1,0:T(8,128)S(1)}, u32[]{:S(2)}, u32[]{:S(2)}) %collective-permute-start.7) | collective-permute-done | bytes 196640 | tf_op jit(solution)/shard_map/ppermute | solution.py:480
  30.1 2.1 %collective-permute-start.2 = (f32[9,64,128]{2,1,0:T(8,128)S(1)}, f32[9,64,128]{2,1,0:T(8,128)S(1)}, u32[]{:S(2)}, u32[]{:S(2)}) collective-permute-start(f32[9,64,128]{2,1,0:T(8,128)S(1)} %get-tuple-element.38), channel_id=1, source_target_pairs={{0,24},{4,12},{8,0},{12,20},{16,8},{20,28},{24,16},{28,4},{1,25},{... | collective-permute-start | bytes 884744 | tf_op jit(solution)/shard_map/ppermute | solution.py:487
  33.6 2.0 %collective-permute-start.17 = (f32[9,64,128]{2,1,0:T(8,128)S(1)}, f32[9,64,128]{2,1,0:T(8,128)S(1)}, u32[]{:S(2)}, u32[]{:S(2)}) collective-permute-start(f32[9,64,128]{2,1,0:T(8,128)S(1)} %get-tuple-element.49), channel_id=1, source_target_pairs={{0,24},{4,12},{8,0},{12,20},{16,8},{20,28},{24,16},{28,4},{1,25},{... | collective-permute-start | bytes 884744 | tf_op jit(solution)/shard_map/ppermute | solution.py:487
  35.8 4.2 %collective-permute-done.2.straight = f32[9,64,128]{2,1,0:T(8,128)S(1)} collective-permute-done((f32[9,64,128]{2,1,0:T(8,128)S(1)}, f32[9,64,128]{2,1,0:T(8,128)S(1)}, u32[]{:S(2)}, u32[]{:S(2)}) %collective-permute-start.2) | collective-permute-done | bytes 294944 | tf_op jit(solution)/shard_map/ppermute | solution.py:487
  40.0 4.7 %shard_map.30 = (f32[12,16,128]{2,1,0:T(8,128)S(1)}, f32[12,16,128]{2,1,0:T(8,128)S(1)}, f32[12,16,128]{2,1,0:T(8,128)S(1)}, f32[12,16,128]{2,1,0:T(8,128)S(1)},...) custom-call(s32[3]{0:T(128)S(1)} %pad_add_fusion.place, ...), custom_call_target="tpu_custom_call" | custom-call | tf_op jit(solution)/shard_map/pallas_call | solution.py:200
  45.8 2.0 %collective-permute-done.16.slanted = f32[9,64,128]{2,1,0:T(8,128)S(1)} collective-permute-done((f32[9,64,128]{2,1,0:T(8,128)S(1)}, f32[9,64,128]{2,1,0:T(8,128)S(1)}, u32[]{:S(2)}, u32[]{:S(2)}) %collective-permute-start.16) | collective-permute-done | bytes 294944 | tf_op jit(solution)/shard_map/ppermute | solution.py:486
  48.3 3.4 %collective-permute-done.17.straight = f32[9,64,128]{2,1,0:T(8,128)S(1)} collective-permute-done((f32[9,64,128]{2,1,0:T(8,128)S(1)}, f32[9,64,128]{2,1,0:T(8,128)S(1)}, u32[]{:S(2)}, u32[]{:S(2)}) %collective-permute-start.17) | collective-permute-done | bytes 294944 | tf_op jit(solution)/shard_map/ppermute | solution.py:487
  54.1 5.7 %shard_map.31 = (f32[12,16,128]{2,1,0:T(8,128)S(1)}, f32[12,16,128]{2,1,0:T(8,128)S(1)}, f32[12,16,128]{2,1,0:T(8,128)S(1)}, f32[12,16,128]{2,1,0:T(8,128)S(1)},...) custom-call(s32[3]{0:T(128)S(1)} %pad_add_fusion.place, ...), custom_call_target="tpu_custom_call" | custom-call | tf_op jit(solution)/shard_map/pallas_call | solution.py:200
  59.7 2.9 %collective-permute-start.18 = (f32[12,16,128]{2,1,0:T(8,128)S(1)}, f32[12,16,128]{2,1,0:T(8,128)S(1)}, u32[]{:S(2)}, u32[]{:S(2)}) collective-permute-start(f32[12,16,128]{2,1,0:T(8,128)S(1)} %get-tuple-element.51), channel_id=1, source_target_pairs={{0,6},{4,2},{1,7},{5,3},{2,4},{6,0},{3,5},{7,1},{8,14},{12,10},{9,... | collective-permute-start | bytes 294920 | tf_op jit(solution)/shard_map/ppermute | solution.py:497
  69.7 2.0 %collective-permute-done.20.refs_8_ = f32[12,16,128]{2,1,0:T(8,128)S(1)} collective-permute-done((f32[12,16,128]{2,1,0:T(8,128)S(1)}, f32[12,16,128]{2,1,0:T(8,128)S(1)}, u32[]{:S(2)}, u32[]{:S(2)}) %collective-permute-start.20) | collective-permute-done | bytes 98336 | tf_op jit(solution)/shard_map/ppermute | solution.py:497
  73.9 2.1 %shard_map.32 = (f32[16,192,128]{2,1,0:T(8,128)S(1)}, f32[32,1,256]{2,1,0:T(1,128)S(1)}, f32[2,2,12,16,128]{4,3,2,1,0:T(8,128)S(1)}) custom-call(s32[3]{0:T(128)S(1)} %pad_add_fusion.place, f32[12,16,128]{2,1,0:T(8,128)S(1)} %collective-permute-done.9.refs_0_, f32[12,16,128]{2,1,0:T(8,128)S(1)} %collective-permute-done.10.refs_1_, ...), custom_call_target="tpu_custom_call" | custom-call | tf_op jit(solution)/shard_map/pallas_call | solution.py:436
  79.8 8.2 %collective-permute-done.26.refs_1_ = f32[2,2,12,16,128]{4,3,2,1,0:T(8,128)S(1)} collective-permute-done((f32[2,2,12,16,128]{4,3,2,1,0:T(8,128)S(1)}, f32[2,2,12,16,128]{4,3,2,1,0:T(8,128)S(1)}, u32[]{:S(2)}, u32[]{:S(2)}) %collective-permute-start.26) | collective-permute-done | bytes 393248 | tf_op jit(solution)/shard_map/ppermute | solution.py:540
  89.8 7.6 %collective-permute-done.28.refs_3_ = f32[2,2,12,16,128]{4,3,2,1,0:T(8,128)S(1)} collective-permute-done((f32[2,2,12,16,128]{4,3,2,1,0:T(8,128)S(1)}, f32[2,2,12,16,128]{4,3,2,1,0:T(8,128)S(1)}, u32[]{:S(2)}, u32[]{:S(2)}) %collective-permute-start.28) | collective-permute-done | bytes 393248 | tf_op jit(solution)/shard_map/ppermute | solution.py:543
  97.4 10.6 %all_to_all.10.copies = f32[32,1,256]{2,1,0:T(1,128)S(1)} all-to-all(f32[32,1,256]{2,1,0:T(1,128)S(1)} %get-tuple-element.59), channel_id=1, replica_groups=mesh['pair'=4,'side'=2,'orb'=4] {'pair','side','orb'}, dimensions={0} | all-to-all | bytes 65536 | tf_op jit(solution)/shard_map/all_to_all | solution.py:525
  108.0 3.4 %shard_map.33 = (f32[16,128]{1,0:T(8,128)S(1)}, f32[32,1,256]{2,1,0:T(1,128)S(1)}) custom-call(f32[32,1,256]{2,1,0:T(1,128)S(1)} %all_to_all.10.copies, f32[16,192,128]{2,1,0:T(8,128)S(1)} %get-tuple-element.60.block), custom_call_target="tpu_custom_call" | custom-call | tf_op jit(solution)/shard_map/pallas_call | solution.py:549
  111.4 9.0 %all_to_all.11.copies = f32[32,1,256]{2,1,0:T(1,128)S(1)} all-to-all(f32[32,1,256]{2,1,0:T(1,128)S(1)} %get-tuple-element.61), channel_id=1, replica_groups=mesh['pair'=4,'side'=2,'orb'=4] {'pair','side','orb'}, dimensions={0} | all-to-all | bytes 65536 | tf_op jit(solution)/shard_map/all_to_all | solution.py:525
  120.4 6.9 %shard_map.34 = f32[4,12,64,128]{3,2,1,0:T(8,128)} custom-call(s32[3]{0:T(128)S(1)} %pad_add_fusion.place, f32[32,1,256]{2,1,0:T(1,128)S(1)} %all_to_all.11.copies, f32[16,128]{1,0:T(8,128)S(1)} %get-tuple-element.62.table, f32[16,192,128]{2,1,0:T(8,128)S(1)} %get-tuple-element.60.block, f32[16,192,128]{2,1,0:T(8,128)S(1)} %collective-permute-done.25.block_near, ...), custom_call_target="tpu_custom_call" | custom-call | tf_op jit(solution)/shard_map/pallas_call | solution.py:557
  (57 shorter events, 22.7 us)
Async XLA Ops:
  2.3 16.3 %collective-permute-start.3 = (f32[12,16,128]{2,1,0:T(8,128)S(1)}, f32[12,16,128]{2,1,0:T(8,128)S(1)}, u32[]{:S(2)}, u32[]{:S(2)}) collective-permute-start(f32[12,16,128]{2,1,0:T(8,128)S(1)} %get-tuple-element.39), channel_id=1, source_target_pairs={{0,4},{4,0},{1,5},{5,1},{2,6},{6,2},{3,7},{7,3},{8,12},{12,8},{9,1... | collective-permute-start | bytes 294920 | tf_op jit(solution)/shard_map/ppermute | solution.py:468
  5.4 28.3 %collective-permute-start.1 = (f32[9,64,128]{2,1,0:T(8,128)S(1)}, f32[9,64,128]{2,1,0:T(8,128)S(1)}, u32[]{:S(2)}, u32[]{:S(2)}) collective-permute-start(f32[9,64,128]{2,1,0:T(8,128)S(1)} %get-tuple-element.37), channel_id=1, source_target_pairs={{0,28},{4,8},{8,4},{12,16},{16,12},{20,24},{24,20},{28,0},{1,29},{... | collective-permute-start | bytes 884744 | tf_op jit(solution)/shard_map/ppermute | solution.py:486
  9.3 9.3 %collective-permute-start.4 = (f32[6,16,128]{2,1,0:T(8,128)S(1)}, f32[6,16,128]{2,1,0:T(8,128)S(1)}, u32[]{:S(2)}, u32[]{:S(2)}) collective-permute-start(f32[6,16,128]{2,1,0:T(8,128)S(1)} %get-tuple-element.40), channel_id=1, source_target_pairs={{0,28},{4,8},{8,4},{12,16},{16,12},{20,24},{24,20},{28,0},{1,29},{... | collective-permute-start | bytes 147464 | tf_op jit(solution)/shard_map/ppermute | solution.py:469
  18.7 11.4 %collective-permute-start.7 = (f32[24,16,128]{2,1,0:T(8,128)S(1)}, f32[24,16,128]{2,1,0:T(8,128)S(1)}, u32[]{:S(2)}, u32[]{:S(2)}) collective-permute-start(f32[24,16,128]{2,1,0:T(8,128)S(1)} %shard_map.29.rest_0_), channel_id=1, source_target_pairs={{0,2},{1,3},{2,0},{3,1},{4,6},{5,7},{6,4},{7,5},{8,10},{9,11},{10,... | collective-permute-start | bytes 589832 | tf_op jit(solution)/shard_map/ppermute | solution.py:480
  20.3 11.9 %collective-permute-start.6 = (f32[24,16,128]{2,1,0:T(8,128)S(1)}, f32[24,16,128]{2,1,0:T(8,128)S(1)}, u32[]{:S(2)}, u32[]{:S(2)}) collective-permute-start(f32[24,16,128]{2,1,0:T(8,128)S(1)} %shard_map.29.rest_0_), channel_id=1, source_target_pairs={{0,1},{1,0},{2,3},{3,2},{4,5},{5,4},{6,7},{7,6},{8,9},{9,8},{10,11... | collective-permute-start | bytes 589832 | tf_op jit(solution)/shard_map/ppermute | solution.py:480
  20.5 19.4 %collective-permute-start = (f32[12,64,128]{2,1,0:T(8,128)S(1)}, f32[12,64,128]{2,1,0:T(8,128)S(1)}, u32[]{:S(2)}, u32[]{:S(2)}) collective-permute-start(f32[12,64,128]{2,1,0:T(8,128)S(1)} %get-tuple-element.36), channel_id=1, source_target_pairs={{0,4},{4,0},{1,5},{5,1},{2,6},{6,2},{3,7},{7,3},{8,12},{12,8},{9,1... | collective-permute-start | bytes 1179656 | tf_op jit(solution)/shard_map/ppermute | solution.py:485
  25.8 26.2 %collective-permute-start.15 = (f32[12,64,128]{2,1,0:T(8,128)S(1)}, f32[12,64,128]{2,1,0:T(8,128)S(1)}, u32[]{:S(2)}, u32[]{:S(2)}) collective-permute-start(f32[12,64,128]{2,1,0:T(8,128)S(1)} %get-tuple-element.47), channel_id=1, source_target_pairs={{0,4},{4,0},{1,5},{5,1},{2,6},{6,2},{3,7},{7,3},{8,12},{12,8},{9,1... | collective-permute-start | bytes 1179656 | tf_op jit(solution)/shard_map/ppermute | solution.py:485
  30.1 9.9 %collective-permute-start.2 = (f32[9,64,128]{2,1,0:T(8,128)S(1)}, f32[9,64,128]{2,1,0:T(8,128)S(1)}, u32[]{:S(2)}, u32[]{:S(2)}) collective-permute-start(f32[9,64,128]{2,1,0:T(8,128)S(1)} %get-tuple-element.38), channel_id=1, source_target_pairs={{0,24},{4,12},{8,0},{12,20},{16,8},{20,28},{24,16},{28,4},{1,25},{... | collective-permute-start | bytes 884744 | tf_op jit(solution)/shard_map/ppermute | solution.py:487
  32.2 15.6 %collective-permute-start.16 = (f32[9,64,128]{2,1,0:T(8,128)S(1)}, f32[9,64,128]{2,1,0:T(8,128)S(1)}, u32[]{:S(2)}, u32[]{:S(2)}) collective-permute-start(f32[9,64,128]{2,1,0:T(8,128)S(1)} %get-tuple-element.48), channel_id=1, source_target_pairs={{0,28},{4,8},{8,4},{12,16},{16,12},{20,24},{24,20},{28,0},{1,29},{... | collective-permute-start | bytes 884744 | tf_op jit(solution)/shard_map/ppermute | solution.py:486
  33.6 18.1 %collective-permute-start.17 = (f32[9,64,128]{2,1,0:T(8,128)S(1)}, f32[9,64,128]{2,1,0:T(8,128)S(1)}, u32[]{:S(2)}, u32[]{:S(2)}) collective-permute-start(f32[9,64,128]{2,1,0:T(8,128)S(1)} %get-tuple-element.49), channel_id=1, source_target_pairs={{0,24},{4,12},{8,0},{12,20},{16,8},{20,28},{24,16},{28,4},{1,25},{... | collective-permute-start | bytes 884744 | tf_op jit(solution)/shard_map/ppermute | solution.py:487
  44.7 15.0 %collective-permute-start.9 = (f32[12,16,128]{2,1,0:T(8,128)S(1)}, f32[12,16,128]{2,1,0:T(8,128)S(1)}, u32[]{:S(2)}, u32[]{:S(2)}) collective-permute-start(f32[12,16,128]{2,1,0:T(8,128)S(1)} %get-tuple-element.41), channel_id=1, source_target_pairs={{0,6},{4,2},{1,7},{5,3},{2,4},{6,0},{3,5},{7,1},{8,14},{12,10},{9,... | collective-permute-start | bytes 294920 | tf_op jit(solution)/shard_map/ppermute | solution.py:497
  45.5 14.2 %collective-permute-start.10 = (f32[12,16,128]{2,1,0:T(8,128)S(1)}, f32[12,16,128]{2,1,0:T(8,128)S(1)}, u32[]{:S(2)}, u32[]{:S(2)}) collective-permute-start(f32[12,16,128]{2,1,0:T(8,128)S(1)} %get-tuple-element.42), channel_id=1, source_target_pairs={{0,7},{4,3},{1,6},{5,2},{2,5},{6,1},{3,4},{7,0},{8,15},{12,11},{9,... | collective-permute-start | bytes 294920 | tf_op jit(solution)/shard_map/ppermute | solution.py:497
  47.8 14.8 %collective-permute-start.11 = (f32[12,16,128]{2,1,0:T(8,128)S(1)}, f32[12,16,128]{2,1,0:T(8,128)S(1)}, u32[]{:S(2)}, u32[]{:S(2)}) collective-permute-start(f32[12,16,128]{2,1,0:T(8,128)S(1)} %get-tuple-element.43), channel_id=1, source_target_pairs={{0,2},{4,6},{1,3},{5,7},{2,0},{6,4},{3,1},{7,5},{8,10},{12,14},{9,... | collective-permute-start | bytes 294920 | tf_op jit(solution)/shard_map/ppermute | solution.py:497
  51.7 10.9 %collective-permute-start.12 = (f32[12,16,128]{2,1,0:T(8,128)S(1)}, f32[12,16,128]{2,1,0:T(8,128)S(1)}, u32[]{:S(2)}, u32[]{:S(2)}) collective-permute-start(f32[12,16,128]{2,1,0:T(8,128)S(1)} %get-tuple-element.44), channel_id=1, source_target_pairs={{0,3},{4,7},{1,2},{5,6},{2,1},{6,5},{3,0},{7,4},{8,11},{12,15},{9,... | collective-permute-start | bytes 294920 | tf_op jit(solution)/shard_map/ppermute | solution.py:497
  52.1 10.8 %collective-permute-start.13 = (f32[12,16,128]{2,1,0:T(8,128)S(1)}, f32[12,16,128]{2,1,0:T(8,128)S(1)}, u32[]{:S(2)}, u32[]{:S(2)}) collective-permute-start(f32[12,16,128]{2,1,0:T(8,128)S(1)} %get-tuple-element.45), channel_id=1, source_target_pairs={{0,4},{4,0},{1,5},{5,1},{2,6},{6,2},{3,7},{7,3},{8,12},{12,8},{9,1... | collective-permute-start | bytes 294920 | tf_op jit(solution)/shard_map/ppermute | solution.py:497
  62.7 11.2 %collective-permute-start.24 = (f32[2,12,16,128]{3,2,1,0:T(8,128)S(1)}, f32[2,12,16,128]{3,2,1,0:T(8,128)S(1)}, u32[]{:S(2)}, u32[]{:S(2)}) collective-permute-start(f32[2,12,16,128]{3,2,1,0:T(8,128)S(1)} %get-tuple-element.58), channel_id=1, source_target_pairs={{0,1},{4,5},{1,0},{5,4},{2,3},{6,7},{3,2},{7,6},{8,9},{12,13},{9,8... | collective-permute-start | bytes 589832 | tf_op jit(solution)/shard_map/ppermute | solution.py:497
  76.0 44.4 %collective-permute-start.25 = (f32[16,192,128]{2,1,0:T(8,128)S(1)}, f32[16,192,128]{2,1,0:T(8,128)S(1)}, u32[]{:S(2)}, u32[]{:S(2)}) collective-permute-start(f32[16,192,128]{2,1,0:T(8,128)S(1)} %get-tuple-element.60.block), channel_id=1, source_target_pairs={{0,1},{1,0},{2,3},{3,2},{4,5},{5,4},{6,7},{7,6},{8,9},{9,8},{10,11... | collective-permute-start | bytes 4718600 | tf_op jit(solution)/shard_map/ppermute | solution.py:544
  77.0 11.1 %collective-permute-start.26 = (f32[2,2,12,16,128]{4,3,2,1,0:T(8,128)S(1)}, f32[2,2,12,16,128]{4,3,2,1,0:T(8,128)S(1)}, u32[]{:S(2)}, u32[]{:S(2)}) collective-permute-start(f32[2,2,12,16,128]{4,3,2,1,0:T(8,128)S(1)} %get-tuple-element.64), channel_id=1, source_target_pairs={{0,4},{4,0},{1,5},{5,1},{2,6},{6,2},{3,7},{7,3},{8,12},{12,8},{9,1... | collective-permute-start | bytes 1179656 | tf_op jit(solution)/shard_map/ppermute | solution.py:540
  77.8 12.0 %collective-permute-start.27 = (f32[2,2,12,16,128]{4,3,2,1,0:T(8,128)S(1)}, f32[2,2,12,16,128]{4,3,2,1,0:T(8,128)S(1)}, u32[]{:S(2)}, u32[]{:S(2)}) collective-permute-start(f32[2,2,12,16,128]{4,3,2,1,0:T(8,128)S(1)} %get-tuple-element.65), channel_id=1, source_target_pairs={{0,2},{1,3},{2,0},{3,1},{4,6},{5,7},{6,4},{7,5},{8,10},{9,11},{10,... | collective-permute-start | bytes 1179656 | tf_op jit(solution)/shard_map/ppermute | solution.py:541
  78.4 19.0 %collective-permute-start.28 = (f32[2,2,12,16,128]{4,3,2,1,0:T(8,128)S(1)}, f32[2,2,12,16,128]{4,3,2,1,0:T(8,128)S(1)}, u32[]{:S(2)}, u32[]{:S(2)}) collective-permute-start(f32[2,2,12,16,128]{4,3,2,1,0:T(8,128)S(1)} %get-tuple-element.66), channel_id=1, source_target_pairs={{0,2},{1,3},{2,0},{3,1},{4,6},{5,7},{6,4},{7,5},{8,10},{9,11},{10,... | collective-permute-start | bytes 1179656 | tf_op jit(solution)/shard_map/ppermute | solution.py:543
  79.8 40.5 %collective-permute-start.29 = (f32[2,2,12,16,128]{4,3,2,1,0:T(8,128)S(1)}, f32[2,2,12,16,128]{4,3,2,1,0:T(8,128)S(1)}, u32[]{:S(2)}, u32[]{:S(2)}) collective-permute-start(f32[2,2,12,16,128]{4,3,2,1,0:T(8,128)S(1)} %get-tuple-element.63.refs_0_), channel_id=1, source_target_pairs={{0,1},{1,0},{2,3},{3,2},{4,5},{5,4},{6,7},{7,6},{8,9},{9,8},{10,11... | collective-permute-start | bytes 1179656 | tf_op jit(solution)/shard_map/ppermute | solution.py:546
  88.1 32.3 %collective-permute-start.30 = (f32[2,2,12,16,128]{4,3,2,1,0:T(8,128)S(1)}, f32[2,2,12,16,128]{4,3,2,1,0:T(8,128)S(1)}, u32[]{:S(2)}, u32[]{:S(2)}) collective-permute-start(f32[2,2,12,16,128]{4,3,2,1,0:T(8,128)S(1)} %collective-permute-done.26.refs_1_), channel_id=1, source_target_pairs={{0,1},{1,0},{2,3},{3,2},{4,5},{5,4},{6,7},{7,6},{8,9},{9,8},{10,11... | collective-permute-start | bytes 1179656 | tf_op jit(solution)/shard_map/ppermute | solution.py:546
  89.8 30.6 %collective-permute-start.31 = (f32[2,2,12,16,128]{4,3,2,1,0:T(8,128)S(1)}, f32[2,2,12,16,128]{4,3,2,1,0:T(8,128)S(1)}, u32[]{:S(2)}, u32[]{:S(2)}) collective-permute-start(f32[2,2,12,16,128]{4,3,2,1,0:T(8,128)S(1)} %collective-permute-done.27.refs_2_), channel_id=1, source_target_pairs={{0,1},{1,0},{2,3},{3,2},{4,5},{5,4},{6,7},{7,6},{8,9},{9,8},{10,11... | collective-permute-start | bytes 1179656 | tf_op jit(solution)/shard_map/ppermute | solution.py:546
  97.4 23.0 %collective-permute-start.32 = (f32[2,2,12,16,128]{4,3,2,1,0:T(8,128)S(1)}, f32[2,2,12,16,128]{4,3,2,1,0:T(8,128)S(1)}, u32[]{:S(2)}, u32[]{:S(2)}) collective-permute-start(f32[2,2,12,16,128]{4,3,2,1,0:T(8,128)S(1)} %collective-permute-done.28.refs_3_), channel_id=1, source_target_pairs={{0,1},{1,0},{2,3},{3,2},{4,5},{5,4},{6,7},{7,6},{8,9},{9,8},{10,11... | collective-permute-start | bytes 1179656 | tf_op jit(solution)/shard_map/ppermute | solution.py:547
  (11 other events, 142.5 us)

commit v13 on v12

--- a/solution.py
+++ b/solution.py
@@ -87,8 +87,8 @@
     )
 
 
-def filter_kernel(at, shares, early, late, place, own, swapped, slanted, straight, own_pot, lane_table, *rest):
-    pot_far, before, outs = rest[:shares], rest[shares : shares + at], rest[shares + at : -4]
+def filter_kernel(at, shares, early, place, own, swapped, slanted, straight, own_pot, lane_table, *rest):
+    pot_far, outs = rest[:shares], rest[shares:-4]
     field, first, second, weight = rest[-4:]
     outs, sorted_pieces = outs[:-1], outs[-1]
     side, me, orb = place[0], place[1], place[2]
@@ -170,19 +170,21 @@
     step(second, first, 2 * REACH, 2 * REACH, both, store_out)
     for apart, out in zip(early, outs):
         out[...] = sorted_pieces[me ^ apart]
-    stages = (*before, sorted_pieces)
-    for apart, out in zip(late, outs[len(early) :]):
-        for stage, pieces in enumerate(stages):
+
+
+def late_kernel(stages, late, place, *refs):
+    given, outs = refs[:stages], refs[stages:]
+    side, me, orb = place[0], place[1], place[2]
+    for stage, pieces in enumerate(given):
+        for apart, out in zip(late, outs):
             out[stage] = pieces[me ^ apart]
-    for index, out in enumerate(outs[len(early) + len(late) :]):
-        chip = orb // CORES ^ (1 if index < 2 else 0)
-        slab = side ^ (index % 2)
-        for stage, pieces in enumerate(stages):
+        for index, out in enumerate(outs[len(late) :]):
+            chip = orb // CORES ^ (1 if index < 2 else 0)
             for core in range(CORES):
-                out[stage, core] = pieces[2 * (CORES * chip + core) + slab]
-
-
-def filtered_pieces(at, place, own, fetched, own_pot, pot_far, group, before, early, late, spares):
+                out[stage, core] = pieces[2 * (CORES * chip + core) + (side ^ (index % 2))]
+
+
+def filtered_pieces(at, place, own, fetched, own_pot, pot_far, group, early):
     slanted, swapped, straight = fetched
     rows, cols, width = own.shape[1:]
     both = 2 * rows
@@ -196,11 +198,11 @@
         return pltpu.VMEM((both + 2 * margin, cols + 2 * EIGHT, width), jnp.float32)
 
     piece = (rows, 2 * cols // group, width)
-    shapes = [piece] * len(early) + [(at + 1, *piece)] * len(late) + [(at + 1, CORES, *piece)] * spares + [(group, *piece)]
+    shapes = [piece] * len(early) + [(group, *piece)]
     return pl.pallas_call(
-        functools.partial(filter_kernel, at, len(pot_far), early, late),
+        functools.partial(filter_kernel, at, len(pot_far), early),
         out_shape=[jax.ShapeDtypeStruct(shape, jnp.float32) for shape in shapes],
-        in_specs=[SMEM] + [VMEM] * (6 + len(pot_far) + at),
+        in_specs=[SMEM] + [VMEM] * (6 + len(pot_far)),
         out_specs=[VMEM] * len(shapes),
         scratch_shapes=[
             scratch(DEEP),
@@ -209,7 +211,7 @@
             pltpu.VMEM((both + 2 * WIDE, cols, width), jnp.float32),
         ],
         compiler_params=pltpu.CompilerParams(vmem_limit_bytes=24 * 1024 * 1024),
-    )(place, own, swapped, slanted, straight, own_pot, lane_table.astype(jnp.bfloat16), *pot_far, *before)
+    )(place, own, swapped, slanted, straight, own_pot, lane_table.astype(jnp.bfloat16), *pot_far)
 
 
 LANES = 128
@@ -299,13 +301,15 @@
     return jnp.concatenate(tiles, axis=1)
 
 
-def first_kernel(early, late, kept, forwards, place, *refs):
-    outs = 2 + len(forwards[:1])
-    given, (block, message, *forward) = refs[:-outs], refs[-outs:]
-    if forward:
-        for slot, apart in enumerate(forwards):
-            for at in range(kept):
-                forward[0][slot, at] = given[at * len(early) + early.index(apart)][...]
+def forward_kernel(place, block, out):
+    kept, held = out.shape[1], 2 * out.shape[1]
+    for flip in range(CORES):
+        for at in range(kept):
+            out[flip, at] = block[(place[2] ^ flip) * held + (place[0] ^ 1) * kept + at].reshape(out.shape[2:])
+
+
+def first_kernel(early, late, kept, place, *refs):
+    given, (block, message) = refs[:-2], refs[-2:]
     me, shape = place[1], block.shape[1:]
     for at in range(kept):
         for index, apart in enumerate(early):
@@ -496,26 +500,21 @@
             return piece
         return lax.ppermute(piece, ("side", "orb"), [(flat_of(i), flat_of(i ^ m)) for i in range(group)])
 
-    parts, before = [], []
+    parts, stages = [], []
     for at in range(kept):
-        final = at == kept - 1
-        outs = filtered_pieces(
-            at,
-            place,
-            orbitals,
-            fetched[at],
-            potential,
-            pot_far,
-            group,
-            before,
-            early,
-            late if final else (),
-            spares if final else 0,
-        )
+        *outs, pieces = filtered_pieces(at, place, orbitals, fetched[at], potential, pot_far, group, early)
         parts += [to_partner(piece, m) for piece, m in zip(outs, early)]
-        before.append(outs[-1])
-    parts += [to_partner(piece, m) for piece, m in zip(outs[len(early) :], late)]
-    spare = outs[len(early) + len(late) : -1]
+        stages.append(pieces)
+    piece = (rows, part, width)
+    shapes = [(kept, *piece)] * len(late) + [(kept, CORES, *piece)] * spares
+    outs = small_call(
+        functools.partial(late_kernel, kept, late),
+        [jax.ShapeDtypeStruct(shape, jnp.float32) for shape in shapes],
+        [SMEM] + [VMEM] * kept,
+        *(place, *stages),
+    )
+    parts += [to_partner(piece, m) for piece, m in zip(outs, late)]
+    spare = outs[len(late) :]
     total, devices = held * orb_count, slabs * orb_count
     cell_total = rows * part * width * devices
     block_shape = jax.ShapeDtypeStruct((total, rows * part, width), jnp.float32)
@@ -524,11 +523,9 @@
     def exchanged(message):
         return lax.all_to_all(message, ALL, 0, 0)
 
-    forwards = (1, 1 + CORES) if spares else ()
-    forward_shape = jax.ShapeDtypeStruct((CORES, kept, rows, part, width), jnp.float32)
-    block, message, *forward = small_call(
-        functools.partial(first_kernel, early, late, kept, forwards),
-        [block_shape, message_shape] + [forward_shape] * len(forwards[:1]),
+    block, message = small_call(
+        functools.partial(first_kernel, early, late, kept),
+        [block_shape, message_shape],
         [SMEM] + [VMEM] * len(parts),
         *(place, *parts),
     )
@@ -540,7 +537,10 @@
             lax.ppermute(spare[1], "side", swap),
             lax.ppermute(spare[2], "orb", across),
         ]
-        given.append(lax.ppermute(forward[0], "orb", across))
+        forward = small_call(
+            forward_kernel, jax.ShapeDtypeStruct((CORES, kept, rows, part, width), jnp.float32), [SMEM, VMEM], place, block
+        )
+        given.append(lax.ppermute(forward, "orb", across))
         block_near = lax.ppermute(block, "orb", cores)
         table_shape = jax.ShapeDtypeStruct((total, LANES), jnp.float32)
         near = [lax.ppermute(piece, "orb", cores) for piece in given[:-1]]

time: 127 us -> 127 us (level)
    pallas_call x1 -> x3, Pallas kernels: 2.14 us -> 3.35 us  [small_call(): pl.pallas_call(kernel, out_shape=out_shape, in_specs=specs, out_specs=jax...]
where the time goes in v13:
time: 127 us
  waiting for transfers between devices  49.4 us (39%)
  starting transfers between devices  32.6 us (26%)
  Pallas kernels  25.2 us (20%)
  blocking collectives  19.6 us (15%)
    all_to_all x2, blocking collectives, exchanged(): return lax.all_to_all(message, ALL, 0, 0)  19.6 us
    ppermute x13, starting transfers between devices, to_partner(): lax.ppermute(piece, ('side', 'orb'), [(flat_of(i), flat_of(i ^ m)) for i...  11.8 us
    ppermute x3, waiting for transfers between devices, whole(): lax.ppermute(joined, 'orb', [(i, i ^ m) for i in range(orb_count)])  9.47 us
    pallas_call x2, Pallas kernels, filtered_pieces(): pl.pallas_call(functools.partial(filter_kernel, at, len(pot_far), early),...  9.35 us
    ppermute x2, waiting for transfers between devices, whole(): straight = lax.ppermute(sent[3 * at + 2], slab_axes, ahead)  7.66 us
    ppermute x1, waiting for transfers between devices, whole(): given.append(lax.ppermute(forward, 'orb', across))  7.61 us
    ppermute x1, waiting for transfers between devices, whole(): lax.ppermute(spare[1], 'side', swap)  7.59 us
    pallas_call x1, Pallas kernels, whole(): pl.pallas_call(functools.partial(last_kernel, cell_total), out_shape=jax....  6.9 us
  transfers between devices with their start and end apart: 33, of which 15 were waited for; matrix products, arithmetic and copies ran while one was open for 0% of the time, Pallas kernels for 11%

profile of v13, /device:TPU:0, one launch (start us, length us, event | category | flops | bytes accessed | tf_op | source)
XLA Modules:
  0.0 127.0 jit_solution(3369964536800171359)
XLA Ops:
  0.1 2.2 %shard_map.28 = (f32[12,16,128]{2,1,0:T(8,128)S(1)}, f32[6,16,128]{2,1,0:T(8,128)S(1)}, f32[9,64,128]{2,1,0:T(8,128)S(1)}, f32[12,64,128]{2,1,0:T(8,128)S(1)}, f...) custom-call(s32[3]{0:T(128)S(1)} %pad_add_fusion.place, ...), custom_call_target="tpu_custom_call" | custom-call | tf_op jit(solution)/shard_map/pallas_call | solution.py:61
  2.3 3.1 %collective-permute-start.3 = (f32[12,16,128]{2,1,0:T(8,128)S(1)}, f32[12,16,128]{2,1,0:T(8,128)S(1)}, u32[]{:S(2)}, u32[]{:S(2)}) collective-permute-start(f32[12,16,128]{2,1,0:T(8,128)S(1)} %get-tuple-element.39), channel_id=1, source_target_pairs={{0,4},{4,0},{1,5},{5,1},{2,6},{6,2},{3,7},{7,3},{8,12},{12,8},{9,1... | collective-permute-start | bytes 294920 | tf_op jit(solution)/shard_map/ppermute | solution.py:472
  5.4 3.5 %collective-permute-start.1 = (f32[9,64,128]{2,1,0:T(8,128)S(1)}, f32[9,64,128]{2,1,0:T(8,128)S(1)}, u32[]{:S(2)}, u32[]{:S(2)}) collective-permute-start(f32[9,64,128]{2,1,0:T(8,128)S(1)} %get-tuple-element.37), channel_id=1, source_target_pairs={{0,28},{4,8},{8,4},{12,16},{16,12},{20,24},{24,20},{28,0},{1,29},{... | collective-permute-start | bytes 884744 | tf_op jit(solution)/shard_map/ppermute | solution.py:490
  9.3 2.4 %collective-permute-start.4 = (f32[6,16,128]{2,1,0:T(8,128)S(1)}, f32[6,16,128]{2,1,0:T(8,128)S(1)}, u32[]{:S(2)}, u32[]{:S(2)}) collective-permute-start(f32[6,16,128]{2,1,0:T(8,128)S(1)} %get-tuple-element.40), channel_id=1, source_target_pairs={{0,28},{4,8},{8,4},{12,16},{16,12},{20,24},{24,20},{28,0},{1,29},{... | collective-permute-start | bytes 147464 | tf_op jit(solution)/shard_map/ppermute | solution.py:473
  11.7 4.7 %collective-permute-done.5.straight = f32[6,16,128]{2,1,0:T(8,128)S(1)} collective-permute-done((f32[6,16,128]{2,1,0:T(8,128)S(1)}, f32[6,16,128]{2,1,0:T(8,128)S(1)}, u32[]{:S(2)}, u32[]{:S(2)}) %collective-permute-start.5) | collective-permute-done | bytes 49184 | tf_op jit(solution)/shard_map/ppermute | solution.py:474
  16.4 2.2 %collective-permute-done.4.slanted = f32[6,16,128]{2,1,0:T(8,128)S(1)} collective-permute-done((f32[6,16,128]{2,1,0:T(8,128)S(1)}, f32[6,16,128]{2,1,0:T(8,128)S(1)}, u32[]{:S(2)}, u32[]{:S(2)}) %collective-permute-start.4) | collective-permute-done | bytes 49184 | tf_op jit(solution)/shard_map/ppermute | solution.py:473
  20.6 5.2 %collective-permute-done.8.rest_3_ = f32[24,16,128]{2,1,0:T(8,128)S(1)} collective-permute-done((f32[24,16,128]{2,1,0:T(8,128)S(1)}, f32[24,16,128]{2,1,0:T(8,128)S(1)}, u32[]{:S(2)}, u32[]{:S(2)}) %collective-permute-start.8) | collective-permute-done | bytes 196640 | tf_op jit(solution)/shard_map/ppermute | solution.py:484
  25.9 4.2 %collective-permute-done.7.rest_2_ = f32[24,16,128]{2,1,0:T(8,128)S(1)} collective-permute-done((f32[24,16,128]{2,1,0:T(8,128)S(1)}, f32[24,16,128]{2,1,0:T(8,128)S(1)}, u32[]{:S(2)}, u32[]{:S(2)}) %collective-permute-start.7) | collective-permute-done | bytes 196640 | tf_op jit(solution)/shard_map/ppermute | solution.py:484
  30.1 2.1 %collective-permute-start.2 = (f32[9,64,128]{2,1,0:T(8,128)S(1)}, f32[9,64,128]{2,1,0:T(8,128)S(1)}, u32[]{:S(2)}, u32[]{:S(2)}) collective-permute-start(f32[9,64,128]{2,1,0:T(8,128)S(1)} %get-tuple-element.38), channel_id=1, source_target_pairs={{0,24},{4,12},{8,0},{12,20},{16,8},{20,28},{24,16},{28,4},{1,25},{... | collective-permute-start | bytes 884744 | tf_op jit(solution)/shard_map/ppermute | solution.py:491
  33.6 2.0 %collective-permute-start.17 = (f32[9,64,128]{2,1,0:T(8,128)S(1)}, f32[9,64,128]{2,1,0:T(8,128)S(1)}, u32[]{:S(2)}, u32[]{:S(2)}) collective-permute-start(f32[9,64,128]{2,1,0:T(8,128)S(1)} %get-tuple-element.49), channel_id=1, source_target_pairs={{0,24},{4,12},{8,0},{12,20},{16,8},{20,28},{24,16},{28,4},{1,25},{... | collective-permute-start | bytes 884744 | tf_op jit(solution)/shard_map/ppermute | solution.py:491
  35.8 4.2 %collective-permute-done.2.straight = f32[9,64,128]{2,1,0:T(8,128)S(1)} collective-permute-done((f32[9,64,128]{2,1,0:T(8,128)S(1)}, f32[9,64,128]{2,1,0:T(8,128)S(1)}, u32[]{:S(2)}, u32[]{:S(2)}) %collective-permute-start.2) | collective-permute-done | bytes 294944 | tf_op jit(solution)/shard_map/ppermute | solution.py:491
  40.0 4.7 %shard_map.30 = (f32[12,16,128]{2,1,0:T(8,128)S(1)}, f32[12,16,128]{2,1,0:T(8,128)S(1)}, f32[12,16,128]{2,1,0:T(8,128)S(1)}, f32[12,16,128]{2,1,0:T(8,128)S(1)},...) custom-call(s32[3]{0:T(128)S(1)} %pad_add_fusion.place, ...), custom_call_target="tpu_custom_call" | custom-call | tf_op jit(solution)/shard_map/pallas_call | solution.py:202
  45.8 2.0 %collective-permute-done.16.slanted = f32[9,64,128]{2,1,0:T(8,128)S(1)} collective-permute-done((f32[9,64,128]{2,1,0:T(8,128)S(1)}, f32[9,64,128]{2,1,0:T(8,128)S(1)}, u32[]{:S(2)}, u32[]{:S(2)}) %collective-permute-start.16) | collective-permute-done | bytes 294944 | tf_op jit(solution)/shard_map/ppermute | solution.py:490
  48.3 3.4 %collective-permute-done.17.straight = f32[9,64,128]{2,1,0:T(8,128)S(1)} collective-permute-done((f32[9,64,128]{2,1,0:T(8,128)S(1)}, f32[9,64,128]{2,1,0:T(8,128)S(1)}, u32[]{:S(2)}, u32[]{:S(2)}) %collective-permute-start.17) | collective-permute-done | bytes 294944 | tf_op jit(solution)/shard_map/ppermute | solution.py:491
  54.1 4.7 %shard_map.31 = (f32[12,16,128]{2,1,0:T(8,128)S(1)}, f32[12,16,128]{2,1,0:T(8,128)S(1)}, f32[12,16,128]{2,1,0:T(8,128)S(1)}, f32[12,16,128]{2,1,0:T(8,128)S(1)},...) custom-call(s32[3]{0:T(128)S(1)} %pad_add_fusion.place, ...), custom_call_target="tpu_custom_call" | custom-call | tf_op jit(solution)/shard_map/pallas_call | solution.py:202
  59.5 2.9 %collective-permute-start.18 = (f32[12,16,128]{2,1,0:T(8,128)S(1)}, f32[12,16,128]{2,1,0:T(8,128)S(1)}, u32[]{:S(2)}, u32[]{:S(2)}) collective-permute-start(f32[12,16,128]{2,1,0:T(8,128)S(1)} %get-tuple-element.50), channel_id=1, source_target_pairs={{0,6},{4,2},{1,7},{5,3},{2,4},{6,0},{3,5},{7,1},{8,14},{12,10},{9,... | collective-permute-start | bytes 294920 | tf_op jit(solution)/shard_map/ppermute | solution.py:501
  69.5 2.0 %collective-permute-done.20.refs_8_ = f32[12,16,128]{2,1,0:T(8,128)S(1)} collective-permute-done((f32[12,16,128]{2,1,0:T(8,128)S(1)}, f32[12,16,128]{2,1,0:T(8,128)S(1)}, u32[]{:S(2)}, u32[]{:S(2)}) %collective-permute-start.20) | collective-permute-done | bytes 98336 | tf_op jit(solution)/shard_map/ppermute | solution.py:501
  73.6 2.1 %shard_map.33 = (f32[16,192,128]{2,1,0:T(8,128)S(1)}, f32[32,1,256]{2,1,0:T(1,128)S(1)}) custom-call(s32[3]{0:T(128)S(1)} %pad_add_fusion.place, f32[12,16,128]{2,1,0:T(8,128)S(1)} %collective-permute-done.9.refs_0_, f32[12,16,128]{2,1,0:T(8,128)S(1)} %collective-permute-done.10.refs_1_, f32[12,16,128]{2,1,0:T(8,128)S(1)} %collective-permute-done.11.refs_2_, ...), custom_call_target="tpu_custom_call" | custom-call | tf_op jit(solution)/shard_map/pallas_call | solution.py:440
  80.2 7.6 %collective-permute-done.26.refs_1_ = f32[2,2,12,16,128]{4,3,2,1,0:T(8,128)S(1)} collective-permute-done((f32[2,2,12,16,128]{4,3,2,1,0:T(8,128)S(1)}, f32[2,2,12,16,128]{4,3,2,1,0:T(8,128)S(1)}, u32[]{:S(2)}, u32[]{:S(2)}) %collective-permute-start.26) | collective-permute-done | bytes 393248 | tf_op jit(solution)/shard_map/ppermute | solution.py:537
  89.5 7.6 %collective-permute-done.28.refs_3_ = f32[2,2,12,16,128]{4,3,2,1,0:T(8,128)S(1)} collective-permute-done((f32[2,2,12,16,128]{4,3,2,1,0:T(8,128)S(1)}, f32[2,2,12,16,128]{4,3,2,1,0:T(8,128)S(1)}, u32[]{:S(2)}, u32[]{:S(2)}) %collective-permute-start.28) | collective-permute-done | bytes 393248 | tf_op jit(solution)/shard_map/ppermute | solution.py:543
  97.1 10.6 %all_to_all.10.copies = f32[32,1,256]{2,1,0:T(1,128)S(1)} all-to-all(f32[32,1,256]{2,1,0:T(1,128)S(1)} %get-tuple-element.60), channel_id=1, replica_groups=mesh['pair'=4,'side'=2,'orb'=4] {'pair','side','orb'}, dimensions={0} | all-to-all | bytes 65536 | tf_op jit(solution)/shard_map/all_to_all | solution.py:524
  107.7 3.4 %shard_map.34 = (f32[16,128]{1,0:T(8,128)S(1)}, f32[32,1,256]{2,1,0:T(1,128)S(1)}) custom-call(f32[32,1,256]{2,1,0:T(1,128)S(1)} %all_to_all.10.copies, f32[16,192,128]{2,1,0:T(8,128)S(1)} %get-tuple-element.61.block), custom_call_target="tpu_custom_call" | custom-call | tf_op jit(solution)/shard_map/pallas_call | solution.py:549
  111.1 9.0 %all_to_all.11.copies = f32[32,1,256]{2,1,0:T(1,128)S(1)} all-to-all(f32[32,1,256]{2,1,0:T(1,128)S(1)} %get-tuple-element.62), channel_id=1, replica_groups=mesh['pair'=4,'side'=2,'orb'=4] {'pair','side','orb'}, dimensions={0} | all-to-all | bytes 65536 | tf_op jit(solution)/shard_map/all_to_all | solution.py:524
  120.1 6.9 %shard_map.36 = f32[4,12,64,128]{3,2,1,0:T(8,128)} custom-call(s32[3]{0:T(128)S(1)} %pad_add_fusion.place, f32[32,1,256]{2,1,0:T(1,128)S(1)} %all_to_all.11.copies, f32[16,128]{1,0:T(8,128)S(1)} %get-tuple-element.63.table, f32[16,192,128]{2,1,0:T(8,128)S(1)} %get-tuple-element.61.block, f32[16,192,128]{2,1,0:T(8,128)S(1)} %collective-permute-done.25.block_near, ...), custom_call_target="tpu_custom_call" | custom-call | tf_op jit(solution)/shard_map/pallas_call | solution.py:557
  (59 shorter events, 24.1 us)
Async XLA Ops:
  2.3 16.3 %collective-permute-start.3 = (f32[12,16,128]{2,1,0:T(8,128)S(1)}, f32[12,16,128]{2,1,0:T(8,128)S(1)}, u32[]{:S(2)}, u32[]{:S(2)}) collective-permute-start(f32[12,16,128]{2,1,0:T(8,128)S(1)} %get-tuple-element.39), channel_id=1, source_target_pairs={{0,4},{4,0},{1,5},{5,1},{2,6},{6,2},{3,7},{7,3},{8,12},{12,8},{9,1... | collective-permute-start | bytes 294920 | tf_op jit(solution)/shard_map/ppermute | solution.py:472
  5.4 28.3 %collective-permute-start.1 = (f32[9,64,128]{2,1,0:T(8,128)S(1)}, f32[9,64,128]{2,1,0:T(8,128)S(1)}, u32[]{:S(2)}, u32[]{:S(2)}) collective-permute-start(f32[9,64,128]{2,1,0:T(8,128)S(1)} %get-tuple-element.37), channel_id=1, source_target_pairs={{0,28},{4,8},{8,4},{12,16},{16,12},{20,24},{24,20},{28,0},{1,29},{... | collective-permute-start | bytes 884744 | tf_op jit(solution)/shard_map/ppermute | solution.py:490
  9.3 9.3 %collective-permute-start.4 = (f32[6,16,128]{2,1,0:T(8,128)S(1)}, f32[6,16,128]{2,1,0:T(8,128)S(1)}, u32[]{:S(2)}, u32[]{:S(2)}) collective-permute-start(f32[6,16,128]{2,1,0:T(8,128)S(1)} %get-tuple-element.40), channel_id=1, source_target_pairs={{0,28},{4,8},{8,4},{12,16},{16,12},{20,24},{24,20},{28,0},{1,29},{... | collective-permute-start | bytes 147464 | tf_op jit(solution)/shard_map/ppermute | solution.py:473
  18.7 11.4 %collective-permute-start.7 = (f32[24,16,128]{2,1,0:T(8,128)S(1)}, f32[24,16,128]{2,1,0:T(8,128)S(1)}, u32[]{:S(2)}, u32[]{:S(2)}) collective-permute-start(f32[24,16,128]{2,1,0:T(8,128)S(1)} %shard_map.29.rest_0_), channel_id=1, source_target_pairs={{0,2},{1,3},{2,0},{3,1},{4,6},{5,7},{6,4},{7,5},{8,10},{9,11},{10,... | collective-permute-start | bytes 589832 | tf_op jit(solution)/shard_map/ppermute | solution.py:484
  20.3 11.9 %collective-permute-start.6 = (f32[24,16,128]{2,1,0:T(8,128)S(1)}, f32[24,16,128]{2,1,0:T(8,128)S(1)}, u32[]{:S(2)}, u32[]{:S(2)}) collective-permute-start(f32[24,16,128]{2,1,0:T(8,128)S(1)} %shard_map.29.rest_0_), channel_id=1, source_target_pairs={{0,1},{1,0},{2,3},{3,2},{4,5},{5,4},{6,7},{7,6},{8,9},{9,8},{10,11... | collective-permute-start | bytes 589832 | tf_op jit(solution)/shard_map/ppermute | solution.py:484
  20.5 19.4 %collective-permute-start = (f32[12,64,128]{2,1,0:T(8,128)S(1)}, f32[12,64,128]{2,1,0:T(8,128)S(1)}, u32[]{:S(2)}, u32[]{:S(2)}) collective-permute-start(f32[12,64,128]{2,1,0:T(8,128)S(1)} %get-tuple-element.36), channel_id=1, source_target_pairs={{0,4},{4,0},{1,5},{5,1},{2,6},{6,2},{3,7},{7,3},{8,12},{12,8},{9,1... | collective-permute-start | bytes 1179656 | tf_op jit(solution)/shard_map/ppermute | solution.py:489
  25.8 26.2 %collective-permute-start.15 = (f32[12,64,128]{2,1,0:T(8,128)S(1)}, f32[12,64,128]{2,1,0:T(8,128)S(1)}, u32[]{:S(2)}, u32[]{:S(2)}) collective-permute-start(f32[12,64,128]{2,1,0:T(8,128)S(1)} %get-tuple-element.47), channel_id=1, source_target_pairs={{0,4},{4,0},{1,5},{5,1},{2,6},{6,2},{3,7},{7,3},{8,12},{12,8},{9,1... | collective-permute-start | bytes 1179656 | tf_op jit(solution)/shard_map/ppermute | solution.py:489
  30.1 9.9 %collective-permute-start.2 = (f32[9,64,128]{2,1,0:T(8,128)S(1)}, f32[9,64,128]{2,1,0:T(8,128)S(1)}, u32[]{:S(2)}, u32[]{:S(2)}) collective-permute-start(f32[9,64,128]{2,1,0:T(8,128)S(1)} %get-tuple-element.38), channel_id=1, source_target_pairs={{0,24},{4,12},{8,0},{12,20},{16,8},{20,28},{24,16},{28,4},{1,25},{... | collective-permute-start | bytes 884744 | tf_op jit(solution)/shard_map/ppermute | solution.py:491
  32.2 15.6 %collective-permute-start.16 = (f32[9,64,128]{2,1,0:T(8,128)S(1)}, f32[9,64,128]{2,1,0:T(8,128)S(1)}, u32[]{:S(2)}, u32[]{:S(2)}) collective-permute-start(f32[9,64,128]{2,1,0:T(8,128)S(1)} %get-tuple-element.48), channel_id=1, source_target_pairs={{0,28},{4,8},{8,4},{12,16},{16,12},{20,24},{24,20},{28,0},{1,29},{... | collective-permute-start | bytes 884744 | tf_op jit(solution)/shard_map/ppermute | solution.py:490
  33.6 18.1 %collective-permute-start.17 = (f32[9,64,128]{2,1,0:T(8,128)S(1)}, f32[9,64,128]{2,1,0:T(8,128)S(1)}, u32[]{:S(2)}, u32[]{:S(2)}) collective-permute-start(f32[9,64,128]{2,1,0:T(8,128)S(1)} %get-tuple-element.49), channel_id=1, source_target_pairs={{0,24},{4,12},{8,0},{12,20},{16,8},{20,28},{24,16},{28,4},{1,25},{... | collective-permute-start | bytes 884744 | tf_op jit(solution)/shard_map/ppermute | solution.py:491
  44.7 14.7 %collective-permute-start.9 = (f32[12,16,128]{2,1,0:T(8,128)S(1)}, f32[12,16,128]{2,1,0:T(8,128)S(1)}, u32[]{:S(2)}, u32[]{:S(2)}) collective-permute-start(f32[12,16,128]{2,1,0:T(8,128)S(1)} %get-tuple-element.41), channel_id=1, source_target_pairs={{0,6},{4,2},{1,7},{5,3},{2,4},{6,0},{3,5},{7,1},{8,14},{12,10},{9,... | collective-permute-start | bytes 294920 | tf_op jit(solution)/shard_map/ppermute | solution.py:501
  45.5 14.0 %collective-permute-start.10 = (f32[12,16,128]{2,1,0:T(8,128)S(1)}, f32[12,16,128]{2,1,0:T(8,128)S(1)}, u32[]{:S(2)}, u32[]{:S(2)}) collective-permute-start(f32[12,16,128]{2,1,0:T(8,128)S(1)} %get-tuple-element.42), channel_id=1, source_target_pairs={{0,7},{4,3},{1,6},{5,2},{2,5},{6,1},{3,4},{7,0},{8,15},{12,11},{9,... | collective-permute-start | bytes 294920 | tf_op jit(solution)/shard_map/ppermute | solution.py:501
  47.8 14.6 %collective-permute-start.11 = (f32[12,16,128]{2,1,0:T(8,128)S(1)}, f32[12,16,128]{2,1,0:T(8,128)S(1)}, u32[]{:S(2)}, u32[]{:S(2)}) collective-permute-start(f32[12,16,128]{2,1,0:T(8,128)S(1)} %get-tuple-element.43), channel_id=1, source_target_pairs={{0,2},{4,6},{1,3},{5,7},{2,0},{6,4},{3,1},{7,5},{8,10},{12,14},{9,... | collective-permute-start | bytes 294920 | tf_op jit(solution)/shard_map/ppermute | solution.py:501
  51.7 10.7 %collective-permute-start.12 = (f32[12,16,128]{2,1,0:T(8,128)S(1)}, f32[12,16,128]{2,1,0:T(8,128)S(1)}, u32[]{:S(2)}, u32[]{:S(2)}) collective-permute-start(f32[12,16,128]{2,1,0:T(8,128)S(1)} %get-tuple-element.44), channel_id=1, source_target_pairs={{0,3},{4,7},{1,2},{5,6},{2,1},{6,5},{3,0},{7,4},{8,11},{12,15},{9,... | collective-permute-start | bytes 294920 | tf_op jit(solution)/shard_map/ppermute | solution.py:501
  52.1 10.5 %collective-permute-start.13 = (f32[12,16,128]{2,1,0:T(8,128)S(1)}, f32[12,16,128]{2,1,0:T(8,128)S(1)}, u32[]{:S(2)}, u32[]{:S(2)}) collective-permute-start(f32[12,16,128]{2,1,0:T(8,128)S(1)} %get-tuple-element.45), channel_id=1, source_target_pairs={{0,4},{4,0},{1,5},{5,1},{2,6},{6,2},{3,7},{7,3},{8,12},{12,8},{9,1... | collective-permute-start | bytes 294920 | tf_op jit(solution)/shard_map/ppermute | solution.py:501
  62.4 11.2 %collective-permute-start.24 = (f32[2,12,16,128]{3,2,1,0:T(8,128)S(1)}, f32[2,12,16,128]{3,2,1,0:T(8,128)S(1)}, u32[]{:S(2)}, u32[]{:S(2)}) collective-permute-start(f32[2,12,16,128]{3,2,1,0:T(8,128)S(1)} %get-tuple-element.59), channel_id=1, source_target_pairs={{0,1},{4,5},{1,0},{5,4},{2,3},{6,7},{3,2},{7,6},{8,9},{12,13},{9,8... | collective-permute-start | bytes 589832 | tf_op jit(solution)/shard_map/ppermute | solution.py:501
  75.8 44.4 %collective-permute-start.25 = (f32[16,192,128]{2,1,0:T(8,128)S(1)}, f32[16,192,128]{2,1,0:T(8,128)S(1)}, u32[]{:S(2)}, u32[]{:S(2)}) collective-permute-start(f32[16,192,128]{2,1,0:T(8,128)S(1)} %get-tuple-element.61.block), channel_id=1, source_target_pairs={{0,1},{1,0},{2,3},{3,2},{4,5},{5,4},{6,7},{7,6},{8,9},{9,8},{10,11... | collective-permute-start | bytes 4718600 | tf_op jit(solution)/shard_map/ppermute | solution.py:544
  76.7 11.1 %collective-permute-start.26 = (f32[2,2,12,16,128]{4,3,2,1,0:T(8,128)S(1)}, f32[2,2,12,16,128]{4,3,2,1,0:T(8,128)S(1)}, u32[]{:S(2)}, u32[]{:S(2)}) collective-permute-start(f32[2,2,12,16,128]{4,3,2,1,0:T(8,128)S(1)} %get-tuple-element.65), channel_id=1, source_target_pairs={{0,4},{4,0},{1,5},{5,1},{2,6},{6,2},{3,7},{7,3},{8,12},{12,8},{9,1... | collective-permute-start | bytes 1179656 | tf_op jit(solution)/shard_map/ppermute | solution.py:537
  77.5 12.0 %collective-permute-start.27 = (f32[2,2,12,16,128]{4,3,2,1,0:T(8,128)S(1)}, f32[2,2,12,16,128]{4,3,2,1,0:T(8,128)S(1)}, u32[]{:S(2)}, u32[]{:S(2)}) collective-permute-start(f32[2,2,12,16,128]{4,3,2,1,0:T(8,128)S(1)} %get-tuple-element.66), channel_id=1, source_target_pairs={{0,2},{1,3},{2,0},{3,1},{4,6},{5,7},{6,4},{7,5},{8,10},{9,11},{10,... | collective-permute-start | bytes 1179656 | tf_op jit(solution)/shard_map/ppermute | solution.py:538
  78.7 18.4 %collective-permute-start.28 = (f32[2,2,12,16,128]{4,3,2,1,0:T(8,128)S(1)}, f32[2,2,12,16,128]{4,3,2,1,0:T(8,128)S(1)}, u32[]{:S(2)}, u32[]{:S(2)}) collective-permute-start(f32[2,2,12,16,128]{4,3,2,1,0:T(8,128)S(1)} %shard_map.35), channel_id=1, source_target_pairs={{0,2},{1,3},{2,0},{3,1},{4,6},{5,7},{6,4},{7,5},{8,10},{9,11},{10,... | collective-permute-start | bytes 1179656 | tf_op jit(solution)/shard_map/ppermute | solution.py:543
  80.2 39.9 %collective-permute-start.29 = (f32[2,2,12,16,128]{4,3,2,1,0:T(8,128)S(1)}, f32[2,2,12,16,128]{4,3,2,1,0:T(8,128)S(1)}, u32[]{:S(2)}, u32[]{:S(2)}) collective-permute-start(f32[2,2,12,16,128]{4,3,2,1,0:T(8,128)S(1)} %get-tuple-element.64.refs_0_), channel_id=1, source_target_pairs={{0,1},{1,0},{2,3},{3,2},{4,5},{5,4},{6,7},{7,6},{8,9},{9,8},{10,11... | collective-permute-start | bytes 1179656 | tf_op jit(solution)/shard_map/ppermute | solution.py:546
  87.8 32.3 %collective-permute-start.30 = (f32[2,2,12,16,128]{4,3,2,1,0:T(8,128)S(1)}, f32[2,2,12,16,128]{4,3,2,1,0:T(8,128)S(1)}, u32[]{:S(2)}, u32[]{:S(2)}) collective-permute-start(f32[2,2,12,16,128]{4,3,2,1,0:T(8,128)S(1)} %collective-permute-done.26.refs_1_), channel_id=1, source_target_pairs={{0,1},{1,0},{2,3},{3,2},{4,5},{5,4},{6,7},{7,6},{8,9},{9,8},{10,11... | collective-permute-start | bytes 1179656 | tf_op jit(solution)/shard_map/ppermute | solution.py:546
  89.5 30.6 %collective-permute-start.31 = (f32[2,2,12,16,128]{4,3,2,1,0:T(8,128)S(1)}, f32[2,2,12,16,128]{4,3,2,1,0:T(8,128)S(1)}, u32[]{:S(2)}, u32[]{:S(2)}) collective-permute-start(f32[2,2,12,16,128]{4,3,2,1,0:T(8,128)S(1)} %collective-permute-done.27.refs_2_), channel_id=1, source_target_pairs={{0,1},{1,0},{2,3},{3,2},{4,5},{5,4},{6,7},{7,6},{8,9},{9,8},{10,11... | collective-permute-start | bytes 1179656 | tf_op jit(solution)/shard_map/ppermute | solution.py:546
  97.1 23.0 %collective-permute-start.32 = (f32[2,2,12,16,128]{4,3,2,1,0:T(8,128)S(1)}, f32[2,2,12,16,128]{4,3,2,1,0:T(8,128)S(1)}, u32[]{:S(2)}, u32[]{:S(2)}) collective-permute-start(f32[2,2,12,16,128]{4,3,2,1,0:T(8,128)S(1)} %collective-permute-done.28.refs_3_), channel_id=1, source_target_pairs={{0,1},{1,0},{2,3},{3,2},{4,5},{5,4},{6,7},{7,6},{8,9},{9,8},{10,11... | collective-permute-start | bytes 1179656 | tf_op jit(solution)/shard_map/ppermute | solution.py:547
  (11 other events, 142.6 us)

commit v14 on v13

--- a/solution.py
+++ b/solution.py
@@ -240,6 +240,16 @@
     return lax.dot_general(a, b, (contract, ((), ())), preferred_element_type=jnp.float32)
 
 
+def picked(values, table):
+    chosen = table.astype(jnp.bfloat16)
+    return sum(product(part, chosen) for part in split(values))
+
+
+def gathered(table, values):
+    chosen = table.astype(jnp.bfloat16)
+    return sum(product(chosen, part) for part in split(values))
+
+
 def gram_message(wide, total):
     tall = total * EIGHT
     high, middle, low = split(wide)
@@ -247,8 +257,8 @@
     mixed = product(doubled, jnp.concatenate([middle, low], axis=1), ((1,), (1,)))
     sums = product(joined, joined, ((1,), (1,))) + (mixed + mixed.T)
     sums = sums * table_of((tall, tall), lambda r, c: r % EIGHT == c % EIGHT)
-    partial = exact_dot(table_of((total, tall), lambda r, c: c // EIGHT == r), sums)
-    spread = exact_dot(partial, table_of((tall, LANES), lambda r, c: r // EIGHT == c % total))
+    partial = gathered(table_of((total, tall), lambda r, c: c // EIGHT == r), sums)
+    spread = picked(partial, table_of((tall, LANES), lambda r, c: r // EIGHT == c % total))
     per = LANES // total
     spread = spread * table_of((total, LANES), lambda r, c: c // total == r % per)
     return jnp.concatenate(
@@ -263,7 +273,7 @@
         [jnp.broadcast_to(row[:, i * LANES : (i + 1) * LANES], (per, LANES)) for i in range(total // per)], axis=0
     )
     wide = wide * table_of((total, LANES), lambda r, c: c // total == r % per)
-    table = exact_dot(wide, table_of((LANES, LANES), lambda r, c: r % total == c))
+    table = picked(wide, table_of((LANES, LANES), lambda r, c: r % total == c))
     table = table + table_of((total, LANES), lambda r, c: c - total == r)
     index = lax.broadcasted_iota(jnp.int32, (total, LANES), 0)
     for start in range(0, total, WIDTH):
@@ -290,8 +300,8 @@
 
 def by_tiles(table, total):
     tall = total * EIGHT
-    wide = exact_dot(table, table_of((LANES, tall), lambda r, c: r - total == c // EIGHT))
-    both = exact_dot(table_of((tall, total), lambda r, c: r // EIGHT == c), wide)
+    wide = picked(table, table_of((LANES, tall), lambda r, c: r - total == c // EIGHT))
+    both = gathered(table_of((tall, total), lambda r, c: r // EIGHT == c), wide)
     return both * table_of((tall, tall), lambda r, c: r % EIGHT == c % EIGHT)
 
 
@@ -374,9 +384,9 @@
         fetch.start()
     second = inverse_factor(copies, total, cell_total)
     pick = table_of((LANES, total), lambda r, c: r - total == c)
-    product = exact_dot(exact_dot(second, pick), exact_dot(table[...], pick))
-    own = exact_dot(table_of((held * EIGHT, total), lambda r, c: orb * held + r // EIGHT == c), product)
-    wide = exact_dot(own, table_of((total, total * width), lambda r, c: c // width == r))
+    both = exact_dot(picked(second, pick), picked(table[...], pick))
+    own = gathered(table_of((held * EIGHT, total), lambda r, c: orb * held + r // EIGHT == c), both)
+    wide = picked(own, table_of((total, total * width), lambda r, c: c // width == r))
     for orbital in range(total):
         splats[orbital] = wide[:, orbital * width : (orbital + 1) * width].reshape(held, EIGHT, width)
 

time: 127 us -> 126 us (level)
  no operation moved by 1% of the time
where the time goes in v14:
time: 126 us
  waiting for transfers between devices  49.4 us (39%)
  starting transfers between devices  32.6 us (26%)
  Pallas kernels  24.4 us (19%)
  blocking collectives  19.6 us (16%)
    all_to_all x2, blocking collectives, exchanged(): return lax.all_to_all(message, ALL, 0, 0)  19.6 us
    ppermute x13, starting transfers between devices, to_partner(): lax.ppermute(piece, ('side', 'orb'), [(flat_of(i), flat_of(i ^ m)) for i...  11.8 us
    ppermute x3, waiting for transfers between devices, whole(): lax.ppermute(joined, 'orb', [(i, i ^ m) for i in range(orb_count)])  9.47 us
    pallas_call x2, Pallas kernels, filtered_pieces(): pl.pallas_call(functools.partial(filter_kernel, at, len(pot_far), early),...  9.35 us
    ppermute x2, waiting for transfers between devices, whole(): straight = lax.ppermute(sent[3 * at + 2], slab_axes, ahead)  7.66 us
    ppermute x1, waiting for transfers between devices, whole(): given.append(lax.ppermute(forward, 'orb', across))  7.61 us
    ppermute x1, waiting for transfers between devices, whole(): lax.ppermute(spare[1], 'side', swap)  7.59 us
    pallas_call x1, Pallas kernels, whole(): pl.pallas_call(functools.partial(last_kernel, cell_total), out_shape=jax....  6.6 us
  transfers between devices with their start and end apart: 33, of which 15 were waited for; matrix products, arithmetic and copies ran while one was open for 0% of the time, Pallas kernels for 11%

profile of v14, /device:TPU:0, one launch (start us, length us, event | category | flops | bytes accessed | tf_op | source)
XLA Modules:
  0.0 126.3 jit_solution(13146932506725424376)
XLA Ops:
  0.1 2.2 %shard_map.28 = (f32[12,16,128]{2,1,0:T(8,128)S(1)}, f32[6,16,128]{2,1,0:T(8,128)S(1)}, f32[9,64,128]{2,1,0:T(8,128)S(1)}, f32[12,64,128]{2,1,0:T(8,128)S(1)}, f...) custom-call(s32[3]{0:T(128)S(1)} %pad_add_fusion.place, ...), custom_call_target="tpu_custom_call" | custom-call | tf_op jit(solution)/shard_map/pallas_call | solution.py:61
  2.3 3.1 %collective-permute-start.3 = (f32[12,16,128]{2,1,0:T(8,128)S(1)}, f32[12,16,128]{2,1,0:T(8,128)S(1)}, u32[]{:S(2)}, u32[]{:S(2)}) collective-permute-start(f32[12,16,128]{2,1,0:T(8,128)S(1)} %get-tuple-element.39), channel_id=1, source_target_pairs={{0,4},{4,0},{1,5},{5,1},{2,6},{6,2},{3,7},{7,3},{8,12},{12,8},{9,1... | collective-permute-start | bytes 294920 | tf_op jit(solution)/shard_map/ppermute | solution.py:482
  5.4 3.5 %collective-permute-start.1 = (f32[9,64,128]{2,1,0:T(8,128)S(1)}, f32[9,64,128]{2,1,0:T(8,128)S(1)}, u32[]{:S(2)}, u32[]{:S(2)}) collective-permute-start(f32[9,64,128]{2,1,0:T(8,128)S(1)} %get-tuple-element.37), channel_id=1, source_target_pairs={{0,28},{4,8},{8,4},{12,16},{16,12},{20,24},{24,20},{28,0},{1,29},{... | collective-permute-start | bytes 884744 | tf_op jit(solution)/shard_map/ppermute | solution.py:500
  9.3 2.4 %collective-permute-start.4 = (f32[6,16,128]{2,1,0:T(8,128)S(1)}, f32[6,16,128]{2,1,0:T(8,128)S(1)}, u32[]{:S(2)}, u32[]{:S(2)}) collective-permute-start(f32[6,16,128]{2,1,0:T(8,128)S(1)} %get-tuple-element.40), channel_id=1, source_target_pairs={{0,28},{4,8},{8,4},{12,16},{16,12},{20,24},{24,20},{28,0},{1,29},{... | collective-permute-start | bytes 147464 | tf_op jit(solution)/shard_map/ppermute | solution.py:483
  11.7 4.7 %collective-permute-done.5.straight = f32[6,16,128]{2,1,0:T(8,128)S(1)} collective-permute-done((f32[6,16,128]{2,1,0:T(8,128)S(1)}, f32[6,16,128]{2,1,0:T(8,128)S(1)}, u32[]{:S(2)}, u32[]{:S(2)}) %collective-permute-start.5) | collective-permute-done | bytes 49184 | tf_op jit(solution)/shard_map/ppermute | solution.py:484
  16.4 2.2 %collective-permute-done.4.slanted = f32[6,16,128]{2,1,0:T(8,128)S(1)} collective-permute-done((f32[6,16,128]{2,1,0:T(8,128)S(1)}, f32[6,16,128]{2,1,0:T(8,128)S(1)}, u32[]{:S(2)}, u32[]{:S(2)}) %collective-permute-start.4) | collective-permute-done | bytes 49184 | tf_op jit(solution)/shard_map/ppermute | solution.py:483
  20.6 5.2 %collective-permute-done.8.rest_3_ = f32[24,16,128]{2,1,0:T(8,128)S(1)} collective-permute-done((f32[24,16,128]{2,1,0:T(8,128)S(1)}, f32[24,16,128]{2,1,0:T(8,128)S(1)}, u32[]{:S(2)}, u32[]{:S(2)}) %collective-permute-start.8) | collective-permute-done | bytes 196640 | tf_op jit(solution)/shard_map/ppermute | solution.py:494
  25.9 4.2 %collective-permute-done.7.rest_2_ = f32[24,16,128]{2,1,0:T(8,128)S(1)} collective-permute-done((f32[24,16,128]{2,1,0:T(8,128)S(1)}, f32[24,16,128]{2,1,0:T(8,128)S(1)}, u32[]{:S(2)}, u32[]{:S(2)}) %collective-permute-start.7) | collective-permute-done | bytes 196640 | tf_op jit(solution)/shard_map/ppermute | solution.py:494
  30.1 2.1 %collective-permute-start.2 = (f32[9,64,128]{2,1,0:T(8,128)S(1)}, f32[9,64,128]{2,1,0:T(8,128)S(1)}, u32[]{:S(2)}, u32[]{:S(2)}) collective-permute-start(f32[9,64,128]{2,1,0:T(8,128)S(1)} %get-tuple-element.38), channel_id=1, source_target_pairs={{0,24},{4,12},{8,0},{12,20},{16,8},{20,28},{24,16},{28,4},{1,25},{... | collective-permute-start | bytes 884744 | tf_op jit(solution)/shard_map/ppermute | solution.py:501
  33.6 2.0 %collective-permute-start.17 = (f32[9,64,128]{2,1,0:T(8,128)S(1)}, f32[9,64,128]{2,1,0:T(8,128)S(1)}, u32[]{:S(2)}, u32[]{:S(2)}) collective-permute-start(f32[9,64,128]{2,1,0:T(8,128)S(1)} %get-tuple-element.49), channel_id=1, source_target_pairs={{0,24},{4,12},{8,0},{12,20},{16,8},{20,28},{24,16},{28,4},{1,25},{... | collective-permute-start | bytes 884744 | tf_op jit(solution)/shard_map/ppermute | solution.py:501
  35.8 4.2 %collective-permute-done.2.straight = f32[9,64,128]{2,1,0:T(8,128)S(1)} collective-permute-done((f32[9,64,128]{2,1,0:T(8,128)S(1)}, f32[9,64,128]{2,1,0:T(8,128)S(1)}, u32[]{:S(2)}, u32[]{:S(2)}) %collective-permute-start.2) | collective-permute-done | bytes 294944 | tf_op jit(solution)/shard_map/ppermute | solution.py:501
  40.0 4.7 %shard_map.30 = (f32[12,16,128]{2,1,0:T(8,128)S(1)}, f32[12,16,128]{2,1,0:T(8,128)S(1)}, f32[12,16,128]{2,1,0:T(8,128)S(1)}, f32[12,16,128]{2,1,0:T(8,128)S(1)},...) custom-call(s32[3]{0:T(128)S(1)} %pad_add_fusion.place, ...), custom_call_target="tpu_custom_call" | custom-call | tf_op jit(solution)/shard_map/pallas_call | solution.py:202
  45.8 2.0 %collective-permute-done.16.slanted = f32[9,64,128]{2,1,0:T(8,128)S(1)} collective-permute-done((f32[9,64,128]{2,1,0:T(8,128)S(1)}, f32[9,64,128]{2,1,0:T(8,128)S(1)}, u32[]{:S(2)}, u32[]{:S(2)}) %collective-permute-start.16) | collective-permute-done | bytes 294944 | tf_op jit(solution)/shard_map/ppermute | solution.py:500
  48.3 3.4 %collective-permute-done.17.straight = f32[9,64,128]{2,1,0:T(8,128)S(1)} collective-permute-done((f32[9,64,128]{2,1,0:T(8,128)S(1)}, f32[9,64,128]{2,1,0:T(8,128)S(1)}, u32[]{:S(2)}, u32[]{:S(2)}) %collective-permute-start.17) | collective-permute-done | bytes 294944 | tf_op jit(solution)/shard_map/ppermute | solution.py:501
  54.1 4.7 %shard_map.31 = (f32[12,16,128]{2,1,0:T(8,128)S(1)}, f32[12,16,128]{2,1,0:T(8,128)S(1)}, f32[12,16,128]{2,1,0:T(8,128)S(1)}, f32[12,16,128]{2,1,0:T(8,128)S(1)},...) custom-call(s32[3]{0:T(128)S(1)} %pad_add_fusion.place, ...), custom_call_target="tpu_custom_call" | custom-call | tf_op jit(solution)/shard_map/pallas_call | solution.py:202
  59.5 2.9 %collective-permute-start.18 = (f32[12,16,128]{2,1,0:T(8,128)S(1)}, f32[12,16,128]{2,1,0:T(8,128)S(1)}, u32[]{:S(2)}, u32[]{:S(2)}) collective-permute-start(f32[12,16,128]{2,1,0:T(8,128)S(1)} %get-tuple-element.50), channel_id=1, source_target_pairs={{0,6},{4,2},{1,7},{5,3},{2,4},{6,0},{3,5},{7,1},{8,14},{12,10},{9,... | collective-permute-start | bytes 294920 | tf_op jit(solution)/shard_map/ppermute | solution.py:511
  69.5 2.0 %collective-permute-done.20.refs_8_ = f32[12,16,128]{2,1,0:T(8,128)S(1)} collective-permute-done((f32[12,16,128]{2,1,0:T(8,128)S(1)}, f32[12,16,128]{2,1,0:T(8,128)S(1)}, u32[]{:S(2)}, u32[]{:S(2)}) %collective-permute-start.20) | collective-permute-done | bytes 98336 | tf_op jit(solution)/shard_map/ppermute | solution.py:511
  73.6 2.0 %shard_map.33 = (f32[16,192,128]{2,1,0:T(8,128)S(1)}, f32[32,1,256]{2,1,0:T(1,128)S(1)}) custom-call(s32[3]{0:T(128)S(1)} %pad_add_fusion.place, f32[12,16,128]{2,1,0:T(8,128)S(1)} %collective-permute-done.9.refs_0_, f32[12,16,128]{2,1,0:T(8,128)S(1)} %collective-permute-done.10.refs_1_, f32[12,16,128]{2,1,0:T(8,128)S(1)} %collective-permute-done.11.refs_2_, ...), custom_call_target="tpu_custom_call" | custom-call | tf_op jit(solution)/shard_map/pallas_call | solution.py:450
  80.1 7.6 %collective-permute-done.26.refs_1_ = f32[2,2,12,16,128]{4,3,2,1,0:T(8,128)S(1)} collective-permute-done((f32[2,2,12,16,128]{4,3,2,1,0:T(8,128)S(1)}, f32[2,2,12,16,128]{4,3,2,1,0:T(8,128)S(1)}, u32[]{:S(2)}, u32[]{:S(2)}) %collective-permute-start.26) | collective-permute-done | bytes 393248 | tf_op jit(solution)/shard_map/ppermute | solution.py:547
  89.4 7.6 %collective-permute-done.28.refs_3_ = f32[2,2,12,16,128]{4,3,2,1,0:T(8,128)S(1)} collective-permute-done((f32[2,2,12,16,128]{4,3,2,1,0:T(8,128)S(1)}, f32[2,2,12,16,128]{4,3,2,1,0:T(8,128)S(1)}, u32[]{:S(2)}, u32[]{:S(2)}) %collective-permute-start.28) | collective-permute-done | bytes 393248 | tf_op jit(solution)/shard_map/ppermute | solution.py:553
  97.0 10.6 %all_to_all.10.copies = f32[32,1,256]{2,1,0:T(1,128)S(1)} all-to-all(f32[32,1,256]{2,1,0:T(1,128)S(1)} %get-tuple-element.60), channel_id=1, replica_groups=mesh['pair'=4,'side'=2,'orb'=4] {'pair','side','orb'}, dimensions={0} | all-to-all | bytes 65536 | tf_op jit(solution)/shard_map/all_to_all | solution.py:534
  107.6 3.1 %shard_map.34 = (f32[16,128]{1,0:T(8,128)S(1)}, f32[32,1,256]{2,1,0:T(1,128)S(1)}) custom-call(f32[32,1,256]{2,1,0:T(1,128)S(1)} %all_to_all.10.copies, f32[16,192,128]{2,1,0:T(8,128)S(1)} %get-tuple-element.61.block), custom_call_target="tpu_custom_call" | custom-call | tf_op jit(solution)/shard_map/pallas_call | solution.py:559
  110.7 9.0 %all_to_all.11.copies = f32[32,1,256]{2,1,0:T(1,128)S(1)} all-to-all(f32[32,1,256]{2,1,0:T(1,128)S(1)} %get-tuple-element.62), channel_id=1, replica_groups=mesh['pair'=4,'side'=2,'orb'=4] {'pair','side','orb'}, dimensions={0} | all-to-all | bytes 65536 | tf_op jit(solution)/shard_map/all_to_all | solution.py:534
  119.7 6.6 %shard_map.36 = f32[4,12,64,128]{3,2,1,0:T(8,128)} custom-call(s32[3]{0:T(128)S(1)} %pad_add_fusion.place, f32[32,1,256]{2,1,0:T(1,128)S(1)} %all_to_all.11.copies, f32[16,128]{1,0:T(8,128)S(1)} %get-tuple-element.63.table, f32[16,192,128]{2,1,0:T(8,128)S(1)} %get-tuple-element.61.block, f32[16,192,128]{2,1,0:T(8,128)S(1)} %collective-permute-done.25.block_near, ...), custom_call_target="tpu_custom_call" | custom-call | tf_op jit(solution)/shard_map/pallas_call | solution.py:567
  (59 shorter events, 24.1 us)
Async XLA Ops:
  2.3 16.3 %collective-permute-start.3 = (f32[12,16,128]{2,1,0:T(8,128)S(1)}, f32[12,16,128]{2,1,0:T(8,128)S(1)}, u32[]{:S(2)}, u32[]{:S(2)}) collective-permute-start(f32[12,16,128]{2,1,0:T(8,128)S(1)} %get-tuple-element.39), channel_id=1, source_target_pairs={{0,4},{4,0},{1,5},{5,1},{2,6},{6,2},{3,7},{7,3},{8,12},{12,8},{9,1... | collective-permute-start | bytes 294920 | tf_op jit(solution)/shard_map/ppermute | solution.py:482
  5.4 28.3 %collective-permute-start.1 = (f32[9,64,128]{2,1,0:T(8,128)S(1)}, f32[9,64,128]{2,1,0:T(8,128)S(1)}, u32[]{:S(2)}, u32[]{:S(2)}) collective-permute-start(f32[9,64,128]{2,1,0:T(8,128)S(1)} %get-tuple-element.37), channel_id=1, source_target_pairs={{0,28},{4,8},{8,4},{12,16},{16,12},{20,24},{24,20},{28,0},{1,29},{... | collective-permute-start | bytes 884744 | tf_op jit(solution)/shard_map/ppermute | solution.py:500
  9.3 9.3 %collective-permute-start.4 = (f32[6,16,128]{2,1,0:T(8,128)S(1)}, f32[6,16,128]{2,1,0:T(8,128)S(1)}, u32[]{:S(2)}, u32[]{:S(2)}) collective-permute-start(f32[6,16,128]{2,1,0:T(8,128)S(1)} %get-tuple-element.40), channel_id=1, source_target_pairs={{0,28},{4,8},{8,4},{12,16},{16,12},{20,24},{24,20},{28,0},{1,29},{... | collective-permute-start | bytes 147464 | tf_op jit(solution)/shard_map/ppermute | solution.py:483
  18.7 11.4 %collective-permute-start.7 = (f32[24,16,128]{2,1,0:T(8,128)S(1)}, f32[24,16,128]{2,1,0:T(8,128)S(1)}, u32[]{:S(2)}, u32[]{:S(2)}) collective-permute-start(f32[24,16,128]{2,1,0:T(8,128)S(1)} %shard_map.29.rest_0_), channel_id=1, source_target_pairs={{0,2},{1,3},{2,0},{3,1},{4,6},{5,7},{6,4},{7,5},{8,10},{9,11},{10,... | collective-permute-start | bytes 589832 | tf_op jit(solution)/shard_map/ppermute | solution.py:494
  20.3 11.9 %collective-permute-start.6 = (f32[24,16,128]{2,1,0:T(8,128)S(1)}, f32[24,16,128]{2,1,0:T(8,128)S(1)}, u32[]{:S(2)}, u32[]{:S(2)}) collective-permute-start(f32[24,16,128]{2,1,0:T(8,128)S(1)} %shard_map.29.rest_0_), channel_id=1, source_target_pairs={{0,1},{1,0},{2,3},{3,2},{4,5},{5,4},{6,7},{7,6},{8,9},{9,8},{10,11... | collective-permute-start | bytes 589832 | tf_op jit(solution)/shard_map/ppermute | solution.py:494
  20.5 19.4 %collective-permute-start = (f32[12,64,128]{2,1,0:T(8,128)S(1)}, f32[12,64,128]{2,1,0:T(8,128)S(1)}, u32[]{:S(2)}, u32[]{:S(2)}) collective-permute-start(f32[12,64,128]{2,1,0:T(8,128)S(1)} %get-tuple-element.36), channel_id=1, source_target_pairs={{0,4},{4,0},{1,5},{5,1},{2,6},{6,2},{3,7},{7,3},{8,12},{12,8},{9,1... | collective-permute-start | bytes 1179656 | tf_op jit(solution)/shard_map/ppermute | solution.py:499
  25.8 26.2 %collective-permute-start.15 = (f32[12,64,128]{2,1,0:T(8,128)S(1)}, f32[12,64,128]{2,1,0:T(8,128)S(1)}, u32[]{:S(2)}, u32[]{:S(2)}) collective-permute-start(f32[12,64,128]{2,1,0:T(8,128)S(1)} %get-tuple-element.47), channel_id=1, source_target_pairs={{0,4},{4,0},{1,5},{5,1},{2,6},{6,2},{3,7},{7,3},{8,12},{12,8},{9,1... | collective-permute-start | bytes 1179656 | tf_op jit(solution)/shard_map/ppermute | solution.py:499
  30.1 9.9 %collective-permute-start.2 = (f32[9,64,128]{2,1,0:T(8,128)S(1)}, f32[9,64,128]{2,1,0:T(8,128)S(1)}, u32[]{:S(2)}, u32[]{:S(2)}) collective-permute-start(f32[9,64,128]{2,1,0:T(8,128)S(1)} %get-tuple-element.38), channel_id=1, source_target_pairs={{0,24},{4,12},{8,0},{12,20},{16,8},{20,28},{24,16},{28,4},{1,25},{... | collective-permute-start | bytes 884744 | tf_op jit(solution)/shard_map/ppermute | solution.py:501
  32.2 15.6 %collective-permute-start.16 = (f32[9,64,128]{2,1,0:T(8,128)S(1)}, f32[9,64,128]{2,1,0:T(8,128)S(1)}, u32[]{:S(2)}, u32[]{:S(2)}) collective-permute-start(f32[9,64,128]{2,1,0:T(8,128)S(1)} %get-tuple-element.48), channel_id=1, source_target_pairs={{0,28},{4,8},{8,4},{12,16},{16,12},{20,24},{24,20},{28,0},{1,29},{... | collective-permute-start | bytes 884744 | tf_op jit(solution)/shard_map/ppermute | solution.py:500
  33.6 18.1 %collective-permute-start.17 = (f32[9,64,128]{2,1,0:T(8,128)S(1)}, f32[9,64,128]{2,1,0:T(8,128)S(1)}, u32[]{:S(2)}, u32[]{:S(2)}) collective-permute-start(f32[9,64,128]{2,1,0:T(8,128)S(1)} %get-tuple-element.49), channel_id=1, source_target_pairs={{0,24},{4,12},{8,0},{12,20},{16,8},{20,28},{24,16},{28,4},{1,25},{... | collective-permute-start | bytes 884744 | tf_op jit(solution)/shard_map/ppermute | solution.py:501
  44.7 14.7 %collective-permute-start.9 = (f32[12,16,128]{2,1,0:T(8,128)S(1)}, f32[12,16,128]{2,1,0:T(8,128)S(1)}, u32[]{:S(2)}, u32[]{:S(2)}) collective-permute-start(f32[12,16,128]{2,1,0:T(8,128)S(1)} %get-tuple-element.41), channel_id=1, source_target_pairs={{0,6},{4,2},{1,7},{5,3},{2,4},{6,0},{3,5},{7,1},{8,14},{12,10},{9,... | collective-permute-start | bytes 294920 | tf_op jit(solution)/shard_map/ppermute | solution.py:511
  45.5 14.0 %collective-permute-start.10 = (f32[12,16,128]{2,1,0:T(8,128)S(1)}, f32[12,16,128]{2,1,0:T(8,128)S(1)}, u32[]{:S(2)}, u32[]{:S(2)}) collective-permute-start(f32[12,16,128]{2,1,0:T(8,128)S(1)} %get-tuple-element.42), channel_id=1, source_target_pairs={{0,7},{4,3},{1,6},{5,2},{2,5},{6,1},{3,4},{7,0},{8,15},{12,11},{9,... | collective-permute-start | bytes 294920 | tf_op jit(solution)/shard_map/ppermute | solution.py:511
  47.8 14.6 %collective-permute-start.11 = (f32[12,16,128]{2,1,0:T(8,128)S(1)}, f32[12,16,128]{2,1,0:T(8,128)S(1)}, u32[]{:S(2)}, u32[]{:S(2)}) collective-permute-start(f32[12,16,128]{2,1,0:T(8,128)S(1)} %get-tuple-element.43), channel_id=1, source_target_pairs={{0,2},{4,6},{1,3},{5,7},{2,0},{6,4},{3,1},{7,5},{8,10},{12,14},{9,... | collective-permute-start | bytes 294920 | tf_op jit(solution)/shard_map/ppermute | solution.py:511
  51.7 10.7 %collective-permute-start.12 = (f32[12,16,128]{2,1,0:T(8,128)S(1)}, f32[12,16,128]{2,1,0:T(8,128)S(1)}, u32[]{:S(2)}, u32[]{:S(2)}) collective-permute-start(f32[12,16,128]{2,1,0:T(8,128)S(1)} %get-tuple-element.44), channel_id=1, source_target_pairs={{0,3},{4,7},{1,2},{5,6},{2,1},{6,5},{3,0},{7,4},{8,11},{12,15},{9,... | collective-permute-start | bytes 294920 | tf_op jit(solution)/shard_map/ppermute | solution.py:511
  52.1 10.5 %collective-permute-start.13 = (f32[12,16,128]{2,1,0:T(8,128)S(1)}, f32[12,16,128]{2,1,0:T(8,128)S(1)}, u32[]{:S(2)}, u32[]{:S(2)}) collective-permute-start(f32[12,16,128]{2,1,0:T(8,128)S(1)} %get-tuple-element.45), channel_id=1, source_target_pairs={{0,4},{4,0},{1,5},{5,1},{2,6},{6,2},{3,7},{7,3},{8,12},{12,8},{9,1... | collective-permute-start | bytes 294920 | tf_op jit(solution)/shard_map/ppermute | solution.py:511
  62.4 11.2 %collective-permute-start.24 = (f32[2,12,16,128]{3,2,1,0:T(8,128)S(1)}, f32[2,12,16,128]{3,2,1,0:T(8,128)S(1)}, u32[]{:S(2)}, u32[]{:S(2)}) collective-permute-start(f32[2,12,16,128]{3,2,1,0:T(8,128)S(1)} %get-tuple-element.59), channel_id=1, source_target_pairs={{0,1},{4,5},{1,0},{5,4},{2,3},{6,7},{3,2},{7,6},{8,9},{12,13},{9,8... | collective-permute-start | bytes 589832 | tf_op jit(solution)/shard_map/ppermute | solution.py:511
  75.7 44.0 %collective-permute-start.25 = (f32[16,192,128]{2,1,0:T(8,128)S(1)}, f32[16,192,128]{2,1,0:T(8,128)S(1)}, u32[]{:S(2)}, u32[]{:S(2)}) collective-permute-start(f32[16,192,128]{2,1,0:T(8,128)S(1)} %get-tuple-element.61.block), channel_id=1, source_target_pairs={{0,1},{1,0},{2,3},{3,2},{4,5},{5,4},{6,7},{7,6},{8,9},{9,8},{10,11... | collective-permute-start | bytes 4718600 | tf_op jit(solution)/shard_map/ppermute | solution.py:554
  76.6 11.1 %collective-permute-start.26 = (f32[2,2,12,16,128]{4,3,2,1,0:T(8,128)S(1)}, f32[2,2,12,16,128]{4,3,2,1,0:T(8,128)S(1)}, u32[]{:S(2)}, u32[]{:S(2)}) collective-permute-start(f32[2,2,12,16,128]{4,3,2,1,0:T(8,128)S(1)} %get-tuple-element.65), channel_id=1, source_target_pairs={{0,4},{4,0},{1,5},{5,1},{2,6},{6,2},{3,7},{7,3},{8,12},{12,8},{9,1... | collective-permute-start | bytes 1179656 | tf_op jit(solution)/shard_map/ppermute | solution.py:547
  77.4 12.0 %collective-permute-start.27 = (f32[2,2,12,16,128]{4,3,2,1,0:T(8,128)S(1)}, f32[2,2,12,16,128]{4,3,2,1,0:T(8,128)S(1)}, u32[]{:S(2)}, u32[]{:S(2)}) collective-permute-start(f32[2,2,12,16,128]{4,3,2,1,0:T(8,128)S(1)} %get-tuple-element.66), channel_id=1, source_target_pairs={{0,2},{1,3},{2,0},{3,1},{4,6},{5,7},{6,4},{7,5},{8,10},{9,11},{10,... | collective-permute-start | bytes 1179656 | tf_op jit(solution)/shard_map/ppermute | solution.py:548
  78.6 18.4 %collective-permute-start.28 = (f32[2,2,12,16,128]{4,3,2,1,0:T(8,128)S(1)}, f32[2,2,12,16,128]{4,3,2,1,0:T(8,128)S(1)}, u32[]{:S(2)}, u32[]{:S(2)}) collective-permute-start(f32[2,2,12,16,128]{4,3,2,1,0:T(8,128)S(1)} %shard_map.35), channel_id=1, source_target_pairs={{0,2},{1,3},{2,0},{3,1},{4,6},{5,7},{6,4},{7,5},{8,10},{9,11},{10,... | collective-permute-start | bytes 1179656 | tf_op jit(solution)/shard_map/ppermute | solution.py:553
  80.1 39.6 %collective-permute-start.29 = (f32[2,2,12,16,128]{4,3,2,1,0:T(8,128)S(1)}, f32[2,2,12,16,128]{4,3,2,1,0:T(8,128)S(1)}, u32[]{:S(2)}, u32[]{:S(2)}) collective-permute-start(f32[2,2,12,16,128]{4,3,2,1,0:T(8,128)S(1)} %get-tuple-element.64.refs_0_), channel_id=1, source_target_pairs={{0,1},{1,0},{2,3},{3,2},{4,5},{5,4},{6,7},{7,6},{8,9},{9,8},{10,11... | collective-permute-start | bytes 1179656 | tf_op jit(solution)/shard_map/ppermute | solution.py:556
  87.7 32.0 %collective-permute-start.30 = (f32[2,2,12,16,128]{4,3,2,1,0:T(8,128)S(1)}, f32[2,2,12,16,128]{4,3,2,1,0:T(8,128)S(1)}, u32[]{:S(2)}, u32[]{:S(2)}) collective-permute-start(f32[2,2,12,16,128]{4,3,2,1,0:T(8,128)S(1)} %collective-permute-done.26.refs_1_), channel_id=1, source_target_pairs={{0,1},{1,0},{2,3},{3,2},{4,5},{5,4},{6,7},{7,6},{8,9},{9,8},{10,11... | collective-permute-start | bytes 1179656 | tf_op jit(solution)/shard_map/ppermute | solution.py:556
  89.4 30.3 %collective-permute-start.31 = (f32[2,2,12,16,128]{4,3,2,1,0:T(8,128)S(1)}, f32[2,2,12,16,128]{4,3,2,1,0:T(8,128)S(1)}, u32[]{:S(2)}, u32[]{:S(2)}) collective-permute-start(f32[2,2,12,16,128]{4,3,2,1,0:T(8,128)S(1)} %collective-permute-done.27.refs_2_), channel_id=1, source_target_pairs={{0,1},{1,0},{2,3},{3,2},{4,5},{5,4},{6,7},{7,6},{8,9},{9,8},{10,11... | collective-permute-start | bytes 1179656 | tf_op jit(solution)/shard_map/ppermute | solution.py:556
  97.0 22.7 %collective-permute-start.32 = (f32[2,2,12,16,128]{4,3,2,1,0:T(8,128)S(1)}, f32[2,2,12,16,128]{4,3,2,1,0:T(8,128)S(1)}, u32[]{:S(2)}, u32[]{:S(2)}) collective-permute-start(f32[2,2,12,16,128]{4,3,2,1,0:T(8,128)S(1)} %collective-permute-done.28.refs_3_), channel_id=1, source_target_pairs={{0,1},{1,0},{2,3},{3,2},{4,5},{5,4},{6,7},{7,6},{8,9},{9,8},{10,11... | collective-permute-start | bytes 1179656 | tf_op jit(solution)/shard_map/ppermute | solution.py:557
  (11 other events, 142.6 us)

commit v15 on v14

--- a/solution.py
+++ b/solution.py
@@ -360,14 +360,11 @@
     put(applied(inverse_factor(copies, block.shape[0], cell_total), block), basis)
 
 
-def table_kernel(cell_total, copies, block, table_out, message_far, message, sem):
+def table_kernel(cell_total, copies, block, table_out, message):
     total = block.shape[0]
     table = inverse_factor(copies, total, cell_total)
     table_out[...] = table
     message[...] = jnp.broadcast_to(gram_message(applied(table, block), total)[None], message.shape)
-    leave = pltpu.make_async_copy(message, message_far, sem)
-    leave.start()
-    leave.wait()
 
 
 def last_kernel(cell_total, place, copies, table, block, block_near, *refs):
@@ -478,11 +475,8 @@
     place = jnp.stack([side, me, orb]).astype(jnp.int32)
     mine, edge, *sent = packed(place, orbitals, potential, orb_count)
 
-    pieces = [
-        lax.ppermute(mine, "side", swap),
-        lax.ppermute(edge, slab_axes, slant),
-        lax.ppermute(edge, slab_axes, ahead),
-    ]
+    pieces = [lax.ppermute(mine, "side", swap)]
+    pieces += [lax.ppermute(edge, slab_axes, slant), lax.ppermute(edge, slab_axes, ahead)]
     joined = pl.pallas_call(
         join_kernel,
         out_shape=jax.ShapeDtypeStruct((rows + 2 * WIDE, part, width), jnp.float32),
@@ -560,8 +554,8 @@
             functools.partial(table_kernel, cell_total),
             out_shape=[table_shape, message_shape],
             in_specs=[VMEM] * 2,
-            out_specs=[VMEM, HBM],
-            scratch_shapes=[pltpu.VMEM(message_shape.shape, jnp.float32), pltpu.SemaphoreType.DMA],
+            out_specs=[VMEM] * 2,
+            input_output_aliases={0: 1},
             compiler_params=pltpu.CompilerParams(vmem_limit_bytes=24 * 1024 * 1024),
         )(copies, block)
         return pl.pallas_call(

time: 126 us -> 126 us (level)
  no operation moved by 1% of the time
where the time goes in v15:
time: 126 us
  waiting for transfers between devices  49.4 us (39%)
  starting transfers between devices  32.6 us (26%)
  Pallas kernels  24.4 us (19%)
  blocking collectives  19.6 us (16%)
    all_to_all x2, blocking collectives, exchanged(): return lax.all_to_all(message, ALL, 0, 0)  19.6 us
    ppermute x13, starting transfers between devices, to_partner(): lax.ppermute(piece, ('side', 'orb'), [(flat_of(i), flat_of(i ^ m)) for i...  11.8 us
    ppermute x3, waiting for transfers between devices, whole(): lax.ppermute(joined, 'orb', [(i, i ^ m) for i in range(orb_count)])  9.47 us
    pallas_call x2, Pallas kernels, filtered_pieces(): pl.pallas_call(functools.partial(filter_kernel, at, len(pot_far), early),...  9.35 us
    ppermute x2, waiting for transfers between devices, whole(): straight = lax.ppermute(sent[3 * at + 2], slab_axes, ahead)  7.66 us
    ppermute x1, waiting for transfers between devices, whole(): given.append(lax.ppermute(forward, 'orb', across))  7.61 us
    ppermute x1, waiting for transfers between devices, whole(): lax.ppermute(spare[1], 'side', swap)  7.59 us
    pallas_call x1, Pallas kernels, whole(): pl.pallas_call(functools.partial(last_kernel, cell_total), out_shape=jax....  6.6 us
  transfers between devices with their start and end apart: 33, of which 15 were waited for; matrix products, arithmetic and copies ran while one was open for 0% of the time, Pallas kernels for 11%

profile of v15, /device:TPU:0, one launch (start us, length us, event | category | flops | bytes accessed | tf_op | source)
XLA Modules:
  0.0 126.2 jit_solution(18256370416485566245)
XLA Ops:
  0.1 2.2 %shard_map.28 = (f32[12,16,128]{2,1,0:T(8,128)S(1)}, f32[6,16,128]{2,1,0:T(8,128)S(1)}, f32[9,64,128]{2,1,0:T(8,128)S(1)}, f32[12,64,128]{2,1,0:T(8,128)S(1)}, f...) custom-call(s32[3]{0:T(128)S(1)} %pad_add_fusion.place, ...), custom_call_target="tpu_custom_call" | custom-call | tf_op jit(solution)/shard_map/pallas_call | solution.py:61
  2.3 3.1 %collective-permute-start.3 = (f32[12,16,128]{2,1,0:T(8,128)S(1)}, f32[12,16,128]{2,1,0:T(8,128)S(1)}, u32[]{:S(2)}, u32[]{:S(2)}) collective-permute-start(f32[12,16,128]{2,1,0:T(8,128)S(1)} %get-tuple-element.39), channel_id=1, source_target_pairs={{0,4},{4,0},{1,5},{5,1},{2,6},{6,2},{3,7},{7,3},{8,12},{12,8},{9,1... | collective-permute-start | bytes 294920 | tf_op jit(solution)/shard_map/ppermute | solution.py:478
  5.4 3.5 %collective-permute-start.1 = (f32[9,64,128]{2,1,0:T(8,128)S(1)}, f32[9,64,128]{2,1,0:T(8,128)S(1)}, u32[]{:S(2)}, u32[]{:S(2)}) collective-permute-start(f32[9,64,128]{2,1,0:T(8,128)S(1)} %get-tuple-element.37), channel_id=1, source_target_pairs={{0,28},{4,8},{8,4},{12,16},{16,12},{20,24},{24,20},{28,0},{1,29},{... | collective-permute-start | bytes 884744 | tf_op jit(solution)/shard_map/ppermute | solution.py:494
  9.3 2.4 %collective-permute-start.4 = (f32[6,16,128]{2,1,0:T(8,128)S(1)}, f32[6,16,128]{2,1,0:T(8,128)S(1)}, u32[]{:S(2)}, u32[]{:S(2)}) collective-permute-start(f32[6,16,128]{2,1,0:T(8,128)S(1)} %get-tuple-element.40), channel_id=1, source_target_pairs={{0,28},{4,8},{8,4},{12,16},{16,12},{20,24},{24,20},{28,0},{1,29},{... | collective-permute-start | bytes 147464 | tf_op jit(solution)/shard_map/ppermute | solution.py:479
  11.7 4.7 %collective-permute-done.5.straight = f32[6,16,128]{2,1,0:T(8,128)S(1)} collective-permute-done((f32[6,16,128]{2,1,0:T(8,128)S(1)}, f32[6,16,128]{2,1,0:T(8,128)S(1)}, u32[]{:S(2)}, u32[]{:S(2)}) %collective-permute-start.5) | collective-permute-done | bytes 49184 | tf_op jit(solution)/shard_map/ppermute | solution.py:479
  16.4 2.2 %collective-permute-done.4.slanted = f32[6,16,128]{2,1,0:T(8,128)S(1)} collective-permute-done((f32[6,16,128]{2,1,0:T(8,128)S(1)}, f32[6,16,128]{2,1,0:T(8,128)S(1)}, u32[]{:S(2)}, u32[]{:S(2)}) %collective-permute-start.4) | collective-permute-done | bytes 49184 | tf_op jit(solution)/shard_map/ppermute | solution.py:479
  20.6 5.2 %collective-permute-done.8.rest_3_ = f32[24,16,128]{2,1,0:T(8,128)S(1)} collective-permute-done((f32[24,16,128]{2,1,0:T(8,128)S(1)}, f32[24,16,128]{2,1,0:T(8,128)S(1)}, u32[]{:S(2)}, u32[]{:S(2)}) %collective-permute-start.8) | collective-permute-done | bytes 196640 | tf_op jit(solution)/shard_map/ppermute | solution.py:488
  25.9 4.2 %collective-permute-done.7.rest_2_ = f32[24,16,128]{2,1,0:T(8,128)S(1)} collective-permute-done((f32[24,16,128]{2,1,0:T(8,128)S(1)}, f32[24,16,128]{2,1,0:T(8,128)S(1)}, u32[]{:S(2)}, u32[]{:S(2)}) %collective-permute-start.7) | collective-permute-done | bytes 196640 | tf_op jit(solution)/shard_map/ppermute | solution.py:488
  30.1 2.1 %collective-permute-start.2 = (f32[9,64,128]{2,1,0:T(8,128)S(1)}, f32[9,64,128]{2,1,0:T(8,128)S(1)}, u32[]{:S(2)}, u32[]{:S(2)}) collective-permute-start(f32[9,64,128]{2,1,0:T(8,128)S(1)} %get-tuple-element.38), channel_id=1, source_target_pairs={{0,24},{4,12},{8,0},{12,20},{16,8},{20,28},{24,16},{28,4},{1,25},{... | collective-permute-start | bytes 884744 | tf_op jit(solution)/shard_map/ppermute | solution.py:495
  33.6 2.0 %collective-permute-start.17 = (f32[9,64,128]{2,1,0:T(8,128)S(1)}, f32[9,64,128]{2,1,0:T(8,128)S(1)}, u32[]{:S(2)}, u32[]{:S(2)}) collective-permute-start(f32[9,64,128]{2,1,0:T(8,128)S(1)} %get-tuple-element.49), channel_id=1, source_target_pairs={{0,24},{4,12},{8,0},{12,20},{16,8},{20,28},{24,16},{28,4},{1,25},{... | collective-permute-start | bytes 884744 | tf_op jit(solution)/shard_map/ppermute | solution.py:495
  35.8 4.2 %collective-permute-done.2.straight = f32[9,64,128]{2,1,0:T(8,128)S(1)} collective-permute-done((f32[9,64,128]{2,1,0:T(8,128)S(1)}, f32[9,64,128]{2,1,0:T(8,128)S(1)}, u32[]{:S(2)}, u32[]{:S(2)}) %collective-permute-start.2) | collective-permute-done | bytes 294944 | tf_op jit(solution)/shard_map/ppermute | solution.py:495
  40.0 4.7 %shard_map.30 = (f32[12,16,128]{2,1,0:T(8,128)S(1)}, f32[12,16,128]{2,1,0:T(8,128)S(1)}, f32[12,16,128]{2,1,0:T(8,128)S(1)}, f32[12,16,128]{2,1,0:T(8,128)S(1)},...) custom-call(s32[3]{0:T(128)S(1)} %pad_add_fusion.place, ...), custom_call_target="tpu_custom_call" | custom-call | tf_op jit(solution)/shard_map/pallas_call | solution.py:202
  45.8 2.0 %collective-permute-done.16.slanted = f32[9,64,128]{2,1,0:T(8,128)S(1)} collective-permute-done((f32[9,64,128]{2,1,0:T(8,128)S(1)}, f32[9,64,128]{2,1,0:T(8,128)S(1)}, u32[]{:S(2)}, u32[]{:S(2)}) %collective-permute-start.16) | collective-permute-done | bytes 294944 | tf_op jit(solution)/shard_map/ppermute | solution.py:494
  48.3 3.4 %collective-permute-done.17.straight = f32[9,64,128]{2,1,0:T(8,128)S(1)} collective-permute-done((f32[9,64,128]{2,1,0:T(8,128)S(1)}, f32[9,64,128]{2,1,0:T(8,128)S(1)}, u32[]{:S(2)}, u32[]{:S(2)}) %collective-permute-start.17) | collective-permute-done | bytes 294944 | tf_op jit(solution)/shard_map/ppermute | solution.py:495
  54.1 4.7 %shard_map.31 = (f32[12,16,128]{2,1,0:T(8,128)S(1)}, f32[12,16,128]{2,1,0:T(8,128)S(1)}, f32[12,16,128]{2,1,0:T(8,128)S(1)}, f32[12,16,128]{2,1,0:T(8,128)S(1)},...) custom-call(s32[3]{0:T(128)S(1)} %pad_add_fusion.place, ...), custom_call_target="tpu_custom_call" | custom-call | tf_op jit(solution)/shard_map/pallas_call | solution.py:202
  59.5 2.9 %collective-permute-start.18 = (f32[12,16,128]{2,1,0:T(8,128)S(1)}, f32[12,16,128]{2,1,0:T(8,128)S(1)}, u32[]{:S(2)}, u32[]{:S(2)}) collective-permute-start(f32[12,16,128]{2,1,0:T(8,128)S(1)} %get-tuple-element.50), channel_id=1, source_target_pairs={{0,6},{4,2},{1,7},{5,3},{2,4},{6,0},{3,5},{7,1},{8,14},{12,10},{9,... | collective-permute-start | bytes 294920 | tf_op jit(solution)/shard_map/ppermute | solution.py:505
  69.5 2.0 %collective-permute-done.20.refs_8_ = f32[12,16,128]{2,1,0:T(8,128)S(1)} collective-permute-done((f32[12,16,128]{2,1,0:T(8,128)S(1)}, f32[12,16,128]{2,1,0:T(8,128)S(1)}, u32[]{:S(2)}, u32[]{:S(2)}) %collective-permute-start.20) | collective-permute-done | bytes 98336 | tf_op jit(solution)/shard_map/ppermute | solution.py:505
  73.6 2.0 %shard_map.33 = (f32[16,192,128]{2,1,0:T(8,128)S(1)}, f32[32,1,256]{2,1,0:T(1,128)S(1)}) custom-call(s32[3]{0:T(128)S(1)} %pad_add_fusion.place, f32[12,16,128]{2,1,0:T(8,128)S(1)} %collective-permute-done.9.refs_0_, f32[12,16,128]{2,1,0:T(8,128)S(1)} %collective-permute-done.10.refs_1_, f32[12,16,128]{2,1,0:T(8,128)S(1)} %collective-permute-done.11.refs_2_, ...), custom_call_target="tpu_custom_call" | custom-call | tf_op jit(solution)/shard_map/pallas_call | solution.py:447
  80.1 7.6 %collective-permute-done.26.refs_1_ = f32[2,2,12,16,128]{4,3,2,1,0:T(8,128)S(1)} collective-permute-done((f32[2,2,12,16,128]{4,3,2,1,0:T(8,128)S(1)}, f32[2,2,12,16,128]{4,3,2,1,0:T(8,128)S(1)}, u32[]{:S(2)}, u32[]{:S(2)}) %collective-permute-start.26) | collective-permute-done | bytes 393248 | tf_op jit(solution)/shard_map/ppermute | solution.py:541
  89.4 7.6 %collective-permute-done.28.refs_3_ = f32[2,2,12,16,128]{4,3,2,1,0:T(8,128)S(1)} collective-permute-done((f32[2,2,12,16,128]{4,3,2,1,0:T(8,128)S(1)}, f32[2,2,12,16,128]{4,3,2,1,0:T(8,128)S(1)}, u32[]{:S(2)}, u32[]{:S(2)}) %collective-permute-start.28) | collective-permute-done | bytes 393248 | tf_op jit(solution)/shard_map/ppermute | solution.py:547
  97.0 10.6 %all_to_all.10.copies = f32[32,1,256]{2,1,0:T(1,128)S(1)} all-to-all(f32[32,1,256]{2,1,0:T(1,128)S(1)} %get-tuple-element.60), channel_id=1, replica_groups=mesh['pair'=4,'side'=2,'orb'=4] {'pair','side','orb'}, dimensions={0} | all-to-all | bytes 65536 | tf_op jit(solution)/shard_map/all_to_all | solution.py:528
  107.6 3.0 %shard_map.34 = (f32[16,128]{1,0:T(8,128)S(1)}, f32[32,1,256]{2,1,0:T(1,128)S(1)}) custom-call(f32[32,1,256]{2,1,0:T(1,128)S(1)} %all_to_all.10.copies, f32[16,192,128]{2,1,0:T(8,128)S(1)} %get-tuple-element.61.block), custom_call_target="tpu_custom_call", output_to_operand_aliasing={{1}: (0, {})} | custom-call | tf_op jit(solution)/shard_map/pallas_call | solution.py:553
  110.7 9.0 %all_to_all.11.copies = f32[32,1,256]{2,1,0:T(1,128)S(1)} all-to-all(f32[32,1,256]{2,1,0:T(1,128)S(1)} %get-tuple-element.62), channel_id=1, replica_groups=mesh['pair'=4,'side'=2,'orb'=4] {'pair','side','orb'}, dimensions={0} | all-to-all | bytes 65536 | tf_op jit(solution)/shard_map/all_to_all | solution.py:528
  119.6 6.6 %shard_map.36 = f32[4,12,64,128]{3,2,1,0:T(8,128)} custom-call(s32[3]{0:T(128)S(1)} %pad_add_fusion.place, f32[32,1,256]{2,1,0:T(1,128)S(1)} %all_to_all.11.copies, f32[16,128]{1,0:T(8,128)S(1)} %get-tuple-element.63.table, f32[16,192,128]{2,1,0:T(8,128)S(1)} %get-tuple-element.61.block, f32[16,192,128]{2,1,0:T(8,128)S(1)} %collective-permute-done.25.block_near, ...), custom_call_target="tpu_custom_call" | custom-call | tf_op jit(solution)/shard_map/pallas_call | solution.py:561
  (59 shorter events, 24.1 us)
Async XLA Ops:
  2.3 16.3 %collective-permute-start.3 = (f32[12,16,128]{2,1,0:T(8,128)S(1)}, f32[12,16,128]{2,1,0:T(8,128)S(1)}, u32[]{:S(2)}, u32[]{:S(2)}) collective-permute-start(f32[12,16,128]{2,1,0:T(8,128)S(1)} %get-tuple-element.39), channel_id=1, source_target_pairs={{0,4},{4,0},{1,5},{5,1},{2,6},{6,2},{3,7},{7,3},{8,12},{12,8},{9,1... | collective-permute-start | bytes 294920 | tf_op jit(solution)/shard_map/ppermute | solution.py:478
  5.4 28.3 %collective-permute-start.1 = (f32[9,64,128]{2,1,0:T(8,128)S(1)}, f32[9,64,128]{2,1,0:T(8,128)S(1)}, u32[]{:S(2)}, u32[]{:S(2)}) collective-permute-start(f32[9,64,128]{2,1,0:T(8,128)S(1)} %get-tuple-element.37), channel_id=1, source_target_pairs={{0,28},{4,8},{8,4},{12,16},{16,12},{20,24},{24,20},{28,0},{1,29},{... | collective-permute-start | bytes 884744 | tf_op jit(solution)/shard_map/ppermute | solution.py:494
  9.3 9.3 %collective-permute-start.4 = (f32[6,16,128]{2,1,0:T(8,128)S(1)}, f32[6,16,128]{2,1,0:T(8,128)S(1)}, u32[]{:S(2)}, u32[]{:S(2)}) collective-permute-start(f32[6,16,128]{2,1,0:T(8,128)S(1)} %get-tuple-element.40), channel_id=1, source_target_pairs={{0,28},{4,8},{8,4},{12,16},{16,12},{20,24},{24,20},{28,0},{1,29},{... | collective-permute-start | bytes 147464 | tf_op jit(solution)/shard_map/ppermute | solution.py:479
  18.7 11.4 %collective-permute-start.7 = (f32[24,16,128]{2,1,0:T(8,128)S(1)}, f32[24,16,128]{2,1,0:T(8,128)S(1)}, u32[]{:S(2)}, u32[]{:S(2)}) collective-permute-start(f32[24,16,128]{2,1,0:T(8,128)S(1)} %shard_map.29.rest_0_), channel_id=1, source_target_pairs={{0,2},{1,3},{2,0},{3,1},{4,6},{5,7},{6,4},{7,5},{8,10},{9,11},{10,... | collective-permute-start | bytes 589832 | tf_op jit(solution)/shard_map/ppermute | solution.py:488
  20.3 11.9 %collective-permute-start.6 = (f32[24,16,128]{2,1,0:T(8,128)S(1)}, f32[24,16,128]{2,1,0:T(8,128)S(1)}, u32[]{:S(2)}, u32[]{:S(2)}) collective-permute-start(f32[24,16,128]{2,1,0:T(8,128)S(1)} %shard_map.29.rest_0_), channel_id=1, source_target_pairs={{0,1},{1,0},{2,3},{3,2},{4,5},{5,4},{6,7},{7,6},{8,9},{9,8},{10,11... | collective-permute-start | bytes 589832 | tf_op jit(solution)/shard_map/ppermute | solution.py:488
  20.5 19.4 %collective-permute-start = (f32[12,64,128]{2,1,0:T(8,128)S(1)}, f32[12,64,128]{2,1,0:T(8,128)S(1)}, u32[]{:S(2)}, u32[]{:S(2)}) collective-permute-start(f32[12,64,128]{2,1,0:T(8,128)S(1)} %get-tuple-element.36), channel_id=1, source_target_pairs={{0,4},{4,0},{1,5},{5,1},{2,6},{6,2},{3,7},{7,3},{8,12},{12,8},{9,1... | collective-permute-start | bytes 1179656 | tf_op jit(solution)/shard_map/ppermute | solution.py:493
  25.8 26.2 %collective-permute-start.15 = (f32[12,64,128]{2,1,0:T(8,128)S(1)}, f32[12,64,128]{2,1,0:T(8,128)S(1)}, u32[]{:S(2)}, u32[]{:S(2)}) collective-permute-start(f32[12,64,128]{2,1,0:T(8,128)S(1)} %get-tuple-element.47), channel_id=1, source_target_pairs={{0,4},{4,0},{1,5},{5,1},{2,6},{6,2},{3,7},{7,3},{8,12},{12,8},{9,1... | collective-permute-start | bytes 1179656 | tf_op jit(solution)/shard_map/ppermute | solution.py:493
  30.1 9.9 %collective-permute-start.2 = (f32[9,64,128]{2,1,0:T(8,128)S(1)}, f32[9,64,128]{2,1,0:T(8,128)S(1)}, u32[]{:S(2)}, u32[]{:S(2)}) collective-permute-start(f32[9,64,128]{2,1,0:T(8,128)S(1)} %get-tuple-element.38), channel_id=1, source_target_pairs={{0,24},{4,12},{8,0},{12,20},{16,8},{20,28},{24,16},{28,4},{1,25},{... | collective-permute-start | bytes 884744 | tf_op jit(solution)/shard_map/ppermute | solution.py:495
  32.2 15.6 %collective-permute-start.16 = (f32[9,64,128]{2,1,0:T(8,128)S(1)}, f32[9,64,128]{2,1,0:T(8,128)S(1)}, u32[]{:S(2)}, u32[]{:S(2)}) collective-permute-start(f32[9,64,128]{2,1,0:T(8,128)S(1)} %get-tuple-element.48), channel_id=1, source_target_pairs={{0,28},{4,8},{8,4},{12,16},{16,12},{20,24},{24,20},{28,0},{1,29},{... | collective-permute-start | bytes 884744 | tf_op jit(solution)/shard_map/ppermute | solution.py:494
  33.6 18.1 %collective-permute-start.17 = (f32[9,64,128]{2,1,0:T(8,128)S(1)}, f32[9,64,128]{2,1,0:T(8,128)S(1)}, u32[]{:S(2)}, u32[]{:S(2)}) collective-permute-start(f32[9,64,128]{2,1,0:T(8,128)S(1)} %get-tuple-element.49), channel_id=1, source_target_pairs={{0,24},{4,12},{8,0},{12,20},{16,8},{20,28},{24,16},{28,4},{1,25},{... | collective-permute-start | bytes 884744 | tf_op jit(solution)/shard_map/ppermute | solution.py:495
  44.7 14.7 %collective-permute-start.9 = (f32[12,16,128]{2,1,0:T(8,128)S(1)}, f32[12,16,128]{2,1,0:T(8,128)S(1)}, u32[]{:S(2)}, u32[]{:S(2)}) collective-permute-start(f32[12,16,128]{2,1,0:T(8,128)S(1)} %get-tuple-element.41), channel_id=1, source_target_pairs={{0,6},{4,2},{1,7},{5,3},{2,4},{6,0},{3,5},{7,1},{8,14},{12,10},{9,... | collective-permute-start | bytes 294920 | tf_op jit(solution)/shard_map/ppermute | solution.py:505
  45.5 14.0 %collective-permute-start.10 = (f32[12,16,128]{2,1,0:T(8,128)S(1)}, f32[12,16,128]{2,1,0:T(8,128)S(1)}, u32[]{:S(2)}, u32[]{:S(2)}) collective-permute-start(f32[12,16,128]{2,1,0:T(8,128)S(1)} %get-tuple-element.42), channel_id=1, source_target_pairs={{0,7},{4,3},{1,6},{5,2},{2,5},{6,1},{3,4},{7,0},{8,15},{12,11},{9,... | collective-permute-start | bytes 294920 | tf_op jit(solution)/shard_map/ppermute | solution.py:505
  47.8 14.6 %collective-permute-start.11 = (f32[12,16,128]{2,1,0:T(8,128)S(1)}, f32[12,16,128]{2,1,0:T(8,128)S(1)}, u32[]{:S(2)}, u32[]{:S(2)}) collective-permute-start(f32[12,16,128]{2,1,0:T(8,128)S(1)} %get-tuple-element.43), channel_id=1, source_target_pairs={{0,2},{4,6},{1,3},{5,7},{2,0},{6,4},{3,1},{7,5},{8,10},{12,14},{9,... | collective-permute-start | bytes 294920 | tf_op jit(solution)/shard_map/ppermute | solution.py:505
  51.7 10.7 %collective-permute-start.12 = (f32[12,16,128]{2,1,0:T(8,128)S(1)}, f32[12,16,128]{2,1,0:T(8,128)S(1)}, u32[]{:S(2)}, u32[]{:S(2)}) collective-permute-start(f32[12,16,128]{2,1,0:T(8,128)S(1)} %get-tuple-element.44), channel_id=1, source_target_pairs={{0,3},{4,7},{1,2},{5,6},{2,1},{6,5},{3,0},{7,4},{8,11},{12,15},{9,... | collective-permute-start | bytes 294920 | tf_op jit(solution)/shard_map/ppermute | solution.py:505
  52.1 10.5 %collective-permute-start.13 = (f32[12,16,128]{2,1,0:T(8,128)S(1)}, f32[12,16,128]{2,1,0:T(8,128)S(1)}, u32[]{:S(2)}, u32[]{:S(2)}) collective-permute-start(f32[12,16,128]{2,1,0:T(8,128)S(1)} %get-tuple-element.45), channel_id=1, source_target_pairs={{0,4},{4,0},{1,5},{5,1},{2,6},{6,2},{3,7},{7,3},{8,12},{12,8},{9,1... | collective-permute-start | bytes 294920 | tf_op jit(solution)/shard_map/ppermute | solution.py:505
  62.4 11.2 %collective-permute-start.24 = (f32[2,12,16,128]{3,2,1,0:T(8,128)S(1)}, f32[2,12,16,128]{3,2,1,0:T(8,128)S(1)}, u32[]{:S(2)}, u32[]{:S(2)}) collective-permute-start(f32[2,12,16,128]{3,2,1,0:T(8,128)S(1)} %get-tuple-element.59), channel_id=1, source_target_pairs={{0,1},{4,5},{1,0},{5,4},{2,3},{6,7},{3,2},{7,6},{8,9},{12,13},{9,8... | collective-permute-start | bytes 589832 | tf_op jit(solution)/shard_map/ppermute | solution.py:505
  75.7 44.0 %collective-permute-start.25 = (f32[16,192,128]{2,1,0:T(8,128)S(1)}, f32[16,192,128]{2,1,0:T(8,128)S(1)}, u32[]{:S(2)}, u32[]{:S(2)}) collective-permute-start(f32[16,192,128]{2,1,0:T(8,128)S(1)} %get-tuple-element.61.block), channel_id=1, source_target_pairs={{0,1},{1,0},{2,3},{3,2},{4,5},{5,4},{6,7},{7,6},{8,9},{9,8},{10,11... | collective-permute-start | bytes 4718600 | tf_op jit(solution)/shard_map/ppermute | solution.py:548
  76.6 11.1 %collective-permute-start.26 = (f32[2,2,12,16,128]{4,3,2,1,0:T(8,128)S(1)}, f32[2,2,12,16,128]{4,3,2,1,0:T(8,128)S(1)}, u32[]{:S(2)}, u32[]{:S(2)}) collective-permute-start(f32[2,2,12,16,128]{4,3,2,1,0:T(8,128)S(1)} %get-tuple-element.65), channel_id=1, source_target_pairs={{0,4},{4,0},{1,5},{5,1},{2,6},{6,2},{3,7},{7,3},{8,12},{12,8},{9,1... | collective-permute-start | bytes 1179656 | tf_op jit(solution)/shard_map/ppermute | solution.py:541
  77.4 12.0 %collective-permute-start.27 = (f32[2,2,12,16,128]{4,3,2,1,0:T(8,128)S(1)}, f32[2,2,12,16,128]{4,3,2,1,0:T(8,128)S(1)}, u32[]{:S(2)}, u32[]{:S(2)}) collective-permute-start(f32[2,2,12,16,128]{4,3,2,1,0:T(8,128)S(1)} %get-tuple-element.66), channel_id=1, source_target_pairs={{0,2},{1,3},{2,0},{3,1},{4,6},{5,7},{6,4},{7,5},{8,10},{9,11},{10,... | collective-permute-start | bytes 1179656 | tf_op jit(solution)/shard_map/ppermute | solution.py:542
  78.6 18.4 %collective-permute-start.28 = (f32[2,2,12,16,128]{4,3,2,1,0:T(8,128)S(1)}, f32[2,2,12,16,128]{4,3,2,1,0:T(8,128)S(1)}, u32[]{:S(2)}, u32[]{:S(2)}) collective-permute-start(f32[2,2,12,16,128]{4,3,2,1,0:T(8,128)S(1)} %shard_map.35), channel_id=1, source_target_pairs={{0,2},{1,3},{2,0},{3,1},{4,6},{5,7},{6,4},{7,5},{8,10},{9,11},{10,... | collective-permute-start | bytes 1179656 | tf_op jit(solution)/shard_map/ppermute | solution.py:547
  80.1 39.5 %collective-permute-start.29 = (f32[2,2,12,16,128]{4,3,2,1,0:T(8,128)S(1)}, f32[2,2,12,16,128]{4,3,2,1,0:T(8,128)S(1)}, u32[]{:S(2)}, u32[]{:S(2)}) collective-permute-start(f32[2,2,12,16,128]{4,3,2,1,0:T(8,128)S(1)} %get-tuple-element.64.refs_0_), channel_id=1, source_target_pairs={{0,1},{1,0},{2,3},{3,2},{4,5},{5,4},{6,7},{7,6},{8,9},{9,8},{10,11... | collective-permute-start | bytes 1179656 | tf_op jit(solution)/shard_map/ppermute | solution.py:550
  87.7 31.9 %collective-permute-start.30 = (f32[2,2,12,16,128]{4,3,2,1,0:T(8,128)S(1)}, f32[2,2,12,16,128]{4,3,2,1,0:T(8,128)S(1)}, u32[]{:S(2)}, u32[]{:S(2)}) collective-permute-start(f32[2,2,12,16,128]{4,3,2,1,0:T(8,128)S(1)} %collective-permute-done.26.refs_1_), channel_id=1, source_target_pairs={{0,1},{1,0},{2,3},{3,2},{4,5},{5,4},{6,7},{7,6},{8,9},{9,8},{10,11... | collective-permute-start | bytes 1179656 | tf_op jit(solution)/shard_map/ppermute | solution.py:550
  89.4 30.2 %collective-permute-start.31 = (f32[2,2,12,16,128]{4,3,2,1,0:T(8,128)S(1)}, f32[2,2,12,16,128]{4,3,2,1,0:T(8,128)S(1)}, u32[]{:S(2)}, u32[]{:S(2)}) collective-permute-start(f32[2,2,12,16,128]{4,3,2,1,0:T(8,128)S(1)} %collective-permute-done.27.refs_2_), channel_id=1, source_target_pairs={{0,1},{1,0},{2,3},{3,2},{4,5},{5,4},{6,7},{7,6},{8,9},{9,8},{10,11... | collective-permute-start | bytes 1179656 | tf_op jit(solution)/shard_map/ppermute | solution.py:550
  97.0 22.6 %collective-permute-start.32 = (f32[2,2,12,16,128]{4,3,2,1,0:T(8,128)S(1)}, f32[2,2,12,16,128]{4,3,2,1,0:T(8,128)S(1)}, u32[]{:S(2)}, u32[]{:S(2)}) collective-permute-start(f32[2,2,12,16,128]{4,3,2,1,0:T(8,128)S(1)} %collective-permute-done.28.refs_3_), channel_id=1, source_target_pairs={{0,1},{1,0},{2,3},{3,2},{4,5},{5,4},{6,7},{7,6},{8,9},{9,8},{10,11... | collective-permute-start | bytes 1179656 | tf_op jit(solution)/shard_map/ppermute | solution.py:551
  (11 other events, 142.6 us)

commit v16 on v15

--- a/solution.py
+++ b/solution.py
@@ -400,7 +400,7 @@
                     out[i, row, pl.ds(column, EIGHT), :] = sums[i]
             return carry
 
-        lax.fori_loop(0, rows, body, 0, unroll=2)
+        lax.fori_loop(0, rows, body, 0, unroll=4)
 
     def at(ref, index):
         def load(row, strip):
@@ -475,8 +475,11 @@
     place = jnp.stack([side, me, orb]).astype(jnp.int32)
     mine, edge, *sent = packed(place, orbitals, potential, orb_count)
 
-    pieces = [lax.ppermute(mine, "side", swap)]
-    pieces += [lax.ppermute(edge, slab_axes, slant), lax.ppermute(edge, slab_axes, ahead)]
+    pieces = [
+        lax.ppermute(mine, "side", swap),
+        lax.ppermute(edge, slab_axes, slant),
+        lax.ppermute(edge, slab_axes, ahead),
+    ]
     joined = pl.pallas_call(
         join_kernel,
         out_shape=jax.ShapeDtypeStruct((rows + 2 * WIDE, part, width), jnp.float32),

time: 126 us -> 126 us (level)
  no operation moved by 1% of the time
where the time goes in v16:
time: 126 us
  waiting for transfers between devices  49.4 us (39%)
  starting transfers between devices  32.6 us (26%)
  Pallas kernels  24.2 us (19%)
  blocking collectives  19.6 us (16%)
    all_to_all x2, blocking collectives, exchanged(): return lax.all_to_all(message, ALL, 0, 0)  19.6 us
    ppermute x13, starting transfers between devices, to_partner(): lax.ppermute(piece, ('side', 'orb'), [(flat_of(i), flat_of(i ^ m)) for i...  11.8 us
    ppermute x3, waiting for transfers between devices, whole(): lax.ppermute(joined, 'orb', [(i, i ^ m) for i in range(orb_count)])  9.47 us
    pallas_call x2, Pallas kernels, filtered_pieces(): pl.pallas_call(functools.partial(filter_kernel, at, len(pot_far), early),...  9.35 us
    ppermute x2, waiting for transfers between devices, whole(): straight = lax.ppermute(sent[3 * at + 2], slab_axes, ahead)  7.66 us
    ppermute x1, waiting for transfers between devices, whole(): given.append(lax.ppermute(forward, 'orb', across))  7.61 us
    ppermute x1, waiting for transfers between devices, whole(): lax.ppermute(spare[1], 'side', swap)  7.59 us
    pallas_call x1, Pallas kernels, whole(): pl.pallas_call(functools.partial(last_kernel, cell_total), out_shape=jax....  6.37 us
  transfers between devices with their start and end apart: 33, of which 15 were waited for; matrix products, arithmetic and copies ran while one was open for 0% of the time, Pallas kernels for 11%

profile of v16, /device:TPU:0, one launch (start us, length us, event | category | flops | bytes accessed | tf_op | source)
XLA Modules:
  0.0 126.0 jit_solution(15518959985663243761)
XLA Ops:
  0.1 2.2 %shard_map.28 = (f32[12,16,128]{2,1,0:T(8,128)S(1)}, f32[6,16,128]{2,1,0:T(8,128)S(1)}, f32[9,64,128]{2,1,0:T(8,128)S(1)}, f32[12,64,128]{2,1,0:T(8,128)S(1)}, f...) custom-call(s32[3]{0:T(128)S(1)} %pad_add_fusion.place, ...), custom_call_target="tpu_custom_call" | custom-call | tf_op jit(solution)/shard_map/pallas_call | solution.py:61
  2.3 3.1 %collective-permute-start.3 = (f32[12,16,128]{2,1,0:T(8,128)S(1)}, f32[12,16,128]{2,1,0:T(8,128)S(1)}, u32[]{:S(2)}, u32[]{:S(2)}) collective-permute-start(f32[12,16,128]{2,1,0:T(8,128)S(1)} %get-tuple-element.39), channel_id=1, source_target_pairs={{0,4},{4,0},{1,5},{5,1},{2,6},{6,2},{3,7},{7,3},{8,12},{12,8},{9,1... | collective-permute-start | bytes 294920 | tf_op jit(solution)/shard_map/ppermute | solution.py:479
  5.4 3.5 %collective-permute-start.1 = (f32[9,64,128]{2,1,0:T(8,128)S(1)}, f32[9,64,128]{2,1,0:T(8,128)S(1)}, u32[]{:S(2)}, u32[]{:S(2)}) collective-permute-start(f32[9,64,128]{2,1,0:T(8,128)S(1)} %get-tuple-element.37), channel_id=1, source_target_pairs={{0,28},{4,8},{8,4},{12,16},{16,12},{20,24},{24,20},{28,0},{1,29},{... | collective-permute-start | bytes 884744 | tf_op jit(solution)/shard_map/ppermute | solution.py:497
  9.3 2.4 %collective-permute-start.4 = (f32[6,16,128]{2,1,0:T(8,128)S(1)}, f32[6,16,128]{2,1,0:T(8,128)S(1)}, u32[]{:S(2)}, u32[]{:S(2)}) collective-permute-start(f32[6,16,128]{2,1,0:T(8,128)S(1)} %get-tuple-element.40), channel_id=1, source_target_pairs={{0,28},{4,8},{8,4},{12,16},{16,12},{20,24},{24,20},{28,0},{1,29},{... | collective-permute-start | bytes 147464 | tf_op jit(solution)/shard_map/ppermute | solution.py:480
  11.7 4.7 %collective-permute-done.5.straight = f32[6,16,128]{2,1,0:T(8,128)S(1)} collective-permute-done((f32[6,16,128]{2,1,0:T(8,128)S(1)}, f32[6,16,128]{2,1,0:T(8,128)S(1)}, u32[]{:S(2)}, u32[]{:S(2)}) %collective-permute-start.5) | collective-permute-done | bytes 49184 | tf_op jit(solution)/shard_map/ppermute | solution.py:481
  16.4 2.2 %collective-permute-done.4.slanted = f32[6,16,128]{2,1,0:T(8,128)S(1)} collective-permute-done((f32[6,16,128]{2,1,0:T(8,128)S(1)}, f32[6,16,128]{2,1,0:T(8,128)S(1)}, u32[]{:S(2)}, u32[]{:S(2)}) %collective-permute-start.4) | collective-permute-done | bytes 49184 | tf_op jit(solution)/shard_map/ppermute | solution.py:480
  20.6 5.2 %collective-permute-done.8.rest_3_ = f32[24,16,128]{2,1,0:T(8,128)S(1)} collective-permute-done((f32[24,16,128]{2,1,0:T(8,128)S(1)}, f32[24,16,128]{2,1,0:T(8,128)S(1)}, u32[]{:S(2)}, u32[]{:S(2)}) %collective-permute-start.8) | collective-permute-done | bytes 196640 | tf_op jit(solution)/shard_map/ppermute | solution.py:491
  25.9 4.2 %collective-permute-done.7.rest_2_ = f32[24,16,128]{2,1,0:T(8,128)S(1)} collective-permute-done((f32[24,16,128]{2,1,0:T(8,128)S(1)}, f32[24,16,128]{2,1,0:T(8,128)S(1)}, u32[]{:S(2)}, u32[]{:S(2)}) %collective-permute-start.7) | collective-permute-done | bytes 196640 | tf_op jit(solution)/shard_map/ppermute | solution.py:491
  30.1 2.1 %collective-permute-start.2 = (f32[9,64,128]{2,1,0:T(8,128)S(1)}, f32[9,64,128]{2,1,0:T(8,128)S(1)}, u32[]{:S(2)}, u32[]{:S(2)}) collective-permute-start(f32[9,64,128]{2,1,0:T(8,128)S(1)} %get-tuple-element.38), channel_id=1, source_target_pairs={{0,24},{4,12},{8,0},{12,20},{16,8},{20,28},{24,16},{28,4},{1,25},{... | collective-permute-start | bytes 884744 | tf_op jit(solution)/shard_map/ppermute | solution.py:498
  33.6 2.0 %collective-permute-start.17 = (f32[9,64,128]{2,1,0:T(8,128)S(1)}, f32[9,64,128]{2,1,0:T(8,128)S(1)}, u32[]{:S(2)}, u32[]{:S(2)}) collective-permute-start(f32[9,64,128]{2,1,0:T(8,128)S(1)} %get-tuple-element.49), channel_id=1, source_target_pairs={{0,24},{4,12},{8,0},{12,20},{16,8},{20,28},{24,16},{28,4},{1,25},{... | collective-permute-start | bytes 884744 | tf_op jit(solution)/shard_map/ppermute | solution.py:498
  35.8 4.2 %collective-permute-done.2.straight = f32[9,64,128]{2,1,0:T(8,128)S(1)} collective-permute-done((f32[9,64,128]{2,1,0:T(8,128)S(1)}, f32[9,64,128]{2,1,0:T(8,128)S(1)}, u32[]{:S(2)}, u32[]{:S(2)}) %collective-permute-start.2) | collective-permute-done | bytes 294944 | tf_op jit(solution)/shard_map/ppermute | solution.py:498
  40.0 4.7 %shard_map.30 = (f32[12,16,128]{2,1,0:T(8,128)S(1)}, f32[12,16,128]{2,1,0:T(8,128)S(1)}, f32[12,16,128]{2,1,0:T(8,128)S(1)}, f32[12,16,128]{2,1,0:T(8,128)S(1)},...) custom-call(s32[3]{0:T(128)S(1)} %pad_add_fusion.place, ...), custom_call_target="tpu_custom_call" | custom-call | tf_op jit(solution)/shard_map/pallas_call | solution.py:202
  45.8 2.0 %collective-permute-done.16.slanted = f32[9,64,128]{2,1,0:T(8,128)S(1)} collective-permute-done((f32[9,64,128]{2,1,0:T(8,128)S(1)}, f32[9,64,128]{2,1,0:T(8,128)S(1)}, u32[]{:S(2)}, u32[]{:S(2)}) %collective-permute-start.16) | collective-permute-done | bytes 294944 | tf_op jit(solution)/shard_map/ppermute | solution.py:497
  48.3 3.4 %collective-permute-done.17.straight = f32[9,64,128]{2,1,0:T(8,128)S(1)} collective-permute-done((f32[9,64,128]{2,1,0:T(8,128)S(1)}, f32[9,64,128]{2,1,0:T(8,128)S(1)}, u32[]{:S(2)}, u32[]{:S(2)}) %collective-permute-start.17) | collective-permute-done | bytes 294944 | tf_op jit(solution)/shard_map/ppermute | solution.py:498
  54.1 4.7 %shard_map.31 = (f32[12,16,128]{2,1,0:T(8,128)S(1)}, f32[12,16,128]{2,1,0:T(8,128)S(1)}, f32[12,16,128]{2,1,0:T(8,128)S(1)}, f32[12,16,128]{2,1,0:T(8,128)S(1)},...) custom-call(s32[3]{0:T(128)S(1)} %pad_add_fusion.place, ...), custom_call_target="tpu_custom_call" | custom-call | tf_op jit(solution)/shard_map/pallas_call | solution.py:202
  59.5 2.9 %collective-permute-start.18 = (f32[12,16,128]{2,1,0:T(8,128)S(1)}, f32[12,16,128]{2,1,0:T(8,128)S(1)}, u32[]{:S(2)}, u32[]{:S(2)}) collective-permute-start(f32[12,16,128]{2,1,0:T(8,128)S(1)} %get-tuple-element.50), channel_id=1, source_target_pairs={{0,6},{4,2},{1,7},{5,3},{2,4},{6,0},{3,5},{7,1},{8,14},{12,10},{9,... | collective-permute-start | bytes 294920 | tf_op jit(solution)/shard_map/ppermute | solution.py:508
  69.5 2.0 %collective-permute-done.20.refs_8_ = f32[12,16,128]{2,1,0:T(8,128)S(1)} collective-permute-done((f32[12,16,128]{2,1,0:T(8,128)S(1)}, f32[12,16,128]{2,1,0:T(8,128)S(1)}, u32[]{:S(2)}, u32[]{:S(2)}) %collective-permute-start.20) | collective-permute-done | bytes 98336 | tf_op jit(solution)/shard_map/ppermute | solution.py:508
  73.6 2.0 %shard_map.33 = (f32[16,192,128]{2,1,0:T(8,128)S(1)}, f32[32,1,256]{2,1,0:T(1,128)S(1)}) custom-call(s32[3]{0:T(128)S(1)} %pad_add_fusion.place, f32[12,16,128]{2,1,0:T(8,128)S(1)} %collective-permute-done.9.refs_0_, f32[12,16,128]{2,1,0:T(8,128)S(1)} %collective-permute-done.10.refs_1_, f32[12,16,128]{2,1,0:T(8,128)S(1)} %collective-permute-done.11.refs_2_, ...), custom_call_target="tpu_custom_call" | custom-call | tf_op jit(solution)/shard_map/pallas_call | solution.py:447
  80.1 7.6 %collective-permute-done.26.refs_1_ = f32[2,2,12,16,128]{4,3,2,1,0:T(8,128)S(1)} collective-permute-done((f32[2,2,12,16,128]{4,3,2,1,0:T(8,128)S(1)}, f32[2,2,12,16,128]{4,3,2,1,0:T(8,128)S(1)}, u32[]{:S(2)}, u32[]{:S(2)}) %collective-permute-start.26) | collective-permute-done | bytes 393248 | tf_op jit(solution)/shard_map/ppermute | solution.py:544
  89.4 7.6 %collective-permute-done.28.refs_3_ = f32[2,2,12,16,128]{4,3,2,1,0:T(8,128)S(1)} collective-permute-done((f32[2,2,12,16,128]{4,3,2,1,0:T(8,128)S(1)}, f32[2,2,12,16,128]{4,3,2,1,0:T(8,128)S(1)}, u32[]{:S(2)}, u32[]{:S(2)}) %collective-permute-start.28) | collective-permute-done | bytes 393248 | tf_op jit(solution)/shard_map/ppermute | solution.py:550
  97.0 10.6 %all_to_all.10.copies = f32[32,1,256]{2,1,0:T(1,128)S(1)} all-to-all(f32[32,1,256]{2,1,0:T(1,128)S(1)} %get-tuple-element.60), channel_id=1, replica_groups=mesh['pair'=4,'side'=2,'orb'=4] {'pair','side','orb'}, dimensions={0} | all-to-all | bytes 65536 | tf_op jit(solution)/shard_map/all_to_all | solution.py:531
  107.6 3.0 %shard_map.34 = (f32[16,128]{1,0:T(8,128)S(1)}, f32[32,1,256]{2,1,0:T(1,128)S(1)}) custom-call(f32[32,1,256]{2,1,0:T(1,128)S(1)} %all_to_all.10.copies, f32[16,192,128]{2,1,0:T(8,128)S(1)} %get-tuple-element.61.block), custom_call_target="tpu_custom_call", output_to_operand_aliasing={{1}: (0, {})} | custom-call | tf_op jit(solution)/shard_map/pallas_call | solution.py:556
  110.7 9.0 %all_to_all.11.copies = f32[32,1,256]{2,1,0:T(1,128)S(1)} all-to-all(f32[32,1,256]{2,1,0:T(1,128)S(1)} %get-tuple-element.62), channel_id=1, replica_groups=mesh['pair'=4,'side'=2,'orb'=4] {'pair','side','orb'}, dimensions={0} | all-to-all | bytes 65536 | tf_op jit(solution)/shard_map/all_to_all | solution.py:531
  119.6 6.4 %shard_map.36 = f32[4,12,64,128]{3,2,1,0:T(8,128)} custom-call(s32[3]{0:T(128)S(1)} %pad_add_fusion.place, f32[32,1,256]{2,1,0:T(1,128)S(1)} %all_to_all.11.copies, f32[16,128]{1,0:T(8,128)S(1)} %get-tuple-element.63.table, f32[16,192,128]{2,1,0:T(8,128)S(1)} %get-tuple-element.61.block, f32[16,192,128]{2,1,0:T(8,128)S(1)} %collective-permute-done.25.block_near, ...), custom_call_target="tpu_custom_call" | custom-call | tf_op jit(solution)/shard_map/pallas_call | solution.py:564
  (59 shorter events, 24.1 us)
Async XLA Ops:
  2.3 16.3 %collective-permute-start.3 = (f32[12,16,128]{2,1,0:T(8,128)S(1)}, f32[12,16,128]{2,1,0:T(8,128)S(1)}, u32[]{:S(2)}, u32[]{:S(2)}) collective-permute-start(f32[12,16,128]{2,1,0:T(8,128)S(1)} %get-tuple-element.39), channel_id=1, source_target_pairs={{0,4},{4,0},{1,5},{5,1},{2,6},{6,2},{3,7},{7,3},{8,12},{12,8},{9,1... | collective-permute-start | bytes 294920 | tf_op jit(solution)/shard_map/ppermute | solution.py:479
  5.4 28.3 %collective-permute-start.1 = (f32[9,64,128]{2,1,0:T(8,128)S(1)}, f32[9,64,128]{2,1,0:T(8,128)S(1)}, u32[]{:S(2)}, u32[]{:S(2)}) collective-permute-start(f32[9,64,128]{2,1,0:T(8,128)S(1)} %get-tuple-element.37), channel_id=1, source_target_pairs={{0,28},{4,8},{8,4},{12,16},{16,12},{20,24},{24,20},{28,0},{1,29},{... | collective-permute-start | bytes 884744 | tf_op jit(solution)/shard_map/ppermute | solution.py:497
  9.3 9.3 %collective-permute-start.4 = (f32[6,16,128]{2,1,0:T(8,128)S(1)}, f32[6,16,128]{2,1,0:T(8,128)S(1)}, u32[]{:S(2)}, u32[]{:S(2)}) collective-permute-start(f32[6,16,128]{2,1,0:T(8,128)S(1)} %get-tuple-element.40), channel_id=1, source_target_pairs={{0,28},{4,8},{8,4},{12,16},{16,12},{20,24},{24,20},{28,0},{1,29},{... | collective-permute-start | bytes 147464 | tf_op jit(solution)/shard_map/ppermute | solution.py:480
  18.7 11.4 %collective-permute-start.7 = (f32[24,16,128]{2,1,0:T(8,128)S(1)}, f32[24,16,128]{2,1,0:T(8,128)S(1)}, u32[]{:S(2)}, u32[]{:S(2)}) collective-permute-start(f32[24,16,128]{2,1,0:T(8,128)S(1)} %shard_map.29.rest_0_), channel_id=1, source_target_pairs={{0,2},{1,3},{2,0},{3,1},{4,6},{5,7},{6,4},{7,5},{8,10},{9,11},{10,... | collective-permute-start | bytes 589832 | tf_op jit(solution)/shard_map/ppermute | solution.py:491
  20.3 11.9 %collective-permute-start.6 = (f32[24,16,128]{2,1,0:T(8,128)S(1)}, f32[24,16,128]{2,1,0:T(8,128)S(1)}, u32[]{:S(2)}, u32[]{:S(2)}) collective-permute-start(f32[24,16,128]{2,1,0:T(8,128)S(1)} %shard_map.29.rest_0_), channel_id=1, source_target_pairs={{0,1},{1,0},{2,3},{3,2},{4,5},{5,4},{6,7},{7,6},{8,9},{9,8},{10,11... | collective-permute-start | bytes 589832 | tf_op jit(solution)/shard_map/ppermute | solution.py:491
  20.5 19.4 %collective-permute-start = (f32[12,64,128]{2,1,0:T(8,128)S(1)}, f32[12,64,128]{2,1,0:T(8,128)S(1)}, u32[]{:S(2)}, u32[]{:S(2)}) collective-permute-start(f32[12,64,128]{2,1,0:T(8,128)S(1)} %get-tuple-element.36), channel_id=1, source_target_pairs={{0,4},{4,0},{1,5},{5,1},{2,6},{6,2},{3,7},{7,3},{8,12},{12,8},{9,1... | collective-permute-start | bytes 1179656 | tf_op jit(solution)/shard_map/ppermute | solution.py:496
  25.8 26.2 %collective-permute-start.15 = (f32[12,64,128]{2,1,0:T(8,128)S(1)}, f32[12,64,128]{2,1,0:T(8,128)S(1)}, u32[]{:S(2)}, u32[]{:S(2)}) collective-permute-start(f32[12,64,128]{2,1,0:T(8,128)S(1)} %get-tuple-element.47), channel_id=1, source_target_pairs={{0,4},{4,0},{1,5},{5,1},{2,6},{6,2},{3,7},{7,3},{8,12},{12,8},{9,1... | collective-permute-start | bytes 1179656 | tf_op jit(solution)/shard_map/ppermute | solution.py:496
  30.1 9.9 %collective-permute-start.2 = (f32[9,64,128]{2,1,0:T(8,128)S(1)}, f32[9,64,128]{2,1,0:T(8,128)S(1)}, u32[]{:S(2)}, u32[]{:S(2)}) collective-permute-start(f32[9,64,128]{2,1,0:T(8,128)S(1)} %get-tuple-element.38), channel_id=1, source_target_pairs={{0,24},{4,12},{8,0},{12,20},{16,8},{20,28},{24,16},{28,4},{1,25},{... | collective-permute-start | bytes 884744 | tf_op jit(solution)/shard_map/ppermute | solution.py:498
  32.2 15.6 %collective-permute-start.16 = (f32[9,64,128]{2,1,0:T(8,128)S(1)}, f32[9,64,128]{2,1,0:T(8,128)S(1)}, u32[]{:S(2)}, u32[]{:S(2)}) collective-permute-start(f32[9,64,128]{2,1,0:T(8,128)S(1)} %get-tuple-element.48), channel_id=1, source_target_pairs={{0,28},{4,8},{8,4},{12,16},{16,12},{20,24},{24,20},{28,0},{1,29},{... | collective-permute-start | bytes 884744 | tf_op jit(solution)/shard_map/ppermute | solution.py:497
  33.6 18.1 %collective-permute-start.17 = (f32[9,64,128]{2,1,0:T(8,128)S(1)}, f32[9,64,128]{2,1,0:T(8,128)S(1)}, u32[]{:S(2)}, u32[]{:S(2)}) collective-permute-start(f32[9,64,128]{2,1,0:T(8,128)S(1)} %get-tuple-element.49), channel_id=1, source_target_pairs={{0,24},{4,12},{8,0},{12,20},{16,8},{20,28},{24,16},{28,4},{1,25},{... | collective-permute-start | bytes 884744 | tf_op jit(solution)/shard_map/ppermute | solution.py:498
  44.7 14.7 %collective-permute-start.9 = (f32[12,16,128]{2,1,0:T(8,128)S(1)}, f32[12,16,128]{2,1,0:T(8,128)S(1)}, u32[]{:S(2)}, u32[]{:S(2)}) collective-permute-start(f32[12,16,128]{2,1,0:T(8,128)S(1)} %get-tuple-element.41), channel_id=1, source_target_pairs={{0,6},{4,2},{1,7},{5,3},{2,4},{6,0},{3,5},{7,1},{8,14},{12,10},{9,... | collective-permute-start | bytes 294920 | tf_op jit(solution)/shard_map/ppermute | solution.py:508
  45.5 14.0 %collective-permute-start.10 = (f32[12,16,128]{2,1,0:T(8,128)S(1)}, f32[12,16,128]{2,1,0:T(8,128)S(1)}, u32[]{:S(2)}, u32[]{:S(2)}) collective-permute-start(f32[12,16,128]{2,1,0:T(8,128)S(1)} %get-tuple-element.42), channel_id=1, source_target_pairs={{0,7},{4,3},{1,6},{5,2},{2,5},{6,1},{3,4},{7,0},{8,15},{12,11},{9,... | collective-permute-start | bytes 294920 | tf_op jit(solution)/shard_map/ppermute | solution.py:508
  47.8 14.6 %collective-permute-start.11 = (f32[12,16,128]{2,1,0:T(8,128)S(1)}, f32[12,16,128]{2,1,0:T(8,128)S(1)}, u32[]{:S(2)}, u32[]{:S(2)}) collective-permute-start(f32[12,16,128]{2,1,0:T(8,128)S(1)} %get-tuple-element.43), channel_id=1, source_target_pairs={{0,2},{4,6},{1,3},{5,7},{2,0},{6,4},{3,1},{7,5},{8,10},{12,14},{9,... | collective-permute-start | bytes 294920 | tf_op jit(solution)/shard_map/ppermute | solution.py:508
  51.7 10.7 %collective-permute-start.12 = (f32[12,16,128]{2,1,0:T(8,128)S(1)}, f32[12,16,128]{2,1,0:T(8,128)S(1)}, u32[]{:S(2)}, u32[]{:S(2)}) collective-permute-start(f32[12,16,128]{2,1,0:T(8,128)S(1)} %get-tuple-element.44), channel_id=1, source_target_pairs={{0,3},{4,7},{1,2},{5,6},{2,1},{6,5},{3,0},{7,4},{8,11},{12,15},{9,... | collective-permute-start | bytes 294920 | tf_op jit(solution)/shard_map/ppermute | solution.py:508
  52.1 10.5 %collective-permute-start.13 = (f32[12,16,128]{2,1,0:T(8,128)S(1)}, f32[12,16,128]{2,1,0:T(8,128)S(1)}, u32[]{:S(2)}, u32[]{:S(2)}) collective-permute-start(f32[12,16,128]{2,1,0:T(8,128)S(1)} %get-tuple-element.45), channel_id=1, source_target_pairs={{0,4},{4,0},{1,5},{5,1},{2,6},{6,2},{3,7},{7,3},{8,12},{12,8},{9,1... | collective-permute-start | bytes 294920 | tf_op jit(solution)/shard_map/ppermute | solution.py:508
  62.4 11.2 %collective-permute-start.24 = (f32[2,12,16,128]{3,2,1,0:T(8,128)S(1)}, f32[2,12,16,128]{3,2,1,0:T(8,128)S(1)}, u32[]{:S(2)}, u32[]{:S(2)}) collective-permute-start(f32[2,12,16,128]{3,2,1,0:T(8,128)S(1)} %get-tuple-element.59), channel_id=1, source_target_pairs={{0,1},{4,5},{1,0},{5,4},{2,3},{6,7},{3,2},{7,6},{8,9},{12,13},{9,8... | collective-permute-start | bytes 589832 | tf_op jit(solution)/shard_map/ppermute | solution.py:508
  75.7 44.0 %collective-permute-start.25 = (f32[16,192,128]{2,1,0:T(8,128)S(1)}, f32[16,192,128]{2,1,0:T(8,128)S(1)}, u32[]{:S(2)}, u32[]{:S(2)}) collective-permute-start(f32[16,192,128]{2,1,0:T(8,128)S(1)} %get-tuple-element.61.block), channel_id=1, source_target_pairs={{0,1},{1,0},{2,3},{3,2},{4,5},{5,4},{6,7},{7,6},{8,9},{9,8},{10,11... | collective-permute-start | bytes 4718600 | tf_op jit(solution)/shard_map/ppermute | solution.py:551
  76.6 11.1 %collective-permute-start.26 = (f32[2,2,12,16,128]{4,3,2,1,0:T(8,128)S(1)}, f32[2,2,12,16,128]{4,3,2,1,0:T(8,128)S(1)}, u32[]{:S(2)}, u32[]{:S(2)}) collective-permute-start(f32[2,2,12,16,128]{4,3,2,1,0:T(8,128)S(1)} %get-tuple-element.65), channel_id=1, source_target_pairs={{0,4},{4,0},{1,5},{5,1},{2,6},{6,2},{3,7},{7,3},{8,12},{12,8},{9,1... | collective-permute-start | bytes 1179656 | tf_op jit(solution)/shard_map/ppermute | solution.py:544
  77.4 12.0 %collective-permute-start.27 = (f32[2,2,12,16,128]{4,3,2,1,0:T(8,128)S(1)}, f32[2,2,12,16,128]{4,3,2,1,0:T(8,128)S(1)}, u32[]{:S(2)}, u32[]{:S(2)}) collective-permute-start(f32[2,2,12,16,128]{4,3,2,1,0:T(8,128)S(1)} %get-tuple-element.66), channel_id=1, source_target_pairs={{0,2},{1,3},{2,0},{3,1},{4,6},{5,7},{6,4},{7,5},{8,10},{9,11},{10,... | collective-permute-start | bytes 1179656 | tf_op jit(solution)/shard_map/ppermute | solution.py:545
  78.6 18.4 %collective-permute-start.28 = (f32[2,2,12,16,128]{4,3,2,1,0:T(8,128)S(1)}, f32[2,2,12,16,128]{4,3,2,1,0:T(8,128)S(1)}, u32[]{:S(2)}, u32[]{:S(2)}) collective-permute-start(f32[2,2,12,16,128]{4,3,2,1,0:T(8,128)S(1)} %shard_map.35), channel_id=1, source_target_pairs={{0,2},{1,3},{2,0},{3,1},{4,6},{5,7},{6,4},{7,5},{8,10},{9,11},{10,... | collective-permute-start | bytes 1179656 | tf_op jit(solution)/shard_map/ppermute | solution.py:550
  80.1 39.5 %collective-permute-start.29 = (f32[2,2,12,16,128]{4,3,2,1,0:T(8,128)S(1)}, f32[2,2,12,16,128]{4,3,2,1,0:T(8,128)S(1)}, u32[]{:S(2)}, u32[]{:S(2)}) collective-permute-start(f32[2,2,12,16,128]{4,3,2,1,0:T(8,128)S(1)} %get-tuple-element.64.refs_0_), channel_id=1, source_target_pairs={{0,1},{1,0},{2,3},{3,2},{4,5},{5,4},{6,7},{7,6},{8,9},{9,8},{10,11... | collective-permute-start | bytes 1179656 | tf_op jit(solution)/shard_map/ppermute | solution.py:553
  87.7 31.9 %collective-permute-start.30 = (f32[2,2,12,16,128]{4,3,2,1,0:T(8,128)S(1)}, f32[2,2,12,16,128]{4,3,2,1,0:T(8,128)S(1)}, u32[]{:S(2)}, u32[]{:S(2)}) collective-permute-start(f32[2,2,12,16,128]{4,3,2,1,0:T(8,128)S(1)} %collective-permute-done.26.refs_1_), channel_id=1, source_target_pairs={{0,1},{1,0},{2,3},{3,2},{4,5},{5,4},{6,7},{7,6},{8,9},{9,8},{10,11... | collective-permute-start | bytes 1179656 | tf_op jit(solution)/shard_map/ppermute | solution.py:553
  89.4 30.2 %collective-permute-start.31 = (f32[2,2,12,16,128]{4,3,2,1,0:T(8,128)S(1)}, f32[2,2,12,16,128]{4,3,2,1,0:T(8,128)S(1)}, u32[]{:S(2)}, u32[]{:S(2)}) collective-permute-start(f32[2,2,12,16,128]{4,3,2,1,0:T(8,128)S(1)} %collective-permute-done.27.refs_2_), channel_id=1, source_target_pairs={{0,1},{1,0},{2,3},{3,2},{4,5},{5,4},{6,7},{7,6},{8,9},{9,8},{10,11... | collective-permute-start | bytes 1179656 | tf_op jit(solution)/shard_map/ppermute | solution.py:553
  97.0 22.6 %collective-permute-start.32 = (f32[2,2,12,16,128]{4,3,2,1,0:T(8,128)S(1)}, f32[2,2,12,16,128]{4,3,2,1,0:T(8,128)S(1)}, u32[]{:S(2)}, u32[]{:S(2)}) collective-permute-start(f32[2,2,12,16,128]{4,3,2,1,0:T(8,128)S(1)} %collective-permute-done.28.refs_3_), channel_id=1, source_target_pairs={{0,1},{1,0},{2,3},{3,2},{4,5},{5,4},{6,7},{7,6},{8,9},{9,8},{10,11... | collective-permute-start | bytes 1179656 | tf_op jit(solution)/shard_map/ppermute | solution.py:554
  (11 other events, 142.6 us)
